TPU v7x, 32 devices: a whole 2x2x4 slice. The times are simulated.
32 devices in a mesh: wide: 16 (over z, y, x), narrow: 2 (over core).
Axes of the slice: x: 2, y: 2, z: 4, core: 2. Of those that a mesh axis runs over, the one named last changes fastest.
Arguments:
- tokens: bfloat16 [16384, 1024], P(('wide', 'narrow')), may hold values from -6 to 6
- cotangent: bfloat16 [16384, 1024], P(('wide', 'narrow'))
- pages: int32 [16384], P('wide'), may hold values from 0 to 3, as said below
- boxes: int32 [2, 16384], P(None, 'wide'), may hold values from 0 to 1000, as said below
- gain_attn: bfloat16 [1024], replicated, may hold values from 0.099609375 to 1.8984375
- gain_ffn: bfloat16 [1024], replicated, may hold values from 0.099609375 to 1.8984375
- bias_tables: bfloat16 [96, 16], replicated, may hold values from -4 to 4
- w_query: bfloat16 [1024, 1024], P('wide', 'narrow'), may hold values from -0.046875 to 0.046875
- w_key: bfloat16 [1024, 1024], P('wide', 'narrow'), may hold values from -0.1875 to 0.1875
- w_value: bfloat16 [1024, 1024], P('wide', 'narrow'), may hold values from -0.1875 to 0.1875
- w_out: bfloat16 [1024, 1024], P('narrow', 'wide'), may hold values from -1 to 1
- w_gate: bfloat16 [1024, 2816], P('wide', 'narrow'), may hold values from -0.1875 to 0.1875
- w_up: bfloat16 [1024, 2816], P('wide', 'narrow'), may hold values from -0.1875 to 0.1875
- w_down: bfloat16 [2816, 1024], P('narrow', 'wide'), may hold values from -0.109375 to 0.109375
Outputs:
- output: bfloat16 [16384, 1024], P(('wide', 'narrow'))
- grad_tokens: float32 [16384, 1024], P(('wide', 'narrow'))
- grad_gain_attn: float32 [1024], replicated
- grad_gain_ffn: float32 [1024], replicated
- grad_bias_tables: float32 [96, 16], replicated
- grad_w_query: float32 [1024, 1024], P('wide', 'narrow')
- grad_w_key: float32 [1024, 1024], P('wide', 'narrow')
- grad_w_value: float32 [1024, 1024], P('wide', 'narrow')
- grad_w_out: float32 [1024, 1024], P('narrow', 'wide')
- grad_w_gate: float32 [1024, 2816], P('wide', 'narrow')
- grad_w_up: float32 [1024, 2816], P('wide', 'narrow')
- grad_w_down: float32 [2816, 1024], P('narrow', 'wide')
Inputs may be any that keep to these rules, and one draw needn't show every extreme that they name: Each aligned block of 1024 rows holds one page of up to 1024 rows or two pages of up to 512 rows each, the second starting at row 512 of the block; a value is the page's number within its block, 0 or 1, plus 2 on padding rows. A page has its patch rows first (784 of them for a page of the whole block, 196 otherwise), then text rows ending in an end token, then padding. Some block holds two pages. `boxes`: row 0 is the horizontal and row 1 the vertical centre of a row's box in thousandths of the page: patch rows carry the centre of their grid cell, text rows their word's box, end tokens 1000 and padding 0.
All inputs are finite; a program needn't handle non-finite values.
Results may differ from a plain program's by a relative error of at most 0.018.
Values may be sent and summed in bfloat16 or wider, within the bound.
A program may use at most 256 MiB of HBM per device.

v0:
```python
import jax
import jax.numpy as jnp
from jax import lax
from jax.sharding import PartitionSpec as P

HEADS = 16
HEAD_DIM = 64
BUCKETS = 32
PAGE = 512


epsilon = 1e-06
bucket_edges = (1, 2, 3, 4, 5, 6, 7, 8, 12, 16, 23, 32, 46, 64, 91)
layout_stretch = 4


def bucket_of(spacing, stretch_factor):
    magnitude = jnp.abs(spacing)
    counted = jnp.zeros(spacing.shape, jnp.int32)
    for border in bucket_edges:
        counted = counted + (magnitude >= border * stretch_factor).astype(jnp.int32)
    return counted + BUCKETS // 2 * (spacing > 0).astype(jnp.int32)


def norm_plain(values, gain_row):
    factor = lax.rsqrt(jnp.mean(values * values, axis=-1, keepdims=True) + epsilon)
    return values * factor * gain_row


def gated_unit(gate_pre, up_pre):
    return jax.nn.gelu(gate_pre, approximate=True) * up_pre


def times_transposed(left_side, right_side):
    return lax.dot_general(
        left_side, right_side, (((1,), (1,)), ((), ())), preferred_element_type=jnp.float32
    )


def transposed_times(left_side, right_side):
    return lax.dot_general(
        left_side, right_side, (((0,), (0,)), ((), ())), preferred_element_type=jnp.float32
    )


def layout_hots(row_start, key_start, row_count, key_count, boxes):
    row_ids = row_start + jnp.arange(row_count, dtype=jnp.int32)
    col_ids = key_start + jnp.arange(key_count, dtype=jnp.int32)
    linear_ids = bucket_of(col_ids[None, :] - row_ids[:, None], 1)
    box_query = lax.dynamic_slice_in_dim(boxes, row_start, row_count, 1)
    across = bucket_of(boxes[0][None, :] - box_query[0][:, None], layout_stretch)
    upward = bucket_of(boxes[1][None, :] - box_query[1][:, None], layout_stretch)
    labels = jnp.arange(BUCKETS, dtype=jnp.int32)[:, None, None]
    return jnp.concatenate(
        [linear_ids[None] == labels, across[None] == labels, upward[None] == labels], axis=0
    ).astype(jnp.bfloat16)


def block_bias(row_start, key_start, head_table_entries, boxes):
    sub_rows = min(128, PAGE)
    bias_parts = []
    for piece_id in range(PAGE // sub_rows):
        indicator_rows = layout_hots(
            row_start + piece_id * sub_rows, key_start, sub_rows, 2 * PAGE, boxes
        )
        bias_parts.append(
            jnp.einsum(
                "ai,anf->inf",
                head_table_entries,
                indicator_rows,
                preferred_element_type=jnp.float32,
            )
        )
    return jnp.concatenate(bias_parts, axis=1)


def block_table_grad(grad_scores, row_start, key_start, boxes, summed):
    sub_rows = min(128, PAGE)
    for piece_id in range(PAGE // sub_rows):
        indicator_rows = layout_hots(
            row_start + piece_id * sub_rows, key_start, sub_rows, 2 * PAGE, boxes
        )
        slice_portion = lax.slice_in_dim(
            grad_scores, piece_id * sub_rows, (piece_id + 1) * sub_rows, axis=1
        )
        summed = summed + jnp.einsum(
            "pru,dru->dp", slice_portion, indicator_rows, preferred_element_type=jnp.float32
        )
    return summed


def block_scores(block_id, query_all, key_all, head_table_entries, pages, boxes):
    row_start = block_id * PAGE
    key_start = block_id // 2 * (2 * PAGE)
    query_rows = lax.dynamic_slice_in_dim(query_all, row_start, PAGE, 0)
    scores = jnp.einsum("qhd,khd->hqk", query_rows, key_all, preferred_element_type=jnp.float32)
    scores = scores + block_bias(row_start, key_start, head_table_entries, boxes)
    page_rows = lax.dynamic_slice_in_dim(pages, row_start, PAGE, 0)
    allowed = pages[None, :] == page_rows[:, None] % 2
    return (jnp.where(allowed[None], scores, -1e30), row_start, key_start)


def local(
    tokens,
    cotangent,
    pages,
    boxes,
    gain_attn,
    gain_ffn,
    bias_tables,
    w_query,
    w_key,
    w_value,
    w_out,
    w_gate,
    w_up,
    w_down,
):
    narrow_size = lax.axis_size("narrow")
    heads_local = HEADS // narrow_size
    rows_local = tokens.shape[0]
    rows_wide = rows_local * narrow_size
    block_count = rows_wide // PAGE
    head_start = lax.axis_index("narrow") * heads_local
    head_table_entries = lax.dynamic_slice_in_dim(bias_tables, head_start, heads_local, 1)
    gathered = (
        lax.all_gather(w_query, "wide", axis=0, tiled=True),
        lax.all_gather(w_key, "wide", axis=0, tiled=True),
        lax.all_gather(w_value, "wide", axis=0, tiled=True),
        lax.all_gather(w_out, "wide", axis=1, tiled=True),
        lax.all_gather(w_gate, "wide", axis=0, tiled=True),
        lax.all_gather(w_up, "wide", axis=0, tiled=True),
        lax.all_gather(w_down, "wide", axis=1, tiled=True),
    )
    full_query, full_key, complete_value, full_out, full_gate, full_up, full_down = gathered
    tokens_float = tokens.astype(jnp.float32)
    gain_one = gain_attn.astype(jnp.float32)
    gain_two = gain_ffn.astype(jnp.float32)
    normed = lax.all_gather(
        norm_plain(tokens_float, gain_one).astype(jnp.bfloat16), "narrow", axis=0, tiled=True
    )
    query_all = (
        jnp.dot(normed, full_query, preferred_element_type=jnp.float32)
        .astype(jnp.bfloat16)
        .reshape(rows_wide, heads_local, HEAD_DIM)
    )
    key_all = (
        jnp.dot(normed, full_key, preferred_element_type=jnp.float32)
        .astype(jnp.bfloat16)
        .reshape(rows_wide, heads_local, HEAD_DIM)
    )
    value_all = (
        jnp.dot(normed, complete_value, preferred_element_type=jnp.float32)
        .astype(jnp.bfloat16)
        .reshape(rows_wide, heads_local, HEAD_DIM)
    )

    def forward_block(state_in, block_id):
        masked, row_start, key_start = block_scores(
            block_id, query_all, key_all, head_table_entries, pages, boxes
        )
        row_peak = jnp.max(masked, axis=-1, keepdims=True)
        powered = jnp.exp(masked - row_peak)
        row_total = jnp.sum(powered, axis=-1, keepdims=True)
        weights_low = (powered / row_total).astype(jnp.bfloat16)
        block_out = jnp.einsum(
            "hqk,khd->qhd", weights_low, value_all, preferred_element_type=jnp.float32
        ).astype(jnp.bfloat16)
        return (state_in, (block_out, row_peak + jnp.log(row_total)))

    block_ids = jnp.arange(block_count, dtype=jnp.int32)
    _, (attended_blocks, log_totals) = lax.scan(forward_block, jnp.int32(0), block_ids)
    attended = attended_blocks.reshape(rows_wide, heads_local * HEAD_DIM)
    hidden = tokens_float + lax.psum_scatter(
        jnp.dot(
            lax.slice_in_dim(attended, 0, rows_local * lax.axis_size("narrow"), axis=0),
            full_out,
            preferred_element_type=jnp.float32,
        ).astype(jnp.bfloat16),
        "narrow",
        scatter_dimension=0,
        tiled=True,
    ).astype(jnp.float32)
    normed_two = lax.all_gather(
        norm_plain(hidden, gain_two).astype(jnp.bfloat16), "narrow", axis=0, tiled=True
    )
    gate_pre = jnp.dot(normed_two, full_gate, preferred_element_type=jnp.float32)
    up_pre = jnp.dot(normed_two, full_up, preferred_element_type=jnp.float32)
    hidden_ff = gated_unit(gate_pre, up_pre).astype(jnp.bfloat16)
    output = (
        hidden
        + lax.psum_scatter(
            jnp.dot(
                lax.slice_in_dim(hidden_ff, 0, rows_local * lax.axis_size("narrow"), axis=0),
                full_down,
                preferred_element_type=jnp.float32,
            ).astype(jnp.bfloat16),
            "narrow",
            scatter_dimension=0,
            tiled=True,
        ).astype(jnp.float32)
    ).astype(jnp.bfloat16)
    gathered = (
        lax.all_gather(w_query, "wide", axis=0, tiled=True),
        lax.all_gather(w_key, "wide", axis=0, tiled=True),
        lax.all_gather(w_value, "wide", axis=0, tiled=True),
        lax.all_gather(w_out, "wide", axis=1, tiled=True),
        lax.all_gather(w_gate, "wide", axis=0, tiled=True),
        lax.all_gather(w_up, "wide", axis=0, tiled=True),
        lax.all_gather(w_down, "wide", axis=1, tiled=True),
    )
    full_query, full_key, complete_value, full_out, full_gate, full_up, full_down = gathered
    grad_output = lax.all_gather(cotangent, "narrow", axis=0, tiled=True)
    grad_w_down = transposed_times(hidden_ff, grad_output)
    grad_ff = times_transposed(grad_output, full_down)
    _, gated_pull = jax.vjp(gated_unit, gate_pre, up_pre)
    grad_gate, grad_up = gated_pull(grad_ff)
    grad_gate = grad_gate.astype(jnp.bfloat16)
    grad_up = grad_up.astype(jnp.bfloat16)
    grad_w_gate = transposed_times(normed_two, grad_gate)
    grad_w_up = transposed_times(normed_two, grad_up)
    gate_rows = lax.slice_in_dim(grad_gate, 0, rows_local * lax.axis_size("narrow"), axis=0)
    up_rows = lax.slice_in_dim(grad_up, 0, rows_local * lax.axis_size("narrow"), axis=0)
    grad_normed_two = lax.psum_scatter(
        (times_transposed(gate_rows, full_gate) + times_transposed(up_rows, full_up)).astype(
            jnp.bfloat16
        ),
        "narrow",
        scatter_dimension=0,
        tiled=True,
    ).astype(jnp.float32)
    _, norm_pull_two = jax.vjp(norm_plain, hidden, gain_two)
    grad_hidden_norm, grad_gain_two = norm_pull_two(grad_normed_two)
    grad_hidden = cotangent.astype(jnp.float32) + grad_hidden_norm
    grad_attn = lax.all_gather(grad_hidden.astype(jnp.bfloat16), "narrow", axis=0, tiled=True)
    grad_w_out = transposed_times(attended, grad_attn)
    grad_attended = (
        times_transposed(grad_attn, full_out)
        .astype(jnp.bfloat16)
        .reshape(block_count, PAGE, heads_local, HEAD_DIM)
    )

    def backward_block(state_in, inputs):
        key_grad, value_grad, table_grad = state_in
        block_id, grad_block, log_total = inputs
        masked, row_start, key_start = block_scores(
            block_id, query_all, key_all, head_table_entries, pages, boxes
        )
        probs = jnp.exp(masked - log_total)
        probs_low = probs.astype(jnp.bfloat16)
        query_rows = lax.dynamic_slice_in_dim(query_all, row_start, PAGE, 0)
        grad_probs = jnp.einsum(
            "qhd,khd->hqk", grad_block, value_all, preferred_element_type=jnp.float32
        )
        inner_row_index = jnp.sum(probs * grad_probs, axis=-1, keepdims=True)
        grad_scores = (probs * (grad_probs - inner_row_index)).astype(jnp.bfloat16)
        grad_query_block = jnp.einsum(
            "hqk,khd->qhd", grad_scores, key_all, preferred_element_type=jnp.float32
        ).astype(jnp.bfloat16)
        key_part = jnp.einsum(
            "hqk,qhd->khd", grad_scores, query_rows, preferred_element_type=jnp.float32
        )
        value_part = jnp.einsum(
            "hqk,qhd->khd", probs_low, grad_block, preferred_element_type=jnp.float32
        )
        key_grad = lax.dynamic_update_slice_in_dim(key_grad, key_grad + key_part, key_start, 0)
        value_grad = lax.dynamic_update_slice_in_dim(
            value_grad, value_grad + value_part, key_start, 0
        )
        table_grad = block_table_grad(grad_scores, row_start, key_start, boxes, table_grad)
        return ((key_grad, value_grad, table_grad), grad_query_block)

    empty_rows = jnp.zeros((rows_wide, heads_local, HEAD_DIM), jnp.float32)
    empty_table = jnp.zeros((3 * BUCKETS, heads_local), jnp.float32)
    (key_grad, value_grad, table_grad), query_blocks = lax.scan(
        backward_block,
        (empty_rows, empty_rows, empty_table),
        (block_ids, grad_attended, log_totals),
    )
    grad_queries = query_blocks.reshape(rows_wide, heads_local * HEAD_DIM)
    grad_keys = key_grad.astype(jnp.bfloat16).reshape(rows_wide, heads_local * HEAD_DIM)
    grad_values = value_grad.astype(jnp.bfloat16).reshape(rows_wide, heads_local * HEAD_DIM)
    grad_w_query = transposed_times(normed, grad_queries)
    grad_w_key = transposed_times(normed, grad_keys)
    grad_w_value = transposed_times(normed, grad_values)
    query_part = times_transposed(
        lax.slice_in_dim(grad_queries, 0, rows_local * lax.axis_size("narrow"), axis=0), full_query
    )
    key_side = times_transposed(grad_keys, full_key)
    value_side = times_transposed(grad_values, complete_value)
    grad_normed = lax.psum_scatter(
        (query_part + key_side + value_side).astype(jnp.bfloat16),
        "narrow",
        scatter_dimension=0,
        tiled=True,
    ).astype(jnp.float32)
    _, norm_pull_one = jax.vjp(norm_plain, tokens_float, gain_one)
    grad_tokens_norm, grad_gain_one = norm_pull_one(grad_normed)
    grad_tokens = grad_hidden + grad_tokens_norm
    table_full = lax.dynamic_update_slice(
        jnp.zeros((3 * BUCKETS, HEADS), jnp.float32), table_grad, (jnp.int32(0), head_start)
    )
    grad_gain_attn, grad_gain_ffn, grad_bias_tables = lax.psum(
        (grad_gain_one, grad_gain_two, table_full), ("wide", "narrow")
    )
    all_parts = (
        lax.psum_scatter(grad_w_query, "wide", scatter_dimension=0, tiled=True),
        lax.psum_scatter(grad_w_key, "wide", scatter_dimension=0, tiled=True),
        lax.psum_scatter(grad_w_value, "wide", scatter_dimension=0, tiled=True),
        lax.psum_scatter(grad_w_out, "wide", scatter_dimension=1, tiled=True),
        lax.psum_scatter(grad_w_gate, "wide", scatter_dimension=0, tiled=True),
        lax.psum_scatter(grad_w_up, "wide", scatter_dimension=0, tiled=True),
        lax.psum_scatter(grad_w_down, "wide", scatter_dimension=1, tiled=True),
    )
    shard_query, shard_key, shard_value, shard_out, shard_gate, shard_up, shard_down = all_parts
    return (
        output,
        grad_tokens,
        grad_gain_attn,
        grad_gain_ffn,
        grad_bias_tables,
        shard_query,
        shard_key,
        shard_value,
        shard_out,
        shard_gate,
        shard_up,
        shard_down,
    )


def solution(mesh):
    in_specs = (
        P(("wide", "narrow"), None),
        P(("wide", "narrow"), None),
        P("wide"),
        P(None, "wide"),
        P(),
        P(),
        P(),
        P("wide", "narrow"),
        P("wide", "narrow"),
        P("wide", "narrow"),
        P("narrow", "wide"),
        P("wide", "narrow"),
        P("wide", "narrow"),
        P("narrow", "wide"),
    )
    out_specs = (
        P(("wide", "narrow"), None),
        P(("wide", "narrow"), None),
        P(),
        P(),
        P(),
        P("wide", "narrow"),
        P("wide", "narrow"),
        P("wide", "narrow"),
        P("narrow", "wide"),
        P("wide", "narrow"),
        P("wide", "narrow"),
        P("narrow", "wide"),
    )
    return jax.shard_map(local, mesh=mesh, in_specs=in_specs, out_specs=out_specs, check_vma=False)
```

profile of v0, /device:TPU:0, one launch (start us, length us, event | category | flops | bytes accessed | tf_op | source)
XLA Modules:
  0.0 1945.9 jit_solution(11280851467745284290)
XLA Ops:
  15.8 53.0 %all-gather.18.cloned.1.call-done = bf16[1024,512]{1,0:T(8,128)(2,1)} async-done(((bf16[64,512]{1,0:T(8,128)(2,1)}), bf16[1024,512]{1,0:T(8,128)(2,1)}) %all-gather.18.cloned.1.call-update) | async-done | bytes 1048592 | tf_op jit(solution)/shard_map/all_gather | solution.py:129
  68.8 11.5 all-gather.12.cloned.1.call-done
  84.6 55.0 %all-gather.16.cloned.1.call-done = bf16[1024,512]{1,0:T(8,128)(2,1)} async-done(((bf16[64,512]{1,0:T(8,128)(2,1)}), bf16[1024,512]{1,0:T(8,128)(2,1)}) %all-gather.16.cloned.1.call-update) | async-done | bytes 1048592 | tf_op jit(solution)/shard_map/all_gather | solution.py:128
  143.1 53.2 %all-gather.14.cloned.1.call-done = bf16[1024,512]{1,0:T(8,128)(2,1)} async-done(((bf16[64,512]{1,0:T(8,128)(2,1)}), bf16[1024,512]{1,0:T(8,128)(2,1)}) %all-gather.14.cloned.1.call-update) | async-done | bytes 1048592 | tf_op jit(solution)/shard_map/all_gather | solution.py:127
  200.9 261.4 %while.33 = (s32[]{:T(128)}, bf16[2,512,8,64]{1,3,2,0:T(8,128)(2,1)}, f32[2,8,512,1]{2,1,3,0:T(8,128)}, s32[1024]{0:T(1024)S(1)}, s32[2]{0:T(128)S(1)}, /*index=...) while((s32[]{:T(128)}, ...), condition=%wide.region_4.5_spmd, body=%wide.region_1.4_spmd.sunk | while | flops 2154040320 | bytes 268903200 | solution.py:172
  249.3 10.0 fusion.580
  259.3 9.4 fusion.579
  377.5 10.0 fusion.580
  387.5 9.6 fusion.579
  484.3 63.8 %all-gather.26.cloned.1.call-done = bf16[1024,1408]{1,0:T(8,128)(2,1)} async-done(((bf16[64,1408]{1,0:T(8,128)(2,1)}), bf16[1024,1408]{1,0:T(8,128)(2,1)}) %all-gather.26.cloned.1.call-update) | async-done | bytes 2883600 | tf_op jit(solution)/shard_map/all_gather | solution.py:132
  548.1 11.9 all-gather.22.cloned.1.call-done
  568.4 61.7 %all-gather.24.cloned.1.call-done = bf16[1024,1408]{1,0:T(8,128)(2,1)} async-done(((bf16[64,1408]{1,0:T(8,128)(2,1)}), bf16[1024,1408]{1,0:T(8,128)(2,1)}) %all-gather.24.cloned.1.call-update) | async-done | bytes 2883600 | tf_op jit(solution)/shard_map/all_gather | solution.py:131
  641.3 70.2 %all-gather.28.cloned.1.call-done = bf16[1408,1024]{0,1:T(8,128)(2,1)} async-done(((bf16[1408,64]{0,1:T(8,128)(2,1)}), bf16[1408,1024]{0,1:T(8,128)(2,1)}) %all-gather.28.cloned.1.call-update) | async-done | bytes 2883600 | tf_op jit(solution)/shard_map/all_gather | solution.py:133
  711.5 13.1 multiply_convert_fusion.1
  747.9 11.8 all-gather.32.cloned.1.call-done
  767.3 425.1 %while.34 = (s32[]{:T(128)}, f32[1024,8,64]{0,2,1:T(8,128)}, f32[1024,8,64]{0,2,1:T(8,128)}, f32[96,8]{0,1:T(8,128)}, bf16[2,512,8,64]{1,3,2,0:T(8,128)(2,1)}, /...) while((s32[]{:T(128)}, f32[1024,8,64]{0,2,1:T(8,128)}, ...), condition=%wide.region_12.13_spmd.clone, body=%wide.region_10.12_spmd.clone.sunk | while | flops 4676918272 | bytes 713860288 | solution.py:275
  815.8 9.2 fusion.605
  885.2 18.8 multiply_reduce_fusion.3
  904.1 11.3 multiply_convert_fusion.5
  956.5 9.1 fusion.610
  1023.8 9.2 fusion.605
  1093.4 18.8 multiply_reduce_fusion.3
  1112.2 11.3 multiply_convert_fusion.5
  1123.6 9.4 bitcast_add_fusion.5
  1165.3 9.1 fusion.610
  1257.5 42.1 %all-reduce = (f32[1024]{0:T(1024)}, f32[1024]{0:T(1024)}, f32[96,16]{0,1:T(8,128)}) all-reduce(f32[1024]{0:T(1024)S(1)} %get-tuple-element.407, f32[1024]{0:T(1024)S(1)} %copy-done.65, f32[96,16]{0,1:T(8,128)S(1)} %constant_dynamic-update-slice_fusion), channel_id=1, replica_groups=mesh['wide'=16,'narrow'=2] {'wide','narrow'}, use_global_device_ids=true, to_apply=%region_16.17 | all-reduce | flops 3584 | bytes 28672 | tf_op jit(solution)/shard_map/psum | solution.py:303
  1311.2 80.4 %reduce-scatter.24.cloned.1.call-done = f32[64,512]{1,0:T(8,128)} async-done(((f32[1024,512]{1,0:T(8,128)}), f32[64,512]{1,0:T(8,128)}) %reduce-scatter.24.cloned.1.call-update) | async-done | bytes 131088 | tf_op jit(solution)/shard_map/reduce_scatter | solution.py:309
  1391.7 80.7 %reduce-scatter.20.cloned.1.call-done = f32[64,512]{1,0:T(8,128)} async-done(((f32[1024,512]{1,0:T(8,128)}), f32[64,512]{1,0:T(8,128)}) %reduce-scatter.20.cloned.1.call-update) | async-done | bytes 131088 | tf_op jit(solution)/shard_map/reduce_scatter | solution.py:307
  1472.4 80.8 %reduce-scatter.22.cloned.1.call-done = f32[64,512]{1,0:T(8,128)} async-done(((f32[1024,512]{1,0:T(8,128)}), f32[64,512]{1,0:T(8,128)}) %reduce-scatter.22.cloned.1.call-update) | async-done | bytes 131088 | tf_op jit(solution)/shard_map/reduce_scatter | solution.py:308
  1553.2 125.8 %reduce-scatter.30.cloned.1.call-done = f32[64,1408]{1,0:T(8,128)} async-done(((f32[1024,1408]{1,0:T(8,128)}), f32[64,1408]{1,0:T(8,128)}) %reduce-scatter.30.cloned.1.call-update) | async-done | bytes 360464 | tf_op jit(solution)/shard_map/reduce_scatter | solution.py:312
  1679.0 129.9 %reduce-scatter.28.cloned.1.call-done = f32[64,1408]{1,0:T(8,128)} async-done(((f32[1024,1408]{1,0:T(8,128)}), f32[64,1408]{1,0:T(8,128)}) %reduce-scatter.28.cloned.1.call-update) | async-done | bytes 360464 | tf_op jit(solution)/shard_map/reduce_scatter | solution.py:311
  1808.9 129.9 %reduce-scatter.32.cloned.1.call-done = f32[1408,64]{0,1:T(8,128)} async-done(((f32[1408,1024]{0,1:T(8,128)}), f32[1408,64]{0,1:T(8,128)}) %reduce-scatter.32.cloned.1.call-update) | async-done | bytes 360464 | tf_op jit(solution)/shard_map/reduce_scatter | solution.py:313
  (501 shorter events, 681.6 us)
Async XLA Ops:
  7.2 61.6 %all-gather.18.cloned.1.call-start = ((), (), s32[]{:S(2)}) async-start(), calls=%async_computation.14 | async-start | bytes 1114112 | tf_op jit(solution)/shard_map/all_gather | solution.py:129
  7.9 72.4 %all-gather.12.cloned.1.call-start = ((), (), s32[]{:S(2)}) async-start(), calls=%async_computation.11 | async-start | bytes 3145728 | tf_op jit(solution)/shard_map/all_gather | solution.py:139
  13.8 125.8 %all-gather.16.cloned.1.call-start = ((), (), s32[]{:S(2)}) async-start(), calls=%async_computation.13 | async-start | bytes 1114112 | tf_op jit(solution)/shard_map/all_gather | solution.py:128
  14.6 181.7 %all-gather.14.cloned.1.call-start = ((), (), s32[]{:S(2)}) async-start(), calls=%async_computation.12 | async-start | bytes 1114112 | tf_op jit(solution)/shard_map/all_gather | solution.py:127
  15.1 449.8 %all-gather.20.cloned.1.call-start = ((), (), s32[]{:S(2)}) async-start(), calls=%async_computation.15 | async-start | bytes 1114112 | tf_op jit(solution)/shard_map/all_gather | solution.py:130
  15.7 462.1 %reduce-scatter.12.cloned.1.call-start = ((), (), s32[]{:S(2)}) async-start(), calls=%async_computation.16 | async-start | bytes 3145728 | tf_op jit(solution)/shard_map/reduce_scatter | solution.py:174
  80.3 59.2 %copy-start.72 = (bf16[1024,1024]{1,0:T(8,128)(2,1)S(1)}, bf16[1024,1024]{1,0:T(8,128)(2,1)}, u32[]{:S(2)}) copy-start(bf16[1024,1024]{1,0:T(8,128)(2,1)} %all-gather.12.cloned.1.call-done) | copy-start | bytes 6291460
  143.1 57.8 %copy-start.40 = (s32[2,1024]{1,0:T(2,128)S(1)}, s32[2,1024]{1,0:T(2,128)}, u32[]{:S(2)}) copy-start(s32[2,1024]{1,0:T(2,128)} %param.21) | copy-start | bytes 24580
  143.1 57.8 %copy-start.48 = (s32[1024]{0:T(1024)S(1)}, s32[1024]{0:T(1024)}, u32[]{:S(2)}) copy-start(s32[1024]{0:T(1024)} %param.20) | copy-start | bytes 12292
  469.3 78.8 %all-gather.26.cloned.1.call-start = ((), (), s32[]{:S(2)}) async-start(), calls=%async_computation.19 | async-start | bytes 3063808 | tf_op jit(solution)/shard_map/all_gather | solution.py:132
  470.0 89.9 %all-gather.22.cloned.1.call-start = ((), (), s32[]{:S(2)}) async-start(), calls=%async_computation.17 | async-start | bytes 3145728 | tf_op jit(solution)/shard_map/all_gather | solution.py:184
  470.1 274.7 %copy-start.53 = (f32[1024]{0:T(1024)}, f32[1024]{0:T(1024)S(1)}, u32[]{:S(2)}) copy-start(f32[1024]{0:T(1024)S(1)} %convert_element_type.3947) | copy-start | bytes 12292
  479.5 265.3 %copy-start.57 = (f32[512]{0:T(512)}, f32[512]{0:T(512)S(1)}, u32[]{:S(2)}) copy-start(f32[512]{0:T(512)S(1)} %fusion.462) | copy-start | bytes 6148
  482.2 148.0 %all-gather.24.cloned.1.call-start = ((), (), s32[]{:S(2)}) async-start(), calls=%async_computation.18 | async-start | bytes 3063808 | tf_op jit(solution)/shard_map/all_gather | solution.py:131
  482.9 158.4 %all-gather.30.cloned.1.call-start = ((), (), s32[]{:S(2)}) async-start(), calls=%async_computation.22 | async-start | bytes 3145728 | tf_op jit(solution)/shard_map/all_gather | solution.py:213
  483.5 228.0 %all-gather.28.cloned.1.call-start = ((), (), s32[]{:S(2)}) async-start(), calls=%async_computation.20 | async-start | bytes 3063808 | tf_op jit(solution)/shard_map/all_gather | solution.py:133
  484.2 257.8 %reduce-scatter.16.cloned.1.call-start = ((), (), s32[]{:S(2)}) async-start(), calls=%async_computation.23 | async-start | bytes 3145728 | tf_op jit(solution)/shard_map/reduce_scatter | solution.py:224
  559.9 70.2 %copy-start.73 = (bf16[1024,1024]{1,0:T(8,128)(2,1)S(1)}, bf16[1024,1024]{1,0:T(8,128)(2,1)}, u32[]{:S(2)}) copy-start(bf16[1024,1024]{1,0:T(8,128)(2,1)} %all-gather.22.cloned.1.call-done) | copy-start | bytes 6291460
  733.2 26.6 %all-gather.32.cloned.1.call-start = ((), (), s32[]{:S(2)}) async-start(), calls=%async_computation.24 | async-start | bytes 3145728 | tf_op jit(solution)/shard_map/all_gather | solution.py:235
  747.8 506.9 %reduce-scatter.18.cloned.1.call-start = ((), (), s32[]{:S(2)}) async-start(), calls=%async_computation.25 | async-start | bytes 3145728 | tf_op jit(solution)/shard_map/reduce_scatter | solution.py:291
  1202.7 97.0 %reduce-scatter.14.cloned.1.call-start = ((), (), s32[]{:S(2)}) async-start(), calls=%async_computation.21 | async-start | bytes 3145728 | tf_op jit(solution)/shard_map/reduce_scatter | solution.py:192
  1210.3 100.9 %reduce-scatter.26.cloned.1.call-start = ((), (), s32[]{:S(2)}) async-start(), calls=%async_computation.29 | async-start | bytes 2228224 | tf_op jit(solution)/shard_map/reduce_scatter | solution.py:310
  1214.7 177.0 %reduce-scatter.24.cloned.1.call-start = ((), (), s32[]{:S(2)}) async-start(), calls=%async_computation.28 | async-start | bytes 2228224 | tf_op jit(solution)/shard_map/reduce_scatter | solution.py:309
  1219.1 253.3 %reduce-scatter.20.cloned.1.call-start = ((), (), s32[]{:S(2)}) async-start(), calls=%async_computation.26 | async-start | bytes 2228224 | tf_op jit(solution)/shard_map/reduce_scatter | solution.py:307
  1223.5 329.7 %reduce-scatter.22.cloned.1.call-start = ((), (), s32[]{:S(2)}) async-start(), calls=%async_computation.27 | async-start | bytes 2228224 | tf_op jit(solution)/shard_map/reduce_scatter | solution.py:308
  1228.1 450.9 %reduce-scatter.30.cloned.1.call-start = ((), (), s32[]{:S(2)}) async-start(), calls=%async_computation.31 | async-start | bytes 6127616 | tf_op jit(solution)/shard_map/reduce_scatter | solution.py:312
  1236.6 572.3 %reduce-scatter.28.cloned.1.call-start = ((), (), s32[]{:S(2)}) async-start(), calls=%async_computation.30 | async-start | bytes 6127616 | tf_op jit(solution)/shard_map/reduce_scatter | solution.py:311
  1245.4 693.5 %reduce-scatter.32.cloned.1.call-start = ((), (), s32[]{:S(2)}) async-start(), calls=%async_computation.32 | async-start | bytes 6127616 | tf_op jit(solution)/shard_map/reduce_scatter | solution.py:313
  1254.1 45.6 %copy-start.34 = (bf16[512,1024]{1,0:T(8,128)(2,1)S(1)}, bf16[512,1024]{1,0:T(8,128)(2,1)}, u32[]{:S(2)}) copy-start(bf16[512,1024]{1,0:T(8,128)(2,1)} %reduce-scatter.12.cloned.1.call-done) | copy-start | bytes 3145732
  1254.1 45.6 %copy-start.37 = (bf16[512,1024]{1,0:T(8,128)(2,1)S(1)}, bf16[512,1024]{1,0:T(8,128)(2,1)}, u32[]{:S(2)}) copy-start(bf16[512,1024]{1,0:T(8,128)(2,1)} %param.19) | copy-start | bytes 3145732
  1254.1 45.6 %copy-start.54 = (f32[1024]{0:T(1024)S(1)}, f32[1024]{0:T(1024)}, u32[]{:S(2)}) copy-start(f32[1024]{0:T(1024)} %copy-done.53) | copy-start | bytes 12292
  1299.7 639.1 %copy-start.1 = (bf16[96,16]{0,1:T(8,128)(2,1)S(1)}, bf16[96,16]{0,1:T(8,128)(2,1)}, u32[]{:S(2)}) copy-start(bf16[96,16]{0,1:T(8,128)(2,1)} %param.24) | copy-start | bytes 9220
  (113 other events, 1015.7 us)
Sparse Core Ops, SparseCore 0:
  10.8 57.9 all-gather.17
  70.9 9.3 all-gather.11
  83.1 56.4 all-gather.15
  142.2 54.0 all-gather.13
  198.9 54.0 all-gather.19
  469.4 8.3 reduce-scatter.11
  481.0 67.0 all-gather.25
  550.3 9.6 all-gather.21
  563.1 67.0 all-gather.23
  631.6 9.6 all-gather.29
  644.4 67.0 all-gather.27
  733.3 8.6 reduce-scatter.15
  748.0 11.7 all-gather.31
  1202.8 10.7 reduce-scatter.17
  1215.8 10.8 reduce-scatter.13
  1229.3 81.8 reduce-scatter.25
  1313.9 77.7 reduce-scatter.23
  1394.4 77.9 reduce-scatter.19
  1475.2 77.9 reduce-scatter.21
  1556.0 123.0 reduce-scatter.29
  1681.9 126.9 reduce-scatter.27
  1811.8 126.9 reduce-scatter.31
where the time goes:
time: 1950 us
  waiting for transfers between devices  1050 us (54%)
  matrix products  432 us (22%)
  other arithmetic  253 us (13%)
  local copies, waits for them, and re-layouts  121 us (6%)
  blocking collectives  42.1 us (2%)
  loops' own time  28.9 us (1%)
    dot_general x16, matrix products, block_bias(): jnp.einsum('ai,anf->inf', head_table_entries, indicator_rows, preferred_e...  139 us
    reduce_scatter x1, waiting for transfers between devices, local(): lax.psum_scatter(grad_w_down, 'wide', scatter_dimension=1, tiled=True)  130 us
    reduce_scatter x1, waiting for transfers between devices, local(): lax.psum_scatter(grad_w_gate, 'wide', scatter_dimension=0, tiled=True)  130 us
    reduce_scatter x1, waiting for transfers between devices, local(): lax.psum_scatter(grad_w_up, 'wide', scatter_dimension=0, tiled=True)  126 us
    dot_general x16, local copies, waits for them, and re-layouts, block_bias(): jnp.einsum('ai,anf->inf', head_table_entries, indicator_rows, preferred_e...  81.3 us
    reduce_scatter x1, waiting for transfers between devices, local(): lax.psum_scatter(grad_w_key, 'wide', scatter_dimension=0, tiled=True)  80.8 us
    reduce_scatter x1, waiting for transfers between devices, local(): lax.psum_scatter(grad_w_query, 'wide', scatter_dimension=0, tiled=True)  80.7 us
    reduce_scatter x1, waiting for transfers between devices, local(): lax.psum_scatter(grad_w_value, 'wide', scatter_dimension=0, tiled=True)  80.4 us
  transfers between devices with their start and end apart: 22, of which 19 were waited for; matrix products, arithmetic and copies ran while one was open for 17% of the time, Pallas kernels for 0%

commit v1 on v0

v1 whole, which is shorter than its diff:
```python
import functools

import jax
import jax.numpy as jnp
from jax import lax
from jax.experimental import pallas as pl
from jax.experimental.pallas import tpu as pltpu
from jax.sharding import PartitionSpec as P

f32, bf16 = jnp.float32, jnp.bfloat16
MESH = pl.DeviceIdType.MESH


EDGES = (1, 2, 3, 4, 5, 6, 7, 8, 12, 16, 23, 32, 46, 64, 91)
NT = (((1,), (1,)), ((), ()))
VM = 56 * 2**20

def lane_take(table, idx):
    return jnp.take_along_axis(table, idx, axis=1, mode="promise_in_bounds")

def bias_kernel(heads, rows, n, steps_ref, tab_ref, box_col, box_row, page_col, page_row, bias_ref, ids_ref):
    start = pl.program_id(0) * rows
    steps = jnp.broadcast_to(steps_ref[...], (rows, 128))
    allowed_col = jnp.broadcast_to(page_col[...] % 2, (rows, 128))
    cols = [jnp.broadcast_to(box_col[:, t:t + 1], (rows, 128)) for t in range(2)]
    own = lax.broadcasted_iota(jnp.int32, (rows, 128), 0) + start
    for c in range(n // 128):
        lanes = pl.ds(c * 128, 128)
        lane_id = lax.broadcasted_iota(jnp.int32, (rows, 128), 1) + c * 128
        ids = []
        for t in range(3):
            gap = (lane_id - own) if t == 0 else (jnp.broadcast_to(box_row[t - 1:t, lanes], (rows, 128)) - cols[t - 1])
            size = jnp.abs(gap)
            if t > 0:
                size = size >> 2
            bucket = lane_take(steps, jnp.minimum(size, 91)) + jnp.where(gap > 0, 16, 0)
            ids.append(bucket)
            ids_ref[t, :, lanes] = bucket.astype(ids_ref.dtype)
        ok = jnp.broadcast_to(page_row[:, lanes], (rows, 128)) == allowed_col
        for h in range(heads):
            total = None
            for t in range(3):
                table = jnp.broadcast_to(tab_ref[t * heads + h:t * heads + h + 1, :], (rows, 128))
                part = lane_take(table, ids[t])
                total = part if total is None else total + part
            bias_ref[h, :, lanes] = jnp.where(ok, total, -1e30)

def make_bias(tables, boxes, pages, ids_dtype=f32):
    heads = tables.shape[1]
    n = pages.shape[0]
    rows = 64
    tab = jnp.pad(tables.astype(f32).reshape(3, 32, heads).transpose(0, 2, 1).reshape(3 * heads, 32), ((0, 0), (0, 96)))
    lane = jnp.arange(128, dtype=jnp.int32)
    steps = sum([(lane >= e).astype(jnp.int32) for e in EDGES])[None]
    return pl.pallas_call(functools.partial(bias_kernel, heads, rows, n),
        grid=(n // rows,),
        out_shape=(jax.ShapeDtypeStruct((heads, n, n), f32), jax.ShapeDtypeStruct((3, n, n), ids_dtype)),
        in_specs=[pl.BlockSpec((1, 128), lambda i: (0, 0)), pl.BlockSpec((3 * heads, 128), lambda i: (0, 0)),
                  pl.BlockSpec((rows, 2), lambda i: (i, 0)), pl.BlockSpec((2, n), lambda i: (0, 0)),
                  pl.BlockSpec((rows, 1), lambda i: (i, 0)), pl.BlockSpec((1, n), lambda i: (0, 0))],
        out_specs=(pl.BlockSpec((heads, rows, n), lambda i: (0, i, 0)), pl.BlockSpec((3, rows, n), lambda i: (0, i, 0))),
        compiler_params=pltpu.CompilerParams(vmem_limit_bytes=VM), name="layout_bias")(steps, tab, boxes.T, boxes, pages[:, None], pages[None])

def half_of(v, e):
    lane = lax.broadcasted_iota(jnp.int32, v.shape, 1)
    return jnp.where((lane >= 64) == (e == 1), v, jnp.zeros_like(v))

def join(a, b):
    lane = lax.broadcasted_iota(jnp.int32, a.shape, 1)
    return jnp.where(lane < 64, a, b)

def fwd_kernel(q_ref, k_ref, v_ref, bias_ref, o_ref, lse_ref):
    q, k, v = q_ref[...], k_ref[...], v_ref[...]
    outs, lses = [], []
    for e in range(2):
        s = lax.dot_general(half_of(q, e), k, NT, preferred_element_type=f32) + bias_ref[e]
        peak = jnp.max(s, axis=1, keepdims=True)
        p = jnp.exp(s - peak)
        total = jnp.sum(p, axis=1, keepdims=True)
        outs.append(jnp.dot(p.astype(bf16), v, preferred_element_type=f32) / total)
        lses.append(peak + jnp.log(total))
    o_ref[...] = join(*outs).astype(bf16)
    lse_ref[0] = jnp.concatenate(lses, axis=1)

def attn_fwd(qkv, bias, tq=256):
    n, width = qkv.shape[0], qkv.shape[1] // 3
    pairs = width // 128
    return pl.pallas_call(fwd_kernel, grid=(pairs, n // tq),
        out_shape=(jax.ShapeDtypeStruct((n, width), bf16), jax.ShapeDtypeStruct((pairs, n, 2), f32)),
        in_specs=[pl.BlockSpec((tq, 128), lambda p, i: (i, p)), pl.BlockSpec((n, 128), lambda p, i: (0, p + pairs)),
                  pl.BlockSpec((n, 128), lambda p, i: (0, p + 2 * pairs)), pl.BlockSpec((2, tq, n), lambda p, i: (p, i, 0))],
        out_specs=(pl.BlockSpec((tq, 128), lambda p, i: (i, p)), pl.BlockSpec((1, tq, 2), lambda p, i: (p, i, 0))),
        compiler_params=pltpu.CompilerParams(vmem_limit_bytes=VM), name="attention")(qkv, qkv, qkv, bias)

def bwd_kernel(q_ref, k_ref, v_ref, bias_ref, o_ref, do_ref, lse_ref, dq_ref, dk_ref, dv_ref, g_ref, dkt, dvt):
    i = pl.program_id(1)
    @pl.when(i == 0)
    def _():
        dkt[...] = jnp.zeros_like(dkt)
        dvt[...] = jnp.zeros_like(dvt)
    q, k, v, do = q_ref[...], k_ref[...], v_ref[...], do_ref[...]
    prod = do.astype(f32) * o_ref[...].astype(f32)
    dqs = []
    for e in range(2):
        qm, dom = half_of(q, e), half_of(do, e)
        s = lax.dot_general(qm, k, NT, preferred_element_type=f32) + bias_ref[e]
        p = jnp.exp(s - lse_ref[0, :, e:e + 1])
        dp = lax.dot_general(dom, v, NT, preferred_element_type=f32)
        inner = jnp.sum(half_of(prod, e), axis=1, keepdims=True)
        g = (p * (dp - inner)).astype(bf16)
        g_ref[e] = g
        dqs.append(jnp.dot(g, k, preferred_element_type=f32))
        dvt[...] += jnp.dot(dom.T, p.astype(bf16), preferred_element_type=f32)
        dkt[...] += jnp.dot(qm.T, g, preferred_element_type=f32)
    dq_ref[...] = join(*dqs).astype(bf16)
    @pl.when(i == pl.num_programs(1) - 1)
    def _():
        dk_ref[...] = dkt[...].T.astype(bf16)
        dv_ref[...] = dvt[...].T.astype(bf16)

def attn_bwd(qkv, bias, o, do, lse, tq=256):
    n, width = qkv.shape[0], qkv.shape[1] // 3
    pairs = width // 128
    tile = pl.BlockSpec((tq, 128), lambda p, i: (i, p))
    full = pl.BlockSpec((n, 128), lambda p, i: (0, p))
    return pl.pallas_call(bwd_kernel, grid=(pairs, n // tq),
        out_shape=(jax.ShapeDtypeStruct((n, width), bf16),) * 3 + (jax.ShapeDtypeStruct((2 * pairs, n, n), bf16),),
        in_specs=[tile, pl.BlockSpec((n, 128), lambda p, i: (0, p + pairs)), pl.BlockSpec((n, 128), lambda p, i: (0, p + 2 * pairs)), pl.BlockSpec((2, tq, n), lambda p, i: (p, i, 0)), tile, tile,
                  pl.BlockSpec((1, tq, 2), lambda p, i: (p, i, 0))],
        out_specs=(tile, full, full, pl.BlockSpec((2, tq, n), lambda p, i: (p, i, 0))),
        scratch_shapes=[pltpu.VMEM((128, n), f32), pltpu.VMEM((128, n), f32)],
        compiler_params=pltpu.CompilerParams(vmem_limit_bytes=VM), name="attention_back")(qkv, qkv, qkv, bias, o, do, lse)

def hist_kernel(heads, rows, n, g_ref, ids_ref, out_ref, gs):
    @pl.when(pl.program_id(0) == 0)
    def _():
        out_ref[...] = jnp.zeros_like(out_ref)
    for h in range(heads):
        for c in range(n // 128):
            gs[c, h * rows:(h + 1) * rows, :] = g_ref[h, :, c * 128:(c + 1) * 128].astype(f32)
    label = lax.broadcasted_iota(jnp.int32, (32, n), 0).astype(bf16)
    one, zero = jnp.ones((32, n), bf16), jnp.zeros((32, n), bf16)
    acc = jnp.zeros((heads, 96), f32)
    for r in range(rows):
        grow = jnp.concatenate([gs[c, pl.ds(r, heads, stride=rows), :] for c in range(n // 128)], axis=1).astype(bf16)
        hots = []
        for t in range(3):
            row = jnp.broadcast_to(ids_ref[t, r:r + 1, :], (32, n)).astype(bf16)
            hots.append(jnp.where(row == label, one, zero))
        acc = acc + lax.dot_general(grow, jnp.concatenate(hots, axis=0), NT, preferred_element_type=f32)
    out_ref[...] += acc

def table_hist(g, ids):
    heads, n, _ = g.shape
    rows = 16
    return pl.pallas_call(functools.partial(hist_kernel, heads, rows, n), grid=(n // rows,),
        out_shape=jax.ShapeDtypeStruct((heads, 96), f32),
        in_specs=[pl.BlockSpec((heads, rows, n), lambda i: (0, i, 0)), pl.BlockSpec((3, rows, n), lambda i: (0, i, 0))],
        out_specs=pl.BlockSpec((heads, 96), lambda i: (0, 0)),
        scratch_shapes=[pltpu.VMEM((n // 128, heads * rows, 128), f32)],
        compiler_params=pltpu.CompilerParams(vmem_limit_bytes=VM), name="table_grad")(g, ids)


def place():
    me = lax.axis_index("wide")
    return me // 4, (me // 2) % 2, me % 2

def wide_id(z, y, x):
    return {"wide": z * 4 + y * 2 + x}

def remote(src, dst, send, recv, target):
    return pltpu.make_async_remote_copy(src_ref=src, dst_ref=dst, send_sem=send, recv_sem=recv, device_id=target, device_id_type=MESH)

def greet(G, far):
    z, y, x = place()
    bar = pltpu.get_barrier_semaphore()
    sig = lambda t: pl.semaphore_signal(bar, inc=1, device_id=t, device_id_type=MESH)
    sig(wide_id(z, 1 - y, x)); sig(wide_id(z, y, 1 - x))
    if far:
        for k in range(1, G):
            sig(wide_id((z + k) % G, y, x))
        pl.semaphore_wait(bar, 2 + G - 1)
    else:
        @pl.when(z > 0)
        def _(): sig(wide_id(z - 1, y, x))
        @pl.when(z < G - 1)
        def _(): sig(wide_id(z + 1, y, x))
        pl.semaphore_wait(bar, 2 + (z > 0).astype(jnp.int32) + (z < G - 1).astype(jnp.int32))

class Gather:
    def __init__(self, G, cut, src, out, local_sem, zs, zr, ns, nr):
        self.G, self.src, self.out, self.local_sem = G, src, out, local_sem
        self.zs, self.zr, self.ns, self.nr = zs, zr, ns, nr
        self.half = (pl.ds(0, cut), pl.ds(cut, src.shape[1] - cut))
        self.z, self.y, self.x = place()
    def hop(self, own, zz, yy, xx, h, tgt, j):
        y, x = self.y, self.x
        target = wide_id(self.z, 1 - y, x) if tgt == "y" else wide_id(self.z, y, 1 - x)
        s = self.src.at[:, self.half[h]] if own else self.out.at[zz, yy, xx, :, self.half[h]]
        return remote(s, self.out.at[zz, yy, xx, :, self.half[h]], self.ns.at[zz * 6 + j], self.nr.at[zz * 6 + j], target)
    def first(self, zz, own=False):
        y, x = self.y, self.x
        return [self.hop(own, zz, y, x, 0, "y", 0), self.hop(own, zz, y, x, 1, "x", 1),
                self.hop(own, zz, y, x, 0, "x", 2), self.hop(own, zz, y, x, 1, "y", 3)]
    def second(self, zz):
        y, x = self.y, self.x
        return [self.hop(False, zz, 1 - y, x, 0, "x", 4), self.hop(False, zz, y, 1 - x, 1, "y", 5)]
    def relay(self, own, zz, step, way):
        s = self.src if own else self.out.at[zz, self.y, self.x]
        slot = way * (self.G - 1) + step
        target = wide_id(self.z + (1 if way == 0 else -1), self.y, self.x)
        return remote(s, self.out.at[zz, self.y, self.x], self.zs.at[slot], self.zr.at[slot], target)
    def can(self, way):
        return self.z < self.G - 1 if way == 0 else self.z > 0
    def source(self, d, way):
        return (self.z - d, self.z - d >= 0) if way == 0 else (self.z + d, self.z + d < self.G)
    def begin(self):
        pltpu.make_async_copy(self.src, self.out.at[self.z, self.y, self.x], self.local_sem).start()
        for way in range(2):
            @pl.when(self.can(way))
            def _(): self.relay(True, self.z, 0, way).start()
        for c in self.first(self.z, True): c.start()
    def turn(self, zz):
        y, x = self.y, self.x
        self.hop(False, zz, 1 - y, x, 0, "y", 0).wait_recv()
        self.hop(False, zz, y, 1 - x, 1, "x", 1).wait_recv()
        for c in self.second(zz): c.start()
    def step(self, d):
        for way in range(2):
            zz, there = self.source(d, way)
            @pl.when(there)
            def _():
                self.relay(False, zz, d - 1, way).wait_recv()
                @pl.when(self.can(way))
                def _():
                    self.relay(False, zz, d, way).start()
                for c in self.first(zz): c.start()
    def turns(self, d):
        if d == 0:
            self.turn(self.z)
            return
        for way in range(2):
            zz, there = self.source(d, way)
            @pl.when(there)
            def _(): self.turn(zz)
    def finish(self):
        y, x = self.y, self.x
        for zz in range(self.G):
            self.hop(False, zz, y, 1 - x, 0, "x", 2).wait_recv()
            self.hop(False, zz, 1 - y, x, 1, "y", 3).wait_recv()
            self.hop(False, zz, 1 - y, 1 - x, 0, "x", 4).wait_recv()
            self.hop(False, zz, 1 - y, 1 - x, 1, "y", 5).wait_recv()
            for c in self.first(zz) + self.second(zz): c.wait_send()
        for way in range(2):
            @pl.when(self.can(way))
            def _():
                self.relay(True, self.z, 0, way).wait_send()
                for d in range(1, self.G - 1):
                    zz, there = self.source(d, way)
                    @pl.when(there)
                    def _(): self.relay(False, zz, d, way).wait_send()
        pltpu.make_async_copy(self.src, self.out.at[self.z, self.y, self.x], self.local_sem).wait()

def gather_sems(G):
    D = pltpu.SemaphoreType.DMA
    return [D, D((2 * (G - 1),)), D((2 * (G - 1),)), D((6 * G,)), D((6 * G,))]

def cut_of(C):
    return (C // 128 + 1) // 2 * 128

def ag_kernel(G, cut, src, out, *sems):
    greet(G, False)
    a = Gather(G, cut, src, out, *sems)
    a.begin()
    a.turns(0)
    for d in range(1, G):
        a.step(d)
        a.turns(d)
    a.finish()

def gather(shard, wide, cid):
    R, C = shard.shape
    G = wide // 4
    out = pl.pallas_call(functools.partial(ag_kernel, G, cut_of(C)),
        out_shape=jax.ShapeDtypeStruct((G, 2, 2, R, C), shard.dtype),
        in_specs=[pl.BlockSpec(memory_space=pl.ANY)], out_specs=pl.BlockSpec(memory_space=pl.ANY),
        scratch_shapes=gather_sems(G),
        compiler_params=pltpu.CompilerParams(collective_id=cid, has_side_effects=True), name="gather")(shard)
    return out.reshape(wide * R, C)

class Scatter:
    def __init__(self, G, cut, part, r1a, r1b, o1a, o1b, r2a, r2b, r3, own, lsem, s1, v1, s2, v2, s3, v3):
        self.__dict__.update(locals())
        C = part.shape[-1]
        self.ha, self.hb = pl.ds(0, cut), pl.ds(cut, C - cut)
        self.z, self.y, self.x = place()
    def zk(self, k):
        return (self.z + k) % self.G
    def ynb(self): return wide_id(self.z, 1 - self.y, self.x)
    def xnb(self): return wide_id(self.z, self.y, 1 - self.x)
    def one(self, k):
        z = self.zk(k)
        return [remote(self.part.at[z, :, 1 - self.x, :, self.ha], self.r1a.at[k], self.s1.at[2 * k], self.v1.at[2 * k], self.xnb()),
                remote(self.part.at[z, 1 - self.y, :, :, self.hb], self.r1b.at[k], self.s1.at[2 * k + 1], self.v1.at[2 * k + 1], self.ynb())]
    def load(self, k):
        z = self.zk(k)
        return [pltpu.make_async_copy(self.part.at[z, :, self.x, :, self.ha], self.o1a.at[k], self.lsem.at[2 * k]),
                pltpu.make_async_copy(self.part.at[z, self.y, :, :, self.hb], self.o1b.at[k], self.lsem.at[2 * k + 1])]
    def two(self, k):
        return [remote(self.o1a.at[k, 1 - self.y], self.r2a.at[k], self.s2.at[2 * k], self.v2.at[2 * k], self.ynb()),
                remote(self.o1b.at[k, 1 - self.x], self.r2b.at[k], self.s2.at[2 * k + 1], self.v2.at[2 * k + 1], self.xnb())]
    def three(self, k):
        return remote(self.own.at[k], self.r3.at[k - 1], self.s3.at[k - 1], self.v3.at[k - 1], wide_id(self.zk(k), self.y, self.x))
    def order(self):
        ks = list(range(1, self.G))
        return sorted(ks, key=lambda k: min(k, self.G - k), reverse=True) + [0]
    def launch(self, k):
        for c in self.one(k) + self.load(k): c.start()
    def begin(self):
        for k in self.order()[:2]: self.launch(k)
    def add_one(self, k):
        R = self.part.shape[3]
        for c in self.one(k): c.wait_recv()
        for c in self.load(k): c.wait()
        step = min(16, R)
        for mine, got in ((self.o1a, self.r1a), (self.o1b, self.r1b)):
            @pl.loop(0, 2 * R // step)
            def _(i):
                j, r = i // (R // step), pl.ds(pl.multiple_of((i % (R // step)) * step, step), step)
                mine[k, j, r, :] = (mine[k, j, r, :].astype(f32) + got[k, j, r, :].astype(f32)).astype(bf16)
        for c in self.two(k): c.start()
        later = self.order()[self.order().index(k) + 2:]
        if later: self.launch(later[0])
    def add_two(self, k):
        R = self.part.shape[3]
        for c in self.two(k): c.wait_recv()
        step = min(16, R)
        for mine, got, me, cols in ((self.o1a, self.r2a, self.y, self.ha), (self.o1b, self.r2b, self.x, self.hb)):
            @pl.loop(0, R // step)
            def _(i):
                r = pl.ds(pl.multiple_of(i * step, step), step)
                self.own[k, r, cols] = (mine[k, me, r, :].astype(f32) + got[k, r, :].astype(f32)).astype(bf16)
        if k:
            self.three(k).start()
    def finish(self, out):
        R = self.part.shape[3]
        for k in range(1, self.G): self.three(k).wait_recv()
        step = min(16, R)
        @pl.loop(0, R // step)
        def _(i):
            r = pl.ds(pl.multiple_of(i * step, step), step)
            total = self.own[0, r, :].astype(f32)
            for k in range(self.G - 1):
                total = total + self.r3[k, r, :].astype(f32)
            out[r, :] = total
        for k in range(self.G):
            for c in self.one(k) + self.two(k): c.wait_send()
            if k: self.three(k).wait_send()

def scatter_scratch(G, R, C):
    cut = cut_of(C)
    D, V = pltpu.SemaphoreType.DMA, lambda *s: pltpu.VMEM(s, bf16)
    return [V(G, 2, R, cut), V(G, 2, R, C - cut), V(G, 2, R, cut), V(G, 2, R, C - cut), V(G, R, cut), V(G, R, C - cut),
            V(G - 1, R, C), V(G, R, C), D((2 * G,)), D((2 * G,)), D((2 * G,)), D((2 * G,)), D((2 * G,)), D((G - 1,)), D((G - 1,))]

def rs_kernel(G, cut, part, out, *scratch):
    greet(G, True)
    s = Scatter(G, cut, part, *scratch)
    s.begin()
    order = s.order()
    for n, k in enumerate(order):
        s.add_one(k)
        if n: s.add_two(order[n - 1])
    s.add_two(order[-1])
    s.finish(out)

def scatter(part, wide, cid):
    R, C, G = part.shape[0] // wide, part.shape[1], wide // 4
    return pl.pallas_call(functools.partial(rs_kernel, G, cut_of(C)),
        out_shape=jax.ShapeDtypeStruct((R, C), f32),
        in_specs=[pl.BlockSpec(memory_space=pl.ANY)], out_specs=pl.BlockSpec(memory_space=pltpu.VMEM),
        scratch_shapes=scatter_scratch(G, R, C),
        compiler_params=pltpu.CompilerParams(collective_id=cid, has_side_effects=True, vmem_limit_bytes=56 * 2**20), name="scatter")(part.reshape(G, 2, 2, R, C))

def sum_kernel(G, src, out, acc, got, gz, s, v, sz, vz):
    z, y, x = place()
    core = {"narrow": 1 - lax.axis_index("narrow")}
    ynb, xnb = wide_id(z, 1 - y, x), wide_id(z, y, 1 - x)
    far = [wide_id((z + k) % G, y, x) for k in range(1, G)]
    bar = pltpu.get_barrier_semaphore()
    for t in [core, ynb, xnb] + far:
        pl.semaphore_signal(bar, inc=1, device_id=t, device_id_type=MESH)
    pl.semaphore_wait(bar, 3 + len(far))
    acc[0] = src[...]
    for n, t in enumerate((core, xnb, ynb)):
        c = remote(acc.at[n], got.at[n], s.at[n], v.at[n], t)
        c.start()
        c.wait()
        acc[n + 1] = acc[n] + got[n]
    gz[z] = acc[3]
    sent = [remote(acc.at[3], gz.at[z], sz.at[k], vz.at[z], t) for k, t in enumerate(far)]
    for c in sent: c.start()
    for k in range(1, G):
        zz = (z + k) % G
        remote(acc.at[3], gz.at[zz], sz.at[k - 1], vz.at[zz], far[k - 1]).wait_recv()
    for c in sent: c.wait_send()
    total = gz[0]
    for k in range(1, G):
        total = total + gz[k]
    out[...] = total

def sum_all(part, wide, cid):
    G, rows = wide // 4, part.shape[0]
    D, V = pltpu.SemaphoreType.DMA, lambda k: pltpu.VMEM((k, rows, 128), f32)
    return pl.pallas_call(functools.partial(sum_kernel, G), out_shape=jax.ShapeDtypeStruct(part.shape, f32),
        in_specs=[pl.BlockSpec(memory_space=pltpu.VMEM)], out_specs=pl.BlockSpec(memory_space=pltpu.VMEM),
        scratch_shapes=[V(4), V(3), V(G), D((3,)), D((3,)), D((G - 1,)), D((G,))],
        compiler_params=pltpu.CompilerParams(collective_id=cid, has_side_effects=True), name="small_sums")(part)


epsilon = 1e-06


def norm_plain(values, gain_row):
    factor = lax.rsqrt(jnp.mean(values * values, axis=-1, keepdims=True) + epsilon)
    return values * factor * gain_row


def gated_unit(gate_pre, up_pre):
    return jax.nn.gelu(gate_pre, approximate=True) * up_pre


def times(a, b):
    return jnp.dot(a, b, preferred_element_type=f32)


def times_transposed(a, b):
    return lax.dot_general(a, b, NT, preferred_element_type=f32)


def transposed_times(a, b):
    return lax.dot_general(a, b, (((0,), (0,)), ((), ())), preferred_element_type=f32)


def swap(a):
    return lax.ppermute(a, "narrow", [(0, 1), (1, 0)])


def both(a):
    return a.astype(f32) + swap(a).astype(f32)


def local(tokens, cotangent, pages, boxes, gain_attn, gain_ffn, bias_tables, w_query, w_key, w_value, w_out, w_gate, w_up, w_down):
    wide, narrow = lax.axis_size("wide"), lax.axis_size("narrow")
    heads_all = bias_tables.shape[1]
    heads = heads_all // narrow
    rows = tokens.shape[0]
    core = lax.axis_index("narrow")
    tables = lax.dynamic_slice_in_dim(bias_tables, core * heads, heads, 1)
    inner, ff = w_query.shape[1], w_gate.shape[1]
    mine = lambda a: lax.dynamic_slice_in_dim(a, core * rows, rows, 0)

    all_tokens = lax.all_gather(tokens, "narrow", axis=0, tiled=True)
    all_cot = lax.all_gather(cotangent, "narrow", axis=0, tiled=True)
    bias, ids = make_bias(tables, boxes, pages)
    w_first = gather(jnp.concatenate([w_query, w_key, w_value], axis=1), wide, 1)
    w_second = gather(jnp.concatenate([w_out.T, w_gate, w_up, w_down.T], axis=1), wide, 2)
    full_out, full_gate, full_up, full_down = jnp.split(w_second, [inner, inner + ff, inner + 2 * ff], axis=1)

    x = all_tokens.astype(f32)
    gain_one, gain_two = gain_attn.astype(f32), gain_ffn.astype(f32)
    normed = norm_plain(x, gain_one).astype(bf16)
    qkv = times(normed, w_first).astype(bf16)
    attended, lse = attn_fwd(qkv, bias)
    hidden = x + both(times_transposed(attended, full_out).astype(bf16))
    normed_two = norm_plain(hidden, gain_two).astype(bf16)
    gate_pre, up_pre = times(normed_two, full_gate), times(normed_two, full_up)
    hidden_ff = gated_unit(gate_pre, up_pre).astype(bf16)
    down = times_transposed(hidden_ff, full_down).astype(bf16)
    output = (mine(hidden) + lax.psum_scatter(down, "narrow", scatter_dimension=0, tiled=True).astype(f32)).astype(bf16)

    grad_w_down = transposed_times(all_cot, hidden_ff)
    grad_ff = times(all_cot, full_down)
    _, gated_pull = jax.vjp(gated_unit, gate_pre, up_pre)
    grad_gate, grad_up = [g.astype(bf16) for g in gated_pull(grad_ff)]
    grad_w_gate = transposed_times(normed_two, grad_gate)
    grad_w_up = transposed_times(normed_two, grad_up)
    grad_two = both((times_transposed(grad_gate, full_gate) + times_transposed(grad_up, full_up)).astype(bf16))
    _, pull_two = jax.vjp(lambda h: norm_plain(h, gain_two), hidden)
    grad_hidden = all_cot.astype(f32) + pull_two(grad_two)[0]
    own_hidden = mine(hidden)
    grad_gain_two = jnp.sum(mine(grad_two) * own_hidden * lax.rsqrt(jnp.mean(own_hidden * own_hidden, axis=-1, keepdims=True) + epsilon), axis=0)
    grad_low = grad_hidden.astype(bf16)
    grad_w_out = transposed_times(grad_low, attended)
    second = jnp.concatenate([g.astype(bf16) for g in (grad_w_out, grad_w_gate, grad_w_up, grad_w_down)], axis=1)
    shard_second = scatter(second, wide, 3)
    grad_attended = times(grad_low, full_out).astype(bf16)
    dq, dk, dv, g = attn_bwd(qkv, bias, attended, grad_attended, lse)
    dqkv = jnp.concatenate([dq, dk, dv], axis=1)
    shard_first = scatter(transposed_times(normed, dqkv).astype(bf16), wide, 4)
    grad_normed = lax.psum_scatter(times_transposed(dqkv, w_first).astype(bf16), "narrow", scatter_dimension=0, tiled=True).astype(f32)
    own = tokens.astype(f32)
    _, pull_one = jax.vjp(norm_plain, own, gain_one)
    grad_tokens_norm, grad_gain_one = pull_one(grad_normed)
    grad_tokens = mine(grad_hidden) + grad_tokens_norm
    table_part = lax.dynamic_update_slice(jnp.zeros((bias_tables.shape[0], heads_all), f32), table_hist(g, ids).T, (jnp.int32(0), core * heads))
    sizes = [gain_one.size, gain_two.size, table_part.size]
    small = sum_all(jnp.concatenate([grad_gain_one, grad_gain_two, table_part.reshape(-1)]).reshape(-1, 128), wide, 5).reshape(-1)
    one, two, table = jnp.split(small, [sizes[0], sizes[0] + sizes[1]])
    s_query, s_key, s_value = jnp.split(shard_first, 3, axis=1)
    s_out, s_gate, s_up, s_down = jnp.split(shard_second, [inner, inner + ff, inner + 2 * ff], axis=1)
    return (output, grad_tokens, one, two, table.reshape(bias_tables.shape), s_query, s_key, s_value, s_out.T, s_gate, s_up, s_down.T)


def solution(mesh):
    rows, cols, tall = P(("wide", "narrow"), None), P("wide", "narrow"), P("narrow", "wide")
    in_specs = (rows, rows, P("wide"), P(None, "wide"), P(), P(), P(), cols, cols, cols, tall, cols, cols, tall)
    out_specs = (rows, rows, P(), P(), P(), cols, cols, cols, tall, cols, cols, tall)
    return jax.shard_map(local, mesh=mesh, in_specs=in_specs, out_specs=out_specs, check_vma=False)
```

time: 1950 us -> 623 us (0.32)
  waiting for transfers between devices: 1050 us -> 0.1 us
  Pallas kernels: 0 us -> 456 us
  matrix products: 432 us -> 83.8 us
  other arithmetic: 253 us -> 35.1 us
  local copies, waits for them, and re-layouts: 121 us -> 23.1 us
  blocking collectives: 42.1 us -> 0 us
  loops' own time: 28.9 us -> 0 us
    reduce_scatter x11 -> x2, waiting for transfers between devices: 651 us -> 0.01 us  [the longest x1 0.01 us: local(): lax.psum_scatter(down, 'narrow', scatter_dimension=0, tiled=True)]
    pallas_call x0 -> x9, Pallas kernels: none -> 456 us  [the longest x2 123 us: scatter(): pl.pallas_call(functools.partial(rs_kernel, G, cut_of(C)), out_shape=jax....]
    all_gather x11 -> x2, waiting for transfers between devices: 396 us -> 0.02 us  [the longest x1 0.02 us: local(): all_cot = lax.all_gather(cotangent, 'narrow', axis=0, tiled=True)]
    dot_general x59 -> x15, matrix products: 432 us -> 83.8 us  [the longest x5 33.8 us: times(): return jnp.dot(a, b, preferred_element_type=f32)]
    eq x44 -> x0, other arithmetic: 153 us -> none  [the longest x8 56.8 us: layout_hots(): linear_ids[None] == labels]
    dot_general x16 -> x0, local copies, waits for them, and re-layouts: 81.3 us -> none  [block_bias(): jnp.einsum('ai,anf->inf', head_table_entries, indicator_rows, preferred_e...]
    add x33 -> x3, other arithmetic: 51.2 us -> 8.63 us  [the longest x1 5.55 us: both(): return a.astype(f32) + swap(a).astype(f32)]
    psum x1 -> x0, blocking collectives: 42.1 us -> none  [local(): lax.psum((grad_gain_one, grad_gain_two, table_full), ('wide', 'narrow'))]
  transfers between devices with their start and end apart: 22 -> 6, of which waited for: 19 -> 0; matrix products, arithmetic and copies ran while one was open for 17% -> 16% of each run, Pallas kernels for 0% -> 72%
where the time goes in v1:
time: 623 us; the launch traced here: 613 us
  Pallas kernels  456 us (73%)
  matrix products  83.8 us (13%)
  other arithmetic  35.1 us (6%)
  local copies, waits for them, and re-layouts  23.1 us (4%)
  between operations  14.6 us (2%)
    pallas_call x2, Pallas kernels, scatter(): pl.pallas_call(functools.partial(rs_kernel, G, cut_of(C)), out_shape=jax....  123 us
    pallas_call x2, Pallas kernels, gather(): pl.pallas_call(functools.partial(ag_kernel, G, cut_of(C)), out_shape=jax....  113 us
    pallas_call x1, Pallas kernels, make_bias(): pl.pallas_call(functools.partial(bias_kernel, heads, rows, n), grid=(n //...  83.1 us
    pallas_call x1, Pallas kernels, table_hist(): pl.pallas_call(functools.partial(hist_kernel, heads, rows, n), grid=(n //...  64.5 us
    dot_general x5, matrix products, times(): return jnp.dot(a, b, preferred_element_type=f32)  33.8 us
    pallas_call x1, Pallas kernels, attn_bwd(): pl.pallas_call(bwd_kernel, grid=(pairs, n // tq), out_shape=(jax.ShapeDty...  32.6 us
    dot_general x5, matrix products, transposed_times(): lax.dot_general(a, b, (((0,), (0,)), ((), ())), preferred_element_type=f32)  27.5 us
    pallas_call x1, Pallas kernels, attn_fwd(): pl.pallas_call(fwd_kernel, grid=(pairs, n // tq), out_shape=(jax.ShapeDty...  25.3 us
  transfers between devices with their start and end apart: 6, of which 0 were waited for; matrix products, arithmetic and copies ran while one was open for 16% of the time, Pallas kernels for 72%

profile of v1, /device:TPU:0, one launch (start us, length us, event | category | flops | bytes accessed | tf_op | source)
XLA Modules:
  0.0 613.4 jit_solution(5056109801235071453)
XLA Ops:
  7.3 2.4 copy.40
  12.4 34.4 %gather.2 = bf16[4,2,2,64,1536]{4,3,2,1,0:T(8,128)(2,1)} custom-call(bf16[64,1536]{1,0:T(8,128)(2,1)} %pad_maximum_fusion.2.src), custom_call_target="tpu_custom_call" | custom-call | tf_op jit(solution)/shard_map/gather/pallas_call | solution.py:284
  50.5 78.7 %gather.3 = bf16[4,2,2,64,4736]{4,3,2,1,0:T(8,128)(2,1)} custom-call(bf16[64,4736]{1,0:T(8,128)(2,1)} %pad_maximum_fusion.1.src), custom_call_target="tpu_custom_call" | custom-call | tf_op jit(solution)/shard_map/gather/pallas_call | solution.py:284
  129.2 83.1 %layout_bias.1 = (f32[8,1024,1024]{2,1,0:T(8,128)}, f32[3,1024,1024]{2,1,0:T(8,128)}) custom-call(s32[1,128]{1,0:T(1,128)} %fusion.58.steps_ref, f32[24,128]{1,0:T(8,128)} %pad_convert_fusion.tab_ref, s32[1024,2]{1,0:T(8,128)} %bitcast.67, s32[2,1024]{1,0:T(2,128)} %box_row.1, s32[1024,1]{1,0:T(8,128)} %copy.43.page_col, s32[1,1024]{1,0:T(1,128)} %bitcast.72), custom_call_target="tpu_custom_call" | custom-call | tf_op jit(solution)/shard_map/layout_bias/pallas_call | solution.py:55
  214.4 7.1 %convolution_convert_fusion.4.q_ref.k_ref.v_ref = bf16[1024,1536]{1,0:T(8,128)(2,1)} fusion(bf16[1024,1536]{1,0:T(8,128)(2,1)S(1)} %bitcast.64, bf16[1024,1024]{0,1:T(8,128)(2,1)} %all-gather.3.cloned.1.call-done, f32[1024]{0:T(1024)S(1)} %convert_element_type.244, f32[1024]{0:T(1024)S(1)} %add_rsqrt_fusion), kind=kOutput, calls=%fused_computation.32 | convolution fusion | flops 3226992640 | bytes 8396800 | tf_op jit(solution)/shard_map/dot_general | solution.py:434
  221.5 25.3 %attention.1 = (bf16[1024,512]{1,0:T(8,128)(2,1)}, f32[4,1024,2]{2,1,0:T(8,128)}) custom-call(bf16[1024,1536]{1,0:T(8,128)(2,1)} %convolution_convert_fusion.4.q_ref.k_ref.v_ref, bf16[1024,1536]{1,0:T(8,128)(2,1)} %convolution_convert_fusion.4.q_ref.k_ref.v_ref, bf16[1024,1536]{1,0:T(8,128)(2,1)} %convolution_convert_fusion.4.q_ref.k_ref.v_ref, ...), custom_call_target="tpu_custom_call" | custom-call | tf_op jit(solution)/shard_map/attention/pallas_call | solution.py:88
  246.8 4.2 convolution_convert_fusion.6
  251.1 8.5 %fusion.13 = f32[1408,1024]{0,1:T(8,128)} fusion(bf16[1024,1024]{0,1:T(8,128)(2,1)} %all-gather.5.cloned.1.call-done, bf16[1024,4736]{1,0:T(8,128)(2,1)} %bitcast.55), kind=kOutput, calls=%fused_computation.41 | convolution fusion | flops 2952790016 | bytes 10747904 | tf_op jit(solution)/shard_map/dot_general | solution.py:434
  259.6 3.8 multiply_reduce_fusion.1
  265.6 3.5 fusion.19
  269.2 10.4 %fusion.6 = (bf16[1024,1408]{1,0:T(8,128)(2,1)}, bf16[1024,1408]{1,0:T(8,128)(2,1)}, bf16[1024,1408]{1,0:T(8,128)(2,1)}) fusion(f32[1024,1408]{1,0:T(8,128)S(1)} %fusion.19, f32[1408,1024]{0,1:T(8,128)S(1)} %bitcast.76, bf16[1024,1024]{0,1:T(8,128)(2,1)S(1)} %multiply_convert_fusion.1, bf16[1024,4736]{1,0:T(8,128)(2,1)S(1)} %bitcast.60), kind=kOutput, calls=%fused_computation.13 | convolution fusion | flops 2990276608 | bytes 25165824 | tf_op jit(solution)/shard_map/dot_general | solution.py:434
  279.6 5.4 fusion.17
  285.0 3.7 add_convert_fusion
  289.3 4.7 fusion.30
  294.3 7.6 %convolution_convert_fusion.1 = bf16[1024,1408]{1,0:T(8,128)(2,1)} fusion(bf16[1024,1024]{0,1:T(8,128)(2,1)} %copy-done.14, bf16[1024,1408]{1,0:T(8,128)(2,1)} %get-tuple-element.57), kind=kOutput, calls=%fused_computation.29 | convolution fusion | flops 2954231808 | bytes 7864320 | tf_op jit(solution)/shard_map/dot_general | solution.py:442
  301.9 2.8 multiply_reduce_fusion
  304.7 5.6 convert_add_fusion.1
  310.3 4.3 convolution_convert_fusion.8.do_ref
  314.6 32.6 %attention_back.1 = (bf16[1024,512]{1,0:T(8,128)(2,1)}, bf16[1024,512]{1,0:T(8,128)(2,1)}, bf16[1024,512]{1,0:T(8,128)(2,1)}, bf16[8,1024,1024]{2,1,0:T(8,128)(2,1)}) custom-call(bf16[1024,1536]{1,0:T(8,128)(2,1)} %convolution_convert_fusion.4.q_ref.k_ref.v_ref, bf16[1024,1536]{1,0:T(8,128)(2,1)} %convolution_convert_fusion.4.q_ref.k_ref.v_ref, ...), custom_call_target="tpu_custom_call" | custom-call | tf_op jit(solution)/shard_map/attention_back/pallas_call | solution.py:126
  351.7 4.6 convolution_convert_fusion.5
  356.4 6.7 %convolution_convert_fusion.2 = bf16[1024,1408]{1,0:T(8,128)(2,1)} fusion(bf16[1024,1024]{0,1:T(8,128)(2,1)S(1)} %copy-done.15, bf16[1024,1408]{1,0:T(8,128)(2,1)} %get-tuple-element.56), kind=kOutput, calls=%fused_computation.30 | convolution fusion | flops 2954231808 | bytes 7864320 | tf_op jit(solution)/shard_map/dot_general | solution.py:442
  363.4 4.7 fusion.12
  368.1 64.5 %table_grad.1 = f32[8,96]{1,0:T(8,128)} custom-call(bf16[8,1024,1024]{2,1,0:T(8,128)(2,1)} %get-tuple-element.26.g_ref, f32[3,1024,1024]{2,1,0:T(8,128)} %get-tuple-element.27.ids_ref), custom_call_target="tpu_custom_call" | custom-call | tf_op jit(solution)/shard_map/table_grad/pallas_call | solution.py:156
  433.8 7.1 %convolution_convert_fusion.3 = bf16[1024,1536]{1,0:T(8,128)(2,1)} fusion(bf16[1024,1536]{1,0:T(8,128)(2,1)} %copy-done.20, bf16[1024,1024]{0,1:T(8,128)(2,1)S(1)} %copy-done.9, f32[1024]{0:T(1024)S(1)} %convert_element_type.244, f32[1024]{0:T(1024)S(1)} %add_rsqrt_fusion), kind=kOutput, calls=%fused_computation.31 | convolution fusion | flops 3226992640 | bytes 8396800 | tf_op jit(solution)/shard_map/dot_general | solution.py:442
  440.9 33.8 %scatter.2 = f32[64,1536]{1,0:T(8,128)} custom-call(bf16[4,2,2,64,1536]{4,3,2,1,0:T(8,128)(2,1)} %bitcast.66), custom_call_target="tpu_custom_call" | custom-call | tf_op jit(solution)/shard_map/scatter/pallas_call | solution.py:379
  476.7 8.8 %pad_maximum_fusion = bf16[1024,4736]{1,0:T(8,128)(2,1)} fusion(bf16[1024,1408]{1,0:T(8,128)(2,1)} %fusion.12, bf16[1024,1408]{1,0:T(8,128)(2,1)} %convolution_convert_fusion.1, bf16[1024,1408]{1,0:T(8,128)(2,1)} %convolution_convert_fusion.2, bf16[1024,512]{1,0:T(8,128)(2,1)S(1)} %copy.53), kind=kLoop, calls=%fused_computation | loop fusion | flops 38797312 | bytes 19398656 | tf_op jit(solution)/shard_map/concatenate | solution.py:495
  485.4 89.3 %scatter.3 = f32[64,4736]{1,0:T(8,128)} custom-call(bf16[4,2,2,64,4736]{4,3,2,1,0:T(8,128)(2,1)} %bitcast.53), custom_call_target="tpu_custom_call" | custom-call | tf_op jit(solution)/shard_map/scatter/pallas_call | solution.py:379
  576.5 2.2 slice_bitcast_fusion
  578.7 2.9 multiply_reduce_fusion.2
  582.9 2.4 fusion.26
  585.9 14.4 %small_sums.1 = f32[28,128]{1,0:T(8,128)} custom-call(f32[28,128]{1,0:T(8,128)} %maximum_bitcast_fusion.src), custom_call_target="tpu_custom_call" | custom-call | tf_op jit(solution)/shard_map/small_sums/pallas_call | solution.py:415
  601.6 2.5 fusion.27
  (138 shorter events, 27.0 us)
Async XLA Ops:
  7.2 39.6 %copy-start = (bf16[96,16]{0,1:T(8,128)(2,1)S(1)}, bf16[96,16]{0,1:T(8,128)(2,1)}, u32[]{:S(2)}) copy-start(bf16[96,16]{0,1:T(8,128)(2,1)} %param.20) | copy-start | bytes 9220
  7.2 205.1 %all-gather.3.cloned.1.call-start = ((), (), s32[]{:S(2)}) async-start(), calls=%async_computation.2 | async-start | bytes 3145728 | tf_op jit(solution)/shard_map/all_gather | solution.py:463
  9.7 37.1 %copy-start.30 = (bf16[1024]{0:T(1024)(128)(2,1)S(1)}, bf16[1024]{0:T(1024)(128)(2,1)}, u32[]{:S(2)}) copy-start(bf16[1024]{0:T(1024)(128)(2,1)} %param.18) | copy-start | bytes 6148
  9.7 37.9 %copy-start.28 = (s32[2,1024]{1,0:T(2,128)S(1)}, s32[2,1024]{1,0:T(2,128)}, u32[]{:S(2)}) copy-start(s32[2,1024]{1,0:T(2,128)} %box_row.1) | copy-start | bytes 24580
  9.7 241.4 %all-gather.5.cloned.1.call-start = ((), (), s32[]{:S(2)}) async-start(), calls=%async_computation.4 | async-start | bytes 3145728 | tf_op jit(solution)/shard_map/all_gather | solution.py:464
  11.1 37.5 %copy-start.29 = (s32[1024]{0:T(1024)S(1)}, s32[1024]{0:T(1024)}, u32[]{:S(2)}) copy-start(s32[1024]{0:T(1024)} %param.16) | copy-start | bytes 12292
  11.1 38.5 %copy-start.21 = (bf16[1408,64]{0,1:T(8,128)(2,1)S(1)}, bf16[1408,64]{0,1:T(8,128)(2,1)}, u32[]{:S(2)}) copy-start(bf16[1408,64]{0,1:T(8,128)(2,1)} %param.27) | copy-start | bytes 540676
  11.1 38.5 %copy-start.22 = (bf16[64,1408]{1,0:T(8,128)(2,1)S(1)}, bf16[64,1408]{1,0:T(8,128)(2,1)}, u32[]{:S(2)}) copy-start(bf16[64,1408]{1,0:T(8,128)(2,1)} %param.26) | copy-start | bytes 540676
  11.1 38.5 %copy-start.23 = (bf16[64,1408]{1,0:T(8,128)(2,1)S(1)}, bf16[64,1408]{1,0:T(8,128)(2,1)}, u32[]{:S(2)}) copy-start(bf16[64,1408]{1,0:T(8,128)(2,1)} %param.25) | copy-start | bytes 540676
  11.1 38.5 %copy-start.24 = (bf16[512,64]{0,1:T(8,128)(2,1)S(1)}, bf16[512,64]{0,1:T(8,128)(2,1)}, u32[]{:S(2)}) copy-start(bf16[512,64]{0,1:T(8,128)(2,1)} %param.24) | copy-start | bytes 196612
  11.2 567.5 %reduce-scatter.3.cloned.1.call-start = ((), (), s32[]{:S(2)}) async-start(), calls=%async_computation.3 | async-start | bytes 3145728 | tf_op jit(solution)/shard_map/reduce_scatter | solution.py:480
  129.2 85.2 %copy-start.10 = (bf16[4,2,2,64,1536]{4,3,2,1,0:T(8,128)(2,1)S(1)}, bf16[4,2,2,64,1536]{4,3,2,1,0:T(8,128)(2,1)}, u32[]{:S(2)}) copy-start(bf16[4,2,2,64,1536]{4,3,2,1,0:T(8,128)(2,1)} %gather.2) | copy-start | bytes 9437188
  251.0 8.6 %collective-permute-start = (bf16[1024,1024]{0,1:T(8,128)(2,1)}, bf16[1024,1024]{0,1:T(8,128)(2,1)}, u32[]{:S(2)}, u32[]{:S(2)}) collective-permute-start(bf16[1024,1024]{0,1:T(8,128)(2,1)} %convolution_convert_fusion.6), channel_id=1, source_target_pairs={{0,1},{1,0},{2,3},{3,2},{4,5},{5,4},{6,7},{7,6},{8,9},{9,8},{10,11... | collective-permute-start | bytes 6291464 | tf_op jit(solution)/shard_map/ppermute | solution.py:446
  251.0 8.6 %copy-start.8 = (bf16[1024,1024]{0,1:T(8,128)(2,1)S(1)}, bf16[1024,1024]{0,1:T(8,128)(2,1)}, u32[]{:S(2)}) copy-start(bf16[1024,1024]{0,1:T(8,128)(2,1)} %all-gather.3.cloned.1.call-done) | copy-start | bytes 6291460
  251.1 14.5 %slice-start = ((s8[9699328]{0:T(1024)(128)(4,1)}), s8[4194304]{0:T(1024)(128)(4,1)S(1)}, s32[]{:S(2)}) async-start(s8[9699328]{0:T(1024)(128)(4,1)} %bitcast.57), calls=%async_computation.6 | async-start | bytes 8388608
  251.1 14.5 %slice-start.1 = ((s8[9699328]{0:T(1024)(128)(4,1)}), s8[4194304]{0:T(1024)(128)(4,1)S(1)}, s32[]{:S(2)}) async-start(s8[9699328]{0:T(1024)(128)(4,1)} %bitcast.57), calls=%async_computation.7 | async-start | bytes 8388608
  259.6 6.0 slice-start.2
  263.5 5.7 slice-start.4
  279.6 5.4 copy-start.32
  288.7 13.2 %collective-permute-start.1 = (bf16[1024,1024]{0,1:T(8,128)(2,1)S(1)}, bf16[1024,1024]{0,1:T(8,128)(2,1)}, u32[]{:S(2)}, u32[]{:S(2)}) collective-permute-start(bf16[1024,1024]{0,1:T(8,128)(2,1)S(1)} %add_convert_fusion), channel_id=1, source_target_pairs={{0,1},{1,0},{2,3},{3,2},{4,5},{5,4},{6,7},{7,6},{8,9},{9,8},{10,11... | collective-permute-start | bytes 6291464 | tf_op jit(solution)/shard_map/ppermute | solution.py:446
  289.2 4.8 copy-start.5
  294.0 289.0 %reduce-scatter.5.cloned.1.call-start = ((), (), s32[]{:S(2)}) async-start(), calls=%async_computation.5 | async-start | bytes 3145728 | tf_op jit(solution)/shard_map/reduce_scatter | solution.py:501
  294.3 7.6 %copy-start.3 = (f32[1024,1024]{0,1:T(8,128)S(1)}, f32[1024,1024]{0,1:T(8,128)}, u32[]{:S(2)}) copy-start(f32[1024,1024]{0,1:T(8,128)} %copy-done.2) | copy-start | bytes 12582916
  351.7 4.6 copy-start.15
  356.4 6.8 %copy-start.4 = (f32[1024,1024]{0,1:T(8,128)S(1)}, f32[1024,1024]{0,1:T(8,128)}, u32[]{:S(2)}) copy-start(f32[1024,1024]{0,1:T(8,128)} %copy-done.2) | copy-start | bytes 12582916
  356.4 7.0 %copy-start.13 = (bf16[1024,1024]{0,1:T(8,128)(2,1)S(1)}, bf16[1024,1024]{0,1:T(8,128)(2,1)}, u32[]{:S(2)}) copy-start(bf16[1024,1024]{0,1:T(8,128)(2,1)} %all-gather.5.cloned.1.call-done) | copy-start | bytes 6291460
  356.4 7.0 %copy-start.34 = (bf16[1024,1408]{1,0:T(8,128)(2,1)S(1)}, bf16[1024,1408]{1,0:T(8,128)(2,1)}, u32[]{:S(2)}) copy-start(bf16[1024,1408]{1,0:T(8,128)(2,1)} %get-tuple-element.58) | copy-start | bytes 8650756
  368.1 65.7 %copy-start.9 = (bf16[1024,1024]{0,1:T(8,128)(2,1)S(1)}, bf16[1024,1024]{0,1:T(8,128)(2,1)}, u32[]{:S(2)}) copy-start(bf16[1024,1024]{0,1:T(8,128)(2,1)} %all-gather.3.cloned.1.call-done) | copy-start | bytes 6291460
  433.8 41.0 %copy-start.7 = (f32[1024,1024]{0,1:T(8,128)S(1)}, f32[1024,1024]{0,1:T(8,128)}, u32[]{:S(2)}) copy-start(f32[1024,1024]{0,1:T(8,128)} %copy-done.6) | copy-start | bytes 12582916
  440.9 33.8 %copy-start.17 = (bf16[1024,512]{1,0:T(8,128)(2,1)S(1)}, bf16[1024,512]{1,0:T(8,128)(2,1)}, u32[]{:S(2)}) copy-start(bf16[1024,512]{1,0:T(8,128)(2,1)} %get-tuple-element.21.o_ref) | copy-start | bytes 3145732
  485.4 89.3 %copy-start.16 = (f32[64,1536]{1,0:T(8,128)S(1)}, f32[64,1536]{1,0:T(8,128)}, u32[]{:S(2)}) copy-start(f32[64,1536]{1,0:T(8,128)} %scatter.2) | copy-start | bytes 1179652
  601.6 5.2 copy-start.1
  (15 other events, 51.8 us)
Sparse Core Ops, SparseCore 0:
  10.2 13.2 all-gather.2
  25.0 11.7 all-gather.4
  294.1 8.8 reduce-scatter.2
  356.5 8.8 reduce-scatter.4

commit v2 on v1

v2 whole, which is shorter than its diff:
```python
import functools

import jax
import jax.numpy as jnp
from jax import lax
from jax.experimental import pallas as pl
from jax.experimental.pallas import tpu as pltpu
from jax.sharding import PartitionSpec as P

f32, bf16 = jnp.float32, jnp.bfloat16
MESH = pl.DeviceIdType.MESH


EDGES = (1, 2, 3, 4, 5, 6, 7, 8, 12, 16, 23, 32, 46, 64, 91)
NT = (((1,), (1,)), ((), ()))
VM = 58 * 2**20


def params(cid):
    return pltpu.CompilerParams(collective_id=cid, has_side_effects=True, vmem_limit_bytes=VM)


def lane_take(table, idx):
    return jnp.take_along_axis(table, idx, axis=1, mode="promise_in_bounds")


def bias_tile(start, heads, rows, n, steps_ref, tab_ref, box_col, box_row, page_col, page_row, bias_ref, ids_ref):
    steps = jnp.broadcast_to(steps_ref[...], (rows, 128))
    allowed_col = jnp.broadcast_to(page_col[...] % 2, (rows, 128))
    cols = [jnp.broadcast_to(box_col[:, t:t + 1], (rows, 128)) for t in range(2)]
    own = lax.broadcasted_iota(jnp.int32, (rows, 128), 0) + start

    @pl.loop(0, n // 128)
    def _(c):
        lanes = pl.ds(pl.multiple_of(c * 128, 128), 128)
        lane_id = lax.broadcasted_iota(jnp.int32, (rows, 128), 1) + c * 128
        ids = []
        for t in range(3):
            gap = (lane_id - own) if t == 0 else (jnp.broadcast_to(box_row[t - 1:t, lanes], (rows, 128)) - cols[t - 1])
            size = jnp.abs(gap)
            if t > 0:
                size = size >> 2
            bucket = lane_take(steps, jnp.minimum(size, 91)) + jnp.where(gap > 0, 16, 0)
            ids.append(bucket)
            ids_ref[t, :, lanes] = bucket.astype(f32)
        ok = jnp.broadcast_to(page_row[:, lanes], (rows, 128)) == allowed_col
        for h in range(heads):
            total = None
            for t in range(3):
                table = jnp.broadcast_to(tab_ref[t * heads + h:t * heads + h + 1, :], (rows, 128))
                part = lane_take(table, ids[t])
                total = part if total is None else total + part
            bias_ref[h, :, lanes] = jnp.where(ok, total, -1e30)


def bias_gather_kernel(heads, rows, n, G, halves, count, *refs):
    ins, srcs = refs[:6], refs[6:6 + count]
    bias_ref, ids_ref = refs[6 + count:8 + count]
    outs, sems = refs[8 + count:8 + 2 * count], refs[8 + 2 * count:]
    now = pl.program_id(0)
    comm = Gather(G, halves, srcs, outs, *sems)
    beside(comm, n // rows, now, lambda: bias_tile(now * rows, heads, rows, n, *ins, bias_ref, ids_ref))


def bias_and_gather(tables, boxes, pages, shards, halves, wide, cid):
    heads, n, G, rows = tables.shape[1], pages.shape[0], wide // 4, 64
    tab = jnp.pad(tables.astype(f32).reshape(3, 32, heads).transpose(0, 2, 1).reshape(3 * heads, 32), ((0, 0), (0, 96)))
    lane = jnp.arange(128, dtype=jnp.int32)
    steps = sum([(lane >= e).astype(jnp.int32) for e in EDGES])[None]
    count = len(shards)
    outs = pl.pallas_call(functools.partial(bias_gather_kernel, heads, rows, n, G, halves, count),
        grid=(n // rows,),
        out_shape=(jax.ShapeDtypeStruct((heads, n, n), f32), jax.ShapeDtypeStruct((3, n, n), f32)) + gathered_shapes(shards, wide),
        in_specs=[pl.BlockSpec((1, 128), lambda i: (0, 0)), pl.BlockSpec((3 * heads, 128), lambda i: (0, 0)),
                  pl.BlockSpec((rows, 2), lambda i: (i, 0)), pl.BlockSpec((2, n), lambda i: (0, 0)),
                  pl.BlockSpec((rows, 1), lambda i: (i, 0)), pl.BlockSpec((1, n), lambda i: (0, 0))] + [ANY] * count,
        out_specs=(pl.BlockSpec((heads, rows, n), lambda i: (0, i, 0)), pl.BlockSpec((3, rows, n), lambda i: (0, i, 0))) + (ANY,) * count,
        scratch_shapes=gather_scratch(G, halves, count), compiler_params=params(cid), name="layout_bias_gather")(
            steps, tab, boxes.T, boxes, pages[:, None], pages[None], *shards)
    return outs[0], outs[1], [flat(a) for a in outs[2:]]


def half_of(v, e):
    lane = lax.broadcasted_iota(jnp.int32, v.shape, 1)
    return jnp.where((lane >= 64) == (e == 1), v, jnp.zeros_like(v))


def join(a, b):
    lane = lax.broadcasted_iota(jnp.int32, a.shape, 1)
    return jnp.where(lane < 64, a, b)


def fwd_tile(q_ref, k_ref, v_ref, bias_ref, o_ref, lse_ref):
    q, k, v = q_ref[...], k_ref[...], v_ref[...]
    outs, lses = [], []
    for e in range(2):
        s = lax.dot_general(half_of(q, e), k, NT, preferred_element_type=f32) + bias_ref[e]
        peak = jnp.max(s, axis=1, keepdims=True)
        p = jnp.exp(s - peak)
        total = jnp.sum(p, axis=1, keepdims=True)
        outs.append(jnp.dot(p.astype(bf16), v, preferred_element_type=f32) / total)
        lses.append(peak + jnp.log(total))
    o_ref[...] = join(*outs).astype(bf16)
    lse_ref[0] = jnp.concatenate(lses, axis=1)


def fwd_kernel(steps, tiles, G, halves, count, *refs):
    ins, srcs = refs[:4], refs[4:4 + count]
    mid = refs[4 + count:6 + count]
    outs, sems = refs[6 + count:6 + 2 * count], refs[6 + 2 * count:]
    now = pl.program_id(0) * tiles + pl.program_id(1)
    beside(Gather(G, halves, srcs, outs, *sems), steps, now, lambda: fwd_tile(*ins, *mid))


def attn_fwd_and_gather(qkv, bias, shards, halves, wide, cid, tq=256):
    n, width = qkv.shape[0], qkv.shape[1] // 3
    pairs, tiles, count, G = width // 128, n // tq, len(shards), wide // 4
    outs = pl.pallas_call(functools.partial(fwd_kernel, pairs * tiles, tiles, G, halves, count), grid=(pairs, tiles),
        out_shape=(jax.ShapeDtypeStruct((n, width), bf16), jax.ShapeDtypeStruct((pairs, n, 2), f32)) + gathered_shapes(shards, wide),
        in_specs=[pl.BlockSpec((tq, 128), lambda p, i: (i, p)), pl.BlockSpec((n, 128), lambda p, i: (0, p + pairs)),
                  pl.BlockSpec((n, 128), lambda p, i: (0, p + 2 * pairs)), pl.BlockSpec((2, tq, n), lambda p, i: (p, i, 0))] + [ANY] * count,
        out_specs=(pl.BlockSpec((tq, 128), lambda p, i: (i, p)), pl.BlockSpec((1, tq, 2), lambda p, i: (p, i, 0))) + (ANY,) * count,
        scratch_shapes=gather_scratch(G, halves, count), compiler_params=params(cid), name="attention_gather")(qkv, qkv, qkv, bias, *shards)
    return outs[0], outs[1], [flat(a) for a in outs[2:]]


def bwd_tile(first, last, q_ref, k_ref, v_ref, bias_ref, o_ref, do_ref, lse_ref, dq_ref, dk_ref, dv_ref, g_ref, dkt, dvt):
    @pl.when(first)
    def _():
        dkt[...] = jnp.zeros_like(dkt)
        dvt[...] = jnp.zeros_like(dvt)

    q, k, v, do = q_ref[...], k_ref[...], v_ref[...], do_ref[...]
    prod = do.astype(f32) * o_ref[...].astype(f32)
    dqs = []
    for e in range(2):
        qm, dom = half_of(q, e), half_of(do, e)
        s = lax.dot_general(qm, k, NT, preferred_element_type=f32) + bias_ref[e]
        p = jnp.exp(s - lse_ref[0, :, e:e + 1])
        dp = lax.dot_general(dom, v, NT, preferred_element_type=f32)
        inner = jnp.sum(half_of(prod, e), axis=1, keepdims=True)
        g = (p * (dp - inner)).astype(bf16)
        g_ref[e] = g
        dqs.append(jnp.dot(g, k, preferred_element_type=f32))
        dvt[...] += jnp.dot(dom.T, p.astype(bf16), preferred_element_type=f32)
        dkt[...] += jnp.dot(qm.T, g, preferred_element_type=f32)
    dq_ref[...] = join(*dqs).astype(bf16)

    @pl.when(last)
    def _():
        dk_ref[...] = dkt[...].T.astype(bf16)
        dv_ref[...] = dvt[...].T.astype(bf16)


def bwd_kernel(steps, tiles, G, halves, count, *refs):
    ins, parts = refs[:7], refs[7:7 + count]
    mid = refs[7 + count:11 + count]
    outs, accs, sems = refs[11 + count:11 + 2 * count], refs[11 + 2 * count:13 + 2 * count], refs[13 + 2 * count:]
    i = pl.program_id(1)
    comm = Scatter(G, halves, parts, outs, *sems)
    beside(comm, steps, pl.program_id(0) * tiles + i, lambda: bwd_tile(i == 0, i == tiles - 1, *ins, *mid, *accs))


def shard_shapes(parts, wide):
    return tuple(jax.ShapeDtypeStruct((p.shape[0] // wide, p.shape[1]), f32) for p in parts)


def attn_bwd_and_scatter(qkv, bias, o, do, lse, parts, halves, wide, cid, tq=256):
    n, width = qkv.shape[0], qkv.shape[1] // 3
    pairs, tiles, count, G = width // 128, n // tq, len(parts), wide // 4
    tile = pl.BlockSpec((tq, 128), lambda p, i: (i, p))
    full = pl.BlockSpec((n, 128), lambda p, i: (0, p))
    outs = pl.pallas_call(functools.partial(bwd_kernel, pairs * tiles, tiles, G, halves, count), grid=(pairs, tiles),
        out_shape=(jax.ShapeDtypeStruct((n, width), bf16),) * 3 + (jax.ShapeDtypeStruct((2 * pairs, n, n), bf16),) + shard_shapes(parts, wide),
        in_specs=[tile, pl.BlockSpec((n, 128), lambda p, i: (0, p + pairs)), pl.BlockSpec((n, 128), lambda p, i: (0, p + 2 * pairs)),
                  pl.BlockSpec((2, tq, n), lambda p, i: (p, i, 0)), tile, tile, pl.BlockSpec((1, tq, 2), lambda p, i: (p, i, 0))] + [ANY] * count,
        out_specs=(tile, full, full, pl.BlockSpec((2, tq, n), lambda p, i: (p, i, 0))) + (whole_vmem(),) * count,
        scratch_shapes=[pltpu.VMEM((128, n), f32), pltpu.VMEM((128, n), f32)] + scatter_scratch(G, halves, parts[0].shape[0] // wide),
        compiler_params=params(cid), name="attention_back_scatter")(qkv, qkv, qkv, bias, o, do, lse, *[spread(p, wide) for p in parts])
    return outs[:4], outs[4:]


def hist_tile(first, heads, rows, n, g_ref, ids_ref, out_ref, gs):
    @pl.when(first)
    def _():
        out_ref[...] = jnp.zeros_like(out_ref)

    for h in range(heads):
        for c in range(n // 128):
            gs[c, h * rows:(h + 1) * rows, :] = g_ref[h, :, c * 128:(c + 1) * 128].astype(f32)
    label = lax.broadcasted_iota(jnp.int32, (32, n), 0).astype(bf16)
    one, zero = jnp.ones((32, n), bf16), jnp.zeros((32, n), bf16)
    acc = jnp.zeros((heads, 96), f32)
    for r in range(rows):
        grow = jnp.concatenate([gs[c, pl.ds(r, heads, stride=rows), :] for c in range(n // 128)], axis=1).astype(bf16)
        hots = []
        for t in range(3):
            row = jnp.broadcast_to(ids_ref[t, r:r + 1, :], (32, n)).astype(bf16)
            hots.append(jnp.where(row == label, one, zero))
        acc = acc + lax.dot_general(grow, jnp.concatenate(hots, axis=0), NT, preferred_element_type=f32)
    out_ref[...] += acc


def hist_kernel(heads, rows, n, G, halves, count, *refs):
    ins, parts, out_ref = refs[:2], refs[2:2 + count], refs[2 + count]
    outs, gs, sems = refs[3 + count:3 + 2 * count], refs[3 + 2 * count], refs[4 + 2 * count:]
    now = pl.program_id(0)
    comm = Scatter(G, halves, parts, outs, *sems)
    beside(comm, n // rows, now, lambda: hist_tile(now == 0, heads, rows, n, *ins, out_ref, gs))


def hist_and_scatter(g, ids, parts, halves, wide, cid):
    heads, n, _ = g.shape
    rows, count, G = 16, len(parts), wide // 4
    outs = pl.pallas_call(functools.partial(hist_kernel, heads, rows, n, G, halves, count), grid=(n // rows,),
        out_shape=(jax.ShapeDtypeStruct((heads, 96), f32),) + shard_shapes(parts, wide),
        in_specs=[pl.BlockSpec((heads, rows, n), lambda i: (0, i, 0)), pl.BlockSpec((3, rows, n), lambda i: (0, i, 0))] + [ANY] * count,
        out_specs=(pl.BlockSpec((heads, 96), lambda i: (0, 0)),) + (whole_vmem(),) * count,
        scratch_shapes=[pltpu.VMEM((n // 128, heads * rows, 128), f32)] + scatter_scratch(G, halves, parts[0].shape[0] // wide),
        compiler_params=params(cid), name="table_grad_scatter")(g, ids, *[spread(p, wide) for p in parts])
    return outs[0], outs[1:]


D = pltpu.SemaphoreType.DMA


def place():
    me = lax.axis_index("wide")
    return me // 4, (me // 2) % 2, me % 2


def wide_id(z, y, x):
    return {"wide": z * 4 + y * 2 + x}


def remote(src, dst, send, recv, target):
    return pltpu.make_async_remote_copy(src_ref=src, dst_ref=dst, send_sem=send, recv_sem=recv, device_id=target, device_id_type=MESH)


def greet(G, far):
    z, y, x = place()
    bar = pltpu.get_barrier_semaphore()
    sig = lambda t: pl.semaphore_signal(bar, inc=1, device_id=t, device_id_type=MESH)
    sig(wide_id(z, 1 - y, x))
    sig(wide_id(z, y, 1 - x))
    if far:
        for k in range(1, G):
            sig(wide_id((z + k) % G, y, x))
        pl.semaphore_wait(bar, 2 + G - 1)
    else:
        @pl.when(z > 0)
        def _():
            sig(wide_id(z - 1, y, x))

        @pl.when(z < G - 1)
        def _():
            sig(wide_id(z + 1, y, x))

        pl.semaphore_wait(bar, 2 + (z > 0).astype(jnp.int32) + (z < G - 1).astype(jnp.int32))


class Gather:
    def __init__(self, G, halves, srcs, outs, local_sem, zs, zr, ns, nr):
        self.G, self.halves, self.srcs, self.outs, self.local_sem = G, halves, srcs, outs, local_sem
        self.zs, self.zr, self.ns, self.nr = zs, zr, ns, nr
        self.most = max(len(h) for h in halves)
        self.z, self.y, self.x = place()

    def hop(self, own, zz, yy, xx, h, way, j):
        target = wide_id(self.z, 1 - self.y, self.x) if way == "y" else wide_id(self.z, self.y, 1 - self.x)
        copies = []
        for n, (a, c, w) in enumerate(self.halves[h]):
            slot = (zz * 6 + j) * self.most + n
            dst = self.outs[a].at[zz, yy, xx, :, pl.ds(c, w)]
            copies.append(remote(self.srcs[a].at[:, pl.ds(c, w)] if own else dst, dst, self.ns.at[slot], self.nr.at[slot], target))
        return copies

    def second_stage(self, zz, own=False):
        return self.hop(own, zz, self.y, self.x, 0, "y", 0) + self.hop(own, zz, self.y, self.x, 1, "x", 1)

    def third_stage(self, zz, own=False):
        return self.hop(own, zz, self.y, self.x, 0, "x", 2) + self.hop(own, zz, self.y, self.x, 1, "y", 3)

    def last_stage(self, zz):
        return self.hop(False, zz, 1 - self.y, self.x, 0, "x", 4) + self.hop(False, zz, self.y, 1 - self.x, 1, "y", 5)

    def relay(self, own, zz, step, way):
        copies = []
        for a in range(len(self.srcs)):
            slot = (way * (self.G - 1) + step) * len(self.srcs) + a
            dst = self.outs[a].at[zz, self.y, self.x]
            copies.append(remote(self.srcs[a] if own else dst, dst, self.zs.at[slot], self.zr.at[slot],
                                 wide_id(self.z + (1 if way == 0 else -1), self.y, self.x)))
        return copies

    def can(self, way):
        return self.z < self.G - 1 if way == 0 else self.z > 0

    def source(self, d, way):
        return (self.z - d, self.z - d >= 0) if way == 0 else (self.z + d, self.z + d < self.G)

    def keep(self):
        return [pltpu.make_async_copy(s, o.at[self.z, self.y, self.x], self.local_sem.at[a]) for a, (s, o) in enumerate(zip(self.srcs, self.outs))]

    def begin(self):
        for way in range(2):
            @pl.when(self.can(way))
            def _():
                for c in self.relay(True, self.z, 0, way):
                    c.start()
        for c in self.second_stage(self.z, True) + self.third_stage(self.z, True) + self.keep():
            c.start()

    def turn(self, zz):
        for c in self.hop(False, zz, 1 - self.y, self.x, 0, "y", 0) + self.hop(False, zz, self.y, 1 - self.x, 1, "x", 1):
            c.wait_recv()
        for c in self.last_stage(zz):
            c.start()

    def step(self, d):
        for way in range(2):
            zz, there = self.source(d, way)

            @pl.when(there)
            def _():
                for c in self.relay(False, zz, d - 1, way):
                    c.wait_recv()

                @pl.when(self.can(way))
                def _():
                    for c in self.relay(False, zz, d, way):
                        c.start()

                for c in self.second_stage(zz):
                    c.start()
        for way in range(2):
            zz, there = self.source(d, way)

            @pl.when(there)
            def _():
                for c in self.third_stage(zz):
                    c.start()

    def turns(self, d):
        if d == 0:
            self.turn(self.z)
            return
        for way in range(2):
            zz, there = self.source(d, way)

            @pl.when(there)
            def _():
                self.turn(zz)

    def finish(self):
        y, x = self.y, self.x

        @pl.loop(0, self.G)
        def _(zz):
            for c in (self.hop(False, zz, y, 1 - x, 0, "x", 2) + self.hop(False, zz, 1 - y, x, 1, "y", 3)
                      + self.hop(False, zz, 1 - y, 1 - x, 0, "x", 4) + self.hop(False, zz, 1 - y, 1 - x, 1, "y", 5)):
                c.wait_recv()
            for c in self.second_stage(zz) + self.third_stage(zz) + self.last_stage(zz):
                c.wait_send()

        for way in range(2):
            @pl.when(self.can(way))
            def _():
                for c in self.relay(True, self.z, 0, way):
                    c.wait_send()
                for d in range(1, self.G - 1):
                    zz, there = self.source(d, way)

                    @pl.when(there)
                    def _():
                        for c in self.relay(False, zz, d, way):
                            c.wait_send()
        for c in self.keep():
            c.wait()

    def events(self):
        G = self.G
        first = lambda: (greet(G, False), self.begin())
        ev = [(0.0, first), (0.7, lambda: self.turns(0))]
        for d in range(1, G):
            ev += [(1.15 * d, functools.partial(self.step, d)), (1.3 * d + 1.2, functools.partial(self.turns, d))]
        return sorted(ev, key=lambda e: e[0]), self.finish


def gather_scratch(G, halves, arrays):
    most = max(len(h) for h in halves)
    return [D((arrays,)), D((2 * (G - 1) * arrays,)), D((2 * (G - 1) * arrays,)), D((6 * G * most,)), D((6 * G * most,))]


class Scatter:
    def __init__(self, G, halves, parts, outs, r1a, r1b, o1a, o1b, r2a, r2b, r3, own, lsem, s1, v1, s2, v2, s3, v3):
        self.__dict__.update(locals())
        self.most = max(len(h) for h in halves)
        self.wa, self.wb = [sum(p[2] for p in h) for h in halves]
        self.R = parts[0].shape[3]
        self.z, self.y, self.x = place()
        self.order = sorted(range(1, G), key=lambda k: min(k, G - k), reverse=True) + [0]

    def zk(self, k):
        return (self.z + k) % self.G

    def neighbour(self, way):
        return wide_id(self.z, 1 - self.y, self.x) if way == "y" else wide_id(self.z, self.y, 1 - self.x)

    def pieces(self, h):
        at, out = 0, []
        for n, (a, c, w) in enumerate(self.halves[h]):
            out.append((n, a, pl.ds(c, w), pl.ds(at, w)))
            at += w
        return out

    def one(self, k):
        z, cs = self.zk(k), []
        for n, a, src, dst in self.pieces(0):
            slot = (2 * k) * self.most + n
            cs.append(remote(self.parts[a].at[z, :, 1 - self.x, :, src], self.r1a.at[k, :, :, dst], self.s1.at[slot], self.v1.at[slot], self.neighbour("x")))
        for n, a, src, dst in self.pieces(1):
            slot = (2 * k + 1) * self.most + n
            cs.append(remote(self.parts[a].at[z, 1 - self.y, :, :, src], self.r1b.at[k, :, :, dst], self.s1.at[slot], self.v1.at[slot], self.neighbour("y")))
        return cs

    def load(self, k):
        z, cs = self.zk(k), []
        for n, a, src, dst in self.pieces(0):
            cs.append(pltpu.make_async_copy(self.parts[a].at[z, :, self.x, :, src], self.o1a.at[k, :, :, dst], self.lsem.at[(2 * k) * self.most + n]))
        for n, a, src, dst in self.pieces(1):
            cs.append(pltpu.make_async_copy(self.parts[a].at[z, self.y, :, :, src], self.o1b.at[k, :, :, dst], self.lsem.at[(2 * k + 1) * self.most + n]))
        return cs

    def two(self, k):
        return [remote(self.o1a.at[k, 1 - self.y], self.r2a.at[k], self.s2.at[2 * k], self.v2.at[2 * k], self.neighbour("y")),
                remote(self.o1b.at[k, 1 - self.x], self.r2b.at[k], self.s2.at[2 * k + 1], self.v2.at[2 * k + 1], self.neighbour("x"))]

    def three(self, k):
        return remote(self.own.at[k], self.r3.at[k - 1], self.s3.at[k - 1], self.v3.at[k - 1], wide_id(self.zk(k), self.y, self.x))

    def launch(self, k):
        for c in self.one(k) + self.load(k):
            c.start()

    def begin(self):
        for k in self.order[:2]:
            self.launch(k)

    def rows(self, count, body):
        step = min(16, count)

        @pl.loop(0, count // step)
        def _(i):
            body(pl.ds(pl.multiple_of(i * step, step), step))

    def add_one(self, n):
        k = self.order[n]
        for c in self.one(k):
            c.wait_recv()
        for c in self.load(k):
            c.wait()
        for mine, got in ((self.o1a, self.r1a), (self.o1b, self.r1b)):
            def body(r):
                for j in range(2):
                    mine[k, j, r, :] = (mine[k, j, r, :].astype(f32) + got[k, j, r, :].astype(f32)).astype(bf16)

            self.rows(self.R, body)
        for c in self.two(k):
            c.start()
        if n + 2 < self.G:
            self.launch(self.order[n + 2])

    def add_two(self, n):
        k = self.order[n]
        for c in self.two(k):
            c.wait_recv()

        def body(r):
            self.own[k, r, pl.ds(0, self.wa)] = (self.o1a[k, self.y, r, :].astype(f32) + self.r2a[k, r, :].astype(f32)).astype(bf16)
            self.own[k, r, pl.ds(self.wa, self.wb)] = (self.o1b[k, self.x, r, :].astype(f32) + self.r2b[k, r, :].astype(f32)).astype(bf16)

        self.rows(self.R, body)
        if k:
            self.three(k).start()

    def finish(self):
        self.add_two(self.G - 1)
        for k in range(1, self.G):
            self.three(k).wait_recv()

        def body(r):
            for h in range(2):
                for _, a, src, dst in self.pieces(h):
                    cols = pl.ds(dst.start + h * self.wa, dst.size)
                    total = self.own[0, r, cols].astype(f32)
                    for k in range(self.G - 1):
                        total = total + self.r3[k, r, cols].astype(f32)
                    self.outs[a][r, src] = total

        self.rows(self.R, body)
        for k in range(self.G):
            for c in self.one(k) + self.two(k):
                c.wait_send()
            if k:
                self.three(k).wait_send()

    def events(self):
        G = self.G
        first = lambda: (greet(G, True), self.begin())
        ev = [(0.0, first), (1.1, lambda: self.add_one(0))]
        for n in range(1, G):
            ev += [(1.5 * n + 0.65, functools.partial(self.add_one, n)), (1.5 * n + 1.1, functools.partial(self.add_two, n - 1))]
        return sorted(ev, key=lambda e: e[0]), self.finish


def scatter_scratch(G, halves, R):
    most = max(len(h) for h in halves)
    a, b = [sum(p[2] for p in h) for h in halves]
    V = lambda *s: pltpu.VMEM(s, bf16)
    return [V(G, 2, R, a), V(G, 2, R, b), V(G, 2, R, a), V(G, 2, R, b), V(G, R, a), V(G, R, b), V(G - 1, R, a + b), V(G, R, a + b),
            D((2 * G * most,)), D((2 * G * most,)), D((2 * G * most,)), D((2 * G,)), D((2 * G,)), D((G - 1,)), D((G - 1,))]


def beside(comm, steps, now, compute):
    events, finish = comm.events()
    units = 1.55 * comm.G
    for n in range(steps):
        here = [act for t, act in events if min(steps - 1, int(-(-t * steps // units))) == n]
        if here:
            @pl.when(now == n)
            def _():
                for act in here:
                    act()
    compute()

    @pl.when(now == steps - 1)
    def _():
        finish()


ANY = pl.BlockSpec(memory_space=pl.ANY)


def whole_vmem():
    return pl.BlockSpec(memory_space=pltpu.VMEM)


def spread(a, wide):
    return a.reshape(wide // 4, 2, 2, a.shape[0] // wide, a.shape[1])


def gathered_shapes(shards, wide):
    return tuple(jax.ShapeDtypeStruct((wide // 4, 2, 2) + s.shape, s.dtype) for s in shards)


def flat(a):
    return a.reshape(-1, a.shape[-1])


def sum_kernel(G, src, out, acc, got, gz, s, v, sz, vz):
    z, y, x = place()
    core = {"narrow": 1 - lax.axis_index("narrow")}
    ynb, xnb = wide_id(z, 1 - y, x), wide_id(z, y, 1 - x)
    far = [wide_id((z + k) % G, y, x) for k in range(1, G)]
    bar = pltpu.get_barrier_semaphore()
    for t in [core, ynb, xnb] + far:
        pl.semaphore_signal(bar, inc=1, device_id=t, device_id_type=MESH)
    pl.semaphore_wait(bar, 3 + len(far))
    acc[0] = src[...]
    for n, t in enumerate((core, xnb, ynb)):
        c = remote(acc.at[n], got.at[n], s.at[n], v.at[n], t)
        c.start()
        c.wait()
        acc[n + 1] = acc[n] + got[n]
    gz[z] = acc[3]
    sent = [remote(acc.at[3], gz.at[z], sz.at[k], vz.at[z], t) for k, t in enumerate(far)]
    for c in sent:
        c.start()
    for k in range(1, G):
        zz = (z + k) % G
        remote(acc.at[3], gz.at[zz], sz.at[k - 1], vz.at[zz], far[k - 1]).wait_recv()
    for c in sent:
        c.wait_send()
    total = gz[0]
    for k in range(1, G):
        total = total + gz[k]
    out[...] = total


def sum_all(part, wide, cid):
    G, rows = wide // 4, part.shape[0]
    V = lambda k: pltpu.VMEM((k, rows, 128), f32)
    return pl.pallas_call(functools.partial(sum_kernel, G), out_shape=jax.ShapeDtypeStruct(part.shape, f32),
        in_specs=[whole_vmem()], out_specs=whole_vmem(),
        scratch_shapes=[V(4), V(3), V(G), D((3,)), D((3,)), D((G - 1,)), D((G,))],
        compiler_params=pltpu.CompilerParams(collective_id=cid, has_side_effects=True), name="small_sums")(part)


epsilon = 1e-06


def norm_plain(values, gain_row):
    factor = lax.rsqrt(jnp.mean(values * values, axis=-1, keepdims=True) + epsilon)
    return values * factor * gain_row


def gated_unit(gate_pre, up_pre):
    return jax.nn.gelu(gate_pre, approximate=True) * up_pre


def times(a, b):
    return jnp.dot(a, b, preferred_element_type=f32)


def times_transposed(a, b):
    return lax.dot_general(a, b, NT, preferred_element_type=f32)


def transposed_times(a, b):
    return lax.dot_general(a, b, (((0,), (0,)), ((), ())), preferred_element_type=f32)


def swap(a):
    return lax.ppermute(a, "narrow", [(0, 1), (1, 0)])


def both(a):
    return a.astype(f32) + swap(a).astype(f32)


def local(tokens, cotangent, pages, boxes, gain_attn, gain_ffn, bias_tables, w_query, w_key, w_value, w_out, w_gate, w_up, w_down):
    wide, narrow = lax.axis_size("wide"), lax.axis_size("narrow")
    heads_all = bias_tables.shape[1]
    heads = heads_all // narrow
    rows = tokens.shape[0]
    core = lax.axis_index("narrow")
    tables = lax.dynamic_slice_in_dim(bias_tables, core * heads, heads, 1)
    inner, ff = w_query.shape[1], w_gate.shape[1]
    mine = lambda a: lax.dynamic_slice_in_dim(a, core * rows, rows, 0)

    all_tokens = lax.all_gather(tokens, "narrow", axis=0, tiled=True)
    all_cot = lax.all_gather(cotangent, "narrow", axis=0, tiled=True)
    keys_to = 2 * inner
    bias, ids, (w_first, full_out, full_gate, full_up) = bias_and_gather(
        tables, boxes, pages, [jnp.concatenate([w_query, w_key, w_value], axis=1), w_out.T, w_gate, w_up],
        (((2, 0, ff), (0, 0, keys_to)), ((3, 0, ff), (1, 0, inner), (0, keys_to, inner))), wide, 1)

    x = all_tokens.astype(f32)
    gain_one, gain_two = gain_attn.astype(f32), gain_ffn.astype(f32)
    normed = norm_plain(x, gain_one).astype(bf16)
    qkv = times(normed, w_first).astype(bf16)
    cut = (ff // 128 + 1) // 2 * 128
    attended, lse, (full_down,) = attn_fwd_and_gather(qkv, bias, [w_down.T], (((0, 0, cut),), ((0, cut, ff - cut),)), wide, 2)
    hidden = x + both(times_transposed(attended, full_out).astype(bf16))
    normed_two = norm_plain(hidden, gain_two).astype(bf16)
    gate_pre, up_pre = times(normed_two, full_gate), times(normed_two, full_up)
    hidden_ff = gated_unit(gate_pre, up_pre).astype(bf16)
    down = times_transposed(hidden_ff, full_down).astype(bf16)
    output = (mine(hidden) + lax.psum_scatter(down, "narrow", scatter_dimension=0, tiled=True).astype(f32)).astype(bf16)

    grad_w_down = transposed_times(all_cot, hidden_ff)
    grad_ff = times(all_cot, full_down)
    _, gated_pull = jax.vjp(gated_unit, gate_pre, up_pre)
    grad_gate, grad_up = [g.astype(bf16) for g in gated_pull(grad_ff)]
    grad_w_gate = transposed_times(normed_two, grad_gate)
    grad_w_up = transposed_times(normed_two, grad_up)
    grad_two = both((times_transposed(grad_gate, full_gate) + times_transposed(grad_up, full_up)).astype(bf16))
    _, pull_two = jax.vjp(lambda h: norm_plain(h, gain_two), hidden)
    grad_hidden = all_cot.astype(f32) + pull_two(grad_two)[0]
    own_hidden = mine(hidden)
    grad_gain_two = jnp.sum(mine(grad_two) * own_hidden * lax.rsqrt(jnp.mean(own_hidden * own_hidden, axis=-1, keepdims=True) + epsilon), axis=0)
    grad_low = grad_hidden.astype(bf16)
    grad_w_out = transposed_times(grad_low, attended)
    grad_attended = times(grad_low, full_out).astype(bf16)
    (dq, dk, dv, g), (s_down, s_out) = attn_bwd_and_scatter(
        qkv, bias, attended, grad_attended, lse, [grad_w_down.astype(bf16), grad_w_out.astype(bf16)],
        (((0, 0, keys_to),), ((0, keys_to, ff - keys_to), (1, 0, inner))), wide, 3)
    dqkv = jnp.concatenate([dq, dk, dv], axis=1)
    mid = 3 * inner // 2
    table_part, (s_gate, s_up, s_first) = hist_and_scatter(
        g, ids, [grad_w_gate.astype(bf16), grad_w_up.astype(bf16), transposed_times(normed, dqkv).astype(bf16)],
        (((0, 0, ff), (2, 0, mid)), ((1, 0, ff), (2, mid, mid))), wide, 4)
    grad_normed = lax.psum_scatter(times_transposed(dqkv, w_first).astype(bf16), "narrow", scatter_dimension=0, tiled=True).astype(f32)
    own = tokens.astype(f32)
    _, pull_one = jax.vjp(norm_plain, own, gain_one)
    grad_tokens_norm, grad_gain_one = pull_one(grad_normed)
    grad_tokens = mine(grad_hidden) + grad_tokens_norm
    table_part = lax.dynamic_update_slice(jnp.zeros((bias_tables.shape[0], heads_all), f32), table_part.T, (jnp.int32(0), core * heads))
    sizes = [gain_one.size, gain_two.size, table_part.size]
    small = sum_all(jnp.concatenate([grad_gain_one, grad_gain_two, table_part.reshape(-1)]).reshape(-1, 128), wide, 5).reshape(-1)
    one, two, table = jnp.split(small, [sizes[0], sizes[0] + sizes[1]])
    s_query, s_key, s_value = jnp.split(s_first, 3, axis=1)
    return (output, grad_tokens, one, two, table.reshape(bias_tables.shape), s_query, s_key, s_value, s_out.T, s_gate, s_up, s_down.T)


def solution(mesh):
    rows, cols, tall = P(("wide", "narrow"), None), P("wide", "narrow"), P("narrow", "wide")
    in_specs = (rows, rows, P("wide"), P(None, "wide"), P(), P(), P(), cols, cols, cols, tall, cols, cols, tall)
    out_specs = (rows, rows, P(), P(), P(), cols, cols, cols, tall, cols, cols, tall)
    return jax.shard_map(local, mesh=mesh, in_specs=in_specs, out_specs=out_specs, check_vma=False)
```

time: 623 us -> 424 us (0.68)
  Pallas kernels: 456 us -> 274 us
  matrix products: 83.8 us -> 73.5 us
  other arithmetic: 35.1 us -> 26.2 us
    pallas_call x8 -> x4, Pallas kernels: 442 us -> 261 us  [the longest x1 100 us: bias_and_gather(): pl.pallas_call(functools.partial(bias_gather_kernel, heads, rows, n, G, h...]
    concatenate x2 -> x0, other arithmetic: 9.63 us -> none  [the longest x1 8.76 us: local(): jnp.concatenate([g.astype(bf16) for g in (grad_w_out, grad_w_gate, grad_w...]
  transfers between devices with their start and end apart: 6 -> 6, of which waited for: 0 -> 0; matrix products, arithmetic and copies ran while one was open for 16% -> 19% of each run, Pallas kernels for 72% -> 63%
where the time goes in v2:
time: 424 us; the launch traced here: 416 us
  Pallas kernels  274 us (65%)
  matrix products  73.5 us (17%)
  other arithmetic  26.2 us (6%)
  local copies, waits for them, and re-layouts  25.8 us (6%)
  between operations  14.5 us (3%)
    pallas_call x1, Pallas kernels, bias_and_gather(): pl.pallas_call(functools.partial(bias_gather_kernel, heads, rows, n, G, h...  100 us
    pallas_call x1, Pallas kernels, hist_and_scatter(): pl.pallas_call(functools.partial(hist_kernel, heads, rows, n, G, halves,...  82.4 us
    pallas_call x1, Pallas kernels, attn_bwd_and_scatter(): pl.pallas_call(functools.partial(bwd_kernel, pairs * tiles, tiles, G, hal...  44.5 us
    pallas_call x1, Pallas kernels, attn_fwd_and_gather(): pl.pallas_call(functools.partial(fwd_kernel, pairs * tiles, tiles, G, hal...  33.4 us
    dot_general x5, matrix products, times(): return jnp.dot(a, b, preferred_element_type=f32)  30.2 us
    dot_general x5, matrix products, transposed_times(): lax.dot_general(a, b, (((0,), (0,)), ((), ())), preferred_element_type=f32)  24.3 us
    unnamed x88, local copies, waits for them, and re-layouts  20.3 us
    dot_general x5, matrix products, times_transposed(): return lax.dot_general(a, b, NT, preferred_element_type=f32)  18.9 us
  transfers between devices with their start and end apart: 6, of which 0 were waited for; matrix products, arithmetic and copies ran while one was open for 19% of the time, Pallas kernels for 63%

profile of v2, /device:TPU:0, one launch (start us, length us, event | category | flops | bytes accessed | tf_op | source)
XLA Modules:
  0.0 415.8 jit_solution(6733358459792680302)
XLA Ops:
  7.3 2.4 copy.38
  15.2 100.3 %layout_bias_gather.1 = (f32[8,1024,1024]{2,1,0:T(8,128)}, f32[3,1024,1024]{2,1,0:T(8,128)}, bf16[4,2,2,64,1536]{4,3,2,1,0:T(8,128)(2,1)}, bf16[4,2,2,64,512]{4,...) custom-call(s32[1,128]{1,0:T(1,128)} %fusion.38.refs_0_, ...), custom_call_target="tpu_custom_call" | custom-call | tf_op jit(solution)/shard_map/layout_bias_gather/pallas_call | solution.py:71
  115.5 2.1 fusion.8
  117.6 7.9 %convolution_convert_fusion.4.refs_0_.refs_1_.refs_2_ = bf16[1024,1536]{1,0:T(8,128)(2,1)} fusion(bf16[1024,1536]{1,0:T(8,128)(2,1)} %bitcast.80, bf16[1024,1024]{0,1:T(8,128)(2,1)} %all-gather.3.cloned.1.call-done, f32[1024]{0:T(1024)S(1)} %convert_element_type.244, f32[1024]{0:T(1024)S(1)} %add_rsqrt_fusion), kind=kOutput, calls=%fused_computation.31 | convolution fusion | flops 3226992640 | bytes 8396800 | tf_op jit(solution)/shard_map/dot_general | solution.py:613
  125.5 33.4 %attention_gather.1 = (bf16[1024,512]{1,0:T(8,128)(2,1)}, f32[4,1024,2]{2,1,0:T(8,128)}, bf16[4,2,2,64,1408]{4,3,2,1,0:T(8,128)(2,1)}) custom-call(bf16[1024,1536]{1,0:T(8,128)(2,1)} %convolution_convert_fusion.4.refs_0_.refs_1_.refs_2_, bf16[1024,1536]{1,0:T(8,128)(2,1)} %convolution_convert_fusion.4.refs_0_.refs_1_.refs_2_, ...), custom_call_target="tpu_custom_call" | custom-call | tf_op jit(solution)/shard_map/attention_gather/pallas_call | solution.py:118
  158.9 2.5 convolution_convert_fusion.7
  161.6 6.3 %fusion.54 = f32[1408,1024]{0,1:T(8,128)S(1)} fusion(bf16[1024,1408]{1,0:T(8,128)(2,1)} %bitcast.86, bf16[1024,1024]{0,1:T(8,128)(2,1)} %all-gather.5.cloned.1.call-done), kind=kOutput, calls=%fused_computation.118 | convolution fusion | flops 2952790016 | bytes 10747904 | tf_op jit(solution)/shard_map/dot_general | solution.py:613
  167.9 2.8 multiply_reduce_fusion.1
  172.8 1.8 copy-done.28
  174.7 3.5 fusion.53
  178.2 10.2 %fusion.7 = (bf16[1024,1408]{1,0:T(8,128)(2,1)}, bf16[1024,1408]{1,0:T(8,128)(2,1)S(1)}, bf16[1024,1408]{1,0:T(8,128)(2,1)}) fusion(f32[1408,1024]{0,1:T(8,128)S(1)} %fusion.54, f32[1024,1408]{1,0:T(8,128)S(1)} %fusion.53, bf16[1024,1024]{0,1:T(8,128)(2,1)S(1)} %multiply_convert_fusion.1, bf16[1024,1408]{1,0:T(8,128)(2,1)S(1)} %bitcast.84), kind=kOutput, calls=%fused_computation.15 | convolution fusion | flops 2990276608 | bytes 25165824 | tf_op jit(solution)/shard_map/dot_general | solution.py:613
  188.4 3.4 fusion.55
  191.9 3.7 add_convert_fusion
  196.1 4.6 %convolution_convert_fusion.6 = bf16[1024,1024]{0,1:T(8,128)(2,1)} fusion(bf16[1024,1408]{1,0:T(8,128)(2,1)S(1)} %copy-done.37, bf16[1024,1408]{1,0:T(8,128)(2,1)S(1)} %bitcast.87), kind=kOutput, calls=%fused_computation.48 | convolution fusion | flops 2953838592 | bytes 7864320 | tf_op jit(solution)/shard_map/dot_general | solution.py:617
  201.3 7.6 %convolution_convert_fusion = bf16[1408,1024]{0,1:T(8,128)(2,1)} fusion(bf16[1024,1024]{0,1:T(8,128)(2,1)} %all-gather.5.cloned.1.call-done, bf16[1024,1408]{1,0:T(8,128)(2,1)} %get-tuple-element.80), kind=kOutput, calls=%fused_computation.27 | convolution fusion | flops 2954231808 | bytes 7864320 | tf_op jit(solution)/shard_map/dot_general | solution.py:621
  208.9 2.7 multiply_reduce_fusion
  211.6 5.6 %convert_add_fusion.1 = (f32[1024,1024]{0,1:T(8,128)}, f32[1024,1024]{0,1:T(8,128)S(1)}) fusion(bf16[1024,1024]{0,1:T(8,128)(2,1)} %collective-permute-done.1, bf16[1024,1024]{0,1:T(8,128)(2,1)S(1)} %add_convert_fusion, f32[1024,1024]{0,1:T(8,128)S(1)} %copy-done.3, f32[1024]{0:T(1024)S(1)} %multiply_multiply_fusion.3, f32[1024]{0:T(1024)S(1)} %fusion.21, ...), kind=kLoop, calls=%fused_computation.23 | loop fusion | flops 10485760 | bytes 18886656 | tf_op jit(solution)/shard_map/add | solution.py:629
  217.2 2.3 convolution_convert_fusion.9.refs_5_
  219.6 2.3 convolution_convert_fusion.8
  221.8 44.5 %attention_back_scatter.1 = (bf16[1024,512]{1,0:T(8,128)(2,1)}, bf16[1024,512]{1,0:T(8,128)(2,1)}, bf16[1024,512]{1,0:T(8,128)(2,1)}, bf16[8,1024,1024]{2,1,0:T(...) custom-call(bf16[1024,1536]{1,0:T(8,128)(2,1)} %convolution_convert_fusion.4.refs_0_.refs_1_.refs_2_, ...), custom_call_target="tpu_custom_call" | custom-call | tf_op jit(solution)/shard_map/attention_back_scatter/pallas_call | solution.py:173
  270.9 4.7 %convolution_convert_fusion.5 = bf16[1024,1024]{0,1:T(8,128)(2,1)} fusion(bf16[1024,1536]{1,0:T(8,128)(2,1)S(1)} %constant_dynamic-update-slice_fusion, bf16[1024,1536]{1,0:T(8,128)(2,1)S(1)} %bitcast.81), kind=kOutput, calls=%fused_computation.47 | convolution fusion | flops 3222274048 | bytes 8388608 | tf_op jit(solution)/shard_map/dot_general | solution.py:617
  275.9 2.0 multiply_reduce_fusion.3
  278.7 4.7 %convolution_convert_fusion.2 = bf16[1024,1408]{1,0:T(8,128)(2,1)} fusion(bf16[1024,1024]{0,1:T(8,128)(2,1)S(1)} %copy-done.10, bf16[1024,1408]{1,0:T(8,128)(2,1)S(1)} %copy-done.36), kind=kOutput, calls=%fused_computation.29 | convolution fusion | flops 2954231808 | bytes 7864320 | tf_op jit(solution)/shard_map/dot_general | solution.py:621
  283.4 4.8 %convolution_convert_fusion.3 = bf16[1024,1408]{1,0:T(8,128)(2,1)} fusion(bf16[1024,1024]{0,1:T(8,128)(2,1)S(1)} %copy-done.10, bf16[1024,1408]{1,0:T(8,128)(2,1)S(1)} %copy-done.34), kind=kOutput, calls=%fused_computation.30 | convolution fusion | flops 2954231808 | bytes 7864320 | tf_op jit(solution)/shard_map/dot_general | solution.py:621
  288.2 5.0 %convolution_convert_fusion.1 = bf16[1024,1536]{1,0:T(8,128)(2,1)} fusion(bf16[1024,1536]{1,0:T(8,128)(2,1)S(1)} %copy-done.18, bf16[1024,1024]{0,1:T(8,128)(2,1)S(1)} %copy-done.7, f32[1024]{0:T(1024)S(1)} %convert_element_type.244, f32[1024]{0:T(1024)S(1)} %add_rsqrt_fusion), kind=kOutput, calls=%fused_computation.28 | convolution fusion | flops 3226992640 | bytes 8396800 | tf_op jit(solution)/shard_map/dot_general | solution.py:621
  293.2 82.4 %table_grad_scatter.1 = (f32[8,96]{1,0:T(8,128)}, f32[64,1408]{1,0:T(8,128)}, f32[64,1408]{1,0:T(8,128)}, f32[64,1536]{1,0:T(8,128)}) custom-call(bf16[8,1024,1024]{2,1,0:T(8,128)(2,1)} %get-tuple-element.42.refs_0_, f32[3,1024,1024]{2,1,0:T(8,128)} %get-tuple-element.43.refs_1_, bf16[4,2,2,64,1408]{4,3,2,1,0:T(8,128)(2,1)} %bitcast.68, ...), custom_call_target="tpu_custom_call" | custom-call | tf_op jit(solution)/shard_map/table_grad_scatter/pallas_call | solution.py:215
  376.8 1.8 fusion.52
  378.6 2.9 multiply_reduce_fusion.2
  382.9 2.4 fusion.13
  385.9 13.9 %small_sums.1 = f32[28,128]{1,0:T(8,128)} custom-call(f32[28,128]{1,0:T(8,128)} %maximum_bitcast_fusion.src), custom_call_target="tpu_custom_call" | custom-call | tf_op jit(solution)/shard_map/small_sums/pallas_call | solution.py:594
  401.0 2.5 fusion.14
  403.6 1.8 copy.51
  (128 shorter events, 22.6 us)
Async XLA Ops:
  7.2 4.5 %copy-start = (bf16[96,16]{0,1:T(8,128)(2,1)S(1)}, bf16[96,16]{0,1:T(8,128)(2,1)}, u32[]{:S(2)}) copy-start(bf16[96,16]{0,1:T(8,128)(2,1)} %param.20) | copy-start | bytes 9220
  7.2 4.5 %copy-start.25 = (bf16[1024]{0:T(1024)(128)(2,1)S(1)}, bf16[1024]{0:T(1024)(128)(2,1)}, u32[]{:S(2)}) copy-start(bf16[1024]{0:T(1024)(128)(2,1)} %param.18) | copy-start | bytes 6148
  7.2 5.2 %copy-start.24 = (s32[1024]{0:T(1024)S(1)}, s32[1024]{0:T(1024)}, u32[]{:S(2)}) copy-start(s32[1024]{0:T(1024)} %param.16) | copy-start | bytes 12292
  7.2 108.2 %all-gather.3.cloned.1.call-start = ((), (), s32[]{:S(2)}) async-start(), calls=%async_computation.2 | async-start | bytes 3145728 | tf_op jit(solution)/shard_map/all_gather | solution.py:642
  9.6 3.8 copy-start.23
  9.6 4.8 %copy-start.20 = (bf16[64,512]{1,0:T(8,128)(2,1)S(1)}, bf16[64,512]{1,0:T(8,128)(2,1)}, u32[]{:S(2)}) copy-start(bf16[64,512]{1,0:T(8,128)(2,1)} %param.23) | copy-start | bytes 196612
  9.6 4.8 %copy-start.21 = (bf16[64,512]{1,0:T(8,128)(2,1)S(1)}, bf16[64,512]{1,0:T(8,128)(2,1)}, u32[]{:S(2)}) copy-start(bf16[64,512]{1,0:T(8,128)(2,1)} %param.22) | copy-start | bytes 196612
  9.6 4.8 %copy-start.22 = (bf16[64,512]{1,0:T(8,128)(2,1)S(1)}, bf16[64,512]{1,0:T(8,128)(2,1)}, u32[]{:S(2)}) copy-start(bf16[64,512]{1,0:T(8,128)(2,1)} %param.21) | copy-start | bytes 196612
  9.7 151.9 %all-gather.5.cloned.1.call-start = ((), (), s32[]{:S(2)}) async-start(), calls=%async_computation.4 | async-start | bytes 3145728 | tf_op jit(solution)/shard_map/all_gather | solution.py:643
  11.1 367.5 %reduce-scatter.3.cloned.1.call-start = ((), (), s32[]{:S(2)}) async-start(), calls=%async_computation.3 | async-start | bytes 3145728 | tf_op jit(solution)/shard_map/reduce_scatter | solution.py:660
  125.5 33.4 %copy-start.31 = (bf16[4,2,2,64,512]{4,3,2,1,0:T(8,128)(2,1)S(1)}, bf16[4,2,2,64,512]{4,3,2,1,0:T(8,128)(2,1)}, u32[]{:S(2)}) copy-start(bf16[4,2,2,64,512]{4,3,2,1,0:T(8,128)(2,1)} %get-tuple-element.34) | copy-start | bytes 3145732
  161.4 6.4 %collective-permute-start = (bf16[1024,1024]{0,1:T(8,128)(2,1)S(1)}, bf16[1024,1024]{0,1:T(8,128)(2,1)}, u32[]{:S(2)}, u32[]{:S(2)}) collective-permute-start(bf16[1024,1024]{0,1:T(8,128)(2,1)S(1)} %convolution_convert_fusion.7), channel_id=1, source_target_pairs={{0,1},{1,0},{2,3},{3,2},{4,5},{5,4},{6,7},{7,6},{8,9},{9,8},{10,11... | collective-permute-start | bytes 6291464 | tf_op jit(solution)/shard_map/ppermute | solution.py:625
  161.6 6.3 %copy-start.6 = (bf16[1024,1024]{0,1:T(8,128)(2,1)S(1)}, bf16[1024,1024]{0,1:T(8,128)(2,1)}, u32[]{:S(2)}) copy-start(bf16[1024,1024]{0,1:T(8,128)(2,1)} %all-gather.3.cloned.1.call-done) | copy-start | bytes 6291460
  170.7 3.9 copy-start.28
  172.8 5.4 %copy-start.9 = (bf16[1024,1024]{0,1:T(8,128)(2,1)}, bf16[1024,1024]{0,1:T(8,128)(2,1)S(1)}, u32[]{:S(2)}) copy-start(bf16[1024,1024]{0,1:T(8,128)(2,1)S(1)} %multiply_convert_fusion.1) | copy-start | bytes 6291460
  174.7 3.5 copy-start.29
  188.4 3.4 copy-start.33
  188.4 3.5 copy-start.35
  191.9 4.2 %copy-start.30 = (bf16[4,2,2,64,1408]{4,3,2,1,0:T(8,128)(2,1)S(1)}, bf16[4,2,2,64,1408]{4,3,2,1,0:T(8,128)(2,1)}, u32[]{:S(2)}) copy-start(bf16[4,2,2,64,1408]{4,3,2,1,0:T(8,128)(2,1)} %get-tuple-element.37) | copy-start | bytes 8650756
  191.9 4.2 %copy-start.37 = (bf16[1024,1408]{1,0:T(8,128)(2,1)S(1)}, bf16[1024,1408]{1,0:T(8,128)(2,1)}, u32[]{:S(2)}) copy-start(bf16[1024,1408]{1,0:T(8,128)(2,1)} %get-tuple-element.80) | copy-start | bytes 8650756
  195.6 13.3 %collective-permute-start.1 = (bf16[1024,1024]{0,1:T(8,128)(2,1)S(1)}, bf16[1024,1024]{0,1:T(8,128)(2,1)}, u32[]{:S(2)}, u32[]{:S(2)}) collective-permute-start(bf16[1024,1024]{0,1:T(8,128)(2,1)S(1)} %add_convert_fusion), channel_id=1, source_target_pairs={{0,1},{1,0},{2,3},{3,2},{4,5},{5,4},{6,7},{7,6},{8,9},{9,8},{10,11... | collective-permute-start | bytes 6291464 | tf_op jit(solution)/shard_map/ppermute | solution.py:625
  200.8 182.1 %reduce-scatter.5.cloned.1.call-start = ((), (), s32[]{:S(2)}) async-start(), calls=%async_computation.5 | async-start | bytes 3145728 | tf_op jit(solution)/shard_map/reduce_scatter | solution.py:684
  201.3 7.6 %copy-start.3 = (f32[1024,1024]{0,1:T(8,128)S(1)}, f32[1024,1024]{0,1:T(8,128)}, u32[]{:S(2)}) copy-start(f32[1024,1024]{0,1:T(8,128)} %copy-done.2) | copy-start | bytes 12582916
  211.6 5.7 %copy-start.32 = (bf16[4,2,2,64,512]{4,3,2,1,0:T(8,128)(2,1)S(1)}, bf16[4,2,2,64,512]{4,3,2,1,0:T(8,128)(2,1)}, u32[]{:S(2)}) copy-start(bf16[4,2,2,64,512]{4,3,2,1,0:T(8,128)(2,1)} %get-tuple-element.34) | copy-start | bytes 3145732
  266.3 4.6 %copy-start.27 = (bf16[4,2,2,64,1536]{4,3,2,1,0:T(8,128)(2,1)S(1)}, bf16[4,2,2,64,1536]{4,3,2,1,0:T(8,128)(2,1)}, u32[]{:S(2)}) copy-start(bf16[4,2,2,64,1536]{4,3,2,1,0:T(8,128)(2,1)} %get-tuple-element.31) | copy-start | bytes 9437188
  270.9 4.7 %copy-start.4 = (bf16[512,1024]{0,1:T(8,128)(2,1)S(1)}, bf16[512,1024]{0,1:T(8,128)(2,1)}, u32[]{:S(2)}) copy-start(bf16[512,1024]{0,1:T(8,128)(2,1)} %copy.38) | copy-start | bytes 3145732
  278.7 4.7 %copy-start.34 = (bf16[1024,1408]{1,0:T(8,128)(2,1)S(1)}, bf16[1024,1408]{1,0:T(8,128)(2,1)}, u32[]{:S(2)}) copy-start(bf16[1024,1408]{1,0:T(8,128)(2,1)} %copy-done.33) | copy-start | bytes 8650756
  283.4 4.8 %copy-start.7 = (bf16[1024,1024]{0,1:T(8,128)(2,1)S(1)}, bf16[1024,1024]{0,1:T(8,128)(2,1)}, u32[]{:S(2)}) copy-start(bf16[1024,1024]{0,1:T(8,128)(2,1)} %all-gather.3.cloned.1.call-done) | copy-start | bytes 6291460
  283.4 4.8 %copy-start.18 = (bf16[1024,1536]{1,0:T(8,128)(2,1)S(1)}, bf16[1024,1536]{1,0:T(8,128)(2,1)}, u32[]{:S(2)}) copy-start(bf16[1024,1536]{1,0:T(8,128)(2,1)} %copy-done.17) | copy-start | bytes 9437188
  401.0 8.1 %copy-start.1 = (bf16[96,16]{0,1:T(8,128)(2,1)S(1)}, bf16[96,16]{0,1:T(8,128)(2,1)}, u32[]{:S(2)}) copy-start(bf16[96,16]{0,1:T(8,128)(2,1)} %param.20) | copy-start | bytes 9220
  403.6 4.0 copy-start.15
  403.6 4.7 %copy-start.14 = (f32[64,1408]{1,0:T(8,128)S(1)}, f32[64,1408]{1,0:T(8,128)}, u32[]{:S(2)}) copy-start(f32[64,1408]{1,0:T(8,128)} %get-tuple-element.49) | copy-start | bytes 1081348
  (13 other events, 32.3 us)
Sparse Core Ops, SparseCore 0:
  10.2 13.2 all-gather.2
  25.6 11.7 all-gather.4
  200.9 8.2 reduce-scatter.2
  275.7 9.4 reduce-scatter.4

commit v3 on v2

--- a/solution.py
+++ b/solution.py
@@ -14,6 +14,8 @@
 EDGES = (1, 2, 3, 4, 5, 6, 7, 8, 12, 16, 23, 32, 46, 64, 91)
 NT = (((1,), (1,)), ((), ()))
 VM = 58 * 2**20
+TABLE_SCALE = 2047.0
+TABLE_LIFT = 8192
 
 
 def params(cid):
@@ -24,58 +26,71 @@
     return jnp.take_along_axis(table, idx, axis=1, mode="promise_in_bounds")
 
 
-def bias_tile(start, heads, rows, n, steps_ref, tab_ref, box_col, box_row, page_col, page_row, bias_ref, ids_ref):
+def buckets_of(gap, steps, shift):
+    return lane_take(steps, jnp.minimum(jnp.abs(gap) >> shift, EDGES[-1])) + jnp.where(gap > 0, 16, 0)
+
+
+def bias_tile(start, heads, rows, n, steps_ref, tab_ref, box_col, box_row, page_col, page_row, bias_ref, ids_ref, lin, lin_ids):
     steps = jnp.broadcast_to(steps_ref[...], (rows, 128))
     allowed_col = jnp.broadcast_to(page_col[...] % 2, (rows, 128))
     cols = [jnp.broadcast_to(box_col[:, t:t + 1], (rows, 128)) for t in range(2)]
-    own = lax.broadcasted_iota(jnp.int32, (rows, 128), 0) + start
+    pairs = heads // 2
+    table = lambda t, p: jnp.broadcast_to(tab_ref[t * pairs + p:t * pairs + p + 1, :], (rows, 128))
+    unit = 1.0 / TABLE_SCALE
+
+    @pl.when(start == 0)
+    def _():
+        @pl.loop(0, 8)
+        def _(k):
+            ids = buckets_of(lax.broadcasted_iota(jnp.int32, (rows, 128), 1) - lax.broadcasted_iota(jnp.int32, (rows, 128), 0) + (k - 4) * rows, steps, 0)
+            lin_ids[k] = ids.astype(f32)
+            for p in range(pairs):
+                lin[k, p] = lane_take(table(0, p), ids)
 
     @pl.loop(0, n // 128)
     def _(c):
         lanes = pl.ds(pl.multiple_of(c * 128, 128), 128)
-        lane_id = lax.broadcasted_iota(jnp.int32, (rows, 128), 1) + c * 128
+        near = jnp.clip((c * 128 - start) // rows + 4, 0, 7)
+        ids_ref[0, :, lanes] = lin_ids[near]
         ids = []
-        for t in range(3):
-            gap = (lane_id - own) if t == 0 else (jnp.broadcast_to(box_row[t - 1:t, lanes], (rows, 128)) - cols[t - 1])
-            size = jnp.abs(gap)
-            if t > 0:
-                size = size >> 2
-            bucket = lane_take(steps, jnp.minimum(size, 91)) + jnp.where(gap > 0, 16, 0)
-            ids.append(bucket)
-            ids_ref[t, :, lanes] = bucket.astype(f32)
+        for t in range(2):
+            ids.append(buckets_of(jnp.broadcast_to(box_row[t:t + 1, lanes], (rows, 128)) - cols[t], steps, 2))
+            ids_ref[t + 1, :, lanes] = ids[t].astype(f32)
         ok = jnp.broadcast_to(page_row[:, lanes], (rows, 128)) == allowed_col
-        for h in range(heads):
-            total = None
-            for t in range(3):
-                table = jnp.broadcast_to(tab_ref[t * heads + h:t * heads + h + 1, :], (rows, 128))
-                part = lane_take(table, ids[t])
-                total = part if total is None else total + part
-            bias_ref[h, :, lanes] = jnp.where(ok, total, -1e30)
+        for p in range(pairs):
+            words = lin[near, p] + lane_take(table(1, p), ids[0]) + lane_take(table(2, p), ids[1])
+            upper = (words >> 16).astype(f32) * unit
+            lower = (words & 0xFFFF).astype(f32) * unit - 3 * TABLE_LIFT * unit
+            bias_ref[2 * p, :, lanes] = jnp.where(ok, upper, -1e30)
+            bias_ref[2 * p + 1, :, lanes] = jnp.where(ok, lower, -1e30)
 
 
 def bias_gather_kernel(heads, rows, n, G, halves, count, *refs):
     ins, srcs = refs[:6], refs[6:6 + count]
     bias_ref, ids_ref = refs[6 + count:8 + count]
-    outs, sems = refs[8 + count:8 + 2 * count], refs[8 + 2 * count:]
+    outs, lins, sems = refs[8 + count:8 + 2 * count], refs[8 + 2 * count:10 + 2 * count], refs[10 + 2 * count:]
     now = pl.program_id(0)
     comm = Gather(G, halves, srcs, outs, *sems)
-    beside(comm, n // rows, now, lambda: bias_tile(now * rows, heads, rows, n, *ins, bias_ref, ids_ref))
+    beside(comm, n // rows, now, lambda: bias_tile(now * rows, heads, rows, n, *ins, bias_ref, ids_ref, *lins))
 
 
 def bias_and_gather(tables, boxes, pages, shards, halves, wide, cid):
     heads, n, G, rows = tables.shape[1], pages.shape[0], wide // 4, 64
-    tab = jnp.pad(tables.astype(f32).reshape(3, 32, heads).transpose(0, 2, 1).reshape(3 * heads, 32), ((0, 0), (0, 96)))
+    fixed = jnp.round(tables.astype(f32) * TABLE_SCALE).astype(jnp.int32).reshape(3, 32, heads // 2, 2)
+    words = fixed[..., 0] * 65536 + fixed[..., 1] + TABLE_LIFT
+    tab = jnp.pad(words.transpose(0, 2, 1).reshape(3 * heads // 2, 32), ((0, 0), (0, 96)))
     lane = jnp.arange(128, dtype=jnp.int32)
     steps = sum([(lane >= e).astype(jnp.int32) for e in EDGES])[None]
     count = len(shards)
     outs = pl.pallas_call(functools.partial(bias_gather_kernel, heads, rows, n, G, halves, count),
         grid=(n // rows,),
         out_shape=(jax.ShapeDtypeStruct((heads, n, n), f32), jax.ShapeDtypeStruct((3, n, n), f32)) + gathered_shapes(shards, wide),
-        in_specs=[pl.BlockSpec((1, 128), lambda i: (0, 0)), pl.BlockSpec((3 * heads, 128), lambda i: (0, 0)),
+        in_specs=[pl.BlockSpec((1, 128), lambda i: (0, 0)), pl.BlockSpec((3 * heads // 2, 128), lambda i: (0, 0)),
                   pl.BlockSpec((rows, 2), lambda i: (i, 0)), pl.BlockSpec((2, n), lambda i: (0, 0)),
                   pl.BlockSpec((rows, 1), lambda i: (i, 0)), pl.BlockSpec((1, n), lambda i: (0, 0))] + [ANY] * count,
         out_specs=(pl.BlockSpec((heads, rows, n), lambda i: (0, i, 0)), pl.BlockSpec((3, rows, n), lambda i: (0, i, 0))) + (ANY,) * count,
-        scratch_shapes=gather_scratch(G, halves, count), compiler_params=params(cid), name="layout_bias_gather")(
+        scratch_shapes=[pltpu.VMEM((8, heads // 2, rows, 128), jnp.int32), pltpu.VMEM((8, rows, 128), f32)] + gather_scratch(G, halves, count),
+        compiler_params=params(cid), name="layout_bias_gather")(
             steps, tab, boxes.T, boxes, pages[:, None], pages[None], *shards)
     return outs[0], outs[1], [flat(a) for a in outs[2:]]
 
@@ -641,17 +656,16 @@
 
     all_tokens = lax.all_gather(tokens, "narrow", axis=0, tiled=True)
     all_cot = lax.all_gather(cotangent, "narrow", axis=0, tiled=True)
-    keys_to = 2 * inner
-    bias, ids, (w_first, full_out, full_gate, full_up) = bias_and_gather(
-        tables, boxes, pages, [jnp.concatenate([w_query, w_key, w_value], axis=1), w_out.T, w_gate, w_up],
-        (((2, 0, ff), (0, 0, keys_to)), ((3, 0, ff), (1, 0, inner), (0, keys_to, inner))), wide, 1)
+    early = inner // 4 * 3
+    bias, ids, (w_first, full_out, full_gate) = bias_and_gather(
+        tables, boxes, pages, [jnp.concatenate([w_query, w_key, w_value], axis=1), w_out.T, w_gate],
+        (((2, 0, ff), (0, 0, early)), ((1, 0, inner), (0, early, 3 * inner - early))), wide, 1)
 
     x = all_tokens.astype(f32)
     gain_one, gain_two = gain_attn.astype(f32), gain_ffn.astype(f32)
     normed = norm_plain(x, gain_one).astype(bf16)
     qkv = times(normed, w_first).astype(bf16)
-    cut = (ff // 128 + 1) // 2 * 128
-    attended, lse, (full_down,) = attn_fwd_and_gather(qkv, bias, [w_down.T], (((0, 0, cut),), ((0, cut, ff - cut),)), wide, 2)
+    attended, lse, (full_up, full_down) = attn_fwd_and_gather(qkv, bias, [w_up, w_down.T], (((0, 0, ff),), ((1, 0, ff),)), wide, 2)
     hidden = x + both(times_transposed(attended, full_out).astype(bf16))
     normed_two = norm_plain(hidden, gain_two).astype(bf16)
     gate_pre, up_pre = times(normed_two, full_gate), times(normed_two, full_up)
@@ -675,7 +689,7 @@
     grad_attended = times(grad_low, full_out).astype(bf16)
     (dq, dk, dv, g), (s_down, s_out) = attn_bwd_and_scatter(
         qkv, bias, attended, grad_attended, lse, [grad_w_down.astype(bf16), grad_w_out.astype(bf16)],
-        (((0, 0, keys_to),), ((0, keys_to, ff - keys_to), (1, 0, inner))), wide, 3)
+        (((0, 0, 2 * inner),), ((0, 2 * inner, ff - 2 * inner), (1, 0, inner))), wide, 3)
     dqkv = jnp.concatenate([dq, dk, dv], axis=1)
     mid = 3 * inner // 2
     table_part, (s_gate, s_up, s_first) = hist_and_scatter(

time: 424 us -> 409 us (0.965)
  Pallas kernels: 274 us -> 260 us
    pallas_call x1, Pallas kernels: 100 us -> 66.4 us  [bias_and_gather(): pl.pallas_call(functools.partial(bias_gather_kernel, heads, rows, n, G, h...]
    pallas_call x1, Pallas kernels: 33.4 us -> 52.8 us  [attn_fwd_and_gather(): pl.pallas_call(functools.partial(fwd_kernel, pairs * tiles, tiles, G, hal...]
    unnamed x88 -> x86, local copies, waits for them, and re-layouts: 20.3 us -> 20.3 us
  transfers between devices with their start and end apart: 6 -> 6, of which waited for: 0 -> 0; matrix products, arithmetic and copies ran while one was open for 19% -> 20% of each run, Pallas kernels for 63% -> 61%
where the time goes in v3:
time: 409 us; the launch traced here: 401 us
  Pallas kernels  260 us (64%)
  matrix products  73 us (18%)
  local copies, waits for them, and re-layouts  26.5 us (6%)
  other arithmetic  25.9 us (6%)
  between operations  14.5 us (4%)
    pallas_call x1, Pallas kernels, hist_and_scatter(): pl.pallas_call(functools.partial(hist_kernel, heads, rows, n, G, halves,...  83.1 us
    pallas_call x1, Pallas kernels, bias_and_gather(): pl.pallas_call(functools.partial(bias_gather_kernel, heads, rows, n, G, h...  66.4 us
    pallas_call x1, Pallas kernels, attn_fwd_and_gather(): pl.pallas_call(functools.partial(fwd_kernel, pairs * tiles, tiles, G, hal...  52.8 us
    pallas_call x1, Pallas kernels, attn_bwd_and_scatter(): pl.pallas_call(functools.partial(bwd_kernel, pairs * tiles, tiles, G, hal...  44.2 us
    dot_general x5, matrix products, times(): return jnp.dot(a, b, preferred_element_type=f32)  29.8 us
    dot_general x5, matrix products, transposed_times(): lax.dot_general(a, b, (((0,), (0,)), ((), ())), preferred_element_type=f32)  24.3 us
    unnamed x86, local copies, waits for them, and re-layouts  20.3 us
    dot_general x5, matrix products, times_transposed(): return lax.dot_general(a, b, NT, preferred_element_type=f32)  18.9 us
  transfers between devices with their start and end apart: 6, of which 0 were waited for; matrix products, arithmetic and copies ran while one was open for 20% of the time, Pallas kernels for 61%

profile of v3, /device:TPU:0, one launch (start us, length us, event | category | flops | bytes accessed | tf_op | source)
XLA Modules:
  0.0 401.3 jit_solution(17744906559244885715)
XLA Ops:
  7.3 2.4 copy.40
  15.2 66.4 %layout_bias_gather.1 = (f32[8,1024,1024]{2,1,0:T(8,128)}, f32[3,1024,1024]{2,1,0:T(8,128)}, bf16[4,2,2,64,1536]{4,3,2,1,0:T(8,128)(2,1)}, bf16[4,2,2,64,512]{4,...) custom-call(s32[1,128]{1,0:T(1,128)} %fusion.40.refs_0_, s32[12,128]{1,0:T(8,128)} %pad.4.refs_1_, s32[1024,2]{1,0:T(8,128)} %bitcast.69, ...), custom_call_target="tpu_custom_call" | custom-call | tf_op jit(solution)/shard_map/layout_bias_gather/pallas_call | solution.py:85
  81.6 2.1 fusion.8
  83.7 7.9 %convolution_convert_fusion.4.refs_0_.refs_1_.refs_2_ = bf16[1024,1536]{1,0:T(8,128)(2,1)} fusion(bf16[1024,1536]{1,0:T(8,128)(2,1)} %bitcast.78, bf16[1024,1024]{0,1:T(8,128)(2,1)} %all-gather.3.cloned.1.call-done, f32[1024]{0:T(1024)S(1)} %convert_element_type.247, f32[1024]{0:T(1024)S(1)} %add_rsqrt_fusion), kind=kOutput, calls=%fused_computation.31 | convolution fusion | flops 3226992640 | bytes 8396800 | tf_op jit(solution)/shard_map/dot_general | solution.py:628
  91.6 52.8 %attention_gather.1 = (bf16[1024,512]{1,0:T(8,128)(2,1)}, f32[4,1024,2]{2,1,0:T(8,128)}, bf16[4,2,2,64,1408]{4,3,2,1,0:T(8,128)(2,1)}, bf16[4,2,2,64,1408]{4,3,2,1,0:T(8,128)(2,1)}) custom-call(bf16[1024,1536]{1,0:T(8,128)(2,1)} %convolution_convert_fusion.4.refs_0_.refs_1_.refs_2_, bf16[1024,1536]{1,0:T(8,128)(2,1)} %convolution_convert_fusion.4.refs_0_.refs_1_.refs_2_, ...), custom_call_target="tpu_custom_call" | custom-call | tf_op jit(solution)/shard_map/attention_gather/pallas_call | solution.py:133
  144.5 2.5 convolution_convert_fusion.7
  147.2 6.1 %fusion.56 = f32[1408,1024]{0,1:T(8,128)S(1)} fusion(bf16[1024,1408]{1,0:T(8,128)(2,1)} %bitcast.82, bf16[1024,1024]{0,1:T(8,128)(2,1)} %all-gather.5.cloned.1.call-done), kind=kOutput, calls=%fused_computation.120 | convolution fusion | flops 2952790016 | bytes 10747904 | tf_op jit(solution)/shard_map/dot_general | solution.py:628
  153.3 3.1 multiply_reduce_fusion.1
  158.5 1.8 copy-done.29
  160.3 3.5 fusion.55
  163.8 10.0 %fusion.7 = (bf16[1024,1408]{1,0:T(8,128)(2,1)}, bf16[1024,1408]{1,0:T(8,128)(2,1)S(1)}, bf16[1024,1408]{1,0:T(8,128)(2,1)}) fusion(f32[1408,1024]{0,1:T(8,128)S(1)} %fusion.56, f32[1024,1408]{1,0:T(8,128)S(1)} %fusion.55, bf16[1024,1024]{0,1:T(8,128)(2,1)S(1)} %multiply_convert_fusion.1, bf16[1024,1408]{1,0:T(8,128)(2,1)S(1)} %bitcast.80), kind=kOutput, calls=%fused_computation.15 | convolution fusion | flops 2990276608 | bytes 25165824 | tf_op jit(solution)/shard_map/dot_general | solution.py:628
  173.8 3.4 fusion.57
  177.3 3.7 add_convert_fusion
  181.5 4.6 %convolution_convert_fusion.6 = bf16[1024,1024]{0,1:T(8,128)(2,1)} fusion(bf16[1024,1408]{1,0:T(8,128)(2,1)S(1)} %copy-done.36, bf16[1024,1408]{1,0:T(8,128)(2,1)S(1)} %bitcast.83), kind=kOutput, calls=%fused_computation.48 | convolution fusion | flops 2953838592 | bytes 7864320 | tf_op jit(solution)/shard_map/dot_general | solution.py:632
  186.7 7.6 %convolution_convert_fusion = bf16[1408,1024]{0,1:T(8,128)(2,1)} fusion(bf16[1024,1024]{0,1:T(8,128)(2,1)} %all-gather.5.cloned.1.call-done, bf16[1024,1408]{1,0:T(8,128)(2,1)} %get-tuple-element.80), kind=kOutput, calls=%fused_computation.27 | convolution fusion | flops 2954231808 | bytes 7864320 | tf_op jit(solution)/shard_map/dot_general | solution.py:636
  194.2 2.7 multiply_reduce_fusion
  197.0 5.7 %convert_add_fusion.1 = (f32[1024,1024]{0,1:T(8,128)}, f32[1024,1024]{0,1:T(8,128)S(1)}) fusion(bf16[1024,1024]{0,1:T(8,128)(2,1)} %collective-permute-done.1, bf16[1024,1024]{0,1:T(8,128)(2,1)S(1)} %add_convert_fusion, f32[1024,1024]{0,1:T(8,128)S(1)} %copy-done.1, f32[1024]{0:T(1024)S(1)} %multiply_multiply_fusion.3, f32[1024]{0:T(1024)S(1)} %fusion.23, ...), kind=kLoop, calls=%fused_computation.23 | loop fusion | flops 10485760 | bytes 18886656 | tf_op jit(solution)/shard_map/add | solution.py:644
  202.7 2.3 convolution_convert_fusion.9.refs_5_
  205.0 2.3 convolution_convert_fusion.8
  207.3 44.2 %attention_back_scatter.1 = (bf16[1024,512]{1,0:T(8,128)(2,1)}, bf16[1024,512]{1,0:T(8,128)(2,1)}, bf16[1024,512]{1,0:T(8,128)(2,1)}, bf16[8,1024,1024]{2,1,0:T(...) custom-call(bf16[1024,1536]{1,0:T(8,128)(2,1)} %convolution_convert_fusion.4.refs_0_.refs_1_.refs_2_, ...), custom_call_target="tpu_custom_call" | custom-call | tf_op jit(solution)/shard_map/attention_back_scatter/pallas_call | solution.py:188
  256.1 4.7 %convolution_convert_fusion.5 = bf16[1024,1024]{0,1:T(8,128)(2,1)} fusion(bf16[1024,1536]{1,0:T(8,128)(2,1)S(1)} %constant_dynamic-update-slice_fusion, bf16[1024,1536]{1,0:T(8,128)(2,1)S(1)} %bitcast.79), kind=kOutput, calls=%fused_computation.47 | convolution fusion | flops 3222274048 | bytes 8388608 | tf_op jit(solution)/shard_map/dot_general | solution.py:632
  261.1 2.0 multiply_reduce_fusion.3
  263.8 4.7 %convolution_convert_fusion.2 = bf16[1024,1408]{1,0:T(8,128)(2,1)} fusion(bf16[1024,1024]{0,1:T(8,128)(2,1)S(1)} %copy-done.8, bf16[1024,1408]{1,0:T(8,128)(2,1)S(1)} %copy-done.35), kind=kOutput, calls=%fused_computation.29 | convolution fusion | flops 2954231808 | bytes 7864320 | tf_op jit(solution)/shard_map/dot_general | solution.py:636
  268.6 4.8 %convolution_convert_fusion.3 = bf16[1024,1408]{1,0:T(8,128)(2,1)} fusion(bf16[1024,1024]{0,1:T(8,128)(2,1)S(1)} %copy-done.8, bf16[1024,1408]{1,0:T(8,128)(2,1)S(1)} %copy-done.33), kind=kOutput, calls=%fused_computation.30 | convolution fusion | flops 2954231808 | bytes 7864320 | tf_op jit(solution)/shard_map/dot_general | solution.py:636
  273.4 5.0 %convolution_convert_fusion.1 = bf16[1024,1536]{1,0:T(8,128)(2,1)} fusion(bf16[1024,1536]{1,0:T(8,128)(2,1)S(1)} %copy-done.16, bf16[1024,1024]{0,1:T(8,128)(2,1)S(1)} %copy-done.5, f32[1024]{0:T(1024)S(1)} %convert_element_type.247, f32[1024]{0:T(1024)S(1)} %add_rsqrt_fusion), kind=kOutput, calls=%fused_computation.28 | convolution fusion | flops 3226992640 | bytes 8396800 | tf_op jit(solution)/shard_map/dot_general | solution.py:636
  278.4 83.1 %table_grad_scatter.1 = (f32[8,96]{1,0:T(8,128)}, f32[64,1408]{1,0:T(8,128)}, f32[64,1408]{1,0:T(8,128)}, f32[64,1536]{1,0:T(8,128)}) custom-call(bf16[8,1024,1024]{2,1,0:T(8,128)(2,1)} %get-tuple-element.42.refs_0_, f32[3,1024,1024]{2,1,0:T(8,128)} %get-tuple-element.43.refs_1_, bf16[4,2,2,64,1408]{4,3,2,1,0:T(8,128)(2,1)} %bitcast.68, ...), custom_call_target="tpu_custom_call" | custom-call | tf_op jit(solution)/shard_map/table_grad_scatter/pallas_call | solution.py:230
  362.7 1.8 fusion.54
  364.5 2.9 multiply_reduce_fusion.2
  368.7 2.3 fusion.13
  371.7 13.5 %small_sums.1 = f32[28,128]{1,0:T(8,128)} custom-call(f32[28,128]{1,0:T(8,128)} %maximum_bitcast_fusion.src), custom_call_target="tpu_custom_call" | custom-call | tf_op jit(solution)/shard_map/small_sums/pallas_call | solution.py:609
  386.5 2.5 fusion.14
  389.1 1.8 copy.53
  (128 shorter events, 22.6 us)
Async XLA Ops:
  7.2 4.5 %copy-start.23 = (bf16[1024]{0:T(1024)(128)(2,1)S(1)}, bf16[1024]{0:T(1024)(128)(2,1)}, u32[]{:S(2)}) copy-start(bf16[1024]{0:T(1024)(128)(2,1)} %param.18) | copy-start | bytes 6148
  7.2 4.5 %copy-start.25 = (bf16[96,16]{0,1:T(8,128)(2,1)S(1)}, bf16[96,16]{0,1:T(8,128)(2,1)}, u32[]{:S(2)}) copy-start(bf16[96,16]{0,1:T(8,128)(2,1)} %param.20) | copy-start | bytes 9220
  7.2 5.2 %copy-start.22 = (s32[1024]{0:T(1024)S(1)}, s32[1024]{0:T(1024)}, u32[]{:S(2)}) copy-start(s32[1024]{0:T(1024)} %param.16) | copy-start | bytes 12292
  7.2 74.4 %all-gather.3.cloned.1.call-start = ((), (), s32[]{:S(2)}) async-start(), calls=%async_computation.2 | async-start | bytes 3145728 | tf_op jit(solution)/shard_map/all_gather | solution.py:657
  9.6 3.8 copy-start.21
  9.6 4.9 %copy-start.18 = (bf16[64,512]{1,0:T(8,128)(2,1)S(1)}, bf16[64,512]{1,0:T(8,128)(2,1)}, u32[]{:S(2)}) copy-start(bf16[64,512]{1,0:T(8,128)(2,1)} %param.23) | copy-start | bytes 196612
  9.6 4.9 %copy-start.19 = (bf16[64,512]{1,0:T(8,128)(2,1)S(1)}, bf16[64,512]{1,0:T(8,128)(2,1)}, u32[]{:S(2)}) copy-start(bf16[64,512]{1,0:T(8,128)(2,1)} %param.22) | copy-start | bytes 196612
  9.6 4.9 %copy-start.20 = (bf16[64,512]{1,0:T(8,128)(2,1)S(1)}, bf16[64,512]{1,0:T(8,128)(2,1)}, u32[]{:S(2)}) copy-start(bf16[64,512]{1,0:T(8,128)(2,1)} %param.21) | copy-start | bytes 196612
  9.7 137.5 %all-gather.5.cloned.1.call-start = ((), (), s32[]{:S(2)}) async-start(), calls=%async_computation.4 | async-start | bytes 3145728 | tf_op jit(solution)/shard_map/all_gather | solution.py:658
  11.1 353.4 %reduce-scatter.3.cloned.1.call-start = ((), (), s32[]{:S(2)}) async-start(), calls=%async_computation.3 | async-start | bytes 3145728 | tf_op jit(solution)/shard_map/reduce_scatter | solution.py:674
  91.6 52.9 %copy-start.30 = (bf16[4,2,2,64,512]{4,3,2,1,0:T(8,128)(2,1)S(1)}, bf16[4,2,2,64,512]{4,3,2,1,0:T(8,128)(2,1)}, u32[]{:S(2)}) copy-start(bf16[4,2,2,64,512]{4,3,2,1,0:T(8,128)(2,1)} %get-tuple-element.34) | copy-start | bytes 3145732
  147.0 6.2 %collective-permute-start = (bf16[1024,1024]{0,1:T(8,128)(2,1)S(1)}, bf16[1024,1024]{0,1:T(8,128)(2,1)}, u32[]{:S(2)}, u32[]{:S(2)}) collective-permute-start(bf16[1024,1024]{0,1:T(8,128)(2,1)S(1)} %convolution_convert_fusion.7), channel_id=1, source_target_pairs={{0,1},{1,0},{2,3},{3,2},{4,5},{5,4},{6,7},{7,6},{8,9},{9,8},{10,11... | collective-permute-start | bytes 6291464 | tf_op jit(solution)/shard_map/ppermute | solution.py:640
  147.1 6.1 %copy-start.4 = (bf16[1024,1024]{0,1:T(8,128)(2,1)S(1)}, bf16[1024,1024]{0,1:T(8,128)(2,1)}, u32[]{:S(2)}) copy-start(bf16[1024,1024]{0,1:T(8,128)(2,1)} %all-gather.3.cloned.1.call-done) | copy-start | bytes 6291460
  156.4 3.9 copy-start.29
  158.5 5.3 %copy-start.7 = (bf16[1024,1024]{0,1:T(8,128)(2,1)}, bf16[1024,1024]{0,1:T(8,128)(2,1)S(1)}, u32[]{:S(2)}) copy-start(bf16[1024,1024]{0,1:T(8,128)(2,1)S(1)} %multiply_convert_fusion.1) | copy-start | bytes 6291460
  160.3 3.5 copy-start.27
  173.8 3.4 copy-start.32
  173.8 3.5 copy-start.34
  177.3 4.2 %copy-start.28 = (bf16[4,2,2,64,1408]{4,3,2,1,0:T(8,128)(2,1)S(1)}, bf16[4,2,2,64,1408]{4,3,2,1,0:T(8,128)(2,1)}, u32[]{:S(2)}) copy-start(bf16[4,2,2,64,1408]{4,3,2,1,0:T(8,128)(2,1)} %get-tuple-element.37) | copy-start | bytes 8650756
  177.3 4.2 %copy-start.36 = (bf16[1024,1408]{1,0:T(8,128)(2,1)S(1)}, bf16[1024,1408]{1,0:T(8,128)(2,1)}, u32[]{:S(2)}) copy-start(bf16[1024,1408]{1,0:T(8,128)(2,1)} %get-tuple-element.80) | copy-start | bytes 8650756
  181.0 13.3 %collective-permute-start.1 = (bf16[1024,1024]{0,1:T(8,128)(2,1)S(1)}, bf16[1024,1024]{0,1:T(8,128)(2,1)}, u32[]{:S(2)}, u32[]{:S(2)}) collective-permute-start(bf16[1024,1024]{0,1:T(8,128)(2,1)S(1)} %add_convert_fusion), channel_id=1, source_target_pairs={{0,1},{1,0},{2,3},{3,2},{4,5},{5,4},{6,7},{7,6},{8,9},{9,8},{10,11... | collective-permute-start | bytes 6291464 | tf_op jit(solution)/shard_map/ppermute | solution.py:640
  186.1 182.6 %reduce-scatter.5.cloned.1.call-start = ((), (), s32[]{:S(2)}) async-start(), calls=%async_computation.5 | async-start | bytes 3145728 | tf_op jit(solution)/shard_map/reduce_scatter | solution.py:698
  186.6 7.6 %copy-start.1 = (f32[1024,1024]{0,1:T(8,128)S(1)}, f32[1024,1024]{0,1:T(8,128)}, u32[]{:S(2)}) copy-start(f32[1024,1024]{0,1:T(8,128)} %copy-done) | copy-start | bytes 12582916
  197.0 5.7 %copy-start.31 = (bf16[4,2,2,64,512]{4,3,2,1,0:T(8,128)(2,1)S(1)}, bf16[4,2,2,64,512]{4,3,2,1,0:T(8,128)(2,1)}, u32[]{:S(2)}) copy-start(bf16[4,2,2,64,512]{4,3,2,1,0:T(8,128)(2,1)} %get-tuple-element.34) | copy-start | bytes 3145732
  251.5 4.6 %copy-start.26 = (bf16[4,2,2,64,1536]{4,3,2,1,0:T(8,128)(2,1)S(1)}, bf16[4,2,2,64,1536]{4,3,2,1,0:T(8,128)(2,1)}, u32[]{:S(2)}) copy-start(bf16[4,2,2,64,1536]{4,3,2,1,0:T(8,128)(2,1)} %get-tuple-element.31) | copy-start | bytes 9437188
  256.1 4.7 %copy-start.2 = (bf16[512,1024]{0,1:T(8,128)(2,1)S(1)}, bf16[512,1024]{0,1:T(8,128)(2,1)}, u32[]{:S(2)}) copy-start(bf16[512,1024]{0,1:T(8,128)(2,1)} %copy.40) | copy-start | bytes 3145732
  263.8 4.7 %copy-start.33 = (bf16[1024,1408]{1,0:T(8,128)(2,1)S(1)}, bf16[1024,1408]{1,0:T(8,128)(2,1)}, u32[]{:S(2)}) copy-start(bf16[1024,1408]{1,0:T(8,128)(2,1)} %copy-done.32) | copy-start | bytes 8650756
  268.6 4.8 %copy-start.5 = (bf16[1024,1024]{0,1:T(8,128)(2,1)S(1)}, bf16[1024,1024]{0,1:T(8,128)(2,1)}, u32[]{:S(2)}) copy-start(bf16[1024,1024]{0,1:T(8,128)(2,1)} %all-gather.3.cloned.1.call-done) | copy-start | bytes 6291460
  268.6 4.8 %copy-start.16 = (bf16[1024,1536]{1,0:T(8,128)(2,1)S(1)}, bf16[1024,1536]{1,0:T(8,128)(2,1)}, u32[]{:S(2)}) copy-start(bf16[1024,1536]{1,0:T(8,128)(2,1)} %copy-done.15) | copy-start | bytes 9437188
  389.1 3.3 copy-start.14
  389.1 4.0 copy-start.13
  389.1 4.7 %copy-start.12 = (f32[64,1408]{1,0:T(8,128)S(1)}, f32[64,1408]{1,0:T(8,128)}, u32[]{:S(2)}) copy-start(f32[64,1408]{1,0:T(8,128)} %get-tuple-element.49) | copy-start | bytes 1081348
  (12 other events, 29.1 us)
Sparse Core Ops, SparseCore 0:
  10.2 13.2 all-gather.2
  25.6 11.7 all-gather.4
  186.2 8.8 reduce-scatter.2
  260.9 9.5 reduce-scatter.4

commit v4 on v3

--- a/solution.py
+++ b/solution.py
@@ -612,6 +612,163 @@
         compiler_params=pltpu.CompilerParams(collective_id=cid, has_side_effects=True), name="small_sums")(part)
 
 
+TILE = 256
+
+
+def nt(a, b):
+    return lax.dot_general(a, b, NT, preferred_element_type=f32)
+
+
+def nn(a, b):
+    return jnp.dot(a, b, preferred_element_type=f32)
+
+
+def gelu_and_slope(v):
+    root = 0.7978845608028654
+    square = v * v
+    t = jnp.tanh(root * v * (1.0 + 0.044715 * square))
+    half = 0.5 * (1.0 + t)
+    return v * half, half + 0.5 * v * (1.0 - t * t) * root * (1.0 + 3 * 0.044715 * square)
+
+
+def mid_kernel(att_h, tok_h, cot_h, wo_h, wg_h, wu_h, wd_h, gain_ref,
+               gout_h, gg_h, gu_h, gd_h, y_ref, gh_ref, ga_ref, ggain_ref,
+               att, tok, cot, wo, wg, wu, wd, part, other, back, hid, n2, n2t, cott, hff, gg, gu, ysend, yown, yother, stage,
+               isem, osem, sp, vp, sb, vb, sy, vy):
+    core = lax.axis_index("narrow")
+    peer = {"narrow": 1 - core}
+    n, d = tok.shape
+    ff = wg.shape[1]
+    tiles = n // TILE
+    half = tiles // 2
+    loads = [pltpu.make_async_copy(s, t, isem.at[k]) for k, (s, t) in enumerate(
+        [(att_h, att), (wo_h, wo), (tok_h, tok), (wg_h, wg), (wu_h, wu), (wd_h, wd), (cot_h, cot)])]
+    for c in loads:
+        c.start()
+    bar = pltpu.get_barrier_semaphore()
+    pl.semaphore_signal(bar, inc=1, device_id=peer, device_id_type=MESH)
+    pl.semaphore_wait(bar, 1)
+    rows_of = lambda t: pl.ds(pl.multiple_of(t * TILE, TILE), TILE)
+    send_part = lambda t: remote(part.at[rows_of(t)], other.at[rows_of(t)], sp.at[t], vp.at[t], peer)
+    send_back = lambda t: remote(part.at[rows_of(t)], back.at[rows_of(t)], sb.at[t], vb.at[t], peer)
+    send_y = lambda j: remote(ysend.at[rows_of(j)], yother.at[rows_of(j)], sy.at[j], vy.at[j], peer)
+    gain = gain_ref[...]
+
+    for c in loads[:2]:
+        c.wait()
+
+    @pl.loop(0, tiles)
+    def _(t):
+        part[rows_of(t), :] = nt(att[rows_of(t), :], wo[...]).astype(bf16)
+        send_part(t).start()
+
+    for c in loads[2:]:
+        c.wait()
+
+    chunks, at = [], 0
+    while at < ff:
+        w = min(384, ff - at)
+        chunks.append((at, w))
+        at += w
+
+    @pl.loop(0, tiles)
+    def _(s):
+        t = (s + half * (1 - core)) % tiles
+        r = rows_of(t)
+        send_part(t).wait()
+        h = tok[r, :].astype(f32) + (part[r, :].astype(f32) + other[r, :].astype(f32))
+        hid[r, :] = h
+        factor = lax.rsqrt(jnp.mean(h * h, axis=1, keepdims=True) + epsilon)
+        low = (h * factor * gain).astype(bf16)
+        n2[r, :] = low
+        n2t[:, r] = low.T
+        ct = cot[r, :]
+        cott[:, r] = ct.T
+        for at, w in chunks:
+            cols = pl.ds(at, w)
+            act, slope = gelu_and_slope(nn(low, wg[:, cols]))
+            up = nn(low, wu[:, cols])
+            gf = nn(ct, wd[:, cols])
+            hff[r, cols] = (act * up).astype(bf16)
+            gg[r, cols] = (gf * up * slope).astype(bf16)
+            gu[r, cols] = (gf * act).astype(bf16)
+        part[r, :] = (nt(gg[r, :], wg[...]) + nt(gu[r, :], wu[...])).astype(bf16)
+        send_back(t).start()
+        y = nt(hff[r, :], wd[...]).astype(bf16)
+
+        @pl.when(s < half)
+        def _():
+            ysend[rows_of(s), :] = y
+            send_y(s).start()
+
+        @pl.when(s >= half)
+        def _():
+            yown[rows_of(s - half), :] = y
+
+    def weight_grad(left, right, out, slot, width):
+        @pl.loop(0, d // TILE)
+        def _(k):
+            b = k % 2
+            copy = lambda kk: pltpu.make_async_copy(stage.at[kk % 2, :, pl.ds(0, width)], out.at[rows_of(kk)], osem.at[2 * slot + kk % 2])
+
+            @pl.when(k >= 2)
+            def _():
+                copy(k - 2).wait()
+
+            stage[b, :, pl.ds(0, width)] = nn(left[rows_of(k), :], right[...]).astype(bf16)
+            copy(k).start()
+
+        for k in range(d // TILE - 2, d // TILE):
+            pltpu.make_async_copy(stage.at[k % 2, :, pl.ds(0, width)], out.at[rows_of(k)], osem.at[2 * slot + k % 2]).wait()
+
+    weight_grad(cott, hff, gd_h, 0, ff)
+    ggain_ref[...] = jnp.zeros_like(ggain_ref)
+
+    @pl.loop(0, tiles)
+    def _(s):
+        t = (s + half * (1 - core)) % tiles
+        r = rows_of(t)
+        send_back(t).wait()
+        total = part[r, :].astype(f32) + back[r, :].astype(f32)
+        h = hid[r, :]
+        factor = lax.rsqrt(jnp.mean(h * h, axis=1, keepdims=True) + epsilon)
+        unit = h * factor
+        g = gain * total
+        gh = cot[r, :].astype(f32) + factor * (g - unit * jnp.mean(g * unit, axis=1, keepdims=True))
+        low = gh.astype(bf16)
+        cott[:, r] = low.T
+        ga_ref[r, :] = nn(low, wo[...]).astype(bf16)
+
+        @pl.when(s >= half)
+        def _():
+            j = rows_of(s - half)
+            gh_ref[j, :] = gh
+            ggain_ref[...] += jnp.sum(total * unit, axis=0, keepdims=True)
+            send_y(s - half).wait()
+            y_ref[j, :] = (h + (yown[j, :].astype(f32) + yother[j, :].astype(f32))).astype(bf16)
+
+    weight_grad(n2t, gg, gg_h, 1, ff)
+    weight_grad(n2t, gu, gu_h, 2, ff)
+    weight_grad(cott, att, gout_h, 3, att.shape[1])
+
+
+def middle(att, tok, cot, wo, wg, wu, wd, gain, cid):
+    n, d = tok.shape
+    units, ff = att.shape[1], wg.shape[1]
+    B = lambda *s: pltpu.VMEM(s, bf16)
+    sds = jax.ShapeDtypeStruct
+    tiles = n // TILE
+    return pl.pallas_call(mid_kernel,
+        out_shape=(sds((d, units), bf16), sds((d, ff), bf16), sds((d, ff), bf16), sds((d, ff), bf16),
+                   sds((n // 2, d), bf16), sds((n // 2, d), f32), sds((n, units), bf16), sds((1, d), f32)),
+        in_specs=[ANY] * 7 + [whole_vmem()], out_specs=(ANY,) * 4 + (whole_vmem(),) * 4,
+        scratch_shapes=[B(n, units), B(n, d), B(n, d), B(d, units), B(d, ff), B(d, ff), B(d, ff), B(n, d), B(n, d), B(n, d),
+                        pltpu.VMEM((n, d), f32), B(n, d), B(d, n), B(d, n), B(n, ff), B(n, ff), B(n, ff),
+                        B(n // 2, d), B(n // 2, d), B(n // 2, d), B(2, TILE, ff),
+                        D((7,)), D((8,)), D((tiles,)), D((tiles,)), D((tiles,)), D((tiles,)), D((tiles // 2,)), D((tiles // 2,))],
+        compiler_params=params(cid), name="feed_forward")(att, tok, cot, wo, wg, wu, wd, gain)
+
+
 epsilon = 1e-06
 
 
@@ -620,10 +777,6 @@
     return values * factor * gain_row
 
 
-def gated_unit(gate_pre, up_pre):
-    return jax.nn.gelu(gate_pre, approximate=True) * up_pre
-
-
 def times(a, b):
     return jnp.dot(a, b, preferred_element_type=f32)
 
@@ -634,14 +787,6 @@
 
 def transposed_times(a, b):
     return lax.dot_general(a, b, (((0,), (0,)), ((), ())), preferred_element_type=f32)
-
-
-def swap(a):
-    return lax.ppermute(a, "narrow", [(0, 1), (1, 0)])
-
-
-def both(a):
-    return a.astype(f32) + swap(a).astype(f32)
 
 
 def local(tokens, cotangent, pages, boxes, gain_attn, gain_ffn, bias_tables, w_query, w_key, w_value, w_out, w_gate, w_up, w_down):
@@ -652,8 +797,6 @@
     core = lax.axis_index("narrow")
     tables = lax.dynamic_slice_in_dim(bias_tables, core * heads, heads, 1)
     inner, ff = w_query.shape[1], w_gate.shape[1]
-    mine = lambda a: lax.dynamic_slice_in_dim(a, core * rows, rows, 0)
-
     all_tokens = lax.all_gather(tokens, "narrow", axis=0, tiled=True)
     all_cot = lax.all_gather(cotangent, "narrow", axis=0, tiled=True)
     early = inner // 4 * 3
@@ -666,43 +809,24 @@
     normed = norm_plain(x, gain_one).astype(bf16)
     qkv = times(normed, w_first).astype(bf16)
     attended, lse, (full_up, full_down) = attn_fwd_and_gather(qkv, bias, [w_up, w_down.T], (((0, 0, ff),), ((1, 0, ff),)), wide, 2)
-    hidden = x + both(times_transposed(attended, full_out).astype(bf16))
-    normed_two = norm_plain(hidden, gain_two).astype(bf16)
-    gate_pre, up_pre = times(normed_two, full_gate), times(normed_two, full_up)
-    hidden_ff = gated_unit(gate_pre, up_pre).astype(bf16)
-    down = times_transposed(hidden_ff, full_down).astype(bf16)
-    output = (mine(hidden) + lax.psum_scatter(down, "narrow", scatter_dimension=0, tiled=True).astype(f32)).astype(bf16)
-
-    grad_w_down = transposed_times(all_cot, hidden_ff)
-    grad_ff = times(all_cot, full_down)
-    _, gated_pull = jax.vjp(gated_unit, gate_pre, up_pre)
-    grad_gate, grad_up = [g.astype(bf16) for g in gated_pull(grad_ff)]
-    grad_w_gate = transposed_times(normed_two, grad_gate)
-    grad_w_up = transposed_times(normed_two, grad_up)
-    grad_two = both((times_transposed(grad_gate, full_gate) + times_transposed(grad_up, full_up)).astype(bf16))
-    _, pull_two = jax.vjp(lambda h: norm_plain(h, gain_two), hidden)
-    grad_hidden = all_cot.astype(f32) + pull_two(grad_two)[0]
-    own_hidden = mine(hidden)
-    grad_gain_two = jnp.sum(mine(grad_two) * own_hidden * lax.rsqrt(jnp.mean(own_hidden * own_hidden, axis=-1, keepdims=True) + epsilon), axis=0)
-    grad_low = grad_hidden.astype(bf16)
-    grad_w_out = transposed_times(grad_low, attended)
-    grad_attended = times(grad_low, full_out).astype(bf16)
+    grad_w_out, grad_w_gate, grad_w_up, grad_w_down, output, grad_hidden, grad_attended, grad_gain_two = middle(
+        attended, all_tokens, all_cot, full_out, full_gate, full_up, full_down, gain_two[None], 6)
     (dq, dk, dv, g), (s_down, s_out) = attn_bwd_and_scatter(
-        qkv, bias, attended, grad_attended, lse, [grad_w_down.astype(bf16), grad_w_out.astype(bf16)],
+        qkv, bias, attended, grad_attended, lse, [grad_w_down, grad_w_out],
         (((0, 0, 2 * inner),), ((0, 2 * inner, ff - 2 * inner), (1, 0, inner))), wide, 3)
     dqkv = jnp.concatenate([dq, dk, dv], axis=1)
     mid = 3 * inner // 2
     table_part, (s_gate, s_up, s_first) = hist_and_scatter(
-        g, ids, [grad_w_gate.astype(bf16), grad_w_up.astype(bf16), transposed_times(normed, dqkv).astype(bf16)],
+        g, ids, [grad_w_gate, grad_w_up, transposed_times(normed, dqkv).astype(bf16)],
         (((0, 0, ff), (2, 0, mid)), ((1, 0, ff), (2, mid, mid))), wide, 4)
     grad_normed = lax.psum_scatter(times_transposed(dqkv, w_first).astype(bf16), "narrow", scatter_dimension=0, tiled=True).astype(f32)
     own = tokens.astype(f32)
     _, pull_one = jax.vjp(norm_plain, own, gain_one)
     grad_tokens_norm, grad_gain_one = pull_one(grad_normed)
-    grad_tokens = mine(grad_hidden) + grad_tokens_norm
+    grad_tokens = grad_hidden + grad_tokens_norm
     table_part = lax.dynamic_update_slice(jnp.zeros((bias_tables.shape[0], heads_all), f32), table_part.T, (jnp.int32(0), core * heads))
     sizes = [gain_one.size, gain_two.size, table_part.size]
-    small = sum_all(jnp.concatenate([grad_gain_one, grad_gain_two, table_part.reshape(-1)]).reshape(-1, 128), wide, 5).reshape(-1)
+    small = sum_all(jnp.concatenate([grad_gain_one, grad_gain_two[0], table_part.reshape(-1)]).reshape(-1, 128), wide, 5).reshape(-1)
     one, two, table = jnp.split(small, [sizes[0], sizes[0] + sizes[1]])
     s_query, s_key, s_value = jnp.split(s_first, 3, axis=1)
     return (output, grad_tokens, one, two, table.reshape(bias_tables.shape), s_query, s_key, s_value, s_out.T, s_gate, s_up, s_down.T)

time: 409 us -> 380 us (0.929); the launches traced: 401 us -> 378 us
  matrix products: 73 us -> 19.2 us
  Pallas kernels: 260 us -> 313 us
  other arithmetic: 25.9 us -> 10.9 us
  local copies, waits for them, and re-layouts: 26.5 us -> 19.7 us
    pallas_call x0 -> x1, Pallas kernels: none -> 55.2 us  [middle(): pl.pallas_call(mid_kernel, out_shape=(sds((d, units), bf16), sds((d, ff),...]
    dot_general x5 -> x1, matrix products: 29.8 us -> 7.66 us  [times(): return jnp.dot(a, b, preferred_element_type=f32)]
    dot_general x5 -> x1, matrix products: 24.3 us -> 6.88 us  [transposed_times(): lax.dot_general(a, b, (((0,), (0,)), ((), ())), preferred_element_type=f32)]
    dot_general x5 -> x1, matrix products: 18.9 us -> 4.62 us  [times_transposed(): return lax.dot_general(a, b, NT, preferred_element_type=f32)]
    unnamed x86 -> x43, local copies, waits for them, and re-layouts: 20.3 us -> 12.1 us
    add x2 -> x1, other arithmetic: 8.18 us -> 3.26 us  [local(): grad_tokens = grad_hidden + grad_tokens_norm]
    reduce_sum x2 -> x0, other arithmetic: 4.91 us -> none  [the longest x1 2.94 us: local(): jnp.sum(mine(grad_two) * own_hidden * lax.rsqrt(jnp.mean(own_hidden * own...]
  transfers between devices with their start and end apart: 6 -> 3, of which waited for: 0 -> 0; matrix products, arithmetic and copies ran while one was open for 20% -> 7% of each run, Pallas kernels for 61% -> 53%
where the time goes in v4:
time: 380 us; the launch traced here: 378 us
  Pallas kernels  313 us (82%)
  local copies, waits for them, and re-layouts  19.7 us (5%)
  matrix products  19.2 us (5%)
  between operations  14 us (4%)
  other arithmetic  10.9 us (3%)
    pallas_call x1, Pallas kernels, hist_and_scatter(): pl.pallas_call(functools.partial(hist_kernel, heads, rows, n, G, halves,...  81.7 us
    pallas_call x1, Pallas kernels, bias_and_gather(): pl.pallas_call(functools.partial(bias_gather_kernel, heads, rows, n, G, h...  66.4 us
    pallas_call x1, Pallas kernels, middle(): pl.pallas_call(mid_kernel, out_shape=(sds((d, units), bf16), sds((d, ff),...  55.2 us
    pallas_call x1, Pallas kernels, attn_fwd_and_gather(): pl.pallas_call(functools.partial(fwd_kernel, pairs * tiles, tiles, G, hal...  52.5 us
    pallas_call x1, Pallas kernels, attn_bwd_and_scatter(): pl.pallas_call(functools.partial(bwd_kernel, pairs * tiles, tiles, G, hal...  43.2 us
    pallas_call x1, Pallas kernels, sum_all(): pl.pallas_call(functools.partial(sum_kernel, G), out_shape=jax.ShapeDtype...  13.5 us
    unnamed x43, local copies, waits for them, and re-layouts  12.1 us
    dot_general x1, matrix products, times(): return jnp.dot(a, b, preferred_element_type=f32)  7.66 us
  transfers between devices with their start and end apart: 3, of which 0 were waited for; matrix products, arithmetic and copies ran while one was open for 7% of the time, Pallas kernels for 53%

profile of v4, /device:TPU:0, one launch (start us, length us, event | category | flops | bytes accessed | tf_op | source)
XLA Modules:
  0.0 378.0 jit_solution(6342209617896414858)
XLA Ops:
  7.3 0.7 all-gather.3.cloned.1.call-update
  8.0 0.7 all-gather.5.cloned.1.call-update
  8.8 0.7 round-nearest-even_convert_fusion
  10.2 1.7 copy.31
  11.9 1.7 copy.32.refs_4_
  14.7 0.7 pad_maximum_fusion.refs_6_
  15.4 66.4 %layout_bias_gather.1 = (f32[8,1024,1024]{2,1,0:T(8,128)}, f32[3,1024,1024]{2,1,0:T(8,128)}, bf16[4,2,2,64,1536]{4,3,2,1,0:T(8,128)(2,1)}, bf16[4,2,2,64,512]{4,...) custom-call(s32[1,128]{1,0:T(1,128)} %fusion.28.refs_0_, s32[12,128]{1,0:T(8,128)} %pad.4.refs_1_, s32[1024,2]{1,0:T(8,128)} %bitcast.43, ...), custom_call_target="tpu_custom_call" | custom-call | tf_op jit(solution)/shard_map/layout_bias_gather/pallas_call | solution.py:85
  81.9 2.1 fusion
  84.0 7.7 %convolution_convert_fusion.1.refs_0_.refs_1_.refs_2_ = bf16[1024,1536]{1,0:T(8,128)(2,1)} fusion(bf16[1024,1536]{1,0:T(8,128)(2,1)} %bitcast.55, bf16[1024,1024]{1,0:T(8,128)(2,1)} %all-gather.3.cloned.1.call-done.tok_h, f32[1024]{0:T(1024)S(1)} %convert_element_type.182, f32[1024]{0:T(1024)S(1)} %add_rsqrt_fusion), kind=kOutput, calls=%fused_computation.6 | convolution fusion | flops 3226992640 | bytes 8396800 | tf_op jit(solution)/shard_map/dot_general | solution.py:781
  91.6 52.5 %attention_gather.1 = (bf16[1024,512]{1,0:T(8,128)(2,1)}, f32[4,1024,2]{2,1,0:T(8,128)}, bf16[4,2,2,64,1408]{4,3,2,1,0:T(8,128)(2,1)}, bf16[4,2,2,64,1408]{4,3,2,1,0:T(8,128)(2,1)}) custom-call(bf16[1024,1536]{1,0:T(8,128)(2,1)} %convolution_convert_fusion.1.refs_0_.refs_1_.refs_2_, bf16[1024,1536]{1,0:T(8,128)(2,1)} %convolution_convert_fusion.1.refs_0_.refs_1_.refs_2_, ...), custom_call_target="tpu_custom_call" | custom-call | tf_op jit(solution)/shard_map/attention_gather/pallas_call | solution.py:133
  144.2 55.2 %feed_forward.1 = (bf16[1024,512]{1,0:T(8,128)(2,1)}, bf16[1024,1408]{1,0:T(8,128)(2,1)}, bf16[1024,1408]{1,0:T(8,128)(2,1)}, bf16[1024,1408]{1,0:T(8,128)(2,1)}...) custom-call(bf16[1024,512]{1,0:T(8,128)(2,1)} %get-tuple-element.41.att_h.refs, ...), custom_call_target="tpu_custom_call" | custom-call | tf_op jit(solution)/shard_map/feed_forward/pallas_call | solution.py:761
  199.5 43.2 %attention_back_scatter.1 = (bf16[1024,512]{1,0:T(8,128)(2,1)}, bf16[1024,512]{1,0:T(8,128)(2,1)}, bf16[1024,512]{1,0:T(8,128)(2,1)}, bf16[8,1024,1024]{2,1,0:T(...) custom-call(bf16[1024,1536]{1,0:T(8,128)(2,1)} %convolution_convert_fusion.1.refs_0_.refs_1_.refs_2_, ...), custom_call_target="tpu_custom_call" | custom-call | tf_op jit(solution)/shard_map/attention_back_scatter/pallas_call | solution.py:188
  242.7 1.4 constant_dynamic-update-slice_fusion.2
  244.1 1.4 constant_dynamic-update-slice_fusion.1
  245.6 1.7 copy-done.8
  247.3 4.6 %convolution_convert_fusion.2 = bf16[1024,1024]{1,0:T(8,128)(2,1)} fusion(bf16[1024,1536]{1,0:T(8,128)(2,1)S(1)} %constant_dynamic-update-slice_fusion, bf16[1024,1536]{1,0:T(8,128)(2,1)S(1)} %bitcast.56), kind=kOutput, calls=%fused_computation.19 | convolution fusion | flops 3222274048 | bytes 8388608 | tf_op jit(solution)/shard_map/dot_general | solution.py:785
  252.3 1.3 copy-done.1
  253.5 6.9 %convolution_convert_fusion = bf16[1024,1536]{1,0:T(8,128)(2,1)} fusion(bf16[1024,1536]{1,0:T(8,128)(2,1)} %copy-done.8, bf16[1024,1024]{1,0:T(8,128)(2,1)S(1)} %copy-done.1, f32[1024]{0:T(1024)S(1)} %convert_element_type.182, f32[1024]{0:T(1024)S(1)} %add_rsqrt_fusion), kind=kOutput, calls=%fused_computation.5 | convolution fusion | flops 3226992640 | bytes 8396800 | tf_op jit(solution)/shard_map/dot_general | solution.py:789
  260.4 81.7 %table_grad_scatter.1 = (f32[8,96]{1,0:T(8,128)}, f32[64,1408]{1,0:T(8,128)}, f32[64,1408]{1,0:T(8,128)}, f32[64,1536]{1,0:T(8,128)}) custom-call(bf16[8,1024,1024]{2,1,0:T(8,128)(2,1)} %get-tuple-element.56.refs_0_, f32[3,1024,1024]{2,1,0:T(8,128)} %get-tuple-element.57.refs_1_, bf16[4,2,2,64,1408]{4,3,2,1,0:T(8,128)(2,1)} %bitcast.37, ...), custom_call_target="tpu_custom_call" | custom-call | tf_op jit(solution)/shard_map/table_grad_scatter/pallas_call | solution.py:230
  342.1 0.9 copy.33
  343.5 1.8 fusion.42
  345.3 2.2 fusion.4
  348.1 13.5 %small_sums.1 = f32[28,128]{1,0:T(8,128)} custom-call(f32[28,128]{1,0:T(8,128)} %maximum_bitcast_fusion.src), custom_call_target="tpu_custom_call" | custom-call | tf_op jit(solution)/shard_map/small_sums/pallas_call | solution.py:609
  361.6 0.7 split.26
  362.3 1.3 slice_bitcast_fusion
  363.6 0.7 copy.34
  364.4 3.3 fusion.5
  367.6 1.0 copy.43
  368.6 0.7 copy.44
  369.3 0.7 copy.45
  370.0 0.7 copy.46
  370.7 0.7 copy.47
  (57 shorter events, 3.6 us)
Async XLA Ops:
  7.2 6.4 %copy-start.14 = (bf16[1024]{0:T(1024)(128)(2,1)S(1)}, bf16[1024]{0:T(1024)(128)(2,1)}, u32[]{:S(2)}) copy-start(bf16[1024]{0:T(1024)(128)(2,1)} %param.18) | copy-start | bytes 6148
  7.2 6.4 %copy-start.15 = (bf16[1024]{0:T(1024)(128)(2,1)S(1)}, bf16[1024]{0:T(1024)(128)(2,1)}, u32[]{:S(2)}) copy-start(bf16[1024]{0:T(1024)(128)(2,1)} %param.19) | copy-start | bytes 6148
  7.2 7.5 %copy-start.12 = (bf16[64,512]{1,0:T(8,128)(2,1)S(1)}, bf16[64,512]{1,0:T(8,128)(2,1)}, u32[]{:S(2)}) copy-start(bf16[64,512]{1,0:T(8,128)(2,1)} %param.21) | copy-start | bytes 196612
  7.2 7.5 %copy-start.11 = (bf16[64,512]{1,0:T(8,128)(2,1)S(1)}, bf16[64,512]{1,0:T(8,128)(2,1)}, u32[]{:S(2)}) copy-start(bf16[64,512]{1,0:T(8,128)(2,1)} %param.22) | copy-start | bytes 196612
  7.2 7.5 %copy-start.10 = (bf16[64,512]{1,0:T(8,128)(2,1)S(1)}, bf16[64,512]{1,0:T(8,128)(2,1)}, u32[]{:S(2)}) copy-start(bf16[64,512]{1,0:T(8,128)(2,1)} %param.23) | copy-start | bytes 196612
  7.2 74.6 %all-gather.3.cloned.1.call-start = ((), (), s32[]{:S(2)}) async-start(), calls=%async_computation.1 | async-start | bytes 3145728 | tf_op jit(solution)/shard_map/all_gather | solution.py:800
  8.0 136.2 %all-gather.5.cloned.1.call-start = ((), (), s32[]{:S(2)}) async-start(), calls=%async_computation.2 | async-start | bytes 3145728 | tf_op jit(solution)/shard_map/all_gather | solution.py:801
  8.7 336.6 %reduce-scatter.2.cloned.1.call-start = ((), (), s32[]{:S(2)}) async-start(), calls=%async_computation.3 | async-start | bytes 3145728 | tf_op jit(solution)/shard_map/reduce_scatter | solution.py:822
  242.7 2.9 copy-start.4
  242.7 4.6 %copy-start.16 = (bf16[4,2,2,64,1536]{4,3,2,1,0:T(8,128)(2,1)S(1)}, bf16[4,2,2,64,1536]{4,3,2,1,0:T(8,128)(2,1)}, u32[]{:S(2)}) copy-start(bf16[4,2,2,64,1536]{4,3,2,1,0:T(8,128)(2,1)} %get-tuple-element.39) | copy-start | bytes 9437188
  245.6 1.7 copy-start.8
  247.3 4.6 %copy-start = (bf16[512,1024]{1,0:T(8,128)(2,1)S(1)}, bf16[512,1024]{1,0:T(8,128)(2,1)}, u32[]{:S(2)}) copy-start(bf16[512,1024]{1,0:T(8,128)(2,1)} %param.14) | copy-start | bytes 3145732
  251.9 1.6 copy-start.1
  342.1 5.3 %copy-start.13 = (f32[1,1024]{1,0:T(1,128)S(1)}, f32[1,1024]{1,0:T(1,128)}, u32[]{:S(2)}) copy-start(f32[1,1024]{1,0:T(1,128)} %get-tuple-element.55) | copy-start | bytes 12292
  342.1 22.2 %copy-start.2 = (f32[512,1024]{1,0:T(8,128)S(1)}, f32[512,1024]{1,0:T(8,128)}, u32[]{:S(2)}) copy-start(f32[512,1024]{1,0:T(8,128)} %get-tuple-element.47) | copy-start | bytes 6291460
  364.3 3.3 copy-start.3
  364.3 4.3 %copy-start.9 = (f32[64,512]{1,0:T(8,128)S(1)}, f32[64,512]{1,0:T(8,128)}, u32[]{:S(2)}) copy-start(f32[64,512]{1,0:T(8,128)} %get-tuple-element.62) | copy-start | bytes 393220
  364.4 4.9 %copy-start.7 = (f32[64,1408]{1,0:T(8,128)S(1)}, f32[64,1408]{1,0:T(8,128)}, u32[]{:S(2)}) copy-start(f32[64,1408]{1,0:T(8,128)} %get-tuple-element.118) | copy-start | bytes 1081348
  364.4 5.6 %copy-start.6 = (f32[64,1408]{1,0:T(8,128)S(1)}, f32[64,1408]{1,0:T(8,128)}, u32[]{:S(2)}) copy-start(f32[64,1408]{1,0:T(8,128)} %get-tuple-element.119) | copy-start | bytes 1081348
  367.6 3.1 copy-start.5
Sparse Core Ops, SparseCore 0:
  9.6 13.2 all-gather.2
  24.5 11.7 all-gather.4
  252.1 9.5 reduce-scatter.1

commit v5 on v4

--- a/solution.py
+++ b/solution.py
@@ -16,6 +16,8 @@
 VM = 58 * 2**20
 TABLE_SCALE = 2047.0
 TABLE_LIFT = 8192
+TILE = 256
+epsilon = 1e-06
 
 
 def params(cid):
@@ -71,7 +73,7 @@
     outs, lins, sems = refs[8 + count:8 + 2 * count], refs[8 + 2 * count:10 + 2 * count], refs[10 + 2 * count:]
     now = pl.program_id(0)
     comm = Gather(G, halves, srcs, outs, *sems)
-    beside(comm, n // rows, now, lambda: bias_tile(now * rows, heads, rows, n, *ins, bias_ref, ids_ref, *lins))
+    beside(comm.events(), G, n // rows, now, lambda: bias_tile(now * rows, heads, rows, n, *ins, bias_ref, ids_ref, *lins))
 
 
 def bias_and_gather(tables, boxes, pages, shards, halves, wide, cid):
@@ -105,42 +107,84 @@
     return jnp.where(lane < 64, a, b)
 
 
-def fwd_tile(q_ref, k_ref, v_ref, bias_ref, o_ref, lse_ref):
-    q, k, v = q_ref[...], k_ref[...], v_ref[...]
+def project(tok_ref, gain_ref, w_ref, normed, qkv):
+    gain = gain_ref[...]
+
+    @pl.loop(0, tok_ref.shape[0] // TILE)
+    def _(t):
+        r = pl.ds(pl.multiple_of(t * TILE, TILE), TILE)
+        x = tok_ref[r, :].astype(f32)
+        low = (x * lax.rsqrt(jnp.mean(x * x, axis=1, keepdims=True) + epsilon) * gain).astype(bf16)
+        normed[r, :] = low
+        qkv[r, :] = jnp.dot(low, w_ref[...], preferred_element_type=f32).astype(bf16)
+
+
+def fwd_tile(p, i, tq, pairs, qkv, bias_ref, o_ref, lse_ref):
+    cols = lambda k: pl.ds(pl.multiple_of((p + k * pairs) * 128, 128), 128)
+    q, k, v = qkv[pl.ds(pl.multiple_of(i * tq, tq), tq), cols(0)], qkv[:, cols(1)], qkv[:, cols(2)]
     outs, lses = [], []
     for e in range(2):
         s = lax.dot_general(half_of(q, e), k, NT, preferred_element_type=f32) + bias_ref[e]
         peak = jnp.max(s, axis=1, keepdims=True)
-        p = jnp.exp(s - peak)
-        total = jnp.sum(p, axis=1, keepdims=True)
-        outs.append(jnp.dot(p.astype(bf16), v, preferred_element_type=f32) / total)
+        w = jnp.exp(s - peak)
+        total = jnp.sum(w, axis=1, keepdims=True)
+        outs.append(jnp.dot(w.astype(bf16), v, preferred_element_type=f32) / total)
         lses.append(peak + jnp.log(total))
     o_ref[...] = join(*outs).astype(bf16)
     lse_ref[0] = jnp.concatenate(lses, axis=1)
 
 
-def fwd_kernel(steps, tiles, G, halves, count, *refs):
-    ins, srcs = refs[:4], refs[4:4 + count]
-    mid = refs[4 + count:6 + count]
-    outs, sems = refs[6 + count:6 + 2 * count], refs[6 + 2 * count:]
-    now = pl.program_id(0) * tiles + pl.program_id(1)
-    beside(Gather(G, halves, srcs, outs, *sems), steps, now, lambda: fwd_tile(*ins, *mid))
-
-
-def attn_fwd_and_gather(qkv, bias, shards, halves, wide, cid, tq=256):
-    n, width = qkv.shape[0], qkv.shape[1] // 3
+def fwd_kernel(pairs, tiles, G, halves, count, *refs):
+    (tok, gain, w, bias_ref), srcs = refs[:4], refs[4:4 + count]
+    o_ref, lse_ref, normed_h, qkv_h = refs[4 + count:8 + count]
+    outs, (normed, qkv, keep), sems = refs[8 + count:8 + 2 * count], refs[8 + 2 * count:11 + 2 * count], refs[11 + 2 * count:]
+    p, i = pl.program_id(0), pl.program_id(1)
+    now, steps = p * tiles + i, pairs * tiles
+    copies = lambda: [pltpu.make_async_copy(normed, normed_h, keep.at[0]), pltpu.make_async_copy(qkv, qkv_h, keep.at[1])]
+
+    def compute():
+        @pl.when(now == 0)
+        def _():
+            project(tok, gain, w, normed, qkv)
+            for c in copies():
+                c.start()
+
+        fwd_tile(p, i, o_ref.shape[0], pairs, qkv, bias_ref, o_ref, lse_ref)
+
+        @pl.when(now == steps - 1)
+        def _():
+            for c in copies():
+                c.wait()
+
+    beside(Gather(G, halves, srcs, outs, *sems).events(), G, steps, now, compute)
+
+
+def attn_fwd_and_gather(tok, gain, w, bias, shards, halves, wide, cid, tq=256):
+    n, d = tok.shape
+    width = w.shape[1] // 3
     pairs, tiles, count, G = width // 128, n // tq, len(shards), wide // 4
-    outs = pl.pallas_call(functools.partial(fwd_kernel, pairs * tiles, tiles, G, halves, count), grid=(pairs, tiles),
-        out_shape=(jax.ShapeDtypeStruct((n, width), bf16), jax.ShapeDtypeStruct((pairs, n, 2), f32)) + gathered_shapes(shards, wide),
-        in_specs=[pl.BlockSpec((tq, 128), lambda p, i: (i, p)), pl.BlockSpec((n, 128), lambda p, i: (0, p + pairs)),
-                  pl.BlockSpec((n, 128), lambda p, i: (0, p + 2 * pairs)), pl.BlockSpec((2, tq, n), lambda p, i: (p, i, 0))] + [ANY] * count,
-        out_specs=(pl.BlockSpec((tq, 128), lambda p, i: (i, p)), pl.BlockSpec((1, tq, 2), lambda p, i: (p, i, 0))) + (ANY,) * count,
-        scratch_shapes=gather_scratch(G, halves, count), compiler_params=params(cid), name="attention_gather")(qkv, qkv, qkv, bias, *shards)
-    return outs[0], outs[1], [flat(a) for a in outs[2:]]
-
-
-def bwd_tile(first, last, q_ref, k_ref, v_ref, bias_ref, o_ref, do_ref, lse_ref, dq_ref, dk_ref, dv_ref, g_ref, dkt, dvt):
-    @pl.when(first)
+    sds = jax.ShapeDtypeStruct
+    const = lambda s: pl.BlockSpec(s, lambda p, i: (0, 0))
+    outs = pl.pallas_call(functools.partial(fwd_kernel, pairs, tiles, G, halves, count), grid=(pairs, tiles),
+        out_shape=(sds((n, width), bf16), sds((pairs, n, 2), f32), sds((n, d), bf16), sds((n, 3 * width), bf16)) + gathered_shapes(shards, wide),
+        in_specs=[const((n, d)), const((1, d)), const(w.shape), pl.BlockSpec((2, tq, n), lambda p, i: (p, i, 0))] + [ANY] * count,
+        out_specs=(pl.BlockSpec((tq, 128), lambda p, i: (i, p)), pl.BlockSpec((1, tq, 2), lambda p, i: (p, i, 0)), ANY, ANY) + (ANY,) * count,
+        scratch_shapes=[pltpu.VMEM((n, d), bf16), pltpu.VMEM((n, 3 * width), bf16), D((2,))] + gather_scratch(G, halves, count),
+        compiler_params=params(cid), name="attention_gather")(tok, gain, w, bias, *shards)
+    return outs[:4], [flat(a) for a in outs[4:]]
+
+
+def bwd_tile(p, i, last_tile, last, q_ref, k_ref, v_ref, bias_ref, o_ref, do_ref, lse_ref, normed_ref, wq_ref, wk_ref, wv_ref,
+             g_ref, dwq_ref, dwk_ref, dwv_ref, dx_ref, dkt, dvt, dqkv, turned, dx):
+    tq, n = q_ref.shape[0], k_ref.shape[0]
+    rows = pl.ds(pl.multiple_of(i * tq, tq), tq)
+
+    @pl.when(p == 0)
+    def _():
+        turned[:, rows] = normed_ref[rows, :].T
+        dx[rows, :] = jnp.zeros((tq, dx.shape[1]), f32)
+
+    @pl.when(i == 0)
     def _():
         dkt[...] = jnp.zeros_like(dkt)
         dvt[...] = jnp.zeros_like(dvt)
@@ -151,48 +195,65 @@
     for e in range(2):
         qm, dom = half_of(q, e), half_of(do, e)
         s = lax.dot_general(qm, k, NT, preferred_element_type=f32) + bias_ref[e]
-        p = jnp.exp(s - lse_ref[0, :, e:e + 1])
+        w = jnp.exp(s - lse_ref[0, :, e:e + 1])
         dp = lax.dot_general(dom, v, NT, preferred_element_type=f32)
         inner = jnp.sum(half_of(prod, e), axis=1, keepdims=True)
-        g = (p * (dp - inner)).astype(bf16)
+        g = (w * (dp - inner)).astype(bf16)
         g_ref[e] = g
         dqs.append(jnp.dot(g, k, preferred_element_type=f32))
-        dvt[...] += jnp.dot(dom.T, p.astype(bf16), preferred_element_type=f32)
+        dvt[...] += jnp.dot(dom.T, w.astype(bf16), preferred_element_type=f32)
         dkt[...] += jnp.dot(qm.T, g, preferred_element_type=f32)
-    dq_ref[...] = join(*dqs).astype(bf16)
-
-    @pl.when(last)
+    dqkv[rows, 0:128] = join(*dqs).astype(bf16)
+
+    @pl.when(last_tile)
     def _():
-        dk_ref[...] = dkt[...].T.astype(bf16)
-        dv_ref[...] = dvt[...].T.astype(bf16)
-
-
-def bwd_kernel(steps, tiles, G, halves, count, *refs):
-    ins, parts = refs[:7], refs[7:7 + count]
-    mid = refs[7 + count:11 + count]
-    outs, accs, sems = refs[11 + count:11 + 2 * count], refs[11 + 2 * count:13 + 2 * count], refs[13 + 2 * count:]
-    i = pl.program_id(1)
+        dqkv[:, 128:256] = dkt[...].T.astype(bf16)
+        dqkv[:, 256:384] = dvt[...].T.astype(bf16)
+
+        @pl.loop(0, n // TILE)
+        def _(t):
+            r = pl.ds(pl.multiple_of(t * TILE, TILE), TILE)
+            part = jnp.dot(turned[r, :], dqkv[...], preferred_element_type=f32).astype(bf16)
+            dwq_ref[r, :], dwk_ref[r, :], dwv_ref[r, :] = part[:, 0:128], part[:, 128:256], part[:, 256:384]
+            weights = jnp.concatenate([wq_ref[...], wk_ref[...], wv_ref[...]], axis=1)
+            dx[r, :] += lax.dot_general(dqkv[r, :], weights, NT, preferred_element_type=f32)
+
+        @pl.when(last)
+        def _():
+            dx_ref[...] = dx[...].astype(bf16)
+
+
+def bwd_kernel(pairs, tiles, G, halves, count, *refs):
+    ins, parts = refs[:11], refs[11:11 + count]
+    mid = refs[11 + count:16 + count]
+    outs, accs, sems = refs[16 + count:16 + 2 * count], refs[16 + 2 * count:21 + 2 * count], refs[21 + 2 * count:]
+    p, i = pl.program_id(0), pl.program_id(1)
     comm = Scatter(G, halves, parts, outs, *sems)
-    beside(comm, steps, pl.program_id(0) * tiles + i, lambda: bwd_tile(i == 0, i == tiles - 1, *ins, *mid, *accs))
+    beside(comm.events(), G, pairs * tiles, p * tiles + i,
+           lambda: bwd_tile(p, i, i == tiles - 1, p == pairs - 1, *ins, *mid, *accs))
 
 
 def shard_shapes(parts, wide):
     return tuple(jax.ShapeDtypeStruct((p.shape[0] // wide, p.shape[1]), f32) for p in parts)
 
 
-def attn_bwd_and_scatter(qkv, bias, o, do, lse, parts, halves, wide, cid, tq=256):
-    n, width = qkv.shape[0], qkv.shape[1] // 3
+def attn_bwd_and_scatter(qkv, bias, o, do, lse, normed, w, parts, halves, wide, cid, tq=256):
+    n, width, d = qkv.shape[0], qkv.shape[1] // 3, normed.shape[1]
     pairs, tiles, count, G = width // 128, n // tq, len(parts), wide // 4
+    sds = jax.ShapeDtypeStruct
     tile = pl.BlockSpec((tq, 128), lambda p, i: (i, p))
-    full = pl.BlockSpec((n, 128), lambda p, i: (0, p))
-    outs = pl.pallas_call(functools.partial(bwd_kernel, pairs * tiles, tiles, G, halves, count), grid=(pairs, tiles),
-        out_shape=(jax.ShapeDtypeStruct((n, width), bf16),) * 3 + (jax.ShapeDtypeStruct((2 * pairs, n, n), bf16),) + shard_shapes(parts, wide),
-        in_specs=[tile, pl.BlockSpec((n, 128), lambda p, i: (0, p + pairs)), pl.BlockSpec((n, 128), lambda p, i: (0, p + 2 * pairs)),
-                  pl.BlockSpec((2, tq, n), lambda p, i: (p, i, 0)), tile, tile, pl.BlockSpec((1, tq, 2), lambda p, i: (p, i, 0))] + [ANY] * count,
-        out_specs=(tile, full, full, pl.BlockSpec((2, tq, n), lambda p, i: (p, i, 0))) + (whole_vmem(),) * count,
-        scratch_shapes=[pltpu.VMEM((128, n), f32), pltpu.VMEM((128, n), f32)] + scatter_scratch(G, halves, parts[0].shape[0] // wide),
-        compiler_params=params(cid), name="attention_back_scatter")(qkv, qkv, qkv, bias, o, do, lse, *[spread(p, wide) for p in parts])
-    return outs[:4], outs[4:]
+    full = lambda rows, k: pl.BlockSpec((rows, 128), lambda p, i: (0, p + k * pairs))
+    const = lambda s: pl.BlockSpec(s, lambda p, i: (0, 0))
+    outs = pl.pallas_call(functools.partial(bwd_kernel, pairs, tiles, G, halves, count), grid=(pairs, tiles),
+        out_shape=(sds((2 * pairs, n, n), bf16),) + (sds((d, width), bf16),) * 3 + (sds((n, d), bf16),) + shard_shapes(parts, wide),
+        in_specs=[tile, full(n, 1), full(n, 2), pl.BlockSpec((2, tq, n), lambda p, i: (p, i, 0)), tile, tile,
+                  pl.BlockSpec((1, tq, 2), lambda p, i: (p, i, 0)), const((n, d)), full(d, 0), full(d, 1), full(d, 2)] + [ANY] * count,
+        out_specs=(pl.BlockSpec((2, tq, n), lambda p, i: (p, i, 0)),) + (full(d, 0),) * 3 + (const((n, d)),) + (whole_vmem(),) * count,
+        scratch_shapes=[pltpu.VMEM((128, n), f32), pltpu.VMEM((128, n), f32), pltpu.VMEM((n, 384), bf16), pltpu.VMEM((d, n), bf16),
+                        pltpu.VMEM((n, d), f32)] + scatter_scratch(G, halves, parts[0].shape[0] // wide),
+        compiler_params=params(cid), name="attention_back_scatter")(
+            qkv, qkv, qkv, bias, o, do, lse, normed, w, w, w, *[spread(p, wide) for p in parts])
+    return outs[:5], outs[5:]
 
 
 def hist_tile(first, heads, rows, n, g_ref, ids_ref, out_ref, gs):
@@ -217,23 +278,68 @@
 
 
 def hist_kernel(heads, rows, n, G, halves, count, *refs):
-    ins, parts, out_ref = refs[:2], refs[2:2 + count], refs[2 + count]
-    outs, gs, sems = refs[3 + count:3 + 2 * count], refs[3 + 2 * count], refs[4 + 2 * count:]
-    now = pl.program_id(0)
+    (g_ref, ids_ref, dx, tok, gh, gain_ref, gain_two), parts = refs[:7], refs[7:7 + count]
+    small_ref, gt_ref = refs[7 + count:9 + count]
+    outs, rest = refs[9 + count:9 + 2 * count], refs[9 + 2 * count:]
+    (gs, table, got, pair_sem), sums, sems = rest[:4], rest[4:11], rest[11:]
+    acc = sums[0]
+    now, steps = pl.program_id(0), n // rows
+    core = lax.axis_index("narrow")
+    mine = tok.shape[0]
+    d = tok.shape[1]
     comm = Scatter(G, halves, parts, outs, *sems)
-    beside(comm, n // rows, now, lambda: hist_tile(now == 0, heads, rows, n, *ins, out_ref, gs))
-
-
-def hist_and_scatter(g, ids, parts, halves, wide, cid):
+    swap = lambda: remote(dx.at[pl.ds(pl.multiple_of((1 - core) * mine, mine), mine)], got, pair_sem.at[0], pair_sem.at[1], {"narrow": 1 - core})
+
+    def compute():
+        @pl.when(now == 0)
+        def _():
+            swap().start()
+            acc[0] = jnp.zeros(acc.shape[1:], f32)
+            for k in range(d // 128):
+                acc[0, d // 128 + k:d // 128 + k + 1, :] = gain_two[:, k * 128:(k + 1) * 128]
+
+        @pl.when(now == steps // 8)
+        def _():
+            swap().wait()
+
+        for t in range(mine // TILE):
+            @pl.when(now == steps // 8 + t)
+            def _():
+                r = pl.ds(t * TILE, TILE)
+                x = tok[r, :].astype(f32)
+                total = dx[pl.ds(pl.multiple_of(core * mine + t * TILE, TILE), TILE), :].astype(f32) + got[r, :].astype(f32)
+                factor = lax.rsqrt(jnp.mean(x * x, axis=1, keepdims=True) + epsilon)
+                unit = x * factor
+                scaled = gain_ref[...] * total
+                gt_ref[r, :] = gh[r, :] + factor * (scaled - unit * jnp.mean(scaled * unit, axis=1, keepdims=True))
+                gain = jnp.sum(total * unit, axis=0, keepdims=True)
+                for k in range(d // 128):
+                    acc[0, k:k + 1, :] += gain[:, k * 128:(k + 1) * 128]
+
+        hist_tile(now == 0, heads, rows, n, g_ref, ids_ref, table, gs)
+
+    def reduce():
+        acc[0, pl.ds(pl.multiple_of(2 * (d // 128) + core * heads, 8), heads), 0:96] = table[...]
+        small_ref[...] = sum_everywhere(G, *sums)
+
+    beside(comm.events(1), G, steps, now, compute, (reduce,))
+
+
+def hist_and_scatter(g, ids, dx, tok, gh, gain, gain_two, parts, halves, wide, cid):
     heads, n, _ = g.shape
-    rows, count, G = 16, len(parts), wide // 4
+    rows, count, G, d = 16, len(parts), wide // 4, tok.shape[1]
+    small = 2 * (d // 128) + 2 * heads
+    sds = jax.ShapeDtypeStruct
+    const = lambda s: pl.BlockSpec(s, lambda i: (0, 0))
     outs = pl.pallas_call(functools.partial(hist_kernel, heads, rows, n, G, halves, count), grid=(n // rows,),
-        out_shape=(jax.ShapeDtypeStruct((heads, 96), f32),) + shard_shapes(parts, wide),
-        in_specs=[pl.BlockSpec((heads, rows, n), lambda i: (0, i, 0)), pl.BlockSpec((3, rows, n), lambda i: (0, i, 0))] + [ANY] * count,
-        out_specs=(pl.BlockSpec((heads, 96), lambda i: (0, 0)),) + (whole_vmem(),) * count,
-        scratch_shapes=[pltpu.VMEM((n // 128, heads * rows, 128), f32)] + scatter_scratch(G, halves, parts[0].shape[0] // wide),
-        compiler_params=params(cid), name="table_grad_scatter")(g, ids, *[spread(p, wide) for p in parts])
-    return outs[0], outs[1:]
+        out_shape=(sds((small, 128), f32), sds(tok.shape, f32)) + shard_shapes(parts, wide),
+        in_specs=[pl.BlockSpec((heads, rows, n), lambda i: (0, i, 0)), pl.BlockSpec((3, rows, n), lambda i: (0, i, 0)),
+                  const(dx.shape), const(tok.shape), const(gh.shape), const(gain.shape), const(gain_two.shape)] + [ANY] * count,
+        out_specs=(const((small, 128)), const(tok.shape)) + (whole_vmem(),) * count,
+        scratch_shapes=[pltpu.VMEM((n // 128, heads * rows, 128), f32), pltpu.VMEM((heads, 96), f32), pltpu.VMEM(tok.shape, bf16), D((2,))]
+        + sum_scratch(G, small) + scatter_scratch(G, halves, parts[0].shape[0] // wide),
+        compiler_params=params(cid), name="table_grad_scatter")(g, ids, dx, tok, gh, gain, gain_two, *[spread(p, wide) for p in parts])
+    return outs[0], outs[1], outs[2:]
 
 
 D = pltpu.SemaphoreType.DMA
@@ -252,16 +358,18 @@
     return pltpu.make_async_remote_copy(src_ref=src, dst_ref=dst, send_sem=send, recv_sem=recv, device_id=target, device_id_type=MESH)
 
 
-def greet(G, far):
+def greet(G, far, pair=0):
     z, y, x = place()
     bar = pltpu.get_barrier_semaphore()
     sig = lambda t: pl.semaphore_signal(bar, inc=1, device_id=t, device_id_type=MESH)
     sig(wide_id(z, 1 - y, x))
     sig(wide_id(z, y, 1 - x))
+    if pair:
+        sig({"narrow": 1 - lax.axis_index("narrow")})
     if far:
         for k in range(1, G):
             sig(wide_id((z + k) % G, y, x))
-        pl.semaphore_wait(bar, 2 + G - 1)
+        pl.semaphore_wait(bar, 2 + pair + G - 1)
     else:
         @pl.when(z > 0)
         def _():
@@ -271,7 +379,7 @@
         def _():
             sig(wide_id(z + 1, y, x))
 
-        pl.semaphore_wait(bar, 2 + (z > 0).astype(jnp.int32) + (z < G - 1).astype(jnp.int32))
+        pl.semaphore_wait(bar, 2 + pair + (z > 0).astype(jnp.int32) + (z < G - 1).astype(jnp.int32))
 
 
 class Gather:
@@ -520,9 +628,9 @@
             if k:
                 self.three(k).wait_send()
 
-    def events(self):
+    def events(self, pair=0):
         G = self.G
-        first = lambda: (greet(G, True), self.begin())
+        first = lambda: (greet(G, True, pair), self.begin())
         ev = [(0.0, first), (1.1, lambda: self.add_one(0))]
         for n in range(1, G):
             ev += [(1.5 * n + 0.65, functools.partial(self.add_one, n)), (1.5 * n + 1.1, functools.partial(self.add_two, n - 1))]
@@ -537,9 +645,9 @@
             D((2 * G * most,)), D((2 * G * most,)), D((2 * G * most,)), D((2 * G,)), D((2 * G,)), D((G - 1,)), D((G - 1,))]
 
 
-def beside(comm, steps, now, compute):
-    events, finish = comm.events()
-    units = 1.55 * comm.G
+def beside(plan, G, steps, now, compute, late=()):
+    events, finish = plan
+    units = 1.55 * G
     for n in range(steps):
         here = [act for t, act in events if min(steps - 1, int(-(-t * steps // units))) == n]
         if here:
@@ -551,6 +659,8 @@
 
     @pl.when(now == steps - 1)
     def _():
+        for act in late:
+            act()
         finish()
 
 
@@ -573,22 +683,16 @@
     return a.reshape(-1, a.shape[-1])
 
 
-def sum_kernel(G, src, out, acc, got, gz, s, v, sz, vz):
+def sum_everywhere(G, acc, got, gz, s, v, sz, vz):
     z, y, x = place()
     core = {"narrow": 1 - lax.axis_index("narrow")}
-    ynb, xnb = wide_id(z, 1 - y, x), wide_id(z, y, 1 - x)
-    far = [wide_id((z + k) % G, y, x) for k in range(1, G)]
-    bar = pltpu.get_barrier_semaphore()
-    for t in [core, ynb, xnb] + far:
-        pl.semaphore_signal(bar, inc=1, device_id=t, device_id_type=MESH)
-    pl.semaphore_wait(bar, 3 + len(far))
-    acc[0] = src[...]
-    for n, t in enumerate((core, xnb, ynb)):
+    for n, t in enumerate((core, wide_id(z, y, 1 - x), wide_id(z, 1 - y, x))):
         c = remote(acc.at[n], got.at[n], s.at[n], v.at[n], t)
         c.start()
         c.wait()
         acc[n + 1] = acc[n] + got[n]
     gz[z] = acc[3]
+    far = [wide_id((z + k) % G, y, x) for k in range(1, G)]
     sent = [remote(acc.at[3], gz.at[z], sz.at[k], vz.at[z], t) for k, t in enumerate(far)]
     for c in sent:
         c.start()
@@ -600,19 +704,12 @@
     total = gz[0]
     for k in range(1, G):
         total = total + gz[k]
-    out[...] = total
-
-
-def sum_all(part, wide, cid):
-    G, rows = wide // 4, part.shape[0]
+    return total
+
+
+def sum_scratch(G, rows):
     V = lambda k: pltpu.VMEM((k, rows, 128), f32)
-    return pl.pallas_call(functools.partial(sum_kernel, G), out_shape=jax.ShapeDtypeStruct(part.shape, f32),
-        in_specs=[whole_vmem()], out_specs=whole_vmem(),
-        scratch_shapes=[V(4), V(3), V(G), D((3,)), D((3,)), D((G - 1,)), D((G,))],
-        compiler_params=pltpu.CompilerParams(collective_id=cid, has_side_effects=True), name="small_sums")(part)
-
-
-TILE = 256
+    return [V(4), V(3), V(G), D((3,)), D((3,)), D((G - 1,)), D((G,))]
 
 
 def nt(a, b):
@@ -769,67 +866,37 @@
         compiler_params=params(cid), name="feed_forward")(att, tok, cot, wo, wg, wu, wd, gain)
 
 
-epsilon = 1e-06
-
-
-def norm_plain(values, gain_row):
-    factor = lax.rsqrt(jnp.mean(values * values, axis=-1, keepdims=True) + epsilon)
-    return values * factor * gain_row
-
-
-def times(a, b):
-    return jnp.dot(a, b, preferred_element_type=f32)
-
-
-def times_transposed(a, b):
-    return lax.dot_general(a, b, NT, preferred_element_type=f32)
-
-
-def transposed_times(a, b):
-    return lax.dot_general(a, b, (((0,), (0,)), ((), ())), preferred_element_type=f32)
-
-
 def local(tokens, cotangent, pages, boxes, gain_attn, gain_ffn, bias_tables, w_query, w_key, w_value, w_out, w_gate, w_up, w_down):
     wide, narrow = lax.axis_size("wide"), lax.axis_size("narrow")
     heads_all = bias_tables.shape[1]
     heads = heads_all // narrow
-    rows = tokens.shape[0]
     core = lax.axis_index("narrow")
     tables = lax.dynamic_slice_in_dim(bias_tables, core * heads, heads, 1)
-    inner, ff = w_query.shape[1], w_gate.shape[1]
+    inner, ff, d = w_query.shape[1], w_gate.shape[1], tokens.shape[1]
+    gain_one, gain_two = gain_attn.astype(f32)[None], gain_ffn.astype(f32)[None]
+
     all_tokens = lax.all_gather(tokens, "narrow", axis=0, tiled=True)
     all_cot = lax.all_gather(cotangent, "narrow", axis=0, tiled=True)
     early = inner // 4 * 3
     bias, ids, (w_first, full_out, full_gate) = bias_and_gather(
         tables, boxes, pages, [jnp.concatenate([w_query, w_key, w_value], axis=1), w_out.T, w_gate],
         (((2, 0, ff), (0, 0, early)), ((1, 0, inner), (0, early, 3 * inner - early))), wide, 1)
-
-    x = all_tokens.astype(f32)
-    gain_one, gain_two = gain_attn.astype(f32), gain_ffn.astype(f32)
-    normed = norm_plain(x, gain_one).astype(bf16)
-    qkv = times(normed, w_first).astype(bf16)
-    attended, lse, (full_up, full_down) = attn_fwd_and_gather(qkv, bias, [w_up, w_down.T], (((0, 0, ff),), ((1, 0, ff),)), wide, 2)
+    (attended, lse, normed, qkv), (full_up, full_down) = attn_fwd_and_gather(
+        all_tokens, gain_one, w_first, bias, [w_up, w_down.T], (((0, 0, ff),), ((1, 0, ff),)), wide, 2)
     grad_w_out, grad_w_gate, grad_w_up, grad_w_down, output, grad_hidden, grad_attended, grad_gain_two = middle(
-        attended, all_tokens, all_cot, full_out, full_gate, full_up, full_down, gain_two[None], 6)
-    (dq, dk, dv, g), (s_down, s_out) = attn_bwd_and_scatter(
-        qkv, bias, attended, grad_attended, lse, [grad_w_down, grad_w_out],
-        (((0, 0, 2 * inner),), ((0, 2 * inner, ff - 2 * inner), (1, 0, inner))), wide, 3)
-    dqkv = jnp.concatenate([dq, dk, dv], axis=1)
-    mid = 3 * inner // 2
-    table_part, (s_gate, s_up, s_first) = hist_and_scatter(
-        g, ids, [grad_w_gate, grad_w_up, transposed_times(normed, dqkv).astype(bf16)],
-        (((0, 0, ff), (2, 0, mid)), ((1, 0, ff), (2, mid, mid))), wide, 4)
-    grad_normed = lax.psum_scatter(times_transposed(dqkv, w_first).astype(bf16), "narrow", scatter_dimension=0, tiled=True).astype(f32)
-    own = tokens.astype(f32)
-    _, pull_one = jax.vjp(norm_plain, own, gain_one)
-    grad_tokens_norm, grad_gain_one = pull_one(grad_normed)
-    grad_tokens = grad_hidden + grad_tokens_norm
-    table_part = lax.dynamic_update_slice(jnp.zeros((bias_tables.shape[0], heads_all), f32), table_part.T, (jnp.int32(0), core * heads))
-    sizes = [gain_one.size, gain_two.size, table_part.size]
-    small = sum_all(jnp.concatenate([grad_gain_one, grad_gain_two[0], table_part.reshape(-1)]).reshape(-1, 128), wide, 5).reshape(-1)
-    one, two, table = jnp.split(small, [sizes[0], sizes[0] + sizes[1]])
-    s_query, s_key, s_value = jnp.split(s_first, 3, axis=1)
-    return (output, grad_tokens, one, two, table.reshape(bias_tables.shape), s_query, s_key, s_value, s_out.T, s_gate, s_up, s_down.T)
+        attended, all_tokens, all_cot, full_out, full_gate, full_up, full_down, gain_two, 3)
+    (g, grad_w_query, grad_w_key, grad_w_value, grad_normed), (s_down, s_out) = attn_bwd_and_scatter(
+        qkv, bias, attended, grad_attended, lse, normed, w_first, [grad_w_down, grad_w_out],
+        (((0, 0, 2 * inner),), ((0, 2 * inner, ff - 2 * inner), (1, 0, inner))), wide, 4)
+    half = inner // 2
+    small, grad_tokens, (s_gate, s_up, s_query, s_key, s_value) = hist_and_scatter(
+        g, ids, grad_normed, tokens, grad_hidden, gain_one, grad_gain_two,
+        [grad_w_gate, grad_w_up, grad_w_query, grad_w_key, grad_w_value],
+        (((0, 0, ff), (2, 0, inner), (3, 0, half)), ((1, 0, ff), (4, 0, inner), (3, half, half))), wide, 5)
+    lines = d // 128
+    one, two = small[:lines].reshape(d), small[lines:2 * lines].reshape(d)
+    table = small[2 * lines:, :bias_tables.shape[0]].T
+    return (output, grad_tokens, one, two, table, s_query, s_key, s_value, s_out.T, s_gate, s_up, s_down.T)
 
 
 def solution(mesh):

time: 380 us -> 358 us (0.942)
  matrix products: 19.2 us -> 0 us
  Pallas kernels: 313 us -> 322 us
  other arithmetic: 10.9 us -> 4.46 us
  local copies, waits for them, and re-layouts: 19.7 us -> 14 us
    dot_general x3 -> x0, matrix products: 19.2 us -> none  [the longest x1 7.66 us: times(): return jnp.dot(a, b, preferred_element_type=f32)]
    pallas_call x1, Pallas kernels: 81.7 us -> 93.6 us  [hist_and_scatter(): pl.pallas_call(functools.partial(hist_kernel, heads, rows, n, G, halves,...]
    reduce_sum x3 -> x0, other arithmetic: 4.5 us -> none  [the longest x2 2.35 us: norm_plain(): jnp.mean(values * values, axis=-1, keepdims=True) + epsilon]
    unnamed x43 -> x34, local copies, waits for them, and re-layouts: 12.1 us -> 8.88 us
    pallas_call x3 -> x2, Pallas kernels: 109 us -> 107 us  [the longest x1 54 us: attn_fwd_and_gather(): pl.pallas_call(functools.partial(fwd_kernel, pairs, tiles, G, halves, cou...]
  transfers between devices with their start and end apart: 3 -> 2, of which waited for: 0 -> 0; matrix products, arithmetic and copies ran while one was open for 7% -> 2% of each run, Pallas kernels for 53% -> 34%
where the time goes in v5:
time: 358 us; the launch traced here: 356 us
  Pallas kernels  322 us (90%)
  between operations  14.2 us (4%)
  local copies, waits for them, and re-layouts  14 us (4%)
  other arithmetic  4.46 us (1%)
    pallas_call x1, Pallas kernels, hist_and_scatter(): pl.pallas_call(functools.partial(hist_kernel, heads, rows, n, G, halves,...  93.6 us
    pallas_call x1, Pallas kernels, bias_and_gather(): pl.pallas_call(functools.partial(bias_gather_kernel, heads, rows, n, G, h...  66.4 us
    pallas_call x1, Pallas kernels, middle(): pl.pallas_call(mid_kernel, out_shape=(sds((d, units), bf16), sds((d, ff),...  55.2 us
    pallas_call x1, Pallas kernels, attn_fwd_and_gather(): pl.pallas_call(functools.partial(fwd_kernel, pairs, tiles, G, halves, cou...  54 us
    pallas_call x1, Pallas kernels, attn_bwd_and_scatter(): pl.pallas_call(functools.partial(bwd_kernel, pairs, tiles, G, halves, cou...  52.8 us
    unnamed x34, local copies, waits for them, and re-layouts  8.88 us
  transfers between devices with their start and end apart: 2, of which 0 were waited for; matrix products, arithmetic and copies ran while one was open for 2% of the time, Pallas kernels for 34%

profile of v5, /device:TPU:0, one launch (start us, length us, event | category | flops | bytes accessed | tf_op | source)
XLA Modules:
  0.0 356.2 jit_solution(12536619518181539155)
XLA Ops:
  7.2 0.0 all-gather.3.cloned.1.call-start
  7.3 0.7 all-gather.3.cloned.1.call-update
  7.9 0.0 all-gather.5.cloned.1.call-start
  8.0 0.7 all-gather.5.cloned.1.call-update
  8.7 1.3 broadcast_in_dim.23
  10.0 1.3 broadcast_in_dim.24
  11.2 0.7 round-nearest-even_convert_fusion
  11.9 0.1 reshape.255
  12.0 0.6 pad.4.refs_1_
  12.7 1.7 copy.31.refs_4_
  14.4 1.7 copy.30
  16.1 0.5 fusion.17.refs_0_
  16.6 0.7 pad_maximum_fusion.refs_6_
  17.3 66.4 %layout_bias_gather.1 = (f32[8,1024,1024]{2,1,0:T(8,128)}, f32[3,1024,1024]{2,1,0:T(8,128)}, bf16[4,2,2,64,1536]{4,3,2,1,0:T(8,128)(2,1)}, bf16[4,2,2,64,512]{4,...) custom-call(s32[1,128]{1,0:T(1,128)} %fusion.17.refs_0_, s32[12,128]{1,0:T(8,128)} %pad.4.refs_1_, s32[1024,2]{1,0:T(8,128)} %bitcast.43, ...), custom_call_target="tpu_custom_call" | custom-call | tf_op jit(solution)/shard_map/layout_bias_gather/pallas_call | solution.py:87
  83.7 0.0 all-gather.3.cloned.1.call-done.refs_0_.tok_h
  83.8 54.0 %attention_gather.1 = (bf16[1024,512]{1,0:T(8,128)(2,1)}, f32[4,1024,2]{2,1,0:T(8,128)}, bf16[1024,1024]{1,0:T(8,128)(2,1)}, bf16[1024,1536]{1,0:T(8,128)(2,1)},...) custom-call(bf16[1024,1024]{1,0:T(8,128)(2,1)} %all-gather.3.cloned.1.call-done.refs_0_.tok_h, ...), custom_call_target="tpu_custom_call" | custom-call | tf_op jit(solution)/shard_map/attention_gather/pallas_call | solution.py:168
  137.8 0.0 all-gather.5.cloned.1.call-done.cot_h
  137.8 55.2 %feed_forward.1 = (bf16[1024,512]{1,0:T(8,128)(2,1)}, bf16[1024,1408]{1,0:T(8,128)(2,1)}, bf16[1024,1408]{1,0:T(8,128)(2,1)}, bf16[1024,1408]{1,0:T(8,128)(2,1)}...) custom-call(bf16[1024,512]{1,0:T(8,128)(2,1)} %get-tuple-element.47.att_h.refs, ...), custom_call_target="tpu_custom_call" | custom-call | tf_op jit(solution)/shard_map/feed_forward/pallas_call | solution.py:858
  193.0 52.8 %attention_back_scatter.1 = (bf16[8,1024,1024]{2,1,0:T(8,128)(2,1)}, bf16[1024,512]{1,0:T(8,128)(2,1)}, bf16[1024,512]{1,0:T(8,128)(2,1)}, bf16[1024,512]{1,0:T(...) custom-call(bf16[1024,1536]{1,0:T(8,128)(2,1)} %get-tuple-element.53.refs_0_.refs_1_.refs_2_, ...), custom_call_target="tpu_custom_call" | custom-call | tf_op jit(solution)/shard_map/attention_back_scatter/pallas_call | solution.py:247
  245.9 93.6 %table_grad_scatter.1 = (f32[32,128]{1,0:T(8,128)}, f32[512,1024]{1,0:T(8,128)}, f32[64,1408]{1,0:T(8,128)}, f32[64,1408]{1,0:T(8,128)}, f32[64,512]{1,0:T(8,128...) custom-call(bf16[8,1024,1024]{2,1,0:T(8,128)(2,1)} %get-tuple-element.59.refs_0_, f32[3,1024,1024]{2,1,0:T(8,128)} %get-tuple-element.60.refs_1_, ...), custom_call_target="tpu_custom_call" | custom-call | tf_op jit(solution)/shard_map/table_grad_scatter/pallas_call | solution.py:334
  339.5 1.4 slice_bitcast_fusion
  340.9 1.3 slice_bitcast_fusion.1
  342.2 1.0 copy.41
  343.2 1.3 copy.42
  344.5 0.7 copy.43
  345.2 0.7 copy.44
  345.8 0.7 copy.45
  346.5 0.7 copy.46
  347.2 0.7 copy.47
  347.9 0.0 copy-done.3
  347.9 0.7 copy.48
  348.6 0.7 copy.49
  (26 shorter events, 0.1 us)
Async XLA Ops:
  7.2 9.4 %copy-start.9 = (bf16[64,512]{1,0:T(8,128)(2,1)S(1)}, bf16[64,512]{1,0:T(8,128)(2,1)}, u32[]{:S(2)}) copy-start(bf16[64,512]{1,0:T(8,128)(2,1)} %param.23) | copy-start | bytes 196612
  7.2 9.4 %copy-start.10 = (bf16[64,512]{1,0:T(8,128)(2,1)S(1)}, bf16[64,512]{1,0:T(8,128)(2,1)}, u32[]{:S(2)}) copy-start(bf16[64,512]{1,0:T(8,128)(2,1)} %param.22) | copy-start | bytes 196612
  7.2 9.4 %copy-start.11 = (bf16[64,512]{1,0:T(8,128)(2,1)S(1)}, bf16[64,512]{1,0:T(8,128)(2,1)}, u32[]{:S(2)}) copy-start(bf16[64,512]{1,0:T(8,128)(2,1)} %param.21) | copy-start | bytes 196612
  7.2 76.6 %all-gather.3.cloned.1.call-start = ((), (), s32[]{:S(2)}) async-start(), calls=%async_computation | async-start | bytes 3145728 | tf_op jit(solution)/shard_map/all_gather | solution.py:878
  7.9 129.8 %all-gather.5.cloned.1.call-start = ((), (), s32[]{:S(2)}) async-start(), calls=%async_computation.1 | async-start | bytes 3145728 | tf_op jit(solution)/shard_map/all_gather | solution.py:879
  245.9 96.3 %copy-start.1 = (bf16[512,1024]{1,0:T(8,128)(2,1)S(1)}, bf16[512,1024]{1,0:T(8,128)(2,1)}, u32[]{:S(2)}) copy-start(bf16[512,1024]{1,0:T(8,128)(2,1)} %get-tuple-element.92) | copy-start | bytes 3145732
  339.4 3.7 %copy-start = (f32[512,1024]{1,0:T(8,128)S(1)}, f32[512,1024]{1,0:T(8,128)}, u32[]{:S(2)}) copy-start(f32[512,1024]{1,0:T(8,128)} %get-tuple-element.93) | copy-start | bytes 6291460
  342.2 2.3 copy-start.8
  342.2 3.0 copy-start.7
  343.2 2.7 copy-start.6
  343.2 3.3 copy-start.5
  343.2 4.0 %copy-start.4 = (f32[64,1408]{1,0:T(8,128)S(1)}, f32[64,1408]{1,0:T(8,128)}, u32[]{:S(2)}) copy-start(f32[64,1408]{1,0:T(8,128)} %get-tuple-element.101) | copy-start | bytes 1081348
  343.2 4.7 %copy-start.3 = (f32[64,1408]{1,0:T(8,128)S(1)}, f32[64,1408]{1,0:T(8,128)}, u32[]{:S(2)}) copy-start(f32[64,1408]{1,0:T(8,128)} %get-tuple-element.102) | copy-start | bytes 1081348
  343.2 5.4 %copy-start.2 = (f32[64,1408]{1,0:T(8,128)S(1)}, f32[64,1408]{1,0:T(8,128)}, u32[]{:S(2)}) copy-start(f32[64,1408]{1,0:T(8,128)} %get-tuple-element.77) | copy-start | bytes 1081348
Sparse Core Ops, SparseCore 0:
  9.6 13.2 all-gather.2
  24.5 11.7 all-gather.4

commit v6 on v5

--- a/solution.py
+++ b/solution.py
@@ -32,7 +32,7 @@
     return lane_take(steps, jnp.minimum(jnp.abs(gap) >> shift, EDGES[-1])) + jnp.where(gap > 0, 16, 0)
 
 
-def bias_tile(start, heads, rows, n, steps_ref, tab_ref, box_col, box_row, page_col, page_row, bias_ref, ids_ref, lin, lin_ids):
+def bias_tile(start, heads, rows, n, steps_ref, tab_ref, box_col, box_row, page_col, page_row, bias_ref, ids_ref, lin_ids, lin):
     steps = jnp.broadcast_to(steps_ref[...], (rows, 128))
     allowed_col = jnp.broadcast_to(page_col[...] % 2, (rows, 128))
     cols = [jnp.broadcast_to(box_col[:, t:t + 1], (rows, 128)) for t in range(2)]
@@ -53,11 +53,10 @@
     def _(c):
         lanes = pl.ds(pl.multiple_of(c * 128, 128), 128)
         near = jnp.clip((c * 128 - start) // rows + 4, 0, 7)
-        ids_ref[0, :, lanes] = lin_ids[near]
         ids = []
         for t in range(2):
             ids.append(buckets_of(jnp.broadcast_to(box_row[t:t + 1, lanes], (rows, 128)) - cols[t], steps, 2))
-            ids_ref[t + 1, :, lanes] = ids[t].astype(f32)
+            ids_ref[t, :, lanes] = ids[t].astype(f32)
         ok = jnp.broadcast_to(page_row[:, lanes], (rows, 128)) == allowed_col
         for p in range(pairs):
             words = lin[near, p] + lane_take(table(1, p), ids[0]) + lane_take(table(2, p), ids[1])
@@ -69,11 +68,11 @@
 
 def bias_gather_kernel(heads, rows, n, G, halves, count, *refs):
     ins, srcs = refs[:6], refs[6:6 + count]
-    bias_ref, ids_ref = refs[6 + count:8 + count]
-    outs, lins, sems = refs[8 + count:8 + 2 * count], refs[8 + 2 * count:10 + 2 * count], refs[10 + 2 * count:]
+    bias_ref, ids_ref, lin_ids = refs[6 + count:9 + count]
+    outs, lin, sems = refs[9 + count:9 + 2 * count], refs[9 + 2 * count], refs[10 + 2 * count:]
     now = pl.program_id(0)
     comm = Gather(G, halves, srcs, outs, *sems)
-    beside(comm.events(), G, n // rows, now, lambda: bias_tile(now * rows, heads, rows, n, *ins, bias_ref, ids_ref, *lins))
+    beside(comm.events(), G, n // rows, now, lambda: bias_tile(now * rows, heads, rows, n, *ins, bias_ref, ids_ref, lin_ids, lin))
 
 
 def bias_and_gather(tables, boxes, pages, shards, halves, wide, cid):
@@ -86,15 +85,16 @@
     count = len(shards)
     outs = pl.pallas_call(functools.partial(bias_gather_kernel, heads, rows, n, G, halves, count),
         grid=(n // rows,),
-        out_shape=(jax.ShapeDtypeStruct((heads, n, n), f32), jax.ShapeDtypeStruct((3, n, n), f32)) + gathered_shapes(shards, wide),
+        out_shape=(jax.ShapeDtypeStruct((heads, n, n), f32), jax.ShapeDtypeStruct((2, n, n), f32), jax.ShapeDtypeStruct((8, rows, 128), f32)) + gathered_shapes(shards, wide),
         in_specs=[pl.BlockSpec((1, 128), lambda i: (0, 0)), pl.BlockSpec((3 * heads // 2, 128), lambda i: (0, 0)),
                   pl.BlockSpec((rows, 2), lambda i: (i, 0)), pl.BlockSpec((2, n), lambda i: (0, 0)),
                   pl.BlockSpec((rows, 1), lambda i: (i, 0)), pl.BlockSpec((1, n), lambda i: (0, 0))] + [ANY] * count,
-        out_specs=(pl.BlockSpec((heads, rows, n), lambda i: (0, i, 0)), pl.BlockSpec((3, rows, n), lambda i: (0, i, 0))) + (ANY,) * count,
-        scratch_shapes=[pltpu.VMEM((8, heads // 2, rows, 128), jnp.int32), pltpu.VMEM((8, rows, 128), f32)] + gather_scratch(G, halves, count),
+        out_specs=(pl.BlockSpec((heads, rows, n), lambda i: (0, i, 0)), pl.BlockSpec((2, rows, n), lambda i: (0, i, 0)),
+                   pl.BlockSpec((8, rows, 128), lambda i: (0, 0, 0))) + (ANY,) * count,
+        scratch_shapes=[pltpu.VMEM((8, heads // 2, rows, 128), jnp.int32)] + gather_scratch(G, halves, count),
         compiler_params=params(cid), name="layout_bias_gather")(
             steps, tab, boxes.T, boxes, pages[:, None], pages[None], *shards)
-    return outs[0], outs[1], [flat(a) for a in outs[2:]]
+    return outs[0], outs[1:3], outs[3:]
 
 
 def half_of(v, e):
@@ -171,11 +171,34 @@
         out_specs=(pl.BlockSpec((tq, 128), lambda p, i: (i, p)), pl.BlockSpec((1, tq, 2), lambda p, i: (p, i, 0)), ANY, ANY) + (ANY,) * count,
         scratch_shapes=[pltpu.VMEM((n, d), bf16), pltpu.VMEM((n, 3 * width), bf16), D((2,))] + gather_scratch(G, halves, count),
         compiler_params=params(cid), name="attention_gather")(tok, gain, w, bias, *shards)
-    return outs[:4], [flat(a) for a in outs[4:]]
+    return outs[:4], outs[4:]
+
+
+def band_sums(i, e, g_ref, band_ref, far_ref):
+    tq, n = g_ref.shape[1], g_ref.shape[2]
+    first = i * (tq // 128) - 1
+
+    @pl.when(i == 0)
+    def _():
+        band_ref[e] = jnp.zeros(band_ref.shape[1:], f32)
+        far_ref[e] = jnp.zeros(far_ref.shape[1:], f32)
+
+    for m in range(tq // 128 + 2):
+        @pl.when((first + m >= 0) & (first + m < n // 128))
+        def _():
+            band_ref[e, :, m * 128:(m + 1) * 128] += g_ref[e, :, pl.ds(pl.multiple_of((first + m) * 128, 128), 128)].astype(f32)
+
+    for c in range(n // 128):
+        @pl.when((c < first) | (c > first + tq // 128 + 1))
+        def _():
+            total = g_ref[e, 0:16, c * 128:(c + 1) * 128].astype(f32)
+            for k in range(1, tq // 16):
+                total = total + g_ref[e, k * 16:(k + 1) * 16, c * 128:(c + 1) * 128].astype(f32)
+            far_ref[e, jnp.where(c < first, 0, 1)] += total
 
 
 def bwd_tile(p, i, last_tile, last, q_ref, k_ref, v_ref, bias_ref, o_ref, do_ref, lse_ref, normed_ref, wq_ref, wk_ref, wv_ref,
-             g_ref, dwq_ref, dwk_ref, dwv_ref, dx_ref, dkt, dvt, dqkv, turned, dx):
+             g_ref, band_ref, far_ref, dwq_ref, dwk_ref, dwv_ref, dx_ref, dkt, dvt, dqkv, turned, dx):
     tq, n = q_ref.shape[0], k_ref.shape[0]
     rows = pl.ds(pl.multiple_of(i * tq, tq), tq)
 
@@ -203,6 +226,7 @@
         dqs.append(jnp.dot(g, k, preferred_element_type=f32))
         dvt[...] += jnp.dot(dom.T, w.astype(bf16), preferred_element_type=f32)
         dkt[...] += jnp.dot(qm.T, g, preferred_element_type=f32)
+        band_sums(i, e, g_ref, band_ref, far_ref)
     dqkv[rows, 0:128] = join(*dqs).astype(bf16)
 
     @pl.when(last_tile)
@@ -225,8 +249,8 @@
 
 def bwd_kernel(pairs, tiles, G, halves, count, *refs):
     ins, parts = refs[:11], refs[11:11 + count]
-    mid = refs[11 + count:16 + count]
-    outs, accs, sems = refs[16 + count:16 + 2 * count], refs[16 + 2 * count:21 + 2 * count], refs[21 + 2 * count:]
+    mid = refs[11 + count:18 + count]
+    outs, accs, sems = refs[18 + count:18 + 2 * count], refs[18 + 2 * count:23 + 2 * count], refs[23 + 2 * count:]
     p, i = pl.program_id(0), pl.program_id(1)
     comm = Scatter(G, halves, parts, outs, *sems)
     beside(comm.events(), G, pairs * tiles, p * tiles + i,
@@ -245,42 +269,67 @@
     full = lambda rows, k: pl.BlockSpec((rows, 128), lambda p, i: (0, p + k * pairs))
     const = lambda s: pl.BlockSpec(s, lambda p, i: (0, 0))
     outs = pl.pallas_call(functools.partial(bwd_kernel, pairs, tiles, G, halves, count), grid=(pairs, tiles),
-        out_shape=(sds((2 * pairs, n, n), bf16),) + (sds((d, width), bf16),) * 3 + (sds((n, d), bf16),) + shard_shapes(parts, wide),
+        out_shape=(sds((2 * pairs, n, n), bf16), sds((2 * pairs, tq, tq + 256), f32), sds((2 * pairs, 2, 16, 128), f32)) + (sds((d, width), bf16),) * 3 + (sds((n, d), bf16),) + shard_shapes(parts, wide),
         in_specs=[tile, full(n, 1), full(n, 2), pl.BlockSpec((2, tq, n), lambda p, i: (p, i, 0)), tile, tile,
                   pl.BlockSpec((1, tq, 2), lambda p, i: (p, i, 0)), const((n, d)), full(d, 0), full(d, 1), full(d, 2)] + [ANY] * count,
-        out_specs=(pl.BlockSpec((2, tq, n), lambda p, i: (p, i, 0)),) + (full(d, 0),) * 3 + (const((n, d)),) + (whole_vmem(),) * count,
+        out_specs=(pl.BlockSpec((2, tq, n), lambda p, i: (p, i, 0)), pl.BlockSpec((2, tq, tq + 256), lambda p, i: (p, 0, 0)),
+                   pl.BlockSpec((2, 2, 16, 128), lambda p, i: (p, 0, 0, 0))) + (full(d, 0),) * 3 + (const((n, d)),) + (whole_vmem(),) * count,
         scratch_shapes=[pltpu.VMEM((128, n), f32), pltpu.VMEM((128, n), f32), pltpu.VMEM((n, 384), bf16), pltpu.VMEM((d, n), bf16),
                         pltpu.VMEM((n, d), f32)] + scatter_scratch(G, halves, parts[0].shape[0] // wide),
         compiler_params=params(cid), name="attention_back_scatter")(
-            qkv, qkv, qkv, bias, o, do, lse, normed, w, w, w, *[spread(p, wide) for p in parts])
-    return outs[:5], outs[5:]
-
-
-def hist_tile(first, heads, rows, n, g_ref, ids_ref, out_ref, gs):
-    @pl.when(first)
-    def _():
-        out_ref[...] = jnp.zeros_like(out_ref)
-
+            qkv, qkv, qkv, bias, o, do, lse, normed, w, w, w, *parts)
+    return outs[:7], outs[7:]
+
+
+def rows_times_hots(src, ids, rows, heads, gs):
+    n = src(0).shape[1]
     for h in range(heads):
+        block = src(h)
         for c in range(n // 128):
-            gs[c, h * rows:(h + 1) * rows, :] = g_ref[h, :, c * 128:(c + 1) * 128].astype(f32)
-    label = lax.broadcasted_iota(jnp.int32, (32, n), 0).astype(bf16)
-    one, zero = jnp.ones((32, n), bf16), jnp.zeros((32, n), bf16)
-    acc = jnp.zeros((heads, 96), f32)
+            gs[c, h * rows:(h + 1) * rows, :] = block[:, c * 128:(c + 1) * 128]
+    labels = [lax.broadcasted_iota(jnp.int32, (16, n), 0).astype(bf16) + float(k) for k in (0, 16)]
+    one, zero = jnp.ones((16, n), bf16), jnp.zeros((16, n), bf16)
+    total = jnp.zeros((heads, 32 * len(ids(0))), f32)
     for r in range(rows):
         grow = jnp.concatenate([gs[c, pl.ds(r, heads, stride=rows), :] for c in range(n // 128)], axis=1).astype(bf16)
         hots = []
-        for t in range(3):
-            row = jnp.broadcast_to(ids_ref[t, r:r + 1, :], (32, n)).astype(bf16)
-            hots.append(jnp.where(row == label, one, zero))
-        acc = acc + lax.dot_general(grow, jnp.concatenate(hots, axis=0), NT, preferred_element_type=f32)
-    out_ref[...] += acc
+        for one_row in ids(r):
+            row = jnp.broadcast_to(one_row, (16, n)).astype(bf16)
+            hots += [jnp.where(row == label, one, zero) for label in labels]
+        total = total + lax.dot_general(grow, jnp.concatenate(hots, axis=0), NT, preferred_element_type=f32)
+    return total
+
+
+def hist_tile(now, heads, g_ref, ids_ref, band_ref, far_ref, lin_ids, table, gs):
+    @pl.when(now == 0)
+    def _():
+        sides = [jnp.sum(jnp.sum(far_ref[:, k], axis=1), axis=1, keepdims=True) for k in range(2)]
+        lane = lax.broadcasted_iota(jnp.int32, (heads, 128), 1)
+        table[0] = jnp.where(lane == 15, sides[0], 0.0) + jnp.where(lane == 31, sides[1], 0.0)
+        table[1] = jnp.zeros_like(table[1])
+
+    big = g_ref.shape[1]
+
+    @pl.loop(0, big // 16)
+    def _(q):
+        block = pl.ds(pl.multiple_of(q * 16, 16), 16)
+        table[1, :, 0:64] += rows_times_hots(lambda h: g_ref[h, block, :].astype(f32), lambda r: [ids_ref.at[t, block][r:r + 1, :] for t in range(2)], 16, heads, gs)
+
+    wide = band_ref.shape[2] // 128
+    per = lin_ids.shape[1]
+    a = now * 16 // per
+    inside = pl.ds(pl.multiple_of(now * 16 % per, 16), 16)
+
+    def band_ids(r):
+        return [jnp.concatenate([lin_ids.at[jnp.clip((m - 1) * (128 // per) - a + 4, 0, 7), inside][r:r + 1, :] for m in range(wide)], axis=1)]
+
+    table[0, :, 0:32] += rows_times_hots(lambda h: band_ref[h], band_ids, 16, heads, gs)
 
 
 def hist_kernel(heads, rows, n, G, halves, count, *refs):
-    (g_ref, ids_ref, dx, tok, gh, gain_ref, gain_two), parts = refs[:7], refs[7:7 + count]
-    small_ref, gt_ref = refs[7 + count:9 + count]
-    outs, rest = refs[9 + count:9 + 2 * count], refs[9 + 2 * count:]
+    (g_ref, ids_ref, band_ref, far_ref, lin_ids, dx, tok, gh, gain_ref, gain_two), parts = refs[:10], refs[10:10 + count]
+    small_ref, gt_ref = refs[10 + count:12 + count]
+    outs, rest = refs[12 + count:12 + 2 * count], refs[12 + 2 * count:]
     (gs, table, got, pair_sem), sums, sems = rest[:4], rest[4:11], rest[11:]
     acc = sums[0]
     now, steps = pl.program_id(0), n // rows
@@ -316,29 +365,32 @@
                 for k in range(d // 128):
                     acc[0, k:k + 1, :] += gain[:, k * 128:(k + 1) * 128]
 
-        hist_tile(now == 0, heads, rows, n, g_ref, ids_ref, table, gs)
+        hist_tile(now, heads, g_ref, ids_ref, band_ref, far_ref, lin_ids, table, gs)
 
     def reduce():
-        acc[0, pl.ds(pl.multiple_of(2 * (d // 128) + core * heads, 8), heads), 0:96] = table[...]
+        acc[0, pl.ds(pl.multiple_of(2 * (d // 128) + core * heads, 8), heads), 0:32] = table[0, :, 0:32]
+        acc[0, pl.ds(pl.multiple_of(2 * (d // 128) + core * heads, 8), heads), 32:96] = table[1, :, 0:64]
         small_ref[...] = sum_everywhere(G, *sums)
 
     beside(comm.events(1), G, steps, now, compute, (reduce,))
 
 
-def hist_and_scatter(g, ids, dx, tok, gh, gain, gain_two, parts, halves, wide, cid):
+def hist_and_scatter(g, band, far, ids, dx, tok, gh, gain, gain_two, parts, halves, wide, cid):
     heads, n, _ = g.shape
-    rows, count, G, d = 16, len(parts), wide // 4, tok.shape[1]
+    rows, count, G, d = n // (band.shape[1] // 16), len(parts), wide // 4, tok.shape[1]
+    box_ids, lin_ids = ids
     small = 2 * (d // 128) + 2 * heads
     sds = jax.ShapeDtypeStruct
     const = lambda s: pl.BlockSpec(s, lambda i: (0, 0))
     outs = pl.pallas_call(functools.partial(hist_kernel, heads, rows, n, G, halves, count), grid=(n // rows,),
         out_shape=(sds((small, 128), f32), sds(tok.shape, f32)) + shard_shapes(parts, wide),
-        in_specs=[pl.BlockSpec((heads, rows, n), lambda i: (0, i, 0)), pl.BlockSpec((3, rows, n), lambda i: (0, i, 0)),
-                  const(dx.shape), const(tok.shape), const(gh.shape), const(gain.shape), const(gain_two.shape)] + [ANY] * count,
+        in_specs=[pl.BlockSpec((heads, rows, n), lambda i: (0, i, 0)), pl.BlockSpec((2, rows, n), lambda i: (0, i, 0)),
+                  pl.BlockSpec((heads, 16, band.shape[2]), lambda i: (0, i, 0)), pl.BlockSpec(far.shape, lambda i: (0, 0, 0, 0)),
+                  pl.BlockSpec(lin_ids.shape, lambda i: (0, 0, 0)), const(dx.shape), const(tok.shape), const(gh.shape), const(gain.shape), const(gain_two.shape)] + [ANY] * count,
         out_specs=(const((small, 128)), const(tok.shape)) + (whole_vmem(),) * count,
-        scratch_shapes=[pltpu.VMEM((n // 128, heads * rows, 128), f32), pltpu.VMEM((heads, 96), f32), pltpu.VMEM(tok.shape, bf16), D((2,))]
+        scratch_shapes=[pltpu.VMEM((n // 128, heads * 16, 128), f32), pltpu.VMEM((2, heads, 128), f32), pltpu.VMEM(tok.shape, bf16), D((2,))]
         + sum_scratch(G, small) + scatter_scratch(G, halves, parts[0].shape[0] // wide),
-        compiler_params=params(cid), name="table_grad_scatter")(g, ids, dx, tok, gh, gain, gain_two, *[spread(p, wide) for p in parts])
+        compiler_params=params(cid), name="table_grad_scatter")(g, box_ids, band, far, lin_ids, dx, tok, gh, gain, gain_two, *parts)
     return outs[0], outs[1], outs[2:]
 
 
@@ -352,6 +404,10 @@
 
 def wide_id(z, y, x):
     return {"wide": z * 4 + y * 2 + x}
+
+
+def shard_rows(z, y, x, R):
+    return pl.ds(pl.multiple_of((z * 4 + y * 2 + x) * R, R), R)
 
 
 def remote(src, dst, send, recv, target):
@@ -384,18 +440,22 @@
 
 class Gather:
     def __init__(self, G, halves, srcs, outs, local_sem, zs, zr, ns, nr):
-        self.G, self.halves, self.srcs, self.outs, self.local_sem = G, halves, srcs, outs, local_sem
+        self.G, self.halves, self.srcs, self.local_sem = G, halves, srcs, local_sem
+        self.outs = [o if isinstance(o, tuple) else (o, 0, 0) for o in outs]
+        self.widths = [sum(w for h in halves for a, _, w in h if a == k) for k in range(len(srcs))]
         self.zs, self.zr, self.ns, self.nr = zs, zr, ns, nr
         self.most = max(len(h) for h in halves)
         self.z, self.y, self.x = place()
+        self.R = srcs[0].shape[0]
 
     def hop(self, own, zz, yy, xx, h, way, j):
         target = wide_id(self.z, 1 - self.y, self.x) if way == "y" else wide_id(self.z, self.y, 1 - self.x)
         copies = []
         for n, (a, c, w) in enumerate(self.halves[h]):
             slot = (zz * 6 + j) * self.most + n
-            dst = self.outs[a].at[zz, yy, xx, :, pl.ds(c, w)]
-            copies.append(remote(self.srcs[a].at[:, pl.ds(c, w)] if own else dst, dst, self.ns.at[slot], self.nr.at[slot], target))
+            out, first, at = self.outs[a]
+            dst = out.at[shard_rows(zz, yy, xx, self.R), pl.ds(first + c, w)]
+            copies.append(remote(self.srcs[a].at[:, pl.ds(at + c, w)] if own else dst, dst, self.ns.at[slot], self.nr.at[slot], target))
         return copies
 
     def second_stage(self, zz, own=False):
@@ -411,11 +471,18 @@
         copies = []
         for a in range(len(self.srcs)):
             slot = (way * (self.G - 1) + step) * len(self.srcs) + a
-            dst = self.outs[a].at[zz, self.y, self.x]
-            copies.append(remote(self.srcs[a] if own else dst, dst, self.zs.at[slot], self.zr.at[slot],
+            dst = self.whole(a, zz)
+            copies.append(remote(self.own(a) if own else dst, dst, self.zs.at[slot], self.zr.at[slot],
                                  wide_id(self.z + (1 if way == 0 else -1), self.y, self.x)))
         return copies
 
+    def whole(self, a, zz):
+        out, first, _ = self.outs[a]
+        return out.at[shard_rows(zz, self.y, self.x, self.R), pl.ds(first, self.widths[a])]
+
+    def own(self, a):
+        return self.srcs[a].at[:, pl.ds(self.outs[a][2], self.widths[a])]
+
     def can(self, way):
         return self.z < self.G - 1 if way == 0 else self.z > 0
 
@@ -423,7 +490,7 @@
         return (self.z - d, self.z - d >= 0) if way == 0 else (self.z + d, self.z + d < self.G)
 
     def keep(self):
-        return [pltpu.make_async_copy(s, o.at[self.z, self.y, self.x], self.local_sem.at[a]) for a, (s, o) in enumerate(zip(self.srcs, self.outs))]
+        return [pltpu.make_async_copy(self.own(a), self.whole(a, self.z), self.local_sem.at[a]) for a in range(len(self.srcs))]
 
     def begin(self):
         for way in range(2):
@@ -520,7 +587,7 @@
         self.__dict__.update(locals())
         self.most = max(len(h) for h in halves)
         self.wa, self.wb = [sum(p[2] for p in h) for h in halves]
-        self.R = parts[0].shape[3]
+        self.R = parts[0].shape[0] // (4 * G)
         self.z, self.y, self.x = place()
         self.order = sorted(range(1, G), key=lambda k: min(k, G - k), reverse=True) + [0]
 
@@ -537,23 +604,23 @@
             at += w
         return out
 
+    def sources(self, k, mine):
+        z, y, x = self.zk(k), self.y, self.x
+        for h in range(2):
+            for n, a, src, dst in self.pieces(h):
+                for j in range(2):
+                    if h == 0:
+                        rows = shard_rows(z, j, x if mine else 1 - x, self.R)
+                    else:
+                        rows = shard_rows(z, y if mine else 1 - y, j, self.R)
+                    yield h, j, dst, ((2 * k + h) * self.most + n) * 2 + j, self.parts[a].at[rows, src]
+
     def one(self, k):
-        z, cs = self.zk(k), []
-        for n, a, src, dst in self.pieces(0):
-            slot = (2 * k) * self.most + n
-            cs.append(remote(self.parts[a].at[z, :, 1 - self.x, :, src], self.r1a.at[k, :, :, dst], self.s1.at[slot], self.v1.at[slot], self.neighbour("x")))
-        for n, a, src, dst in self.pieces(1):
-            slot = (2 * k + 1) * self.most + n
-            cs.append(remote(self.parts[a].at[z, 1 - self.y, :, :, src], self.r1b.at[k, :, :, dst], self.s1.at[slot], self.v1.at[slot], self.neighbour("y")))
-        return cs
+        return [remote(src, (self.r1a, self.r1b)[h].at[k, j, :, dst], self.s1.at[slot], self.v1.at[slot], self.neighbour("xy"[h]))
+                for h, j, dst, slot, src in self.sources(k, False)]
 
     def load(self, k):
-        z, cs = self.zk(k), []
-        for n, a, src, dst in self.pieces(0):
-            cs.append(pltpu.make_async_copy(self.parts[a].at[z, :, self.x, :, src], self.o1a.at[k, :, :, dst], self.lsem.at[(2 * k) * self.most + n]))
-        for n, a, src, dst in self.pieces(1):
-            cs.append(pltpu.make_async_copy(self.parts[a].at[z, self.y, :, :, src], self.o1b.at[k, :, :, dst], self.lsem.at[(2 * k + 1) * self.most + n]))
-        return cs
+        return [pltpu.make_async_copy(src, (self.o1a, self.o1b)[h].at[k, j, :, dst], self.lsem.at[slot]) for h, j, dst, slot, src in self.sources(k, True)]
 
     def two(self, k):
         return [remote(self.o1a.at[k, 1 - self.y], self.r2a.at[k], self.s2.at[2 * k], self.v2.at[2 * k], self.neighbour("y")),
@@ -642,7 +709,7 @@
     a, b = [sum(p[2] for p in h) for h in halves]
     V = lambda *s: pltpu.VMEM(s, bf16)
     return [V(G, 2, R, a), V(G, 2, R, b), V(G, 2, R, a), V(G, 2, R, b), V(G, R, a), V(G, R, b), V(G - 1, R, a + b), V(G, R, a + b),
-            D((2 * G * most,)), D((2 * G * most,)), D((2 * G * most,)), D((2 * G,)), D((2 * G,)), D((G - 1,)), D((G - 1,))]
+            D((4 * G * most,)), D((4 * G * most,)), D((4 * G * most,)), D((2 * G,)), D((2 * G,)), D((G - 1,)), D((G - 1,))]
 
 
 def beside(plan, G, steps, now, compute, late=()):
@@ -671,16 +738,8 @@
     return pl.BlockSpec(memory_space=pltpu.VMEM)
 
 
-def spread(a, wide):
-    return a.reshape(wide // 4, 2, 2, a.shape[0] // wide, a.shape[1])
-
-
 def gathered_shapes(shards, wide):
-    return tuple(jax.ShapeDtypeStruct((wide // 4, 2, 2) + s.shape, s.dtype) for s in shards)
-
-
-def flat(a):
-    return a.reshape(-1, a.shape[-1])
+    return tuple(jax.ShapeDtypeStruct((wide * s.shape[0], s.shape[1]), s.dtype) for s in shards)
 
 
 def sum_everywhere(G, acc, got, gz, s, v, sz, vz):
@@ -728,10 +787,10 @@
     return v * half, half + 0.5 * v * (1.0 - t * t) * root * (1.0 + 3 * 0.044715 * square)
 
 
-def mid_kernel(att_h, tok_h, cot_h, wo_h, wg_h, wu_h, wd_h, gain_ref,
-               gout_h, gg_h, gu_h, gd_h, y_ref, gh_ref, ga_ref, ggain_ref,
-               att, tok, cot, wo, wg, wu, wd, part, other, back, hid, n2, n2t, cott, hff, gg, gu, ysend, yown, yother, stage,
-               isem, osem, sp, vp, sb, vb, sy, vy):
+def mid_kernel(G, cut, att_h, tok_h, cot_h, wo_h, wg_h, wu_h, wd_h, wd_shard, gain_ref,
+               gout_h, gg_h, gu_h, gd_h, y_ref, gh_ref, ga_ref, ggain_ref, sd_ref,
+               att, tok, cot, wo, wg, wu, wd, part, other, back, hid, n2t, cott, hff, gg, gu, ysend, yown, yother, stage,
+               isem, osem, sp, vp, sb, vb, sy, vy, *sems):
     core = lax.axis_index("narrow")
     peer = {"narrow": 1 - core}
     n, d = tok.shape
@@ -739,12 +798,14 @@
     tiles = n // TILE
     half = tiles // 2
     loads = [pltpu.make_async_copy(s, t, isem.at[k]) for k, (s, t) in enumerate(
-        [(att_h, att), (wo_h, wo), (tok_h, tok), (wg_h, wg), (wu_h, wu), (wd_h, wd), (cot_h, cot)])]
+        [(att_h, att), (wo_h, wo), (tok_h, tok), (wg_h, wg), (wu_h, wu), (cot_h, cot), (wd_h, wd.at[:, pl.ds(0, cut)])])]
     for c in loads:
         c.start()
-    bar = pltpu.get_barrier_semaphore()
-    pl.semaphore_signal(bar, inc=1, device_id=peer, device_id_type=MESH)
-    pl.semaphore_wait(bar, 1)
+    mid = cut + (ff - cut) // 256 * 128
+    bring = Gather(G, (((0, 0, mid - cut),), ((0, mid - cut, ff - mid),)), [wd_shard], [(wd, cut, cut)], *sems[:5])
+    give = Scatter(G, (((0, 0, cut),), ((0, cut, ff - cut),)), [gd_h], [sd_ref], *sems[5:])
+    greet(G, True, 1)
+    bring.begin()
     rows_of = lambda t: pl.ds(pl.multiple_of(t * TILE, TILE), TILE)
     send_part = lambda t: remote(part.at[rows_of(t)], other.at[rows_of(t)], sp.at[t], vp.at[t], peer)
     send_back = lambda t: remote(part.at[rows_of(t)], back.at[rows_of(t)], sb.at[t], vb.at[t], peer)
@@ -754,10 +815,21 @@
     for c in loads[:2]:
         c.wait()
 
+    def at_step(s, plan):
+        for k, acts in plan.items():
+            @pl.when(s == k)
+            def _():
+                for act in acts:
+                    act()
+
+    turns = [functools.partial(bring.turns, k) for k in range(G)]
+    steps = [functools.partial(bring.step, k) for k in range(1, G)]
+
     @pl.loop(0, tiles)
     def _(t):
         part[rows_of(t), :] = nt(att[rows_of(t), :], wo[...]).astype(bf16)
         send_part(t).start()
+        at_step(t, {1: turns[:1], 2: steps[:1]})
 
     for c in loads[2:]:
         c.wait()
@@ -767,6 +839,8 @@
         w = min(384, ff - at)
         chunks.append((at, w))
         at += w
+
+    later = [act for pair in zip(turns[1:], steps[1:] + [lambda: None]) for act in pair]
 
     @pl.loop(0, tiles)
     def _(s):
@@ -777,30 +851,16 @@
         hid[r, :] = h
         factor = lax.rsqrt(jnp.mean(h * h, axis=1, keepdims=True) + epsilon)
         low = (h * factor * gain).astype(bf16)
-        n2[r, :] = low
         n2t[:, r] = low.T
-        ct = cot[r, :]
-        cott[:, r] = ct.T
+        cott[:, r] = cot[r, :].T
         for at, w in chunks:
             cols = pl.ds(at, w)
             act, slope = gelu_and_slope(nn(low, wg[:, cols]))
             up = nn(low, wu[:, cols])
-            gf = nn(ct, wd[:, cols])
             hff[r, cols] = (act * up).astype(bf16)
-            gg[r, cols] = (gf * up * slope).astype(bf16)
-            gu[r, cols] = (gf * act).astype(bf16)
-        part[r, :] = (nt(gg[r, :], wg[...]) + nt(gu[r, :], wu[...])).astype(bf16)
-        send_back(t).start()
-        y = nt(hff[r, :], wd[...]).astype(bf16)
-
-        @pl.when(s < half)
-        def _():
-            ysend[rows_of(s), :] = y
-            send_y(s).start()
-
-        @pl.when(s >= half)
-        def _():
-            yown[rows_of(s - half), :] = y
+            gg[r, cols] = (up * slope).astype(bf16)
+            gu[r, cols] = act.astype(bf16)
+        at_step(s, {1: later[:2], 2: later[2:4], 3: later[4:]})
 
     def weight_grad(left, right, out, slot, width):
         @pl.loop(0, d // TILE)
@@ -819,6 +879,36 @@
             pltpu.make_async_copy(stage.at[k % 2, :, pl.ds(0, width)], out.at[rows_of(k)], osem.at[2 * slot + k % 2]).wait()
 
     weight_grad(cott, hff, gd_h, 0, ff)
+    give.begin()
+    bring.finish()
+    ones = [functools.partial(give.add_one, k) for k in range(G)]
+    twos = [functools.partial(give.add_two, k) for k in range(G - 1)]
+
+    @pl.loop(0, tiles)
+    def _(s):
+        t = (s + half * (1 - core)) % tiles
+        r = rows_of(t)
+        ct = cot[r, :]
+        for at, w in chunks:
+            cols = pl.ds(at, w)
+            gf = nn(ct, wd[:, cols])
+            gg[r, cols] = (gf * gg[r, cols].astype(f32)).astype(bf16)
+            gu[r, cols] = (gf * gu[r, cols].astype(f32)).astype(bf16)
+        part[r, :] = (nt(gg[r, :], wg[...]) + nt(gu[r, :], wu[...])).astype(bf16)
+        send_back(t).start()
+        y = nt(hff[r, :], wd[...]).astype(bf16)
+
+        @pl.when(s < half)
+        def _():
+            ysend[rows_of(s), :] = y
+            send_y(s).start()
+
+        @pl.when(s >= half)
+        def _():
+            yown[rows_of(s - half), :] = y
+
+        at_step(s, {0: ones[:1], 1: ones[1:2], 2: twos[:1], 3: ones[2:3] + twos[1:2]})
+
     ggain_ref[...] = jnp.zeros_like(ggain_ref)
 
     @pl.loop(0, tiles)
@@ -844,26 +934,33 @@
             send_y(s - half).wait()
             y_ref[j, :] = (h + (yown[j, :].astype(f32) + yother[j, :].astype(f32))).astype(bf16)
 
+        at_step(s, {2: ones[3:4]})
+
     weight_grad(n2t, gg, gg_h, 1, ff)
+    for act in twos[2:3] + [act for pair in zip(ones[4:], twos[3:]) for act in pair]:
+        act()
     weight_grad(n2t, gu, gu_h, 2, ff)
     weight_grad(cott, att, gout_h, 3, att.shape[1])
-
-
-def middle(att, tok, cot, wo, wg, wu, wd, gain, cid):
+    give.finish()
+
+
+def middle(att, tok, cot, wo, wg, wu, wd, wd_shard, gain, wide, cid):
     n, d = tok.shape
-    units, ff = att.shape[1], wg.shape[1]
+    units, ff, G, cut = att.shape[1], wg.shape[1], wide // 4, wd.shape[1]
     B = lambda *s: pltpu.VMEM(s, bf16)
     sds = jax.ShapeDtypeStruct
     tiles = n // TILE
-    return pl.pallas_call(mid_kernel,
+    halves = (((0, 0, cut),), ((0, cut, ff - cut),))
+    return pl.pallas_call(functools.partial(mid_kernel, G, cut),
         out_shape=(sds((d, units), bf16), sds((d, ff), bf16), sds((d, ff), bf16), sds((d, ff), bf16),
-                   sds((n // 2, d), bf16), sds((n // 2, d), f32), sds((n, units), bf16), sds((1, d), f32)),
-        in_specs=[ANY] * 7 + [whole_vmem()], out_specs=(ANY,) * 4 + (whole_vmem(),) * 4,
+                   sds((n // 2, d), bf16), sds((n // 2, d), f32), sds((n, units), bf16), sds((1, d), f32), sds((d // wide, ff), f32)),
+        in_specs=[ANY] * 8 + [whole_vmem()], out_specs=(ANY,) * 4 + (whole_vmem(),) * 5,
         scratch_shapes=[B(n, units), B(n, d), B(n, d), B(d, units), B(d, ff), B(d, ff), B(d, ff), B(n, d), B(n, d), B(n, d),
-                        pltpu.VMEM((n, d), f32), B(n, d), B(d, n), B(d, n), B(n, ff), B(n, ff), B(n, ff),
+                        pltpu.VMEM((n, d), f32), B(d, n), B(d, n), B(n, ff), B(n, ff), B(n, ff),
                         B(n // 2, d), B(n // 2, d), B(n // 2, d), B(2, TILE, ff),
-                        D((7,)), D((8,)), D((tiles,)), D((tiles,)), D((tiles,)), D((tiles,)), D((tiles // 2,)), D((tiles // 2,))],
-        compiler_params=params(cid), name="feed_forward")(att, tok, cot, wo, wg, wu, wd, gain)
+                        D((7,)), D((8,)), D((tiles,)), D((tiles,)), D((tiles,)), D((tiles,)), D((tiles // 2,)), D((tiles // 2,))]
+        + gather_scratch(G, halves, 1) + scatter_scratch(G, halves, d // wide),
+        compiler_params=params(cid), name="feed_forward")(att, tok, cot, wo, wg, wu, wd, wd_shard, gain)
 
 
 def local(tokens, cotangent, pages, boxes, gain_attn, gain_ffn, bias_tables, w_query, w_key, w_value, w_out, w_gate, w_up, w_down):
@@ -881,18 +978,19 @@
     bias, ids, (w_first, full_out, full_gate) = bias_and_gather(
         tables, boxes, pages, [jnp.concatenate([w_query, w_key, w_value], axis=1), w_out.T, w_gate],
         (((2, 0, ff), (0, 0, early)), ((1, 0, inner), (0, early, 3 * inner - early))), wide, 1)
-    (attended, lse, normed, qkv), (full_up, full_down) = attn_fwd_and_gather(
-        all_tokens, gain_one, w_first, bias, [w_up, w_down.T], (((0, 0, ff),), ((1, 0, ff),)), wide, 2)
-    grad_w_out, grad_w_gate, grad_w_up, grad_w_down, output, grad_hidden, grad_attended, grad_gain_two = middle(
-        attended, all_tokens, all_cot, full_out, full_gate, full_up, full_down, gain_two, 3)
-    (g, grad_w_query, grad_w_key, grad_w_value, grad_normed), (s_down, s_out) = attn_bwd_and_scatter(
-        qkv, bias, attended, grad_attended, lse, normed, w_first, [grad_w_down, grad_w_out],
+    down_shard = w_down.T
+    cut = (ff // 128 + 1) // 2 * 128
+    (attended, lse, normed, qkv), (full_up, most_down) = attn_fwd_and_gather(
+        all_tokens, gain_one, w_first, bias, [w_up, down_shard[:, :cut]],
+        (((0, 0, cut), (1, 0, cut - 384)), ((0, cut, ff - cut), (1, cut - 384, 384))), wide, 2)
+    grad_w_out, grad_w_gate, grad_w_up, _, output, grad_hidden, grad_attended, grad_gain_two, s_down = middle(
+        attended, all_tokens, all_cot, full_out, full_gate, full_up, most_down, down_shard, gain_two, wide, 3)
+    (g, band, far, grad_w_query, grad_w_key, grad_w_value, grad_normed), (s_gate, s_out) = attn_bwd_and_scatter(
+        qkv, bias, attended, grad_attended, lse, normed, w_first, [grad_w_gate, grad_w_out],
         (((0, 0, 2 * inner),), ((0, 2 * inner, ff - 2 * inner), (1, 0, inner))), wide, 4)
-    half = inner // 2
-    small, grad_tokens, (s_gate, s_up, s_query, s_key, s_value) = hist_and_scatter(
-        g, ids, grad_normed, tokens, grad_hidden, gain_one, grad_gain_two,
-        [grad_w_gate, grad_w_up, grad_w_query, grad_w_key, grad_w_value],
-        (((0, 0, ff), (2, 0, inner), (3, 0, half)), ((1, 0, ff), (4, 0, inner), (3, half, half))), wide, 5)
+    small, grad_tokens, (s_up, s_query, s_key, s_value) = hist_and_scatter(
+        g, band, far, ids, grad_normed, tokens, grad_hidden, gain_one, grad_gain_two, [grad_w_up, grad_w_query, grad_w_key, grad_w_value],
+        (((0, 0, ff),), ((1, 0, inner), (2, 0, inner), (3, 0, inner))), wide, 5)
     lines = d // 128
     one, two = small[:lines].reshape(d), small[lines:2 * lines].reshape(d)
     table = small[2 * lines:, :bias_tables.shape[0]].T

time: 358 us -> 348 us (0.972)
  Pallas kernels: 322 us -> 312 us
    pallas_call x1, Pallas kernels: 93.6 us -> 73.6 us  [hist_and_scatter(): pl.pallas_call(functools.partial(hist_kernel, heads, rows, n, G, halves,...]
    pallas_call x1, Pallas kernels: 55.2 us -> 67.6 us  [middle(): pl.pallas_call(functools.partial(mid_kernel, G, cut), out_shape=(sds((d,...]
    pallas_call x1, Pallas kernels: 54 us -> 44.8 us  [attn_fwd_and_gather(): pl.pallas_call(functools.partial(fwd_kernel, pairs, tiles, G, halves, cou...]
    pallas_call x1, Pallas kernels: 52.8 us -> 59.2 us  [attn_bwd_and_scatter(): pl.pallas_call(functools.partial(bwd_kernel, pairs, tiles, G, halves, cou...]
    unnamed x34 -> x36, local copies, waits for them, and re-layouts: 8.88 us -> 8.2 us
  transfers between devices with their start and end apart: 2 -> 2, of which waited for: 0 -> 0; matrix products, arithmetic and copies ran while one was open for 2% -> 3% of each run, Pallas kernels for 34% -> 32%
where the time goes in v6:
time: 348 us; the launch traced here: 347 us
  Pallas kernels  312 us (90%)
  local copies, waits for them, and re-layouts  14.9 us (4%)
  between operations  14.2 us (4%)
  other arithmetic  4.46 us (1%)
    pallas_call x1, Pallas kernels, hist_and_scatter(): pl.pallas_call(functools.partial(hist_kernel, heads, rows, n, G, halves,...  73.6 us
    pallas_call x1, Pallas kernels, middle(): pl.pallas_call(functools.partial(mid_kernel, G, cut), out_shape=(sds((d,...  67.6 us
    pallas_call x1, Pallas kernels, bias_and_gather(): pl.pallas_call(functools.partial(bias_gather_kernel, heads, rows, n, G, h...  66.5 us
    pallas_call x1, Pallas kernels, attn_bwd_and_scatter(): pl.pallas_call(functools.partial(bwd_kernel, pairs, tiles, G, halves, cou...  59.2 us
    pallas_call x1, Pallas kernels, attn_fwd_and_gather(): pl.pallas_call(functools.partial(fwd_kernel, pairs, tiles, G, halves, cou...  44.8 us
    unnamed x36, local copies, waits for them, and re-layouts  8.2 us
  transfers between devices with their start and end apart: 2, of which 0 were waited for; matrix products, arithmetic and copies ran while one was open for 3% of the time, Pallas kernels for 32%

profile of v6, /device:TPU:0, one launch (start us, length us, event | category | flops | bytes accessed | tf_op | source)
XLA Modules:
  0.0 346.8 jit_solution(10340046904181604928)
XLA Ops:
  7.2 0.0 all-gather.3.cloned.1.call-start
  7.3 0.7 all-gather.3.cloned.1.call-update
  8.0 0.0 all-gather.5.cloned.1.call-start
  8.0 0.7 all-gather.5.cloned.1.call-update
  8.7 1.3 broadcast_in_dim.23
  10.0 1.3 broadcast_in_dim.24
  11.3 0.7 round-nearest-even_convert_fusion
  11.9 0.1 reshape.219
  12.1 0.6 pad.4.refs_1_
  12.7 1.5 slice.26.refs_5_
  14.2 1.7 copy.31.refs_4_
  15.9 1.0 copy.30
  16.9 0.5 fusion.17.refs_0_
  17.5 0.7 pad_maximum_fusion.refs_6_
  18.2 66.5 %layout_bias_gather.1 = (f32[8,1024,1024]{2,1,0:T(8,128)}, f32[2,1024,1024]{2,1,0:T(8,128)}, f32[8,64,128]{2,1,0:T(8,128)}, bf16[1024,1536]{1,0:T(8,128)(2,1)}, ...) custom-call(s32[1,128]{1,0:T(1,128)} %fusion.17.refs_0_, s32[12,128]{1,0:T(8,128)} %pad.4.refs_1_, ...), custom_call_target="tpu_custom_call" | custom-call | tf_op jit(solution)/shard_map/layout_bias_gather/pallas_call | solution.py:86
  84.7 0.0 all-gather.3.cloned.1.call-done.refs_0_.tok_h
  84.7 44.8 %attention_gather.1 = (bf16[1024,512]{1,0:T(8,128)(2,1)}, f32[4,1024,2]{2,1,0:T(8,128)}, bf16[1024,1024]{1,0:T(8,128)(2,1)}, bf16[1024,1536]{1,0:T(8,128)(2,1)},...) custom-call(bf16[1024,1024]{1,0:T(8,128)(2,1)} %all-gather.3.cloned.1.call-done.refs_0_.tok_h, f32[1,1024]{1,0:T(1,128)} %bitcast.27, ...), custom_call_target="tpu_custom_call" | custom-call | tf_op jit(solution)/shard_map/attention_gather/pallas_call | solution.py:168
  129.6 0.0 all-gather.5.cloned.1.call-done.cot_h
  129.6 67.6 %feed_forward.1 = (bf16[1024,512]{1,0:T(8,128)(2,1)}, bf16[1024,1408]{1,0:T(8,128)(2,1)}, bf16[1024,1408]{1,0:T(8,128)(2,1)}, bf16[1024,1408]{1,0:T(8,128)(2,1)}...) custom-call(bf16[1024,512]{1,0:T(8,128)(2,1)} %get-tuple-element.49., ...), custom_call_target="tpu_custom_call" | custom-call | tf_op jit(solution)/shard_map/feed_forward/pallas_call | solution.py:954
  197.2 59.2 %attention_back_scatter.1 = (bf16[8,1024,1024]{2,1,0:T(8,128)(2,1)}, f32[8,256,512]{2,1,0:T(8,128)}, f32[8,2,16,128]{3,2,1,0:T(8,128)}, bf16[1024,512]{1,0:T(8,1...) custom-call(bf16[1024,1536]{1,0:T(8,128)(2,1)} %get-tuple-element.55, ...), custom_call_target="tpu_custom_call" | custom-call | tf_op jit(solution)/shard_map/attention_back_scatter/pallas_call | solution.py:271
  256.4 73.6 %table_grad_scatter.1 = (f32[32,128]{1,0:T(8,128)}, f32[512,1024]{1,0:T(8,128)}, f32[64,1408]{1,0:T(8,128)}, f32[64,512]{1,0:T(8,128)}, f32[64,512]{1,0:T(8,128)}, /*index=5*/f32[64,512]{1,0:T(8,128)}) custom-call(bf16[8,1024,1024]{2,1,0:T(8,128)(2,1)} %get-tuple-element.61.refs_0_, f32[2,1024,1024]{2,1,0:T(8,128)} %get-tuple-element.62.refs_1_, ...), custom_call_target="tpu_custom_call" | custom-call | tf_op jit(solution)/shard_map/table_grad_scatter/pallas_call | solution.py:385
  330.1 1.4 slice_bitcast_fusion
  331.5 1.3 slice_bitcast_fusion.1
  332.8 1.0 copy.41
  333.8 1.3 copy.42
  335.1 0.7 copy.43
  335.8 0.7 copy.44
  336.4 0.7 copy.45
  337.1 0.7 copy.46
  337.8 0.7 copy.47
  338.5 0.7 copy.48
  339.2 0.7 copy.49
  (29 shorter events, 0.1 us)
Async XLA Ops:
  7.2 8.7 %copy-start.12 = (s32[2,1024]{1,0:T(2,128)S(1)}, s32[2,1024]{1,0:T(2,128)}, u32[]{:S(2)}) copy-start(s32[2,1024]{1,0:T(2,128)} %refs_3_.1) | copy-start | bytes 24580
  7.2 10.3 %copy-start.9 = (bf16[64,512]{1,0:T(8,128)(2,1)S(1)}, bf16[64,512]{1,0:T(8,128)(2,1)}, u32[]{:S(2)}) copy-start(bf16[64,512]{1,0:T(8,128)(2,1)} %param.23) | copy-start | bytes 196612
  7.2 10.3 %copy-start.10 = (bf16[64,512]{1,0:T(8,128)(2,1)S(1)}, bf16[64,512]{1,0:T(8,128)(2,1)}, u32[]{:S(2)}) copy-start(bf16[64,512]{1,0:T(8,128)(2,1)} %param.22) | copy-start | bytes 196612
  7.2 10.3 %copy-start.11 = (bf16[64,512]{1,0:T(8,128)(2,1)S(1)}, bf16[64,512]{1,0:T(8,128)(2,1)}, u32[]{:S(2)}) copy-start(bf16[64,512]{1,0:T(8,128)(2,1)} %param.21) | copy-start | bytes 196612
  7.2 77.5 %all-gather.3.cloned.1.call-start = ((), (), s32[]{:S(2)}) async-start(), calls=%async_computation | async-start | bytes 3145728 | tf_op jit(solution)/shard_map/all_gather | solution.py:975
  8.0 121.6 %all-gather.5.cloned.1.call-start = ((), (), s32[]{:S(2)}) async-start(), calls=%async_computation.1 | async-start | bytes 3145728 | tf_op jit(solution)/shard_map/all_gather | solution.py:976
  256.4 76.4 %copy-start.1 = (bf16[512,1024]{1,0:T(8,128)(2,1)S(1)}, bf16[512,1024]{1,0:T(8,128)(2,1)}, u32[]{:S(2)}) copy-start(bf16[512,1024]{1,0:T(8,128)(2,1)} %get-tuple-element.96) | copy-start | bytes 3145732
  330.0 3.7 %copy-start = (f32[512,1024]{1,0:T(8,128)S(1)}, f32[512,1024]{1,0:T(8,128)}, u32[]{:S(2)}) copy-start(f32[512,1024]{1,0:T(8,128)} %get-tuple-element.97) | copy-start | bytes 6291460
  332.8 2.3 copy-start.8
  332.8 3.0 copy-start.7
  333.8 2.7 copy-start.6
  333.8 3.3 copy-start.5
  333.8 4.0 %copy-start.3 = (f32[64,1408]{1,0:T(8,128)S(1)}, f32[64,1408]{1,0:T(8,128)}, u32[]{:S(2)}) copy-start(f32[64,1408]{1,0:T(8,128)} %get-tuple-element.105) | copy-start | bytes 1081348
  333.8 4.7 %copy-start.4 = (f32[64,1408]{1,0:T(8,128)S(1)}, f32[64,1408]{1,0:T(8,128)}, u32[]{:S(2)}) copy-start(f32[64,1408]{1,0:T(8,128)} %get-tuple-element.106) | copy-start | bytes 1081348
  333.8 5.4 %copy-start.2 = (f32[64,1408]{1,0:T(8,128)S(1)}, f32[64,1408]{1,0:T(8,128)}, u32[]{:S(2)}) copy-start(f32[64,1408]{1,0:T(8,128)} %get-tuple-element.81) | copy-start | bytes 1081348
Sparse Core Ops, SparseCore 0:
  9.6 13.2 all-gather.2
  24.5 11.7 all-gather.4

commit v7 on v6

--- a/solution.py
+++ b/solution.py
@@ -197,15 +197,14 @@
             far_ref[e, jnp.where(c < first, 0, 1)] += total
 
 
-def bwd_tile(p, i, last_tile, last, q_ref, k_ref, v_ref, bias_ref, o_ref, do_ref, lse_ref, normed_ref, wq_ref, wk_ref, wv_ref,
-             g_ref, band_ref, far_ref, dwq_ref, dwk_ref, dwv_ref, dx_ref, dkt, dvt, dqkv, turned, dx):
+def bwd_tile(p, pairs, i, last_tile, last, q_ref, k_ref, v_ref, bias_ref, o_ref, do_ref, lse_ref, normed_ref, w_ref,
+             g_ref, band_ref, far_ref, dw_ref, dx_ref, dkt, dvt, dqkv, turned):
     tq, n = q_ref.shape[0], k_ref.shape[0]
     rows = pl.ds(pl.multiple_of(i * tq, tq), tq)
 
     @pl.when(p == 0)
     def _():
         turned[:, rows] = normed_ref[rows, :].T
-        dx[rows, :] = jnp.zeros((tq, dx.shape[1]), f32)
 
     @pl.when(i == 0)
     def _():
@@ -227,34 +226,31 @@
         dvt[...] += jnp.dot(dom.T, w.astype(bf16), preferred_element_type=f32)
         dkt[...] += jnp.dot(qm.T, g, preferred_element_type=f32)
         band_sums(i, e, g_ref, band_ref, far_ref)
-    dqkv[rows, 0:128] = join(*dqs).astype(bf16)
+    columns = lambda k: pl.ds(pl.multiple_of((p + k * pairs) * 128, 128), 128)
+    dqkv[rows, columns(0)] = join(*dqs).astype(bf16)
 
     @pl.when(last_tile)
     def _():
-        dqkv[:, 128:256] = dkt[...].T.astype(bf16)
-        dqkv[:, 256:384] = dvt[...].T.astype(bf16)
-
-        @pl.loop(0, n // TILE)
-        def _(t):
-            r = pl.ds(pl.multiple_of(t * TILE, TILE), TILE)
-            part = jnp.dot(turned[r, :], dqkv[...], preferred_element_type=f32).astype(bf16)
-            dwq_ref[r, :], dwk_ref[r, :], dwv_ref[r, :] = part[:, 0:128], part[:, 128:256], part[:, 256:384]
-            weights = jnp.concatenate([wq_ref[...], wk_ref[...], wv_ref[...]], axis=1)
-            dx[r, :] += lax.dot_general(dqkv[r, :], weights, NT, preferred_element_type=f32)
+        dqkv[:, columns(1)] = dkt[...].T.astype(bf16)
+        dqkv[:, columns(2)] = dvt[...].T.astype(bf16)
 
         @pl.when(last)
         def _():
-            dx_ref[...] = dx[...].astype(bf16)
+            @pl.loop(0, n // TILE)
+            def _(t):
+                r = pl.ds(pl.multiple_of(t * TILE, TILE), TILE)
+                dw_ref[r, :] = jnp.dot(turned[r, :], dqkv[...], preferred_element_type=f32).astype(bf16)
+                dx_ref[r, :] = lax.dot_general(dqkv[r, :], w_ref[...], NT, preferred_element_type=f32).astype(bf16)
 
 
 def bwd_kernel(pairs, tiles, G, halves, count, *refs):
-    ins, parts = refs[:11], refs[11:11 + count]
-    mid = refs[11 + count:18 + count]
-    outs, accs, sems = refs[18 + count:18 + 2 * count], refs[18 + 2 * count:23 + 2 * count], refs[23 + 2 * count:]
+    ins, parts = refs[:9], refs[9:9 + count]
+    mid = refs[9 + count:14 + count]
+    outs, accs, sems = refs[14 + count:14 + 2 * count], refs[14 + 2 * count:18 + 2 * count], refs[18 + 2 * count:]
     p, i = pl.program_id(0), pl.program_id(1)
     comm = Scatter(G, halves, parts, outs, *sems)
     beside(comm.events(), G, pairs * tiles, p * tiles + i,
-           lambda: bwd_tile(p, i, i == tiles - 1, p == pairs - 1, *ins, *mid, *accs))
+           lambda: bwd_tile(p, pairs, i, i == tiles - 1, p == pairs - 1, *ins, *mid, *accs))
 
 
 def shard_shapes(parts, wide):
@@ -269,16 +265,15 @@
     full = lambda rows, k: pl.BlockSpec((rows, 128), lambda p, i: (0, p + k * pairs))
     const = lambda s: pl.BlockSpec(s, lambda p, i: (0, 0))
     outs = pl.pallas_call(functools.partial(bwd_kernel, pairs, tiles, G, halves, count), grid=(pairs, tiles),
-        out_shape=(sds((2 * pairs, n, n), bf16), sds((2 * pairs, tq, tq + 256), f32), sds((2 * pairs, 2, 16, 128), f32)) + (sds((d, width), bf16),) * 3 + (sds((n, d), bf16),) + shard_shapes(parts, wide),
+        out_shape=(sds((2 * pairs, n, n), bf16), sds((2 * pairs, tq, tq + 256), f32), sds((2 * pairs, 2, 16, 128), f32)) + (sds((d, 3 * width), bf16), sds((n, d), bf16)) + shard_shapes(parts, wide),
         in_specs=[tile, full(n, 1), full(n, 2), pl.BlockSpec((2, tq, n), lambda p, i: (p, i, 0)), tile, tile,
-                  pl.BlockSpec((1, tq, 2), lambda p, i: (p, i, 0)), const((n, d)), full(d, 0), full(d, 1), full(d, 2)] + [ANY] * count,
+                  pl.BlockSpec((1, tq, 2), lambda p, i: (p, i, 0)), const((n, d)), const(w.shape)] + [ANY] * count,
         out_specs=(pl.BlockSpec((2, tq, n), lambda p, i: (p, i, 0)), pl.BlockSpec((2, tq, tq + 256), lambda p, i: (p, 0, 0)),
-                   pl.BlockSpec((2, 2, 16, 128), lambda p, i: (p, 0, 0, 0))) + (full(d, 0),) * 3 + (const((n, d)),) + (whole_vmem(),) * count,
-        scratch_shapes=[pltpu.VMEM((128, n), f32), pltpu.VMEM((128, n), f32), pltpu.VMEM((n, 384), bf16), pltpu.VMEM((d, n), bf16),
-                        pltpu.VMEM((n, d), f32)] + scatter_scratch(G, halves, parts[0].shape[0] // wide),
+                   pl.BlockSpec((2, 2, 16, 128), lambda p, i: (p, 0, 0, 0))) + (const(w.shape), const((n, d))) + (whole_vmem(),) * count,
+        scratch_shapes=[pltpu.VMEM((128, n), f32), pltpu.VMEM((128, n), f32), pltpu.VMEM((n, 3 * width), bf16), pltpu.VMEM((d, n), bf16)] + scatter_scratch(G, halves, parts[0].shape[0] // wide),
         compiler_params=params(cid), name="attention_back_scatter")(
-            qkv, qkv, qkv, bias, o, do, lse, normed, w, w, w, *parts)
-    return outs[:7], outs[7:]
+            qkv, qkv, qkv, bias, o, do, lse, normed, w, *parts)
+    return outs[:5], outs[5:]
 
 
 def rows_times_hots(src, ids, rows, heads, gs):
@@ -289,31 +284,73 @@
             gs[c, h * rows:(h + 1) * rows, :] = block[:, c * 128:(c + 1) * 128]
     labels = [lax.broadcasted_iota(jnp.int32, (16, n), 0).astype(bf16) + float(k) for k in (0, 16)]
     one, zero = jnp.ones((16, n), bf16), jnp.zeros((16, n), bf16)
-    total = jnp.zeros((heads, 32 * len(ids(0))), f32)
-    for r in range(rows):
-        grow = jnp.concatenate([gs[c, pl.ds(r, heads, stride=rows), :] for c in range(n // 128)], axis=1).astype(bf16)
-        hots = []
-        for one_row in ids(r):
-            row = jnp.broadcast_to(one_row, (16, n)).astype(bf16)
-            hots += [jnp.where(row == label, one, zero) for label in labels]
-        total = total + lax.dot_general(grow, jnp.concatenate(hots, axis=0), NT, preferred_element_type=f32)
+    group = 4 // len(ids(0))
+    total = jnp.zeros((heads * group, 128), f32)
+    for first in range(0, rows, group):
+        grow, hots = [], []
+        for r in range(first, first + group):
+            grow.append(jnp.concatenate([gs[c, pl.ds(r, heads, stride=rows), :] for c in range(n // 128)], axis=1))
+            for one_row in ids(r):
+                row = jnp.broadcast_to(one_row, (16, n)).astype(bf16)
+                hots += [jnp.where(row == label, one, zero) for label in labels]
+        total = total + lax.dot_general(jnp.concatenate(grow, axis=0).astype(bf16), jnp.concatenate(hots, axis=0), NT, preferred_element_type=f32)
     return total
 
 
-def hist_tile(now, heads, g_ref, ids_ref, band_ref, far_ref, lin_ids, table, gs):
+def own_blocks(total, heads, width):
+    out = total[0:heads, 0:width]
+    for k in range(1, 128 // width):
+        out = out + total[k * heads:(k + 1) * heads, k * width:(k + 1) * width]
+    return out
+
+
+def halves_times_hots(g_ref, ids_ref, block, heads, gs, low):
+    rows, n = 16, g_ref.shape[2]
+    for h in range(heads):
+        for c in range(n // 128):
+            gs[c, h * rows:(h + 1) * rows, :] = g_ref[h, block, c * 128:(c + 1) * 128].astype(f32)
+    for t in range(2):
+        ids = ids_ref[t, block, :]
+        low[t] = jnp.where(ids >= 16.0, ids - 16.0, ids)
+    label = lax.broadcasted_iota(jnp.int32, (16, n), 0).astype(bf16)
+    one, zero = jnp.ones((16, n), bf16), jnp.zeros((16, n), bf16)
+    total = jnp.zeros((64, 64), f32)
+    for first in range(0, rows, 2):
+        left, hots = [], []
+        for r in range(first, first + 2):
+            grow = jnp.concatenate([gs[c, pl.ds(r, heads, stride=rows), :] for c in range(n // 128)], axis=1)
+            for t in range(2):
+                upper = jnp.broadcast_to(ids_ref.at[t, block][r:r + 1, :], (heads, n)) >= 16.0
+                left += [jnp.where(upper, 0.0, grow), jnp.where(upper, grow, 0.0)]
+                row = jnp.broadcast_to(low[t, r:r + 1, :], (16, n)).astype(bf16)
+                hots.append(jnp.where(row == label, one, zero))
+        total = total + lax.dot_general(jnp.concatenate(left, axis=0).astype(bf16), jnp.concatenate(hots, axis=0), NT, preferred_element_type=f32)
+    return total
+
+
+def own_halves(total, heads):
+    out = 0.0
+    for k in range(2):
+        part = lambda t, up: total[k * 32 + (2 * t + up) * heads:k * 32 + (2 * t + up + 1) * heads, k * 32 + t * 16:k * 32 + t * 16 + 16]
+        out = out + jnp.concatenate([part(0, 0), part(0, 1), part(1, 0), part(1, 1)], axis=1)
+    return out
+
+
+def hist_tile(now, heads, g_ref, ids_ref, band_ref, far_ref, lin_ids, table, boxes, gs, low):
     @pl.when(now == 0)
     def _():
         sides = [jnp.sum(jnp.sum(far_ref[:, k], axis=1), axis=1, keepdims=True) for k in range(2)]
         lane = lax.broadcasted_iota(jnp.int32, (heads, 128), 1)
-        table[0] = jnp.where(lane == 15, sides[0], 0.0) + jnp.where(lane == 31, sides[1], 0.0)
-        table[1] = jnp.zeros_like(table[1])
+        table[...] = jnp.zeros_like(table)
+        boxes[...] = jnp.zeros_like(boxes)
+        table[0:heads, :] = jnp.where(lane == 15, sides[0], 0.0) + jnp.where(lane == 31, sides[1], 0.0)
 
     big = g_ref.shape[1]
 
     @pl.loop(0, big // 16)
     def _(q):
         block = pl.ds(pl.multiple_of(q * 16, 16), 16)
-        table[1, :, 0:64] += rows_times_hots(lambda h: g_ref[h, block, :].astype(f32), lambda r: [ids_ref.at[t, block][r:r + 1, :] for t in range(2)], 16, heads, gs)
+        boxes[...] += halves_times_hots(g_ref, ids_ref, block, heads, gs, low)
 
     wide = band_ref.shape[2] // 128
     per = lin_ids.shape[1]
@@ -323,14 +360,14 @@
     def band_ids(r):
         return [jnp.concatenate([lin_ids.at[jnp.clip((m - 1) * (128 // per) - a + 4, 0, 7), inside][r:r + 1, :] for m in range(wide)], axis=1)]
 
-    table[0, :, 0:32] += rows_times_hots(lambda h: band_ref[h], band_ids, 16, heads, gs)
+    table[...] += rows_times_hots(lambda h: band_ref[h], band_ids, 16, heads, gs)
 
 
 def hist_kernel(heads, rows, n, G, halves, count, *refs):
     (g_ref, ids_ref, band_ref, far_ref, lin_ids, dx, tok, gh, gain_ref, gain_two), parts = refs[:10], refs[10:10 + count]
     small_ref, gt_ref = refs[10 + count:12 + count]
     outs, rest = refs[12 + count:12 + 2 * count], refs[12 + 2 * count:]
-    (gs, table, got, pair_sem), sums, sems = rest[:4], rest[4:11], rest[11:]
+    (gs, low, table, boxes, got, pair_sem), sums, sems = rest[:6], rest[6:13], rest[13:]
     acc = sums[0]
     now, steps = pl.program_id(0), n // rows
     core = lax.axis_index("narrow")
@@ -365,11 +402,11 @@
                 for k in range(d // 128):
                     acc[0, k:k + 1, :] += gain[:, k * 128:(k + 1) * 128]
 
-        hist_tile(now, heads, g_ref, ids_ref, band_ref, far_ref, lin_ids, table, gs)
+        hist_tile(now, heads, g_ref, ids_ref, band_ref, far_ref, lin_ids, table, boxes, gs, low)
 
     def reduce():
-        acc[0, pl.ds(pl.multiple_of(2 * (d // 128) + core * heads, 8), heads), 0:32] = table[0, :, 0:32]
-        acc[0, pl.ds(pl.multiple_of(2 * (d // 128) + core * heads, 8), heads), 32:96] = table[1, :, 0:64]
+        acc[0, pl.ds(pl.multiple_of(2 * (d // 128) + core * heads, 8), heads), 0:32] = own_blocks(table[...], heads, 32)
+        acc[0, pl.ds(pl.multiple_of(2 * (d // 128) + core * heads, 8), heads), 32:96] = own_halves(boxes[...], heads)
         small_ref[...] = sum_everywhere(G, *sums)
 
     beside(comm.events(1), G, steps, now, compute, (reduce,))
@@ -388,7 +425,7 @@
                   pl.BlockSpec((heads, 16, band.shape[2]), lambda i: (0, i, 0)), pl.BlockSpec(far.shape, lambda i: (0, 0, 0, 0)),
                   pl.BlockSpec(lin_ids.shape, lambda i: (0, 0, 0)), const(dx.shape), const(tok.shape), const(gh.shape), const(gain.shape), const(gain_two.shape)] + [ANY] * count,
         out_specs=(const((small, 128)), const(tok.shape)) + (whole_vmem(),) * count,
-        scratch_shapes=[pltpu.VMEM((n // 128, heads * 16, 128), f32), pltpu.VMEM((2, heads, 128), f32), pltpu.VMEM(tok.shape, bf16), D((2,))]
+        scratch_shapes=[pltpu.VMEM((n // 128, heads * 16, 128), f32), pltpu.VMEM((2, 16, n), f32), pltpu.VMEM((4 * heads, 128), f32), pltpu.VMEM((64, 64), f32), pltpu.VMEM(tok.shape, bf16), D((2,))]
         + sum_scratch(G, small) + scatter_scratch(G, halves, parts[0].shape[0] // wide),
         compiler_params=params(cid), name="table_grad_scatter")(g, box_ids, band, far, lin_ids, dx, tok, gh, gain, gain_two, *parts)
     return outs[0], outs[1], outs[2:]
@@ -788,7 +825,7 @@
 
 
 def mid_kernel(G, cut, att_h, tok_h, cot_h, wo_h, wg_h, wu_h, wd_h, wd_shard, gain_ref,
-               gout_h, gg_h, gu_h, gd_h, y_ref, gh_ref, ga_ref, ggain_ref, sd_ref,
+               gout_h, gg_h, gu_h, gd_h, y_ref, gh_ref, ga_ref, ggain_ref,
                att, tok, cot, wo, wg, wu, wd, part, other, back, hid, n2t, cott, hff, gg, gu, ysend, yown, yother, stage,
                isem, osem, sp, vp, sb, vb, sy, vy, *sems):
     core = lax.axis_index("narrow")
@@ -802,9 +839,8 @@
     for c in loads:
         c.start()
     mid = cut + (ff - cut) // 256 * 128
-    bring = Gather(G, (((0, 0, mid - cut),), ((0, mid - cut, ff - mid),)), [wd_shard], [(wd, cut, cut)], *sems[:5])
-    give = Scatter(G, (((0, 0, cut),), ((0, cut, ff - cut),)), [gd_h], [sd_ref], *sems[5:])
-    greet(G, True, 1)
+    bring = Gather(G, (((0, 0, mid - cut),), ((0, mid - cut, ff - mid),)), [wd_shard], [(wd, cut, cut)], *sems)
+    greet(G, False, 1)
     bring.begin()
     rows_of = lambda t: pl.ds(pl.multiple_of(t * TILE, TILE), TILE)
     send_part = lambda t: remote(part.at[rows_of(t)], other.at[rows_of(t)], sp.at[t], vp.at[t], peer)
@@ -879,10 +915,7 @@
             pltpu.make_async_copy(stage.at[k % 2, :, pl.ds(0, width)], out.at[rows_of(k)], osem.at[2 * slot + k % 2]).wait()
 
     weight_grad(cott, hff, gd_h, 0, ff)
-    give.begin()
     bring.finish()
-    ones = [functools.partial(give.add_one, k) for k in range(G)]
-    twos = [functools.partial(give.add_two, k) for k in range(G - 1)]
 
     @pl.loop(0, tiles)
     def _(s):
@@ -906,8 +939,6 @@
         @pl.when(s >= half)
         def _():
             yown[rows_of(s - half), :] = y
-
-        at_step(s, {0: ones[:1], 1: ones[1:2], 2: twos[:1], 3: ones[2:3] + twos[1:2]})
 
     ggain_ref[...] = jnp.zeros_like(ggain_ref)
 
@@ -934,14 +965,9 @@
             send_y(s - half).wait()
             y_ref[j, :] = (h + (yown[j, :].astype(f32) + yother[j, :].astype(f32))).astype(bf16)
 
-        at_step(s, {2: ones[3:4]})
-
     weight_grad(n2t, gg, gg_h, 1, ff)
-    for act in twos[2:3] + [act for pair in zip(ones[4:], twos[3:]) for act in pair]:
-        act()
     weight_grad(n2t, gu, gu_h, 2, ff)
     weight_grad(cott, att, gout_h, 3, att.shape[1])
-    give.finish()
 
 
 def middle(att, tok, cot, wo, wg, wu, wd, wd_shard, gain, wide, cid):
@@ -953,13 +979,13 @@
     halves = (((0, 0, cut),), ((0, cut, ff - cut),))
     return pl.pallas_call(functools.partial(mid_kernel, G, cut),
         out_shape=(sds((d, units), bf16), sds((d, ff), bf16), sds((d, ff), bf16), sds((d, ff), bf16),
-                   sds((n // 2, d), bf16), sds((n // 2, d), f32), sds((n, units), bf16), sds((1, d), f32), sds((d // wide, ff), f32)),
-        in_specs=[ANY] * 8 + [whole_vmem()], out_specs=(ANY,) * 4 + (whole_vmem(),) * 5,
+                   sds((n // 2, d), bf16), sds((n // 2, d), f32), sds((n, units), bf16), sds((1, d), f32)),
+        in_specs=[ANY] * 8 + [whole_vmem()], out_specs=(ANY,) * 4 + (whole_vmem(),) * 4,
         scratch_shapes=[B(n, units), B(n, d), B(n, d), B(d, units), B(d, ff), B(d, ff), B(d, ff), B(n, d), B(n, d), B(n, d),
                         pltpu.VMEM((n, d), f32), B(d, n), B(d, n), B(n, ff), B(n, ff), B(n, ff),
                         B(n // 2, d), B(n // 2, d), B(n // 2, d), B(2, TILE, ff),
                         D((7,)), D((8,)), D((tiles,)), D((tiles,)), D((tiles,)), D((tiles,)), D((tiles // 2,)), D((tiles // 2,))]
-        + gather_scratch(G, halves, 1) + scatter_scratch(G, halves, d // wide),
+        + gather_scratch(G, halves, 1),
         compiler_params=params(cid), name="feed_forward")(att, tok, cot, wo, wg, wu, wd, wd_shard, gain)
 
 
@@ -983,14 +1009,15 @@
     (attended, lse, normed, qkv), (full_up, most_down) = attn_fwd_and_gather(
         all_tokens, gain_one, w_first, bias, [w_up, down_shard[:, :cut]],
         (((0, 0, cut), (1, 0, cut - 384)), ((0, cut, ff - cut), (1, cut - 384, 384))), wide, 2)
-    grad_w_out, grad_w_gate, grad_w_up, _, output, grad_hidden, grad_attended, grad_gain_two, s_down = middle(
+    grad_w_out, grad_w_gate, grad_w_up, grad_w_down, output, grad_hidden, grad_attended, grad_gain_two = middle(
         attended, all_tokens, all_cot, full_out, full_gate, full_up, most_down, down_shard, gain_two, wide, 3)
-    (g, band, far, grad_w_query, grad_w_key, grad_w_value, grad_normed), (s_gate, s_out) = attn_bwd_and_scatter(
-        qkv, bias, attended, grad_attended, lse, normed, w_first, [grad_w_gate, grad_w_out],
-        (((0, 0, 2 * inner),), ((0, 2 * inner, ff - 2 * inner), (1, 0, inner))), wide, 4)
-    small, grad_tokens, (s_up, s_query, s_key, s_value) = hist_and_scatter(
-        g, band, far, ids, grad_normed, tokens, grad_hidden, gain_one, grad_gain_two, [grad_w_up, grad_w_query, grad_w_key, grad_w_value],
-        (((0, 0, ff),), ((1, 0, inner), (2, 0, inner), (3, 0, inner))), wide, 5)
+    (g, band, far, grad_w_first, grad_normed), (s_gate, s_down) = attn_bwd_and_scatter(
+        qkv, bias, attended, grad_attended, lse, normed, w_first, [grad_w_gate, grad_w_down], (((0, 0, ff),), ((1, 0, ff),)), wide, 4)
+    most = 2 * inner
+    small, grad_tokens, (s_up, s_out, s_first) = hist_and_scatter(
+        g, band, far, ids, grad_normed, tokens, grad_hidden, gain_one, grad_gain_two, [grad_w_up, grad_w_out, grad_w_first],
+        (((0, 0, ff), (2, most, inner // 2)), ((1, 0, inner), (2, 0, most), (2, most + inner // 2, inner // 2))), wide, 5)
+    s_query, s_key, s_value = jnp.split(s_first, 3, axis=1)
     lines = d // 128
     one, two = small[:lines].reshape(d), small[lines:2 * lines].reshape(d)
     table = small[2 * lines:, :bias_tables.shape[0]].T

time: 348 us -> 351 us (level)
    pallas_call x1, Pallas kernels: 67.6 us -> 61.8 us  [middle(): pl.pallas_call(functools.partial(mid_kernel, G, cut), out_shape=(sds((d,...]
    pallas_call x1, Pallas kernels: 59.2 us -> 64.7 us  [attn_bwd_and_scatter(): pl.pallas_call(functools.partial(bwd_kernel, pairs, tiles, G, halves, cou...]
    pallas_call x1, Pallas kernels: 73.6 us -> 77.6 us  [hist_and_scatter(): pl.pallas_call(functools.partial(hist_kernel, heads, rows, n, G, halves,...]
    unnamed x36 -> x27, local copies, waits for them, and re-layouts: 8.2 us -> 6.22 us
where the time goes in v7:
time: 351 us; the launch traced here: 350 us
  Pallas kernels  315 us (90%)
  local copies, waits for them, and re-layouts  14.7 us (4%)
  between operations  14.2 us (4%)
  other arithmetic  4.46 us (1%)
    pallas_call x1, Pallas kernels, hist_and_scatter(): pl.pallas_call(functools.partial(hist_kernel, heads, rows, n, G, halves,...  77.6 us
    pallas_call x1, Pallas kernels, bias_and_gather(): pl.pallas_call(functools.partial(bias_gather_kernel, heads, rows, n, G, h...  66.5 us
    pallas_call x1, Pallas kernels, attn_bwd_and_scatter(): pl.pallas_call(functools.partial(bwd_kernel, pairs, tiles, G, halves, cou...  64.7 us
    pallas_call x1, Pallas kernels, middle(): pl.pallas_call(functools.partial(mid_kernel, G, cut), out_shape=(sds((d,...  61.8 us
    pallas_call x1, Pallas kernels, attn_fwd_and_gather(): pl.pallas_call(functools.partial(fwd_kernel, pairs, tiles, G, halves, cou...  44.9 us
  transfers between devices with their start and end apart: 2, of which 0 were waited for; matrix products, arithmetic and copies ran while one was open for 3% of the time, Pallas kernels for 32%

profile of v7, /device:TPU:0, one launch (start us, length us, event | category | flops | bytes accessed | tf_op | source)
XLA Modules:
  0.0 350.3 jit_solution(11634862726268078718)
XLA Ops:
  7.2 0.0 copy-start.9
  7.2 0.0 all-gather.3.cloned.1.call-start
  7.3 0.7 all-gather.3.cloned.1.call-update
  8.0 0.0 all-gather.5.cloned.1.call-start
  8.0 0.7 all-gather.5.cloned.1.call-update
  8.7 1.3 broadcast_in_dim.23
  10.0 1.3 broadcast_in_dim.24
  11.3 0.7 round-nearest-even_convert_fusion
  11.9 0.1 reshape.219
  12.1 0.6 pad.4.refs_1_
  12.7 1.5 slice.26.refs_5_
  14.2 1.7 copy.31.refs_4_
  15.9 1.0 copy.30
  16.9 0.5 fusion.17.refs_0_
  17.5 0.0 copy-done.8
  17.5 0.7 pad_maximum_fusion.refs_6_
  18.2 66.5 %layout_bias_gather.1 = (f32[8,1024,1024]{2,1,0:T(8,128)}, f32[2,1024,1024]{2,1,0:T(8,128)}, f32[8,64,128]{2,1,0:T(8,128)}, bf16[1024,1536]{1,0:T(8,128)(2,1)}, ...) custom-call(s32[1,128]{1,0:T(1,128)} %fusion.17.refs_0_, s32[12,128]{1,0:T(8,128)} %pad.4.refs_1_, ...), custom_call_target="tpu_custom_call" | custom-call | tf_op jit(solution)/shard_map/layout_bias_gather/pallas_call | solution.py:86
  84.7 0.0 all-gather.3.cloned.1.call-done.refs_0_.tok_h
  84.7 44.9 %attention_gather.1 = (bf16[1024,512]{1,0:T(8,128)(2,1)}, f32[4,1024,2]{2,1,0:T(8,128)}, bf16[1024,1024]{1,0:T(8,128)(2,1)}, bf16[1024,1536]{1,0:T(8,128)(2,1)},...) custom-call(bf16[1024,1024]{1,0:T(8,128)(2,1)} %all-gather.3.cloned.1.call-done.refs_0_.tok_h, f32[1,1024]{1,0:T(1,128)} %bitcast.27, ...), custom_call_target="tpu_custom_call" | custom-call | tf_op jit(solution)/shard_map/attention_gather/pallas_call | solution.py:168
  129.6 0.0 all-gather.5.cloned.1.call-done.cot_h
  129.6 61.8 %feed_forward.1 = (bf16[1024,512]{1,0:T(8,128)(2,1)}, bf16[1024,1408]{1,0:T(8,128)(2,1)}, bf16[1024,1408]{1,0:T(8,128)(2,1)}, bf16[1024,1408]{1,0:T(8,128)(2,1)}...) custom-call(bf16[1024,512]{1,0:T(8,128)(2,1)} %get-tuple-element.46.att_h.refs, ...), custom_call_target="tpu_custom_call" | custom-call | tf_op jit(solution)/shard_map/feed_forward/pallas_call | solution.py:980
  191.4 64.7 %attention_back_scatter.1 = (bf16[8,1024,1024]{2,1,0:T(8,128)(2,1)}, f32[8,256,512]{2,1,0:T(8,128)}, f32[8,2,16,128]{3,2,1,0:T(8,128)}, bf16[1024,1536]{1,0:T(8,...) custom-call(bf16[1024,1536]{1,0:T(8,128)(2,1)} %get-tuple-element.52.refs_0_.refs_1_.refs_2_, ...), custom_call_target="tpu_custom_call" | custom-call | tf_op jit(solution)/shard_map/attention_back_scatter/pallas_call | solution.py:267
  256.2 77.6 %table_grad_scatter.1 = (f32[32,128]{1,0:T(8,128)}, f32[512,1024]{1,0:T(8,128)}, f32[64,1408]{1,0:T(8,128)}, f32[64,512]{1,0:T(8,128)}, f32[64,1536]{1,0:T(8,128)}) custom-call(bf16[8,1024,1024]{2,1,0:T(8,128)(2,1)} %get-tuple-element.58.refs_0_, f32[2,1024,1024]{2,1,0:T(8,128)} %get-tuple-element.59.refs_1_, f32[8,256,512]{2,1,0:T(8,128)} %get-tuple-element.60.refs_2_, ...), custom_call_target="tpu_custom_call" | custom-call | tf_op jit(solution)/shard_map/table_grad_scatter/pallas_call | solution.py:422
  333.8 1.4 slice_bitcast_fusion
  335.2 1.3 slice_bitcast_fusion.1
  336.5 1.8 fusion.31
  338.3 1.0 copy.38
  339.3 1.3 copy.39
  340.6 0.7 copy.40
  341.2 0.7 copy.41
  342.0 0.7 copy.42
  342.7 0.7 copy.43
  (21 shorter events, 0.1 us)
Async XLA Ops:
  7.2 8.7 %copy-start.9 = (s32[2,1024]{1,0:T(2,128)S(1)}, s32[2,1024]{1,0:T(2,128)}, u32[]{:S(2)}) copy-start(s32[2,1024]{1,0:T(2,128)} %refs_3_.1) | copy-start | bytes 24580
  7.2 10.3 %copy-start.6 = (bf16[64,512]{1,0:T(8,128)(2,1)S(1)}, bf16[64,512]{1,0:T(8,128)(2,1)}, u32[]{:S(2)}) copy-start(bf16[64,512]{1,0:T(8,128)(2,1)} %param.23) | copy-start | bytes 196612
  7.2 10.3 %copy-start.7 = (bf16[64,512]{1,0:T(8,128)(2,1)S(1)}, bf16[64,512]{1,0:T(8,128)(2,1)}, u32[]{:S(2)}) copy-start(bf16[64,512]{1,0:T(8,128)(2,1)} %param.22) | copy-start | bytes 196612
  7.2 10.3 %copy-start.8 = (bf16[64,512]{1,0:T(8,128)(2,1)S(1)}, bf16[64,512]{1,0:T(8,128)(2,1)}, u32[]{:S(2)}) copy-start(bf16[64,512]{1,0:T(8,128)(2,1)} %param.21) | copy-start | bytes 196612
  7.2 77.5 %all-gather.3.cloned.1.call-start = ((), (), s32[]{:S(2)}) async-start(), calls=%async_computation | async-start | bytes 3145728 | tf_op jit(solution)/shard_map/all_gather | solution.py:1001
  8.0 121.6 %all-gather.5.cloned.1.call-start = ((), (), s32[]{:S(2)}) async-start(), calls=%async_computation.1 | async-start | bytes 3145728 | tf_op jit(solution)/shard_map/all_gather | solution.py:1002
  256.2 82.1 %copy-start.1 = (bf16[512,1024]{1,0:T(8,128)(2,1)S(1)}, bf16[512,1024]{1,0:T(8,128)(2,1)}, u32[]{:S(2)}) copy-start(bf16[512,1024]{1,0:T(8,128)(2,1)} %get-tuple-element.93) | copy-start | bytes 3145732
  333.8 5.5 %copy-start = (f32[512,1024]{1,0:T(8,128)S(1)}, f32[512,1024]{1,0:T(8,128)}, u32[]{:S(2)}) copy-start(f32[512,1024]{1,0:T(8,128)} %get-tuple-element.94) | copy-start | bytes 6291460
  338.3 2.3 copy-start.5
  338.3 3.0 copy-start.3
  339.3 2.7 copy-start.4
  339.3 3.5 copy-start.2
Sparse Core Ops, SparseCore 0:
  9.6 13.2 all-gather.2
  24.5 11.7 all-gather.4

commit v8 on v7

--- a/solution.py
+++ b/solution.py
@@ -825,7 +825,7 @@
 
 
 def mid_kernel(G, cut, att_h, tok_h, cot_h, wo_h, wg_h, wu_h, wd_h, wd_shard, gain_ref,
-               gout_h, gg_h, gu_h, gd_h, y_ref, gh_ref, ga_ref, ggain_ref,
+               gout_h, gg_h, gu_h, gd_h, y_ref, gh_ref, ga_ref, ggain_ref, sd_ref,
                att, tok, cot, wo, wg, wu, wd, part, other, back, hid, n2t, cott, hff, gg, gu, ysend, yown, yother, stage,
                isem, osem, sp, vp, sb, vb, sy, vy, *sems):
     core = lax.axis_index("narrow")
@@ -838,9 +838,11 @@
         [(att_h, att), (wo_h, wo), (tok_h, tok), (wg_h, wg), (wu_h, wu), (cot_h, cot), (wd_h, wd.at[:, pl.ds(0, cut)])])]
     for c in loads:
         c.start()
+    part_cols = sd_ref.shape[1]
     mid = cut + (ff - cut) // 256 * 128
-    bring = Gather(G, (((0, 0, mid - cut),), ((0, mid - cut, ff - mid),)), [wd_shard], [(wd, cut, cut)], *sems)
-    greet(G, False, 1)
+    bring = Gather(G, (((0, 0, mid - cut),), ((0, mid - cut, ff - mid),)), [wd_shard], [(wd, cut, cut)], *sems[:5])
+    give = Scatter(G, (((0, 0, part_cols // 2),), ((0, part_cols // 2, part_cols // 2),)), [gd_h], [sd_ref], *sems[5:])
+    greet(G, True, 1)
     bring.begin()
     rows_of = lambda t: pl.ds(pl.multiple_of(t * TILE, TILE), TILE)
     send_part = lambda t: remote(part.at[rows_of(t)], other.at[rows_of(t)], sp.at[t], vp.at[t], peer)
@@ -899,23 +901,23 @@
         at_step(s, {1: later[:2], 2: later[2:4], 3: later[4:]})
 
     def weight_grad(left, right, out, slot, width):
-        @pl.loop(0, d // TILE)
-        def _(k):
-            b = k % 2
-            copy = lambda kk: pltpu.make_async_copy(stage.at[kk % 2, :, pl.ds(0, width)], out.at[rows_of(kk)], osem.at[2 * slot + kk % 2])
-
-            @pl.when(k >= 2)
-            def _():
+        rows = stage.shape[1]
+        block = lambda k: pl.ds(k * rows, rows)
+        copy = lambda k: pltpu.make_async_copy(stage.at[k % 2, :, pl.ds(0, width)], out.at[block(k)], osem.at[2 * slot + k % 2])
+        count = d // rows
+        for k in range(count):
+            if k >= 2:
                 copy(k - 2).wait()
-
-            stage[b, :, pl.ds(0, width)] = nn(left[rows_of(k), :], right[...]).astype(bf16)
+            stage[k % 2, :, pl.ds(0, width)] = nn(left[block(k), :], right[...]).astype(bf16)
             copy(k).start()
-
-        for k in range(d // TILE - 2, d // TILE):
-            pltpu.make_async_copy(stage.at[k % 2, :, pl.ds(0, width)], out.at[rows_of(k)], osem.at[2 * slot + k % 2]).wait()
-
-    weight_grad(cott, hff, gd_h, 0, ff)
+        return [copy(k) for k in range(max(0, count - 2), count)]
+
+    for c in weight_grad(cott, hff, gd_h, 0, ff):
+        c.wait()
+    give.begin()
     bring.finish()
+    ones = [functools.partial(give.add_one, k) for k in range(G)]
+    twos = [functools.partial(give.add_two, k) for k in range(G - 1)]
 
     @pl.loop(0, tiles)
     def _(s):
@@ -939,6 +941,8 @@
         @pl.when(s >= half)
         def _():
             yown[rows_of(s - half), :] = y
+
+        at_step(s, {0: ones[:1], 1: ones[1:2], 2: twos[:1] + ones[2:3], 3: twos[1:2]})
 
     ggain_ref[...] = jnp.zeros_like(ggain_ref)
 
@@ -965,12 +969,17 @@
             send_y(s - half).wait()
             y_ref[j, :] = (h + (yown[j, :].astype(f32) + yother[j, :].astype(f32))).astype(bf16)
 
-    weight_grad(n2t, gg, gg_h, 1, ff)
-    weight_grad(n2t, gu, gu_h, 2, ff)
-    weight_grad(cott, att, gout_h, 3, att.shape[1])
-
-
-def middle(att, tok, cot, wo, wg, wu, wd, wd_shard, gain, wide, cid):
+        at_step(s, {0: ones[3:4], 3: twos[2:3]})
+
+    for act in [act for pair in zip(ones[4:], twos[3:]) for act in pair]:
+        act()
+    for left, right, out, slot in ((n2t, gg, gg_h, 1), (n2t, gu, gu_h, 2), (cott, att, gout_h, 3)):
+        for c in weight_grad(left, right, out, slot, right.shape[1]):
+            c.wait()
+    give.finish()
+
+
+def middle(att, tok, cot, wo, wg, wu, wd, wd_shard, gain, here, wide, cid):
     n, d = tok.shape
     units, ff, G, cut = att.shape[1], wg.shape[1], wide // 4, wd.shape[1]
     B = lambda *s: pltpu.VMEM(s, bf16)
@@ -979,13 +988,13 @@
     halves = (((0, 0, cut),), ((0, cut, ff - cut),))
     return pl.pallas_call(functools.partial(mid_kernel, G, cut),
         out_shape=(sds((d, units), bf16), sds((d, ff), bf16), sds((d, ff), bf16), sds((d, ff), bf16),
-                   sds((n // 2, d), bf16), sds((n // 2, d), f32), sds((n, units), bf16), sds((1, d), f32)),
-        in_specs=[ANY] * 8 + [whole_vmem()], out_specs=(ANY,) * 4 + (whole_vmem(),) * 4,
+                   sds((n // 2, d), bf16), sds((n // 2, d), f32), sds((n, units), bf16), sds((1, d), f32), sds((d // wide, here), f32)),
+        in_specs=[ANY] * 8 + [whole_vmem()], out_specs=(ANY,) * 4 + (whole_vmem(),) * 5,
         scratch_shapes=[B(n, units), B(n, d), B(n, d), B(d, units), B(d, ff), B(d, ff), B(d, ff), B(n, d), B(n, d), B(n, d),
                         pltpu.VMEM((n, d), f32), B(d, n), B(d, n), B(n, ff), B(n, ff), B(n, ff),
-                        B(n // 2, d), B(n // 2, d), B(n // 2, d), B(2, TILE, ff),
+                        B(n // 2, d), B(n // 2, d), B(n // 2, d), B(2, 512, ff),
                         D((7,)), D((8,)), D((tiles,)), D((tiles,)), D((tiles,)), D((tiles,)), D((tiles // 2,)), D((tiles // 2,))]
-        + gather_scratch(G, halves, 1),
+        + gather_scratch(G, halves, 1) + scatter_scratch(G, (((0, 0, here // 2),), ((0, here // 2, here // 2),)), d // wide),
         compiler_params=params(cid), name="feed_forward")(att, tok, cot, wo, wg, wu, wd, wd_shard, gain)
 
 
@@ -1009,14 +1018,17 @@
     (attended, lse, normed, qkv), (full_up, most_down) = attn_fwd_and_gather(
         all_tokens, gain_one, w_first, bias, [w_up, down_shard[:, :cut]],
         (((0, 0, cut), (1, 0, cut - 384)), ((0, cut, ff - cut), (1, cut - 384, 384))), wide, 2)
-    grad_w_out, grad_w_gate, grad_w_up, grad_w_down, output, grad_hidden, grad_attended, grad_gain_two = middle(
-        attended, all_tokens, all_cot, full_out, full_gate, full_up, most_down, down_shard, gain_two, wide, 3)
-    (g, band, far, grad_w_first, grad_normed), (s_gate, s_down) = attn_bwd_and_scatter(
-        qkv, bias, attended, grad_attended, lse, normed, w_first, [grad_w_gate, grad_w_down], (((0, 0, ff),), ((1, 0, ff),)), wide, 4)
-    most = 2 * inner
-    small, grad_tokens, (s_up, s_out, s_first) = hist_and_scatter(
-        g, band, far, ids, grad_normed, tokens, grad_hidden, gain_one, grad_gain_two, [grad_w_up, grad_w_out, grad_w_first],
-        (((0, 0, ff), (2, most, inner // 2)), ((1, 0, inner), (2, 0, most), (2, most + inner // 2, inner // 2))), wide, 5)
+    here = 2 * inner
+    grad_w_out, grad_w_gate, grad_w_up, grad_w_down, output, grad_hidden, grad_attended, grad_gain_two, s_down = middle(
+        attended, all_tokens, all_cot, full_out, full_gate, full_up, most_down, down_shard, gain_two, here, wide, 3)
+    even = (ff + inner + ff - here) // 2
+    (g, band, far, grad_w_first, grad_normed), (s_gate, s_out, more_down) = attn_bwd_and_scatter(
+        qkv, bias, attended, grad_attended, lse, normed, w_first, [grad_w_gate, grad_w_out, grad_w_down],
+        (((0, 0, even),), ((0, even, ff - even), (1, 0, inner), (2, here, ff - here))), wide, 4)
+    s_down = jnp.concatenate([s_down, more_down[:, here:]], axis=1)
+    small, grad_tokens, (s_up, s_first) = hist_and_scatter(
+        g, band, far, ids, grad_normed, tokens, grad_hidden, gain_one, grad_gain_two, [grad_w_up, grad_w_first],
+        (((0, 0, ff),), ((1, 0, 3 * inner),)), wide, 5)
     s_query, s_key, s_value = jnp.split(s_first, 3, axis=1)
     lines = d // 128
     one, two = small[:lines].reshape(d), small[lines:2 * lines].reshape(d)

time: 351 us -> 338 us (0.963)
  Pallas kernels: 315 us -> 301 us
    pallas_call x1, Pallas kernels: 77.6 us -> 68.3 us  [hist_and_scatter(): pl.pallas_call(functools.partial(hist_kernel, heads, rows, n, G, halves,...]
    pallas_call x1, Pallas kernels: 64.7 us -> 58.1 us  [attn_bwd_and_scatter(): pl.pallas_call(functools.partial(bwd_kernel, pairs, tiles, G, halves, cou...]
  transfers between devices with their start and end apart: 2 -> 2, of which waited for: 0 -> 0; matrix products, arithmetic and copies ran while one was open for 3% -> 3% of each run, Pallas kernels for 32% -> 33%
where the time goes in v8:
time: 338 us; the launch traced here: 337 us
  Pallas kernels  301 us (89%)
  local copies, waits for them, and re-layouts  14.8 us (4%)
  between operations  14.2 us (4%)
  other arithmetic  5.22 us (2%)
    pallas_call x1, Pallas kernels, hist_and_scatter(): pl.pallas_call(functools.partial(hist_kernel, heads, rows, n, G, halves,...  68.3 us
    pallas_call x1, Pallas kernels, bias_and_gather(): pl.pallas_call(functools.partial(bias_gather_kernel, heads, rows, n, G, h...  66.5 us
    pallas_call x1, Pallas kernels, middle(): pl.pallas_call(functools.partial(mid_kernel, G, cut), out_shape=(sds((d,...  63.6 us
    pallas_call x1, Pallas kernels, attn_bwd_and_scatter(): pl.pallas_call(functools.partial(bwd_kernel, pairs, tiles, G, halves, cou...  58.1 us
    pallas_call x1, Pallas kernels, attn_fwd_and_gather(): pl.pallas_call(functools.partial(fwd_kernel, pairs, tiles, G, halves, cou...  44.9 us
  transfers between devices with their start and end apart: 2, of which 0 were waited for; matrix products, arithmetic and copies ran while one was open for 3% of the time, Pallas kernels for 33%

profile of v8, /device:TPU:0, one launch (start us, length us, event | category | flops | bytes accessed | tf_op | source)
XLA Modules:
  0.0 337.1 jit_solution(4396719136292986456)
XLA Ops:
  7.2 0.0 copy-start.9
  7.2 0.0 all-gather.3.cloned.1.call-start
  7.3 0.7 all-gather.3.cloned.1.call-update
  8.0 0.0 all-gather.5.cloned.1.call-start
  8.0 0.7 all-gather.5.cloned.1.call-update
  8.7 1.3 broadcast_in_dim.23
  10.0 1.3 broadcast_in_dim.24
  11.3 0.7 round-nearest-even_convert_fusion
  11.9 0.1 reshape.219
  12.1 0.6 pad.4.refs_1_
  12.7 1.5 slice.30.refs_5_
  14.2 1.7 copy.31.refs_4_
  15.9 1.0 copy.30
  16.9 0.5 fusion.17.refs_0_
  17.5 0.7 pad_maximum_fusion.refs_6_
  18.2 66.5 %layout_bias_gather.1 = (f32[8,1024,1024]{2,1,0:T(8,128)}, f32[2,1024,1024]{2,1,0:T(8,128)}, f32[8,64,128]{2,1,0:T(8,128)}, bf16[1024,1536]{1,0:T(8,128)(2,1)}, ...) custom-call(s32[1,128]{1,0:T(1,128)} %fusion.17.refs_0_, s32[12,128]{1,0:T(8,128)} %pad.4.refs_1_, ...), custom_call_target="tpu_custom_call" | custom-call | tf_op jit(solution)/shard_map/layout_bias_gather/pallas_call | solution.py:86
  84.7 0.0 all-gather.3.cloned.1.call-done.refs_0_.tok_h
  84.7 44.9 %attention_gather.1 = (bf16[1024,512]{1,0:T(8,128)(2,1)}, f32[4,1024,2]{2,1,0:T(8,128)}, bf16[1024,1024]{1,0:T(8,128)(2,1)}, bf16[1024,1536]{1,0:T(8,128)(2,1)},...) custom-call(bf16[1024,1024]{1,0:T(8,128)(2,1)} %all-gather.3.cloned.1.call-done.refs_0_.tok_h, f32[1,1024]{1,0:T(1,128)} %bitcast.27, ...), custom_call_target="tpu_custom_call" | custom-call | tf_op jit(solution)/shard_map/attention_gather/pallas_call | solution.py:168
  129.6 0.0 all-gather.5.cloned.1.call-done.cot_h
  129.6 63.6 %feed_forward.1 = (bf16[1024,512]{1,0:T(8,128)(2,1)}, bf16[1024,1408]{1,0:T(8,128)(2,1)}, bf16[1024,1408]{1,0:T(8,128)(2,1)}, bf16[1024,1408]{1,0:T(8,128)(2,1)}...) custom-call(bf16[1024,512]{1,0:T(8,128)(2,1)} %get-tuple-element.47., ...), custom_call_target="tpu_custom_call" | custom-call | tf_op jit(solution)/shard_map/feed_forward/pallas_call | solution.py:989
  193.2 58.1 %attention_back_scatter.1 = (bf16[8,1024,1024]{2,1,0:T(8,128)(2,1)}, f32[8,256,512]{2,1,0:T(8,128)}, f32[8,2,16,128]{3,2,1,0:T(8,128)}, bf16[1024,1536]{1,0:T(8,...) custom-call(bf16[1024,1536]{1,0:T(8,128)(2,1)} %get-tuple-element.53.refs_0, ...), custom_call_target="tpu_custom_call" | custom-call | tf_op jit(solution)/shard_map/attention_back_scatter/pallas_call | solution.py:267
  251.3 68.3 %table_grad_scatter.1 = (f32[32,128]{1,0:T(8,128)}, f32[512,1024]{1,0:T(8,128)}, f32[64,1408]{1,0:T(8,128)}, f32[64,1536]{1,0:T(8,128)}) custom-call(bf16[8,1024,1024]{2,1,0:T(8,128)(2,1)} %get-tuple-element.60.refs_0_, f32[2,1024,1024]{2,1,0:T(8,128)} %get-tuple-element.61.refs_1_, f32[8,256,512]{2,1,0:T(8,128)} %get-tuple-element.62.refs_2_, ...), custom_call_target="tpu_custom_call" | custom-call | tf_op jit(solution)/shard_map/table_grad_scatter/pallas_call | solution.py:422
  319.6 1.4 slice_bitcast_fusion
  321.1 1.3 slice_bitcast_fusion.1
  322.4 0.9 slice.27
  323.3 1.8 fusion.31
  325.0 0.8 maximum_bitcast_fusion
  325.8 1.0 copy.37
  326.8 1.3 copy.38
  328.1 0.7 copy.39
  328.8 0.7 copy.40
  329.5 0.7 copy.41
  (22 shorter events, 0.1 us)
Async XLA Ops:
  7.2 8.7 %copy-start.9 = (s32[2,1024]{1,0:T(2,128)S(1)}, s32[2,1024]{1,0:T(2,128)}, u32[]{:S(2)}) copy-start(s32[2,1024]{1,0:T(2,128)} %refs_3_.1) | copy-start | bytes 24580
  7.2 10.3 %copy-start.6 = (bf16[64,512]{1,0:T(8,128)(2,1)S(1)}, bf16[64,512]{1,0:T(8,128)(2,1)}, u32[]{:S(2)}) copy-start(bf16[64,512]{1,0:T(8,128)(2,1)} %param.23) | copy-start | bytes 196612
  7.2 10.3 %copy-start.7 = (bf16[64,512]{1,0:T(8,128)(2,1)S(1)}, bf16[64,512]{1,0:T(8,128)(2,1)}, u32[]{:S(2)}) copy-start(bf16[64,512]{1,0:T(8,128)(2,1)} %param.22) | copy-start | bytes 196612
  7.2 10.3 %copy-start.8 = (bf16[64,512]{1,0:T(8,128)(2,1)S(1)}, bf16[64,512]{1,0:T(8,128)(2,1)}, u32[]{:S(2)}) copy-start(bf16[64,512]{1,0:T(8,128)(2,1)} %param.21) | copy-start | bytes 196612
  7.2 77.5 %all-gather.3.cloned.1.call-start = ((), (), s32[]{:S(2)}) async-start(), calls=%async_computation | async-start | bytes 3145728 | tf_op jit(solution)/shard_map/all_gather | solution.py:1010
  8.0 121.6 %all-gather.5.cloned.1.call-start = ((), (), s32[]{:S(2)}) async-start(), calls=%async_computation.1 | async-start | bytes 3145728 | tf_op jit(solution)/shard_map/all_gather | solution.py:1011
  251.3 73.8 %copy-start.4 = (f32[64,1024]{1,0:T(8,128)S(1)}, f32[64,1024]{1,0:T(8,128)}, u32[]{:S(2)}) copy-start(f32[64,1024]{1,0:T(8,128)} %get-tuple-element.76) | copy-start | bytes 786436
  251.3 74.5 %copy-start.1 = (bf16[512,1024]{1,0:T(8,128)(2,1)S(1)}, bf16[512,1024]{1,0:T(8,128)(2,1)}, u32[]{:S(2)}) copy-start(bf16[512,1024]{1,0:T(8,128)(2,1)} %get-tuple-element.95) | copy-start | bytes 3145732
  319.6 7.2 %copy-start = (f32[512,1024]{1,0:T(8,128)S(1)}, f32[512,1024]{1,0:T(8,128)}, u32[]{:S(2)}) copy-start(f32[512,1024]{1,0:T(8,128)} %get-tuple-element.96) | copy-start | bytes 6291460
  325.8 2.3 copy-start.5
  325.8 3.0 copy-start.2
  326.8 2.7 copy-start.3
Sparse Core Ops, SparseCore 0:
  9.6 13.2 all-gather.2
  24.5 11.7 all-gather.4

commit v9 on v8

--- a/solution.py
+++ b/solution.py
@@ -32,22 +32,39 @@
     return lane_take(steps, jnp.minimum(jnp.abs(gap) >> shift, EDGES[-1])) + jnp.where(gap > 0, 16, 0)
 
 
-def bias_tile(start, heads, rows, n, steps_ref, tab_ref, box_col, box_row, page_col, page_row, bias_ref, ids_ref, lin_ids, lin):
-    steps = jnp.broadcast_to(steps_ref[...], (rows, 128))
-    allowed_col = jnp.broadcast_to(page_col[...] % 2, (rows, 128))
-    cols = [jnp.broadcast_to(box_col[:, t:t + 1], (rows, 128)) for t in range(2)]
+def bias_tile(start, heads, rows, n, tab_ref, box_row, page_row, bias_ref, ids_ref, lin_ids, lin, words_ref):
+    lane = lax.broadcasted_iota(jnp.int32, (rows, 128), 1)
+    down = lax.broadcasted_iota(jnp.int32, (rows, 128), 0)
+    steps = sum([(lane >= e).astype(jnp.int32) for e in EDGES])
     pairs = heads // 2
-    table = lambda t, p: jnp.broadcast_to(tab_ref[t * pairs + p:t * pairs + p + 1, :], (rows, 128))
-    unit = 1.0 / TABLE_SCALE
+
+    def column(row_ref, t):
+        values = jnp.broadcast_to(row_ref[t:t + 1, pl.ds(pl.multiple_of(start // 128 * 128, 128), 128)], (rows, 128)).astype(f32)
+        return jnp.broadcast_to(jnp.sum(jnp.where(lane == down + start % 128, values, 0.0), axis=1, keepdims=True), (rows, 128)).astype(jnp.int32)
+
+    allowed_col = column(page_row, 0) % 2
+    cols = [column(box_row, t) for t in range(2)]
 
     @pl.when(start == 0)
     def _():
+        first = lax.axis_index("narrow") * heads
+        row = lax.broadcasted_iota(jnp.int32, (heads, tab_ref.shape[0]), 0)
+        wanted = first + jnp.where(row < pairs, 2 * row, 2 * (row - pairs) + 1)
+        pick = jnp.where(lax.broadcasted_iota(jnp.int32, row.shape, 1) == wanted, 1.0, 0.0).astype(bf16)
+        picked = jnp.dot(pick, tab_ref[...], preferred_element_type=f32)
+        fixed = jnp.round(picked * TABLE_SCALE).astype(jnp.int32)
+        words_ref[...] = jnp.zeros_like(words_ref)
+        words_ref[0:pairs, 0:picked.shape[1]] = fixed[0:pairs] * 65536 + fixed[pairs:heads] + TABLE_LIFT
+
         @pl.loop(0, 8)
         def _(k):
-            ids = buckets_of(lax.broadcasted_iota(jnp.int32, (rows, 128), 1) - lax.broadcasted_iota(jnp.int32, (rows, 128), 0) + (k - 4) * rows, steps, 0)
+            ids = buckets_of(lane - down + (k - 4) * rows, steps, 0)
             lin_ids[k] = ids.astype(f32)
             for p in range(pairs):
-                lin[k, p] = lane_take(table(0, p), ids)
+                lin[k, p] = lane_take(jnp.broadcast_to(words_ref[p:p + 1, :], (rows, 128)), ids)
+
+    unit = 1.0 / TABLE_SCALE
+    tables = [jnp.broadcast_to(words_ref[p:p + 1, :], (rows, 128)) for p in range(pairs)]
 
     @pl.loop(0, n // 128)
     def _(c):
@@ -59,41 +76,36 @@
             ids_ref[t, :, lanes] = ids[t].astype(f32)
         ok = jnp.broadcast_to(page_row[:, lanes], (rows, 128)) == allowed_col
         for p in range(pairs):
-            words = lin[near, p] + lane_take(table(1, p), ids[0]) + lane_take(table(2, p), ids[1])
+            words = lin[near, p] + lane_take(tables[p], ids[0] + 32) + lane_take(tables[p], ids[1] + 64)
             upper = (words >> 16).astype(f32) * unit
             lower = (words & 0xFFFF).astype(f32) * unit - 3 * TABLE_LIFT * unit
             bias_ref[2 * p, :, lanes] = jnp.where(ok, upper, -1e30)
             bias_ref[2 * p + 1, :, lanes] = jnp.where(ok, lower, -1e30)
 
 
-def bias_gather_kernel(heads, rows, n, G, halves, count, *refs):
-    ins, srcs = refs[:6], refs[6:6 + count]
-    bias_ref, ids_ref, lin_ids = refs[6 + count:9 + count]
-    outs, lin, sems = refs[9 + count:9 + 2 * count], refs[9 + 2 * count], refs[10 + 2 * count:]
+def bias_gather_kernel(heads, rows, n, G, halves, count, into, *refs):
+    ins, srcs = refs[:3], refs[3:3 + count]
+    bias_ref, ids_ref, lin_ids = refs[3 + count:6 + count]
+    kinds = len(set(k for k, _ in into))
+    outs, scratch, sems = refs[6 + count:6 + count + kinds], refs[6 + count + kinds:8 + count + kinds], refs[8 + count + kinds:]
     now = pl.program_id(0)
-    comm = Gather(G, halves, srcs, outs, *sems)
-    beside(comm.events(), G, n // rows, now, lambda: bias_tile(now * rows, heads, rows, n, *ins, bias_ref, ids_ref, lin_ids, lin))
-
-
-def bias_and_gather(tables, boxes, pages, shards, halves, wide, cid):
-    heads, n, G, rows = tables.shape[1], pages.shape[0], wide // 4, 64
-    fixed = jnp.round(tables.astype(f32) * TABLE_SCALE).astype(jnp.int32).reshape(3, 32, heads // 2, 2)
-    words = fixed[..., 0] * 65536 + fixed[..., 1] + TABLE_LIFT
-    tab = jnp.pad(words.transpose(0, 2, 1).reshape(3 * heads // 2, 32), ((0, 0), (0, 96)))
-    lane = jnp.arange(128, dtype=jnp.int32)
-    steps = sum([(lane >= e).astype(jnp.int32) for e in EDGES])[None]
+    comm = Gather(G, halves, srcs, [(outs[k], c, 0) for k, c in into], *sems)
+    beside(comm.events(), G, n // rows, now, lambda: bias_tile(now * rows, heads, rows, n, *ins, bias_ref, ids_ref, lin_ids, *scratch))
+
+
+def bias_and_gather(tables, heads, boxes, pages, shards, into, halves, wide, cid):
+    n, G, rows = pages.shape[0], wide // 4, 64
     count = len(shards)
-    outs = pl.pallas_call(functools.partial(bias_gather_kernel, heads, rows, n, G, halves, count),
+    widths = [sum(a.shape[1] for a, (j, _) in zip(shards, into) if j == k) for k in sorted(set(k for k, _ in into))]
+    outs = pl.pallas_call(functools.partial(bias_gather_kernel, heads, rows, n, G, halves, count, into),
         grid=(n // rows,),
-        out_shape=(jax.ShapeDtypeStruct((heads, n, n), f32), jax.ShapeDtypeStruct((2, n, n), f32), jax.ShapeDtypeStruct((8, rows, 128), f32)) + gathered_shapes(shards, wide),
-        in_specs=[pl.BlockSpec((1, 128), lambda i: (0, 0)), pl.BlockSpec((3 * heads // 2, 128), lambda i: (0, 0)),
-                  pl.BlockSpec((rows, 2), lambda i: (i, 0)), pl.BlockSpec((2, n), lambda i: (0, 0)),
-                  pl.BlockSpec((rows, 1), lambda i: (i, 0)), pl.BlockSpec((1, n), lambda i: (0, 0))] + [ANY] * count,
+        out_shape=(jax.ShapeDtypeStruct((heads, n, n), f32), jax.ShapeDtypeStruct((2, n, n), f32), jax.ShapeDtypeStruct((8, rows, 128), f32)) + gathered_shapes([(shards[0].shape[0], w) for w in widths], wide),
+        in_specs=[pl.BlockSpec(tables.shape, lambda i: (0, 0)), pl.BlockSpec((2, n), lambda i: (0, 0)), pl.BlockSpec((1, n), lambda i: (0, 0))] + [ANY] * count,
         out_specs=(pl.BlockSpec((heads, rows, n), lambda i: (0, i, 0)), pl.BlockSpec((2, rows, n), lambda i: (0, i, 0)),
-                   pl.BlockSpec((8, rows, 128), lambda i: (0, 0, 0))) + (ANY,) * count,
-        scratch_shapes=[pltpu.VMEM((8, heads // 2, rows, 128), jnp.int32)] + gather_scratch(G, halves, count),
+                   pl.BlockSpec((8, rows, 128), lambda i: (0, 0, 0))) + (ANY,) * len(widths),
+        scratch_shapes=[pltpu.VMEM((8, heads // 2, rows, 128), jnp.int32), pltpu.VMEM((8, 128), jnp.int32)] + gather_scratch(G, halves, count),
         compiler_params=params(cid), name="layout_bias_gather")(
-            steps, tab, boxes.T, boxes, pages[:, None], pages[None], *shards)
+            tables, boxes, pages[None], *shards)
     return outs[0], outs[1:3], outs[3:]
 
 
@@ -108,7 +120,7 @@
 
 
 def project(tok_ref, gain_ref, w_ref, normed, qkv):
-    gain = gain_ref[...]
+    gain = gain_ref[0:1, :].astype(f32)
 
     @pl.loop(0, tok_ref.shape[0] // TILE)
     def _(t):
@@ -137,15 +149,19 @@
 def fwd_kernel(pairs, tiles, G, halves, count, *refs):
     (tok, gain, w, bias_ref), srcs = refs[:4], refs[4:4 + count]
     o_ref, lse_ref, normed_h, qkv_h = refs[4 + count:8 + count]
-    outs, (normed, qkv, keep), sems = refs[8 + count:8 + 2 * count], refs[8 + 2 * count:11 + 2 * count], refs[11 + 2 * count:]
+    outs, (tok_s, w_s, normed, qkv, keep, load), sems = refs[8 + count:8 + 2 * count], refs[8 + 2 * count:14 + 2 * count], refs[14 + 2 * count:]
     p, i = pl.program_id(0), pl.program_id(1)
     now, steps = p * tiles + i, pairs * tiles
     copies = lambda: [pltpu.make_async_copy(normed, normed_h, keep.at[0]), pltpu.make_async_copy(qkv, qkv_h, keep.at[1])]
 
+    loads = lambda: [pltpu.make_async_copy(tok, tok_s, load.at[0]), pltpu.make_async_copy(w, w_s, load.at[1])]
+
     def compute():
         @pl.when(now == 0)
         def _():
-            project(tok, gain, w, normed, qkv)
+            for c in loads():
+                c.wait()
+            project(tok_s, gain, w_s, normed, qkv)
             for c in copies():
                 c.start()
 
@@ -156,20 +172,20 @@
             for c in copies():
                 c.wait()
 
-    beside(Gather(G, halves, srcs, outs, *sems).events(), G, steps, now, compute)
-
-
-def attn_fwd_and_gather(tok, gain, w, bias, shards, halves, wide, cid, tq=256):
+    beside(Gather(G, halves, srcs, outs, *sems).events(), G, steps, now, compute, early=[lambda: [c.start() for c in loads()]])
+
+
+def attn_fwd_and_gather(tok, gain, w, bias, shards, widths, halves, wide, cid, tq=256):
     n, d = tok.shape
     width = w.shape[1] // 3
     pairs, tiles, count, G = width // 128, n // tq, len(shards), wide // 4
     sds = jax.ShapeDtypeStruct
     const = lambda s: pl.BlockSpec(s, lambda p, i: (0, 0))
     outs = pl.pallas_call(functools.partial(fwd_kernel, pairs, tiles, G, halves, count), grid=(pairs, tiles),
-        out_shape=(sds((n, width), bf16), sds((pairs, n, 2), f32), sds((n, d), bf16), sds((n, 3 * width), bf16)) + gathered_shapes(shards, wide),
-        in_specs=[const((n, d)), const((1, d)), const(w.shape), pl.BlockSpec((2, tq, n), lambda p, i: (p, i, 0))] + [ANY] * count,
+        out_shape=(sds((n, width), bf16), sds((pairs, n, 2), f32), sds((n, d), bf16), sds((n, 3 * width), bf16)) + gathered_shapes([(shards[0].shape[0], c) for c in widths], wide),
+        in_specs=[ANY, const(gain.shape), ANY, pl.BlockSpec((2, tq, n), lambda p, i: (p, i, 0))] + [ANY] * count,
         out_specs=(pl.BlockSpec((tq, 128), lambda p, i: (i, p)), pl.BlockSpec((1, tq, 2), lambda p, i: (p, i, 0)), ANY, ANY) + (ANY,) * count,
-        scratch_shapes=[pltpu.VMEM((n, d), bf16), pltpu.VMEM((n, 3 * width), bf16), D((2,))] + gather_scratch(G, halves, count),
+        scratch_shapes=[pltpu.VMEM((n, d), bf16), pltpu.VMEM(w.shape, bf16), pltpu.VMEM((n, d), bf16), pltpu.VMEM((n, 3 * width), bf16), D((2,)), D((2,))] + gather_scratch(G, halves, count),
         compiler_params=params(cid), name="attention_gather")(tok, gain, w, bias, *shards)
     return outs[:4], outs[4:]
 
@@ -246,11 +262,22 @@
 def bwd_kernel(pairs, tiles, G, halves, count, *refs):
     ins, parts = refs[:9], refs[9:9 + count]
     mid = refs[9 + count:14 + count]
-    outs, accs, sems = refs[14 + count:14 + 2 * count], refs[14 + 2 * count:18 + 2 * count], refs[18 + 2 * count:]
+    outs, accs, sems = refs[14 + count:14 + 2 * count], refs[14 + 2 * count:18 + 2 * count], refs[21 + 2 * count:]
+    normed_s, w_s, load = refs[18 + 2 * count:21 + 2 * count]
+    loads = [lambda: pltpu.make_async_copy(ins[7], normed_s, load.at[0]), lambda: pltpu.make_async_copy(ins[8], w_s, load.at[1])]
     p, i = pl.program_id(0), pl.program_id(1)
     comm = Scatter(G, halves, parts, outs, *sems)
-    beside(comm.events(), G, pairs * tiles, p * tiles + i,
-           lambda: bwd_tile(p, pairs, i, i == tiles - 1, p == pairs - 1, *ins, *mid, *accs))
+    now, steps = p * tiles + i, pairs * tiles
+
+    def compute():
+        for n, step in ((0, 0), (1, steps - 1)):
+            @pl.when(now == step)
+            def _():
+                loads[n]().wait()
+
+        bwd_tile(p, pairs, i, i == tiles - 1, p == pairs - 1, *ins[:7], normed_s, w_s, *mid, *accs)
+
+    beside(comm.events(), G, steps, now, compute, early=[lambda: [c().start() for c in loads]])
 
 
 def shard_shapes(parts, wide):
@@ -267,10 +294,11 @@
     outs = pl.pallas_call(functools.partial(bwd_kernel, pairs, tiles, G, halves, count), grid=(pairs, tiles),
         out_shape=(sds((2 * pairs, n, n), bf16), sds((2 * pairs, tq, tq + 256), f32), sds((2 * pairs, 2, 16, 128), f32)) + (sds((d, 3 * width), bf16), sds((n, d), bf16)) + shard_shapes(parts, wide),
         in_specs=[tile, full(n, 1), full(n, 2), pl.BlockSpec((2, tq, n), lambda p, i: (p, i, 0)), tile, tile,
-                  pl.BlockSpec((1, tq, 2), lambda p, i: (p, i, 0)), const((n, d)), const(w.shape)] + [ANY] * count,
+                  pl.BlockSpec((1, tq, 2), lambda p, i: (p, i, 0)), ANY, ANY] + [ANY] * count,
         out_specs=(pl.BlockSpec((2, tq, n), lambda p, i: (p, i, 0)), pl.BlockSpec((2, tq, tq + 256), lambda p, i: (p, 0, 0)),
                    pl.BlockSpec((2, 2, 16, 128), lambda p, i: (p, 0, 0, 0))) + (const(w.shape), const((n, d))) + (whole_vmem(),) * count,
-        scratch_shapes=[pltpu.VMEM((128, n), f32), pltpu.VMEM((128, n), f32), pltpu.VMEM((n, 3 * width), bf16), pltpu.VMEM((d, n), bf16)] + scatter_scratch(G, halves, parts[0].shape[0] // wide),
+        scratch_shapes=[pltpu.VMEM((128, n), f32), pltpu.VMEM((128, n), f32), pltpu.VMEM((n, 3 * width), bf16), pltpu.VMEM((d, n), bf16),
+                        pltpu.VMEM((n, d), bf16), pltpu.VMEM(w.shape, bf16), D((2,))] + scatter_scratch(G, halves, parts[0].shape[0] // wide),
         compiler_params=params(cid), name="attention_back_scatter")(
             qkv, qkv, qkv, bias, o, do, lse, normed, w, *parts)
     return outs[:5], outs[5:]
@@ -364,17 +392,19 @@
 
 
 def hist_kernel(heads, rows, n, G, halves, count, *refs):
-    (g_ref, ids_ref, band_ref, far_ref, lin_ids, dx, tok, gh, gain_ref, gain_two), parts = refs[:10], refs[10:10 + count]
+    (g_ref, ids_ref, band_ref, far_ref, lin_ids, dx_h, tok_h, gh_h, gain_ref, gain_two), parts = refs[:10], refs[10:10 + count]
     small_ref, gt_ref = refs[10 + count:12 + count]
     outs, rest = refs[12 + count:12 + 2 * count], refs[12 + 2 * count:]
-    (gs, low, table, boxes, got, pair_sem), sums, sems = rest[:6], rest[6:13], rest[13:]
+    (gs, low, table, boxes, got, dx, tok, gh, load, pair_sem), sums, sems = rest[:10], rest[10:17], rest[17:]
     acc = sums[0]
     now, steps = pl.program_id(0), n // rows
     core = lax.axis_index("narrow")
     mine = tok.shape[0]
     d = tok.shape[1]
     comm = Scatter(G, halves, parts, outs, *sems)
-    swap = lambda: remote(dx.at[pl.ds(pl.multiple_of((1 - core) * mine, mine), mine)], got, pair_sem.at[0], pair_sem.at[1], {"narrow": 1 - core})
+    loads = lambda: [pltpu.make_async_copy(dx_h.at[pl.ds(pl.multiple_of(core * mine, mine), mine)], dx, load.at[0]),
+                     pltpu.make_async_copy(tok_h, tok, load.at[1]), pltpu.make_async_copy(gh_h, gh, load.at[2])]
+    swap = lambda: remote(dx_h.at[pl.ds(pl.multiple_of((1 - core) * mine, mine), mine)], got, pair_sem.at[0], pair_sem.at[1], {"narrow": 1 - core})
 
     def compute():
         @pl.when(now == 0)
@@ -387,16 +417,18 @@
         @pl.when(now == steps // 8)
         def _():
             swap().wait()
+            for c in loads():
+                c.wait()
 
         for t in range(mine // TILE):
             @pl.when(now == steps // 8 + t)
             def _():
                 r = pl.ds(t * TILE, TILE)
                 x = tok[r, :].astype(f32)
-                total = dx[pl.ds(pl.multiple_of(core * mine + t * TILE, TILE), TILE), :].astype(f32) + got[r, :].astype(f32)
+                total = dx[r, :].astype(f32) + got[r, :].astype(f32)
                 factor = lax.rsqrt(jnp.mean(x * x, axis=1, keepdims=True) + epsilon)
                 unit = x * factor
-                scaled = gain_ref[...] * total
+                scaled = gain_ref[0:1, :].astype(f32) * total
                 gt_ref[r, :] = gh[r, :] + factor * (scaled - unit * jnp.mean(scaled * unit, axis=1, keepdims=True))
                 gain = jnp.sum(total * unit, axis=0, keepdims=True)
                 for k in range(d // 128):
@@ -407,9 +439,11 @@
     def reduce():
         acc[0, pl.ds(pl.multiple_of(2 * (d // 128) + core * heads, 8), heads), 0:32] = own_blocks(table[...], heads, 32)
         acc[0, pl.ds(pl.multiple_of(2 * (d // 128) + core * heads, 8), heads), 32:96] = own_halves(boxes[...], heads)
-        small_ref[...] = sum_everywhere(G, *sums)
-
-    beside(comm.events(1), G, steps, now, compute, (reduce,))
+
+    events, _ = comm.events(1)
+    stages = sum_everywhere(G, small_ref, *sums)
+    beside((events, lambda: None), G, steps, now, compute, [reduce] + [act for pair in zip(stages, comm.ending()) for act in pair],
+           [lambda: [c.start() for c in loads()]])
 
 
 def hist_and_scatter(g, band, far, ids, dx, tok, gh, gain, gain_two, parts, halves, wide, cid):
@@ -423,9 +457,10 @@
         out_shape=(sds((small, 128), f32), sds(tok.shape, f32)) + shard_shapes(parts, wide),
         in_specs=[pl.BlockSpec((heads, rows, n), lambda i: (0, i, 0)), pl.BlockSpec((2, rows, n), lambda i: (0, i, 0)),
                   pl.BlockSpec((heads, 16, band.shape[2]), lambda i: (0, i, 0)), pl.BlockSpec(far.shape, lambda i: (0, 0, 0, 0)),
-                  pl.BlockSpec(lin_ids.shape, lambda i: (0, 0, 0)), const(dx.shape), const(tok.shape), const(gh.shape), const(gain.shape), const(gain_two.shape)] + [ANY] * count,
+                  pl.BlockSpec(lin_ids.shape, lambda i: (0, 0, 0)), ANY, ANY, ANY, const(gain.shape), const(gain_two.shape)] + [ANY] * count,
         out_specs=(const((small, 128)), const(tok.shape)) + (whole_vmem(),) * count,
-        scratch_shapes=[pltpu.VMEM((n // 128, heads * 16, 128), f32), pltpu.VMEM((2, 16, n), f32), pltpu.VMEM((4 * heads, 128), f32), pltpu.VMEM((64, 64), f32), pltpu.VMEM(tok.shape, bf16), D((2,))]
+        scratch_shapes=[pltpu.VMEM((n // 128, heads * 16, 128), f32), pltpu.VMEM((2, 16, n), f32), pltpu.VMEM((4 * heads, 128), f32), pltpu.VMEM((64, 64), f32), pltpu.VMEM(tok.shape, bf16),
+                        pltpu.VMEM(tok.shape, bf16), pltpu.VMEM(tok.shape, bf16), pltpu.VMEM(tok.shape, f32), D((3,)), D((2,))]
         + sum_scratch(G, small) + scatter_scratch(G, halves, parts[0].shape[0] // wide),
         compiler_params=params(cid), name="table_grad_scatter")(g, box_ids, band, far, lin_ids, dx, tok, gh, gain, gain_two, *parts)
     return outs[0], outs[1], outs[2:]
@@ -711,11 +746,11 @@
         if k:
             self.three(k).start()
 
-    def finish(self):
-        self.add_two(self.G - 1)
+    def arrived(self):
         for k in range(1, self.G):
             self.three(k).wait_recv()
 
+    def write_out(self):
         def body(r):
             for h in range(2):
                 for _, a, src, dst in self.pieces(h):
@@ -726,11 +761,20 @@
                     self.outs[a][r, src] = total
 
         self.rows(self.R, body)
+
+    def all_sent(self):
         for k in range(self.G):
             for c in self.one(k) + self.two(k):
                 c.wait_send()
             if k:
                 self.three(k).wait_send()
+
+    def ending(self):
+        return [lambda: self.add_two(self.G - 1), self.arrived, self.write_out, self.all_sent, lambda: None]
+
+    def finish(self):
+        for act in self.ending():
+            act()
 
     def events(self, pair=0):
         G = self.G
@@ -749,9 +793,14 @@
             D((4 * G * most,)), D((4 * G * most,)), D((4 * G * most,)), D((2 * G,)), D((2 * G,)), D((G - 1,)), D((G - 1,))]
 
 
-def beside(plan, G, steps, now, compute, late=()):
+def beside(plan, G, steps, now, compute, late=(), early=()):
     events, finish = plan
     units = 1.55 * G
+    if early:
+        @pl.when(now == 0)
+        def _():
+            for act in early:
+                act()
     for n in range(steps):
         here = [act for t, act in events if min(steps - 1, int(-(-t * steps // units))) == n]
         if here:
@@ -776,31 +825,41 @@
 
 
 def gathered_shapes(shards, wide):
-    return tuple(jax.ShapeDtypeStruct((wide * s.shape[0], s.shape[1]), s.dtype) for s in shards)
-
-
-def sum_everywhere(G, acc, got, gz, s, v, sz, vz):
+    return tuple(jax.ShapeDtypeStruct((wide * rows, columns), bf16) for rows, columns in shards)
+
+
+def sum_everywhere(G, out, acc, got, gz, s, v, sz, vz):
     z, y, x = place()
-    core = {"narrow": 1 - lax.axis_index("narrow")}
-    for n, t in enumerate((core, wide_id(z, y, 1 - x), wide_id(z, 1 - y, x))):
-        c = remote(acc.at[n], got.at[n], s.at[n], v.at[n], t)
-        c.start()
-        c.wait()
+    targets = [{"narrow": 1 - lax.axis_index("narrow")}, wide_id(z, y, 1 - x), wide_id(z, 1 - y, x)]
+    near = lambda n: remote(acc.at[n], got.at[n], s.at[n], v.at[n], targets[n])
+    far = lambda k, zz: remote(acc.at[3], gz.at[zz], sz.at[k - 1], vz.at[zz], wide_id((z + k) % G, y, x))
+
+    def take(n):
+        near(n).wait()
         acc[n + 1] = acc[n] + got[n]
-    gz[z] = acc[3]
-    far = [wide_id((z + k) % G, y, x) for k in range(1, G)]
-    sent = [remote(acc.at[3], gz.at[z], sz.at[k], vz.at[z], t) for k, t in enumerate(far)]
-    for c in sent:
-        c.start()
-    for k in range(1, G):
-        zz = (z + k) % G
-        remote(acc.at[3], gz.at[zz], sz.at[k - 1], vz.at[zz], far[k - 1]).wait_recv()
-    for c in sent:
-        c.wait_send()
-    total = gz[0]
-    for k in range(1, G):
-        total = total + gz[k]
-    return total
+
+    def next_near(n):
+        if n:
+            take(n - 1)
+        near(n).start()
+
+    def spread_far():
+        take(2)
+        gz[z] = acc[3]
+        for k in range(1, G):
+            far(k, z).start()
+
+    def total():
+        for k in range(1, G):
+            far(k, (z + k) % G).wait_recv()
+        for k in range(1, G):
+            far(k, z).wait_send()
+        value = gz[0]
+        for k in range(1, G):
+            value = value + gz[k]
+        out[...] = value
+
+    return [functools.partial(next_near, n) for n in range(3)] + [spread_far, total]
 
 
 def sum_scratch(G, rows):
@@ -848,7 +907,7 @@
     send_part = lambda t: remote(part.at[rows_of(t)], other.at[rows_of(t)], sp.at[t], vp.at[t], peer)
     send_back = lambda t: remote(part.at[rows_of(t)], back.at[rows_of(t)], sb.at[t], vb.at[t], peer)
     send_y = lambda j: remote(ysend.at[rows_of(j)], yother.at[rows_of(j)], sy.at[j], vy.at[j], peer)
-    gain = gain_ref[...]
+    gain = gain_ref[1:2, :].astype(f32)
 
     for c in loads[:2]:
         c.wait()
@@ -1000,34 +1059,31 @@
 
 def local(tokens, cotangent, pages, boxes, gain_attn, gain_ffn, bias_tables, w_query, w_key, w_value, w_out, w_gate, w_up, w_down):
     wide, narrow = lax.axis_size("wide"), lax.axis_size("narrow")
-    heads_all = bias_tables.shape[1]
-    heads = heads_all // narrow
-    core = lax.axis_index("narrow")
-    tables = lax.dynamic_slice_in_dim(bias_tables, core * heads, heads, 1)
+    heads = bias_tables.shape[1] // narrow
     inner, ff, d = w_query.shape[1], w_gate.shape[1], tokens.shape[1]
-    gain_one, gain_two = gain_attn.astype(f32)[None], gain_ffn.astype(f32)[None]
+    gains = jnp.stack([gain_attn, gain_ffn])
 
     all_tokens = lax.all_gather(tokens, "narrow", axis=0, tiled=True)
     all_cot = lax.all_gather(cotangent, "narrow", axis=0, tiled=True)
     early = inner // 4 * 3
     bias, ids, (w_first, full_out, full_gate) = bias_and_gather(
-        tables, boxes, pages, [jnp.concatenate([w_query, w_key, w_value], axis=1), w_out.T, w_gate],
-        (((2, 0, ff), (0, 0, early)), ((1, 0, inner), (0, early, 3 * inner - early))), wide, 1)
+        bias_tables.T, heads, boxes, pages, [w_query, w_key, w_value, w_out.T, w_gate], ((0, 0), (0, inner), (0, 2 * inner), (1, 0), (2, 0)),
+        (((4, 0, ff), (0, 0, early)), ((3, 0, inner), (0, early, inner - early), (1, 0, inner), (2, 0, inner))), wide, 1)
     down_shard = w_down.T
     cut = (ff // 128 + 1) // 2 * 128
     (attended, lse, normed, qkv), (full_up, most_down) = attn_fwd_and_gather(
-        all_tokens, gain_one, w_first, bias, [w_up, down_shard[:, :cut]],
+        all_tokens, gains, w_first, bias, [w_up, down_shard], (ff, cut),
         (((0, 0, cut), (1, 0, cut - 384)), ((0, cut, ff - cut), (1, cut - 384, 384))), wide, 2)
     here = 2 * inner
     grad_w_out, grad_w_gate, grad_w_up, grad_w_down, output, grad_hidden, grad_attended, grad_gain_two, s_down = middle(
-        attended, all_tokens, all_cot, full_out, full_gate, full_up, most_down, down_shard, gain_two, here, wide, 3)
+        attended, all_tokens, all_cot, full_out, full_gate, full_up, most_down, down_shard, gains, here, wide, 3)
     even = (ff + inner + ff - here) // 2
     (g, band, far, grad_w_first, grad_normed), (s_gate, s_out, more_down) = attn_bwd_and_scatter(
         qkv, bias, attended, grad_attended, lse, normed, w_first, [grad_w_gate, grad_w_out, grad_w_down],
         (((0, 0, even),), ((0, even, ff - even), (1, 0, inner), (2, here, ff - here))), wide, 4)
     s_down = jnp.concatenate([s_down, more_down[:, here:]], axis=1)
     small, grad_tokens, (s_up, s_first) = hist_and_scatter(
-        g, band, far, ids, grad_normed, tokens, grad_hidden, gain_one, grad_gain_two, [grad_w_up, grad_w_first],
+        g, band, far, ids, grad_normed, tokens, grad_hidden, gains, grad_gain_two, [grad_w_up, grad_w_first],
         (((0, 0, ff),), ((1, 0, 3 * inner),)), wide, 5)
     s_query, s_key, s_value = jnp.split(s_first, 3, axis=1)
     lines = d // 128

time: 338 us -> 330 us (0.976)
  other arithmetic: 5.22 us -> 1.37 us
  local copies, waits for them, and re-layouts: 14.8 us -> 11.2 us
  transfers between devices with their start and end apart: 2 -> 2, of which waited for: 0 -> 0; matrix products, arithmetic and copies ran while one was open for 3% -> 1% of each run, Pallas kernels for 33% -> 34%
where the time goes in v9:
time: 330 us; the launch traced here: 329 us
  Pallas kernels  301 us (91%)
  between operations  14.1 us (4%)
  local copies, waits for them, and re-layouts  11.2 us (3%)
    pallas_call x1, Pallas kernels, hist_and_scatter(): pl.pallas_call(functools.partial(hist_kernel, heads, rows, n, G, halves,...  67.8 us
    pallas_call x1, Pallas kernels, bias_and_gather(): pl.pallas_call(functools.partial(bias_gather_kernel, heads, rows, n, G, h...  67.6 us
    pallas_call x1, Pallas kernels, middle(): pl.pallas_call(functools.partial(mid_kernel, G, cut), out_shape=(sds((d,...  64.4 us
    pallas_call x1, Pallas kernels, attn_bwd_and_scatter(): pl.pallas_call(functools.partial(bwd_kernel, pairs, tiles, G, halves, cou...  56.2 us
    pallas_call x1, Pallas kernels, attn_fwd_and_gather(): pl.pallas_call(functools.partial(fwd_kernel, pairs, tiles, G, halves, cou...  44.6 us
  transfers between devices with their start and end apart: 2, of which 0 were waited for; matrix products, arithmetic and copies ran while one was open for 1% of the time, Pallas kernels for 34%

profile of v9, /device:TPU:0, one launch (start us, length us, event | category | flops | bytes accessed | tf_op | source)
XLA Modules:
  0.0 328.8 jit_solution(18247044297215774369)
XLA Ops:
  7.2 0.0 all-gather.3.cloned.1.call-start
  7.2 0.7 all-gather.3.cloned.1.call-update
  7.9 0.0 all-gather.5.cloned.1.call-start
  8.0 0.7 all-gather.5.cloned.1.call-update
  8.7 0.7 stack.9
  9.3 0.7 stack.10
  10.0 67.6 %layout_bias_gather.1 = (f32[8,1024,1024]{2,1,0:T(8,128)}, f32[2,1024,1024]{2,1,0:T(8,128)}, f32[8,64,128]{2,1,0:T(8,128)}, bf16[1024,1536]{1,0:T(8,128)(2,1)}, ...) custom-call(bf16[16,96]{1,0:T(8,128)(2,1)} %bitcast.17, s32[2,1024]{1,0:T(2,128)} %refs_1_.1, s32[1,1024]{1,0:T(1,128)} %bitcast.18, ...), custom_call_target="tpu_custom_call" | custom-call | tf_op jit(solution)/shard_map/layout_bias_gather/pallas_call | solution.py:100
  77.6 0.6 pad_maximum_fusion.refs_1_.gain_ref.refs_8_
  78.2 44.6 %attention_gather.1 = (bf16[1024,512]{1,0:T(8,128)(2,1)}, f32[4,1024,2]{2,1,0:T(8,128)}, bf16[1024,1024]{1,0:T(8,128)(2,1)}, bf16[1024,1536]{1,0:T(8,128)(2,1)},...) custom-call(bf16[1024,1024]{1,0:T(8,128)(2,1)} %all-gather.3.cloned.1.call-done.refs_0_.tok_h, ...), custom_call_target="tpu_custom_call" | custom-call | tf_op jit(solution)/shard_map/attention_gather/pallas_call | solution.py:184
  122.8 0.0 all-gather.5.cloned.1.call-done.cot_h
  122.8 64.4 %feed_forward.1 = (bf16[1024,512]{1,0:T(8,128)(2,1)}, bf16[1024,1408]{1,0:T(8,128)(2,1)}, bf16[1024,1408]{1,0:T(8,128)(2,1)}, bf16[1024,1408]{1,0:T(8,128)(2,1)}...) custom-call(bf16[1024,512]{1,0:T(8,128)(2,1)} %get-tuple-element.47., ...), custom_call_target="tpu_custom_call" | custom-call | tf_op jit(solution)/shard_map/feed_forward/pallas_call | solution.py:1048
  187.2 56.2 %attention_back_scatter.1 = (bf16[8,1024,1024]{2,1,0:T(8,128)(2,1)}, f32[8,256,512]{2,1,0:T(8,128)}, f32[8,2,16,128]{3,2,1,0:T(8,128)}, bf16[1024,1536]{1,0:T(8,...) custom-call(bf16[1024,1536]{1,0:T(8,128)(2,1)} %get-tuple-element.53.refs_0, ...), custom_call_target="tpu_custom_call" | custom-call | tf_op jit(solution)/shard_map/attention_back_scatter/pallas_call | solution.py:294
  243.5 0.0 copy-start.4
  243.5 0.0 copy-start.1
  243.5 67.8 %table_grad_scatter.1 = (f32[32,128]{1,0:T(8,128)}, f32[512,1024]{1,0:T(8,128)}, f32[64,1408]{1,0:T(8,128)}, f32[64,1536]{1,0:T(8,128)}) custom-call(bf16[8,1024,1024]{2,1,0:T(8,128)(2,1)} %get-tuple-element.60.refs_0_, f32[2,1024,1024]{2,1,0:T(8,128)} %get-tuple-element.61.refs_1_, f32[8,256,512]{2,1,0:T(8,128)} %get-tuple-element.62.refs_2_, ...), custom_call_target="tpu_custom_call" | custom-call | tf_op jit(solution)/shard_map/table_grad_scatter/pallas_call | solution.py:456
  311.3 0.0 copy-start
  311.3 1.4 slice_bitcast_fusion
  312.8 1.3 slice_bitcast_fusion.1
  314.1 0.9 slice.15
  315.0 1.8 fusion
  316.7 0.0 copy-done.4
  316.7 0.8 maximum_bitcast_fusion
  317.5 0.0 copy-done.1
  317.5 1.0 copy.31
  318.5 0.0 copy-done
  318.5 1.3 copy.32
  319.8 0.0 copy-done.5
  319.8 0.7 copy.33
  320.5 0.0 copy-done.2
  320.5 0.7 copy.34
  321.2 0.0 copy-done.3
  321.2 0.7 copy.35
  (4 shorter events, 0.0 us)
Async XLA Ops:
  7.2 71.0 %all-gather.3.cloned.1.call-start = ((), (), s32[]{:S(2)}) async-start(), calls=%async_computation | async-start | bytes 3145728 | tf_op jit(solution)/shard_map/all_gather | solution.py:1066
  7.9 114.9 %all-gather.5.cloned.1.call-start = ((), (), s32[]{:S(2)}) async-start(), calls=%async_computation.1 | async-start | bytes 3145728 | tf_op jit(solution)/shard_map/all_gather | solution.py:1067
  243.5 73.3 %copy-start.4 = (f32[64,1024]{1,0:T(8,128)S(1)}, f32[64,1024]{1,0:T(8,128)}, u32[]{:S(2)}) copy-start(f32[64,1024]{1,0:T(8,128)} %get-tuple-element.76) | copy-start | bytes 786436
  243.5 74.0 %copy-start.1 = (bf16[512,1024]{1,0:T(8,128)(2,1)S(1)}, bf16[512,1024]{1,0:T(8,128)(2,1)}, u32[]{:S(2)}) copy-start(bf16[512,1024]{1,0:T(8,128)(2,1)} %get-tuple-element.95) | copy-start | bytes 3145732
  311.3 7.2 %copy-start = (f32[512,1024]{1,0:T(8,128)S(1)}, f32[512,1024]{1,0:T(8,128)}, u32[]{:S(2)}) copy-start(f32[512,1024]{1,0:T(8,128)} %get-tuple-element.96) | copy-start | bytes 6291460
  317.5 2.3 copy-start.5
  317.5 3.0 copy-start.2
  318.5 2.7 copy-start.3
Sparse Core Ops, SparseCore 0:
  9.6 13.2 all-gather.2
  24.4 11.7 all-gather.4

commit v10 on v9

--- a/solution.py
+++ b/solution.py
@@ -28,14 +28,14 @@
     return jnp.take_along_axis(table, idx, axis=1, mode="promise_in_bounds")
 
 
-def buckets_of(gap, steps, shift):
-    return lane_take(steps, jnp.minimum(jnp.abs(gap) >> shift, EDGES[-1])) + jnp.where(gap > 0, 16, 0)
+def buckets_of(gap, shift):
+    size = jnp.minimum(jnp.abs(gap) >> shift, EDGES[-1])
+    return jnp.where(size < 8, size, 33 - lax.clz(size * size)) + jnp.where(gap > 0, 16, 0)
 
 
 def bias_tile(start, heads, rows, n, tab_ref, box_row, page_row, bias_ref, ids_ref, lin_ids, lin, words_ref):
     lane = lax.broadcasted_iota(jnp.int32, (rows, 128), 1)
     down = lax.broadcasted_iota(jnp.int32, (rows, 128), 0)
-    steps = sum([(lane >= e).astype(jnp.int32) for e in EDGES])
     pairs = heads // 2
 
     def column(row_ref, t):
@@ -58,7 +58,7 @@
 
         @pl.loop(0, 8)
         def _(k):
-            ids = buckets_of(lane - down + (k - 4) * rows, steps, 0)
+            ids = buckets_of(lane - down + (k - 4) * rows, 0)
             lin_ids[k] = ids.astype(f32)
             for p in range(pairs):
                 lin[k, p] = lane_take(jnp.broadcast_to(words_ref[p:p + 1, :], (rows, 128)), ids)
@@ -72,7 +72,7 @@
         near = jnp.clip((c * 128 - start) // rows + 4, 0, 7)
         ids = []
         for t in range(2):
-            ids.append(buckets_of(jnp.broadcast_to(box_row[t:t + 1, lanes], (rows, 128)) - cols[t], steps, 2))
+            ids.append(buckets_of(jnp.broadcast_to(box_row[t:t + 1, lanes], (rows, 128)) - cols[t], 2))
             ids_ref[t, :, lanes] = ids[t].astype(f32)
         ok = jnp.broadcast_to(page_row[:, lanes], (rows, 128)) == allowed_col
         for p in range(pairs):
@@ -119,7 +119,7 @@
     return jnp.where(lane < 64, a, b)
 
 
-def project(tok_ref, gain_ref, w_ref, normed, qkv):
+def project(tok_ref, gain_ref, w_ref, normed, qkv, between):
     gain = gain_ref[0:1, :].astype(f32)
 
     @pl.loop(0, tok_ref.shape[0] // TILE)
@@ -129,6 +129,8 @@
         low = (x * lax.rsqrt(jnp.mean(x * x, axis=1, keepdims=True) + epsilon) * gain).astype(bf16)
         normed[r, :] = low
         qkv[r, :] = jnp.dot(low, w_ref[...], preferred_element_type=f32).astype(bf16)
+        for k, act in between:
+            pl.when(t == k)(act)
 
 
 def fwd_tile(p, i, tq, pairs, qkv, bias_ref, o_ref, lse_ref):
@@ -154,6 +156,7 @@
     now, steps = p * tiles + i, pairs * tiles
     copies = lambda: [pltpu.make_async_copy(normed, normed_h, keep.at[0]), pltpu.make_async_copy(qkv, qkv_h, keep.at[1])]
 
+    events, finish = Gather(G, halves, srcs, outs, *sems).events()
     loads = lambda: [pltpu.make_async_copy(tok, tok_s, load.at[0]), pltpu.make_async_copy(w, w_s, load.at[1])]
 
     def compute():
@@ -161,7 +164,7 @@
         def _():
             for c in loads():
                 c.wait()
-            project(tok_s, gain, w_s, normed, qkv)
+            project(tok_s, gain, w_s, normed, qkv, [(1, events[1][1]), (3, events[2][1])])
             for c in copies():
                 c.start()
 
@@ -172,7 +175,7 @@
             for c in copies():
                 c.wait()
 
-    beside(Gather(G, halves, srcs, outs, *sems).events(), G, steps, now, compute, early=[lambda: [c.start() for c in loads()]])
+    beside((events[:1] + events[3:], finish), G, steps, now, compute, early=[lambda: [c.start() for c in loads()]], pace=0.36, lead=1.7)
 
 
 def attn_fwd_and_gather(tok, gain, w, bias, shards, widths, halves, wide, cid, tq=256):
@@ -443,7 +446,7 @@
     events, _ = comm.events(1)
     stages = sum_everywhere(G, small_ref, *sums)
     beside((events, lambda: None), G, steps, now, compute, [reduce] + [act for pair in zip(stages, comm.ending()) for act in pair],
-           [lambda: [c.start() for c in loads()]])
+           [lambda: [c.start() for c in loads()]], pace=0.3875)
 
 
 def hist_and_scatter(g, band, far, ids, dx, tok, gh, gain, gain_two, parts, halves, wide, cid):
@@ -467,6 +470,7 @@
 
 
 D = pltpu.SemaphoreType.DMA
+AHEAD = 2
 
 
 def place():
@@ -706,7 +710,7 @@
             c.start()
 
     def begin(self):
-        for k in self.order[:2]:
+        for k in self.order[:AHEAD]:
             self.launch(k)
 
     def rows(self, count, body):
@@ -730,8 +734,8 @@
             self.rows(self.R, body)
         for c in self.two(k):
             c.start()
-        if n + 2 < self.G:
-            self.launch(self.order[n + 2])
+        if n + AHEAD < self.G:
+            self.launch(self.order[n + AHEAD])
 
     def add_two(self, n):
         k = self.order[n]
@@ -793,16 +797,15 @@
             D((4 * G * most,)), D((4 * G * most,)), D((4 * G * most,)), D((2 * G,)), D((2 * G,)), D((G - 1,)), D((G - 1,))]
 
 
-def beside(plan, G, steps, now, compute, late=(), early=()):
+def beside(plan, G, steps, now, compute, late=(), early=(), pace=0.3875, lead=0.0):
     events, finish = plan
-    units = 1.55 * G
     if early:
         @pl.when(now == 0)
         def _():
             for act in early:
                 act()
     for n in range(steps):
-        here = [act for t, act in events if min(steps - 1, int(-(-t * steps // units))) == n]
+        here = [act for t, act in events if min(steps - 1, max(0, int(-((lead - t) // pace)))) == n]
         if here:
             @pl.when(now == n)
             def _():
@@ -885,7 +888,7 @@
 
 def mid_kernel(G, cut, att_h, tok_h, cot_h, wo_h, wg_h, wu_h, wd_h, wd_shard, gain_ref,
                gout_h, gg_h, gu_h, gd_h, y_ref, gh_ref, ga_ref, ggain_ref, sd_ref,
-               att, tok, cot, wo, wg, wu, wd, part, other, back, hid, n2t, cott, hff, gg, gu, ysend, yown, yother, stage,
+               att, tok, cot, wo, wg, wu, wd, part, other, back, hid, n2t, cott, hff, gg, gu, yother, stage,
                isem, osem, sp, vp, sb, vb, sy, vy, *sems):
     core = lax.axis_index("narrow")
     peer = {"narrow": 1 - core}
@@ -904,9 +907,10 @@
     greet(G, True, 1)
     bring.begin()
     rows_of = lambda t: pl.ds(pl.multiple_of(t * TILE, TILE), TILE)
+    kept = lambda j: rows_of(j + half)
     send_part = lambda t: remote(part.at[rows_of(t)], other.at[rows_of(t)], sp.at[t], vp.at[t], peer)
     send_back = lambda t: remote(part.at[rows_of(t)], back.at[rows_of(t)], sb.at[t], vb.at[t], peer)
-    send_y = lambda j: remote(ysend.at[rows_of(j)], yother.at[rows_of(j)], sy.at[j], vy.at[j], peer)
+    send_y = lambda j: remote(tok.at[rows_of(j)], yother.at[rows_of(j)], sy.at[j], vy.at[j], peer)
     gain = gain_ref[1:2, :].astype(f32)
 
     for c in loads[:2]:
@@ -926,7 +930,6 @@
     def _(t):
         part[rows_of(t), :] = nt(att[rows_of(t), :], wo[...]).astype(bf16)
         send_part(t).start()
-        at_step(t, {1: turns[:1], 2: steps[:1]})
 
     for c in loads[2:]:
         c.wait()
@@ -957,7 +960,7 @@
             hff[r, cols] = (act * up).astype(bf16)
             gg[r, cols] = (up * slope).astype(bf16)
             gu[r, cols] = act.astype(bf16)
-        at_step(s, {1: later[:2], 2: later[2:4], 3: later[4:]})
+        at_step(s, {0: turns[:1] + steps[:1], 1: later[:2], 2: later[2:4], 3: later[4:]})
 
     def weight_grad(left, right, out, slot, width):
         rows = stage.shape[1]
@@ -994,14 +997,14 @@
 
         @pl.when(s < half)
         def _():
-            ysend[rows_of(s), :] = y
+            tok[rows_of(s), :] = y
             send_y(s).start()
 
         @pl.when(s >= half)
         def _():
-            yown[rows_of(s - half), :] = y
-
-        at_step(s, {0: ones[:1], 1: ones[1:2], 2: twos[:1] + ones[2:3], 3: twos[1:2]})
+            tok[rows_of(s), :] = y
+
+        at_step(s, {1: ones[:1], 2: ones[1:2], 3: twos[:1]})
 
     ggain_ref[...] = jnp.zeros_like(ggain_ref)
 
@@ -1026,13 +1029,14 @@
             gh_ref[j, :] = gh
             ggain_ref[...] += jnp.sum(total * unit, axis=0, keepdims=True)
             send_y(s - half).wait()
-            y_ref[j, :] = (h + (yown[j, :].astype(f32) + yother[j, :].astype(f32))).astype(bf16)
-
-        at_step(s, {0: ones[3:4], 3: twos[2:3]})
-
-    for act in [act for pair in zip(ones[4:], twos[3:]) for act in pair]:
-        act()
+            y_ref[j, :] = (h + (tok[kept(s - half), :].astype(f32) + yother[j, :].astype(f32))).astype(bf16)
+
+        at_step(s, {0: ones[2:3], 1: twos[1:2], 3: ones[3:4]})
+
     for left, right, out, slot in ((n2t, gg, gg_h, 1), (n2t, gu, gu_h, 2), (cott, att, gout_h, 3)):
+        if slot == 2:
+            for act in twos[2:3] + [act for pair in zip(ones[4:], twos[3:]) for act in pair]:
+                act()
         for c in weight_grad(left, right, out, slot, right.shape[1]):
             c.wait()
     give.finish()
@@ -1051,7 +1055,7 @@
         in_specs=[ANY] * 8 + [whole_vmem()], out_specs=(ANY,) * 4 + (whole_vmem(),) * 5,
         scratch_shapes=[B(n, units), B(n, d), B(n, d), B(d, units), B(d, ff), B(d, ff), B(d, ff), B(n, d), B(n, d), B(n, d),
                         pltpu.VMEM((n, d), f32), B(d, n), B(d, n), B(n, ff), B(n, ff), B(n, ff),
-                        B(n // 2, d), B(n // 2, d), B(n // 2, d), B(2, 512, ff),
+                        B(n // 2, d), B(2, 512, ff),
                         D((7,)), D((8,)), D((tiles,)), D((tiles,)), D((tiles,)), D((tiles,)), D((tiles // 2,)), D((tiles // 2,))]
         + gather_scratch(G, halves, 1) + scatter_scratch(G, (((0, 0, here // 2),), ((0, here // 2, here // 2),)), d // wide),
         compiler_params=params(cid), name="feed_forward")(att, tok, cot, wo, wg, wu, wd, wd_shard, gain)
@@ -1074,17 +1078,18 @@
     (attended, lse, normed, qkv), (full_up, most_down) = attn_fwd_and_gather(
         all_tokens, gains, w_first, bias, [w_up, down_shard], (ff, cut),
         (((0, 0, cut), (1, 0, cut - 384)), ((0, cut, ff - cut), (1, cut - 384, 384))), wide, 2)
-    here = 2 * inner
+    here, upto = ff // 256 * 256, ff // 256 * 256 - 128
     grad_w_out, grad_w_gate, grad_w_up, grad_w_down, output, grad_hidden, grad_attended, grad_gain_two, s_down = middle(
         attended, all_tokens, all_cot, full_out, full_gate, full_up, most_down, down_shard, gains, here, wide, 3)
-    even = (ff + inner + ff - here) // 2
-    (g, band, far, grad_w_first, grad_normed), (s_gate, s_out, more_down) = attn_bwd_and_scatter(
-        qkv, bias, attended, grad_attended, lse, normed, w_first, [grad_w_gate, grad_w_out, grad_w_down],
-        (((0, 0, even),), ((0, even, ff - even), (1, 0, inner), (2, here, ff - here))), wide, 4)
+    even = (ff + inner + ff - here + ff - upto) // 2
+    (g, band, far, grad_w_first, grad_normed), (s_gate, s_out, more_down, more_up) = attn_bwd_and_scatter(
+        qkv, bias, attended, grad_attended, lse, normed, w_first, [grad_w_gate, grad_w_out, grad_w_down, grad_w_up],
+        (((0, 0, even),), ((0, even, ff - even), (1, 0, inner), (2, here, ff - here), (3, upto, ff - upto))), wide, 4)
     s_down = jnp.concatenate([s_down, more_down[:, here:]], axis=1)
     small, grad_tokens, (s_up, s_first) = hist_and_scatter(
         g, band, far, ids, grad_normed, tokens, grad_hidden, gains, grad_gain_two, [grad_w_up, grad_w_first],
-        (((0, 0, ff),), ((1, 0, 3 * inner),)), wide, 5)
+        (((0, 0, upto), (1, 0, 128)), ((1, 128, 3 * inner - 128),)), wide, 5)
+    s_up = jnp.concatenate([s_up[:, :upto], more_up[:, upto:]], axis=1)
     s_query, s_key, s_value = jnp.split(s_first, 3, axis=1)
     lines = d // 128
     one, two = small[:lines].reshape(d), small[lines:2 * lines].reshape(d)

time: 330 us -> 328 us (level)
  no operation moved by 1% of the time
where the time goes in v10:
time: 328 us; the launch traced here: 327 us
  Pallas kernels  298 us (91%)
  between operations  14.1 us (4%)
  local copies, waits for them, and re-layouts  12.2 us (4%)
    pallas_call x1, Pallas kernels, bias_and_gather(): pl.pallas_call(functools.partial(bias_gather_kernel, heads, rows, n, G, h...  67.5 us
    pallas_call x1, Pallas kernels, hist_and_scatter(): pl.pallas_call(functools.partial(hist_kernel, heads, rows, n, G, halves,...  65.1 us
    pallas_call x1, Pallas kernels, middle(): pl.pallas_call(functools.partial(mid_kernel, G, cut), out_shape=(sds((d,...  63.9 us
    pallas_call x1, Pallas kernels, attn_bwd_and_scatter(): pl.pallas_call(functools.partial(bwd_kernel, pairs, tiles, G, halves, cou...  56.7 us
    pallas_call x1, Pallas kernels, attn_fwd_and_gather(): pl.pallas_call(functools.partial(fwd_kernel, pairs, tiles, G, halves, cou...  44.3 us
  transfers between devices with their start and end apart: 2, of which 0 were waited for; matrix products, arithmetic and copies ran while one was open for 1% of the time, Pallas kernels for 34%

profile of v10, /device:TPU:0, one launch (start us, length us, event | category | flops | bytes accessed | tf_op | source)
XLA Modules:
  0.0 326.8 jit_solution(11986218794870811228)
XLA Ops:
  7.2 0.0 all-gather.3.cloned.1.call-start
  7.2 0.7 all-gather.3.cloned.1.call-update
  7.9 0.0 all-gather.5.cloned.1.call-start
  8.0 0.7 all-gather.5.cloned.1.call-update
  8.7 0.7 stack.9
  9.3 0.7 stack.10
  10.0 67.5 %layout_bias_gather.1 = (f32[8,1024,1024]{2,1,0:T(8,128)}, f32[2,1024,1024]{2,1,0:T(8,128)}, f32[8,64,128]{2,1,0:T(8,128)}, bf16[1024,1536]{1,0:T(8,128)(2,1)}, ...) custom-call(bf16[16,96]{1,0:T(8,128)(2,1)} %bitcast.17, s32[2,1024]{1,0:T(2,128)} %refs_1_.1, s32[1,1024]{1,0:T(1,128)} %bitcast.18, ...), custom_call_target="tpu_custom_call" | custom-call | tf_op jit(solution)/shard_map/layout_bias_gather/pallas_call | solution.py:100
  77.6 0.6 pad_maximum_fusion.1.refs_1_.gain_ref.refs_8_
  78.2 44.3 %attention_gather.1 = (bf16[1024,512]{1,0:T(8,128)(2,1)}, f32[4,1024,2]{2,1,0:T(8,128)}, bf16[1024,1024]{1,0:T(8,128)(2,1)}, bf16[1024,1536]{1,0:T(8,128)(2,1)},...) custom-call(bf16[1024,1024]{1,0:T(8,128)(2,1)} %all-gather.3.cloned.1.call-done.refs_0_.tok_h, ...), custom_call_target="tpu_custom_call" | custom-call | tf_op jit(solution)/shard_map/attention_gather/pallas_call | solution.py:187
  122.4 0.0 all-gather.5.cloned.1.call-done.cot_h
  122.5 63.9 %feed_forward.1 = (bf16[1024,512]{1,0:T(8,128)(2,1)}, bf16[1024,1408]{1,0:T(8,128)(2,1)}, bf16[1024,1408]{1,0:T(8,128)(2,1)}, bf16[1024,1408]{1,0:T(8,128)(2,1)}...) custom-call(bf16[1024,512]{1,0:T(8,128)(2,1)} %get-tuple-element.48., ...), custom_call_target="tpu_custom_call" | custom-call | tf_op jit(solution)/shard_map/feed_forward/pallas_call | solution.py:1052
  186.4 56.7 %attention_back_scatter.1 = (bf16[8,1024,1024]{2,1,0:T(8,128)(2,1)}, f32[8,256,512]{2,1,0:T(8,128)}, f32[8,2,16,128]{3,2,1,0:T(8,128)}, bf16[1024,1536]{1,0:T(8,...) custom-call(bf16[1024,1536]{1,0:T(8,128)(2,1)} %get-tuple-element.54, ...), custom_call_target="tpu_custom_call" | custom-call | tf_op jit(solution)/shard_map/attention_back_scatter/pallas_call | solution.py:297
  243.1 0.0 copy-start.3
  243.1 0.0 copy-start.1
  243.1 65.1 %table_grad_scatter.1 = (f32[32,128]{1,0:T(8,128)}, f32[512,1024]{1,0:T(8,128)}, f32[64,1408]{1,0:T(8,128)}, f32[64,1536]{1,0:T(8,128)}) custom-call(bf16[8,1024,1024]{2,1,0:T(8,128)(2,1)} %get-tuple-element.62.refs_0_, f32[2,1024,1024]{2,1,0:T(8,128)} %get-tuple-element.63.refs_1_, f32[8,256,512]{2,1,0:T(8,128)} %get-tuple-element.64.refs_2_, ...), custom_call_target="tpu_custom_call" | custom-call | tf_op jit(solution)/shard_map/table_grad_scatter/pallas_call | solution.py:459
  308.3 0.0 copy-start
  308.3 1.4 slice_bitcast_fusion
  309.7 1.3 slice_bitcast_fusion.1
  311.0 0.8 slice.23
  311.8 0.8 slice.22
  312.6 1.0 slice.21
  313.6 1.8 fusion
  315.4 0.0 copy-done.3
  315.4 0.9 pad_maximum_fusion
  316.3 0.0 copy-done.1
  316.3 1.0 copy.30
  317.3 0.0 copy-done
  317.3 1.3 copy.31
  318.6 0.0 copy-done.4
  318.6 0.7 copy.32
  319.2 0.0 copy-done.2
  319.2 0.7 copy.33
  (3 shorter events, 0.0 us)
Async XLA Ops:
  7.2 71.0 %all-gather.3.cloned.1.call-start = ((), (), s32[]{:S(2)}) async-start(), calls=%async_computation | async-start | bytes 3145728 | tf_op jit(solution)/shard_map/all_gather | solution.py:1070
  7.9 114.6 %all-gather.5.cloned.1.call-start = ((), (), s32[]{:S(2)}) async-start(), calls=%async_computation.1 | async-start | bytes 3145728 | tf_op jit(solution)/shard_map/all_gather | solution.py:1071
  243.1 72.3 %copy-start.3 = (f32[64,1280]{1,0:T(8,128)S(1)}, f32[64,1280]{1,0:T(8,128)}, u32[]{:S(2)}) copy-start(f32[64,1280]{1,0:T(8,128)} %get-tuple-element.78) | copy-start | bytes 983044
  243.1 73.2 %copy-start.1 = (bf16[512,1024]{1,0:T(8,128)(2,1)S(1)}, bf16[512,1024]{1,0:T(8,128)(2,1)}, u32[]{:S(2)}) copy-start(bf16[512,1024]{1,0:T(8,128)(2,1)} %get-tuple-element.99) | copy-start | bytes 3145732
  308.3 9.0 %copy-start = (f32[512,1024]{1,0:T(8,128)S(1)}, f32[512,1024]{1,0:T(8,128)}, u32[]{:S(2)}) copy-start(f32[512,1024]{1,0:T(8,128)} %get-tuple-element.100) | copy-start | bytes 6291460
  316.3 2.3 copy-start.4
  316.3 3.0 copy-start.2
Sparse Core Ops, SparseCore 0:
  9.6 13.2 all-gather.2
  24.4 11.7 all-gather.4

commit v11 on v10

--- a/solution.py
+++ b/solution.py
@@ -280,7 +280,7 @@
 
         bwd_tile(p, pairs, i, i == tiles - 1, p == pairs - 1, *ins[:7], normed_s, w_s, *mid, *accs)
 
-    beside(comm.events(), G, steps, now, compute, early=[lambda: [c().start() for c in loads]])
+    beside(comm.events(), G, steps, now, compute, early=[lambda: [c().start() for c in loads]], pace=0.36)
 
 
 def shard_shapes(parts, wide):

time: 328 us -> 328 us (level)
  no operation moved by 1% of the time
where the time goes in v11:
time: 328 us; the launch traced here: 327 us
  Pallas kernels  298 us (91%)
  between operations  14.1 us (4%)
  local copies, waits for them, and re-layouts  12.2 us (4%)
    pallas_call x1, Pallas kernels, bias_and_gather(): pl.pallas_call(functools.partial(bias_gather_kernel, heads, rows, n, G, h...  67.5 us
    pallas_call x1, Pallas kernels, hist_and_scatter(): pl.pallas_call(functools.partial(hist_kernel, heads, rows, n, G, halves,...  66.6 us
    pallas_call x1, Pallas kernels, middle(): pl.pallas_call(functools.partial(mid_kernel, G, cut), out_shape=(sds((d,...  63.9 us
    pallas_call x1, Pallas kernels, attn_bwd_and_scatter(): pl.pallas_call(functools.partial(bwd_kernel, pairs, tiles, G, halves, cou...  55.8 us
    pallas_call x1, Pallas kernels, attn_fwd_and_gather(): pl.pallas_call(functools.partial(fwd_kernel, pairs, tiles, G, halves, cou...  44.3 us
  transfers between devices with their start and end apart: 2, of which 0 were waited for; matrix products, arithmetic and copies ran while one was open for 1% of the time, Pallas kernels for 34%

profile of v11, /device:TPU:0, one launch (start us, length us, event | category | flops | bytes accessed | tf_op | source)
XLA Modules:
  0.0 327.4 jit_solution(17711333590324873397)
XLA Ops:
  7.2 0.0 all-gather.3.cloned.1.call-start
  7.2 0.7 all-gather.3.cloned.1.call-update
  7.9 0.0 all-gather.5.cloned.1.call-start
  8.0 0.7 all-gather.5.cloned.1.call-update
  8.7 0.7 stack.9
  9.3 0.7 stack.10
  10.0 67.5 %layout_bias_gather.1 = (f32[8,1024,1024]{2,1,0:T(8,128)}, f32[2,1024,1024]{2,1,0:T(8,128)}, f32[8,64,128]{2,1,0:T(8,128)}, bf16[1024,1536]{1,0:T(8,128)(2,1)}, ...) custom-call(bf16[16,96]{1,0:T(8,128)(2,1)} %bitcast.17, s32[2,1024]{1,0:T(2,128)} %refs_1_.1, s32[1,1024]{1,0:T(1,128)} %bitcast.18, ...), custom_call_target="tpu_custom_call" | custom-call | tf_op jit(solution)/shard_map/layout_bias_gather/pallas_call | solution.py:100
  77.6 0.6 pad_maximum_fusion.1.refs_1_.gain_ref.refs_8_
  78.2 44.3 %attention_gather.1 = (bf16[1024,512]{1,0:T(8,128)(2,1)}, f32[4,1024,2]{2,1,0:T(8,128)}, bf16[1024,1024]{1,0:T(8,128)(2,1)}, bf16[1024,1536]{1,0:T(8,128)(2,1)},...) custom-call(bf16[1024,1024]{1,0:T(8,128)(2,1)} %all-gather.3.cloned.1.call-done.refs_0_.tok_h, ...), custom_call_target="tpu_custom_call" | custom-call | tf_op jit(solution)/shard_map/attention_gather/pallas_call | solution.py:187
  122.4 0.0 all-gather.5.cloned.1.call-done.cot_h
  122.5 63.9 %feed_forward.1 = (bf16[1024,512]{1,0:T(8,128)(2,1)}, bf16[1024,1408]{1,0:T(8,128)(2,1)}, bf16[1024,1408]{1,0:T(8,128)(2,1)}, bf16[1024,1408]{1,0:T(8,128)(2,1)}...) custom-call(bf16[1024,512]{1,0:T(8,128)(2,1)} %get-tuple-element.48., ...), custom_call_target="tpu_custom_call" | custom-call | tf_op jit(solution)/shard_map/feed_forward/pallas_call | solution.py:1052
  186.4 55.8 %attention_back_scatter.1 = (bf16[8,1024,1024]{2,1,0:T(8,128)(2,1)}, f32[8,256,512]{2,1,0:T(8,128)}, f32[8,2,16,128]{3,2,1,0:T(8,128)}, bf16[1024,1536]{1,0:T(8,...) custom-call(bf16[1024,1536]{1,0:T(8,128)(2,1)} %get-tuple-element.54, ...), custom_call_target="tpu_custom_call" | custom-call | tf_op jit(solution)/shard_map/attention_back_scatter/pallas_call | solution.py:297
  242.2 0.0 copy-start.3
  242.2 0.0 copy-start.1
  242.2 66.6 %table_grad_scatter.1 = (f32[32,128]{1,0:T(8,128)}, f32[512,1024]{1,0:T(8,128)}, f32[64,1408]{1,0:T(8,128)}, f32[64,1536]{1,0:T(8,128)}) custom-call(bf16[8,1024,1024]{2,1,0:T(8,128)(2,1)} %get-tuple-element.62.refs_0_, f32[2,1024,1024]{2,1,0:T(8,128)} %get-tuple-element.63.refs_1_, f32[8,256,512]{2,1,0:T(8,128)} %get-tuple-element.64.refs_2_, ...), custom_call_target="tpu_custom_call" | custom-call | tf_op jit(solution)/shard_map/table_grad_scatter/pallas_call | solution.py:459
  308.8 0.0 copy-start
  308.8 1.4 slice_bitcast_fusion
  310.3 1.3 slice_bitcast_fusion.1
  311.6 0.8 slice.23
  312.3 0.8 slice.22
  313.2 1.0 slice.21
  314.1 1.8 fusion
  315.9 0.0 copy-done.3
  315.9 0.9 pad_maximum_fusion
  316.8 0.0 copy-done.1
  316.8 1.0 copy.30
  317.8 0.0 copy-done
  317.8 1.3 copy.31
  319.1 0.0 copy-done.4
  319.1 0.7 copy.32
  319.8 0.0 copy-done.2
  319.8 0.7 copy.33
  (3 shorter events, 0.0 us)
Async XLA Ops:
  7.2 71.0 %all-gather.3.cloned.1.call-start = ((), (), s32[]{:S(2)}) async-start(), calls=%async_computation | async-start | bytes 3145728 | tf_op jit(solution)/shard_map/all_gather | solution.py:1070
  7.9 114.6 %all-gather.5.cloned.1.call-start = ((), (), s32[]{:S(2)}) async-start(), calls=%async_computation.1 | async-start | bytes 3145728 | tf_op jit(solution)/shard_map/all_gather | solution.py:1071
  242.2 73.7 %copy-start.3 = (f32[64,1280]{1,0:T(8,128)S(1)}, f32[64,1280]{1,0:T(8,128)}, u32[]{:S(2)}) copy-start(f32[64,1280]{1,0:T(8,128)} %get-tuple-element.78) | copy-start | bytes 983044
  242.2 74.6 %copy-start.1 = (bf16[512,1024]{1,0:T(8,128)(2,1)S(1)}, bf16[512,1024]{1,0:T(8,128)(2,1)}, u32[]{:S(2)}) copy-start(bf16[512,1024]{1,0:T(8,128)(2,1)} %get-tuple-element.99) | copy-start | bytes 3145732
  308.8 9.0 %copy-start = (f32[512,1024]{1,0:T(8,128)S(1)}, f32[512,1024]{1,0:T(8,128)}, u32[]{:S(2)}) copy-start(f32[512,1024]{1,0:T(8,128)} %get-tuple-element.100) | copy-start | bytes 6291460
  316.8 2.3 copy-start.4
  316.8 3.0 copy-start.2
Sparse Core Ops, SparseCore 0:
  9.6 13.2 all-gather.2
  24.4 11.7 all-gather.4
